TPU v7x, 32 devices: a whole 2x2x4 slice. The times are simulated.
32 devices in a mesh: rows: 8 (over z, y), group: 4 (over x, core).
Axes of the slice: x: 2, y: 2, z: 4, core: 2. Of those that a mesh axis runs over, the one named last changes fastest.
Arguments:
- inputs: bfloat16 [32, 2048, 768], P('rows', 'group'), may hold values from -6 to 6
- lengths: int32 [32, 4], P('rows'), may hold values from 1 to 1024, 2048 in all within a row
- params: float32 [6, 768], replicated
- first_moment: float32 [6, 768], replicated, may hold values from -0.0234375 to 0.0234375
- second_moment: float32 [6, 768], replicated, may hold values from 1.08506946e-07 to 8.6805557e-07
- cotangent: bfloat16 [32, 1024, 768], P('rows', 'group')
Outputs:
- output: bfloat16 [32, 1024, 768], P('rows', 'group')
- grad_inputs: bfloat16 [32, 2048, 768], P('rows', 'group')
- grad_norm: float32 [], replicated
- new_params: float32 [6, 768], replicated
- new_first: float32 [6, 768], replicated
- new_second: float32 [6, 768], replicated
Inputs may be any that keep to these rules, and one draw needn't show every extreme that they name: Each row's 4 lengths sum to 2048.
All inputs are finite; a program needn't handle non-finite values.
Results may differ from a plain program's by a relative error of at most 0.0005.
Values may be sent and summed in bfloat16 or wider, within the bound.
No kernel may reach another device: no remote copies, remote signals or barrier semaphores. Data moves between devices by JAX's collectives and lax.ppermute only.
A program may use at most 256 MiB of HBM per device.

v0:
```python
import jax
import jax.numpy as jnp
from jax import lax
from jax.sharding import PartitionSpec as P

STEP = 10


beta_one = 0.9
beta_two = 0.999
learn_rate = 0.2
decay_rate = 0.01
adam_eps = 1e-08
clip_limit = 1.0


def passed_along(value, axis, steps):
    count = lax.axis_size(axis)
    initial, last = (max(0, -steps), min(count, count - steps))
    return lax.ppermute(value, axis, [(source, source + steps) for source in range(initial, last)])


def offsets(row_lengths, positions):
    seg_ends = jnp.cumsum(row_lengths)
    seg_starts = seg_ends - row_lengths
    inside = (positions[:, None] >= seg_starts[None, :]) & (positions[:, None] < seg_ends[None, :])
    chosen_start = jnp.sum(jnp.where(inside, seg_starts[None, :], 0), axis=1)
    chosen_end = jnp.sum(jnp.where(inside, seg_ends[None, :], 0), axis=1)
    return (positions - chosen_start, chosen_end - positions)


def mix_window(padded, off_ext, rem_ext, weights):
    span = padded.shape[0] - 9
    conv_rows = span + 6
    off_conv = off_ext[3 : 3 + conv_rows]
    conv_out = jnp.zeros((conv_rows, padded.shape[1]), padded.dtype) + weights[4]
    for k in range(4):
        keep_mask = (off_conv >= k).astype(padded.dtype)[:, None]
        conv_out = conv_out + keep_mask * weights[k] * padded[3 - k : 3 - k + conv_rows]
    off_own = off_ext[6 : 6 + span]
    rem_own = rem_ext[6 : 6 + span]
    pooled = []
    for block_size in range(1, 5):
        within = off_own % block_size
        upper = jnp.minimum(block_size - within, rem_own)
        count = jnp.maximum(within + upper, 1)
        running = jnp.zeros((span, padded.shape[1]), padded.dtype)
        for j in range(1 - block_size, block_size):
            keep_mask = ((j >= -within) & (j < upper)).astype(padded.dtype)[:, None]
            running = running + keep_mask * conv_out[3 + j : 3 + j + span]
        pooled.append(running / count.astype(padded.dtype)[:, None])
    stacked = jnp.stack(pooled)
    logits = jnp.sum(stacked * weights[5], axis=2)
    largest = jnp.max(logits, axis=0, keepdims=True)
    shares = jnp.exp(logits - largest)
    shares = shares / jnp.sum(shares, axis=0, keepdims=True)
    mixed = jnp.sum(shares[:, :, None] * stacked, axis=0)
    return jnp.mean(mixed.reshape(span // 2, 2, padded.shape[1]), axis=1)


def window_info(lengths, first_position, window_rows):
    positions = lax.iota(jnp.int32, window_rows) + first_position
    return jax.vmap(lambda row_lengths: offsets(row_lengths, positions))(lengths)


def apply_rows(values, info, weights):
    return jax.vmap(
        lambda row_values, row_off, row_rem: mix_window(row_values, row_off, row_rem, weights)
    )(values, info[0], info[1])


def adam_update(grads, weights, first_old, second_old):
    first_new = beta_one * first_old + (1.0 - beta_one) * grads
    second_new = beta_two * second_old + (1.0 - beta_two) * grads * grads
    first_hat = first_new / (1.0 - beta_one**STEP)
    second_hat = second_new / (1.0 - beta_two**STEP)
    updated = weights - learn_rate * (
        first_hat / (jnp.sqrt(second_hat) + adam_eps) + decay_rate * weights
    )
    return (updated, first_new, second_new)


def per_device(inputs, lengths, params, first_moment, second_moment, cotangent):
    rows_here, length_here, features = inputs.shape
    cot_rows = cotangent.shape[1]
    before_rows, after_rows, cot_before, cot_after = (6, 3, 0, 0)
    send_up = jnp.concatenate(
        [inputs[:, length_here - before_rows :], cotangent[:, cot_rows - cot_before :]], axis=1
    )
    from_below = passed_along(send_up, "group", 1)
    send_down = jnp.concatenate([inputs[:, :after_rows], cotangent[:, :cot_after]], axis=1)
    from_above = passed_along(send_down, "group", -1)
    group_start = lax.axis_index("group") * length_here
    padded = jnp.concatenate([from_below, inputs, from_above], axis=1).astype(jnp.float32)
    main_info = window_info(lengths, group_start - 6, length_here + 9)

    def forward(values, weights):
        return apply_rows(values, main_info, weights)

    output, pullback = jax.vjp(forward, padded, params)
    grad_padded, grad_local = pullback(cotangent.astype(jnp.float32))
    grad_values = grad_padded[:, 6 : 6 + length_here]
    returned_low = passed_along(grad_padded[:, :6].astype(jnp.bfloat16), "group", -1).astype(
        jnp.float32
    )
    returned_high = passed_along(
        grad_padded[:, 6 + length_here :].astype(jnp.bfloat16), "group", 1
    ).astype(jnp.float32)
    grad_values = grad_values + jnp.concatenate(
        [jnp.zeros((rows_here, length_here - 6, features), jnp.float32), returned_low], axis=1
    )
    grad_values = grad_values + jnp.concatenate(
        [returned_high, jnp.zeros((rows_here, length_here - 3, features), jnp.float32)], axis=1
    )
    grad_params = lax.psum(grad_local, ("rows", "group"))
    grad_norm = jnp.sqrt(jnp.sum(grad_params * grad_params))
    clip_scale = jnp.minimum(1.0, clip_limit / (grad_norm + 1e-06))
    new_params, new_first, new_second = adam_update(
        grad_params * clip_scale, params, first_moment, second_moment
    )
    return (
        output.astype(jnp.bfloat16),
        grad_values.astype(jnp.bfloat16),
        grad_norm,
        new_params,
        new_first,
        new_second,
    )


def solution(mesh):
    in_specs = (P("rows", "group", None), P("rows", None), P(), P(), P(), P("rows", "group", None))
    out_specs = (P("rows", "group", None), P("rows", "group", None), P(), P(), P(), P())
    return jax.shard_map(
        per_device, mesh=mesh, in_specs=in_specs, out_specs=out_specs, check_vma=False
    )
```

profile of v0, /device:TPU:0, one launch (start us, length us, event | category | flops | bytes accessed | tf_op | source)
XLA Modules:
  0.0 249.5 jit_solution(8609651600042316704)
XLA Ops:
  0.6 0.8 slice.91
  1.4 1.3 collective-permute-start.1
  2.7 0.8 slice.90
  3.6 3.0 %collective-permute-start = (bf16[4,6,768]{2,1,0:T(8,128)(2,1)S(1)}, bf16[4,6,768]{2,1,0:T(8,128)(2,1)S(1)}, u32[]{:S(2)}, u32[]{:S(2)}) collective-permute-start(bf16[4,6,768]{2,1,0:T(8,128)(2,1)S(1)} %slice.90), channel_id=1, source_target_pairs={{0,1},{1,2},{2,3},{4,5},{5,6},{6,7},{8,9},{9,10},{10,11},{12,13},{... | collective-permute-start | bytes 110600 | tf_op jit(solution)/shard_map/ppermute | solution.py:20
  6.6 0.9 reduce_window_sum.11
  7.5 0.7 sub.50
  8.2 0.1 slice.112
  8.2 0.1 select_reduce_fusion.1
  8.4 0.1 compare_convert_fusion.3
  8.5 0.1 compare_convert_fusion.4
  8.5 0.1 and_convert_fusion.14
  8.6 0.1 maximum_convert_fusion.3
  8.7 0.1 and_convert_fusion.13
  8.9 1.7 convert_multiply_fusion
  10.6 1.0 slice_reduce_fusion.5
  11.6 4.7 %broadcast_in_dim.41 = f32[4,256,2,768]{3,2,1,0:T(2,128)} broadcast(f32[4,256,768]{2,1,0:T(8,128)S(1)} %convert_multiply_fusion), dimensions={0,1,3} | broadcast | bytes 9437184 | tf_op jit(solution)/shard_map/transpose(jvp(vmap()))/broadcast_in_dim | solution.py:58
  16.2 0.0 copy-start.4
  16.2 8.7 %reshape.120 = f32[4,512,768]{2,1,0:T(8,128)} reshape(f32[4,256,2,768]{3,2,1,0:T(2,128)} %broadcast_in_dim.41) | data formatting | bytes 12582912 | tf_op jit(solution)/shard_map/transpose(jvp(vmap()))/reshape | solution.py:58
  24.9 0.0 collective-permute-done.1
  24.9 0.0 collective-permute-done
  24.9 0.0 copy-done.4
  24.9 0.7 maximum_convert_fusion
  25.6 0.0 copy-start
  25.6 4.8 %fusion.3 = f32[4,518,768]{2,1,0:T(8,128)S(1)} fusion(f32[4,521,768]{2,1,0:T(8,128)S(1)} %maximum_convert_fusion, f32[768]{0:T(1024)S(1)} %get-tuple-element.16, f32[4,518]{1,0:T(4,128)S(1)} %get-tuple-element.86, f32[768]{0:T(1024)S(1)} %get-tuple-element.17, f32[4,518]{1,0:T(4,128)S(1)} %get-tuple-element.85, f32[768]{0:T(1024)S(1)} %get-tuple-element.18, ...), kind=kLoop, calls=%fused_computation.18 | loop fusion | flops 19095552 | bytes 31874432 | tf_op jit(solution)/shard_map/jvp(vmap())/add | solution.py:39
  30.5 0.0 copy-done
  30.5 6.4 %divide_bitcast_fusion.1 = (f32[1,4,512,768]{3,2,1,0:T(8,128)S(1)}, f32[1,4,512,768]{3,2,1,0:T(8,128)S(1)}) fusion(f32[4,518,768]{2,1,0:T(8,128)S(1)} %fusion.3, f32[4,512]{1,0:T(4,128)S(1)} %get-tuple-element.75, f32[4,512]{1,0:T(4,128)S(1)} %get-tuple-element.72, f32[4,512]{1,0:T(4,128)S(1)} %get-tuple-element.66, f32[4,512]{1,0:T(4,128)S(1)} %get-tuple-element.35, ...), kind=kLoop, calls=%fused_computation.48 | loop fusion | flops 25165824 | bytes 44122112 | tf_op jit(solution)/shard_map/jvp(vmap())/stack | solution.py:52
  36.9 0.0 copy-start.1
  36.9 0.0 copy-start.2
  36.9 8.8 %divide_bitcast_fusion.2 = (f32[1,4,512,768]{3,2,1,0:T(8,128)S(1)}, f32[1,4,512,768]{3,2,1,0:T(8,128)}) fusion(f32[4,518,768]{2,1,0:T(8,128)S(1)} %fusion.3, f32[4,512]{1,0:T(4,128)S(1)} %get-tuple-element.87, f32[4,512]{1,0:T(4,128)S(1)} %get-tuple-element.33, f32[4,512]{1,0:T(4,128)S(1)} %get-tuple-element.76, f32[4,512]{1,0:T(4,128)S(1)} %get-tuple-element.71, ...), kind=kLoop, calls=%fused_computation.49 | loop fusion | flops 25165824 | bytes 56705024 | tf_op jit(solution)/shard_map/jvp(vmap())/stack | solution.py:52
  45.7 0.0 copy-start.3
  45.7 0.0 copy-done.1
  45.7 0.0 copy-done.2
  45.7 17.0 %multiply_reduce_fusion.1 = (f32[4,4,512]{2,0,1:T(4,128)S(1)}, f32[4,4,512]{2,0,1:T(4,128)S(1)}) fusion(f32[4,512,768]{2,1,0:T(8,128)} %reshape.120, f32[1,4,512,768]{3,2,1,0:T(8,128)} %get-tuple-element.61, f32[1,4,512,768]{3,2,1,0:T(8,128)S(1)} %get-tuple-element.63, f32[1,4,512,768]{3,2,1,0:T(8,128)S(1)} %get-tuple-element.62, ...), kind=kLoop, calls=%fused_computation.3 | loop fusion | flops 44023808 | bytes 31525888 | tf_op jit(solution)/shard_map/transpose(jvp(vmap()))/reduce_sum | solution.py:57
  62.7 0.0 copy-done.3
  62.9 14.1 %multiply_reduce_fusion = (f32[768]{0:T(1024)S(1)}, f32[4,512,768]{2,1,0:T(8,128)}) fusion(f32[4,4,512]{2,0,1:T(4,128)S(1)} %select_add_fusion, f32[1,4,512,768]{3,2,1,0:T(8,128)} %get-tuple-element.61, f32[1,4,512,768]{3,2,1,0:T(8,128)} %copy-done.2, f32[1,4,512,768]{3,2,1,0:T(8,128)} %copy-done.1, f32[1,4,512,768]{3,2,1,0:T(8,128)} %copy-done.3, ...), kind=kLoop, calls=%fused_computation.1 | loop fusion | flops 42466560 | bytes 31525888 | tf_op jit(solution)/shard_map/transpose(jvp(vmap()))/reduce_sum | solution.py:53
  77.1 11.4 %multiply_add_fusion = f32[4,4,512,768]{3,2,0,1:T(8,128)} fusion(f32[4,4,512]{2,0,1:T(4,128)S(1)} %copy.31, f32[4,512,768]{2,1,0:T(8,128)} %reshape.120, f32[4,4,512]{2,0,1:T(4,128)S(1)} %copy.30, f32[768]{0:T(1024)S(1)} %get-tuple-element.20), kind=kLoop, calls=%fused_computation.2 | loop fusion | flops 18874368 | bytes 31525888 | tf_op jit(solution)/shard_map/transpose(jvp(vmap()))/add_any | solution.py:53
  88.5 0.0 slice-start
  88.5 20.8 %broadcast_multiply_fusion.7 = (f32[4,512,768]{2,1,0:T(8,128)}, f32[4,512,768]{2,1,0:T(8,128)}, f32[4,512,768]{2,1,0:T(8,128)}, f32[4,512,768]{2,1,0:T(8,128)}, ...) fusion(f32[4,512]{1,0:T(4,128)S(1)} %get-tuple-element.80, ...), kind=kLoop, calls=%fused_computation.61 | loop fusion | flops 15728640 | bytes 62996480 | tf_op jit(solution)/shard_map/transpose(jvp(vmap()))/mul | solution.py:50
  109.2 0.0 slice-start.1
  109.2 20.6 %broadcast_multiply_fusion = (f32[4,512,768]{2,1,0:T(8,128)}, f32[4,512,768]{2,1,0:T(8,128)}, f32[4,512,768]{2,1,0:T(8,128)}, f32[4,512,768]{2,1,0:T(8,128)}, f3...) fusion(f32[4,512]{1,0:T(4,128)S(1)} %get-tuple-element.71, ...), kind=kLoop, calls=%fused_computation.54 | loop fusion | flops 15728640 | bytes 62996480 | tf_op jit(solution)/shard_map/transpose(jvp(vmap()))/mul | solution.py:50
  129.8 0.0 slice-done
  129.8 0.0 slice-done.1
  129.8 36.3 %multiply_reduce_fusion.7 = (f32[768]{0:T(1024)S(1)}, f32[768]{0:T(1024)S(1)}, f32[768]{0:T(1024)S(1)}, f32[768]{0:T(1024)S(1)}, f32[768]{0:T(1024)S(1)}, /*index=5*/f32[4,518,768]{2,1,0:T(8,128)}) fusion(f32[4,521,768]{2,1,0:T(8,128)S(1)} %bitcast.77, f32[4,518]{1,0:T(4,128)S(1)} %get-tuple-element.86, f32[4,518]{1,0:T(4,128)S(1)} %get-tuple-element.83, ...), kind=kLoop, calls=%fused_computation.22 | loop fusion | flops 44552448 | bytes 132537728 | tf_op jit(solution)/shard_map/transpose(jvp(vmap()))/reduce_sum | solution.py:39
  166.1 7.7 %multiply_multiply_fusion = (f32[4,518,768]{2,1,0:T(8,128)S(1)}, f32[4,518,768]{2,1,0:T(8,128)S(1)}, f32[4,518,768]{2,1,0:T(8,128)S(1)}, f32[4,518,768]{2,1,0:T(8,128)}) fusion(f32[4,518,768]{2,1,0:T(8,128)} %get-tuple-element.26, f32[768]{0:T(1024)S(1)} %get-tuple-element.16, f32[4,518]{1,0:T(4,128)S(1)} %get-tuple-element.86, ...), kind=kLoop, calls=%fused_computation.6 | loop fusion | flops 12730368 | bytes 31871360 | tf_op jit(solution)/shard_map/transpose(jvp(vmap()))/mul | solution.py:39
  173.8 6.8 %fusion.23 = (bf16[4,521,768]{2,1,0:T(8,128)(2,1)}, f32[4,521,768]{2,1,0:T(8,128)}) fusion(f32[4,518,768]{2,1,0:T(8,128)S(1)} %get-tuple-element.57, f32[4,518,768]{2,1,0:T(8,128)S(1)} %get-tuple-element.58, f32[4,518,768]{2,1,0:T(8,128)} %get-tuple-element.59, f32[4,518,768]{2,1,0:T(8,128)S(1)} %get-tuple-element.56), kind=kLoop, calls=%fused_computation.131 | loop fusion | flops 6402048 | bytes 35063808 | tf_op jit(solution)/shard_map/convert.5
  180.6 0.9 slice.128
  181.5 0.8 slice.127
  182.3 0.0 copy-start.5
  182.3 0.0 copy-start.6
  182.3 0.0 copy-start.7
  182.3 8.7 %bitcast_reduce_fusion = f32[4,256,768]{2,0,1:T(4,128)S(1)} fusion(f32[4,512,768]{2,1,0:T(8,128)} %get-tuple-element.7), kind=kLoop, calls=%fused_computation.46 | loop fusion | flops 786432 | bytes 9437184 | tf_op jit(solution)/shard_map/jvp(vmap())/reduce_sum | solution.py:58
  191.0 1.7 fusion.19
  192.8 42.2 %psum.7 = f32[6,768]{1,0:T(8,128)S(1)} all-reduce(f32[6,768]{1,0:T(8,128)S(1)} %pad_add_fusion.2), channel_id=1, replica_groups=mesh['rows'=8,'group'=4] {'rows','group'}, use_global_device_ids=true, to_apply=%region_18.19 | all-reduce | flops 4608 | bytes 36864 | tf_op jit(solution)/shard_map/psum | solution.py:115
  235.0 0.6 multiply_reduce_fusion.9
  236.3 1.3 collective-permute-start.3
  237.6 1.3 collective-permute-start.2
  238.9 0.0 copy-done.5
  238.9 0.0 copy-done.6
  238.9 0.0 copy-done.7
  239.0 0.6 multiply_subtract_fusion
  239.6 0.0 collective-permute-done.3
  239.6 3.7 %collective-permute-done.2 = bf16[4,6,768]{2,1,0:T(8,128)(2,1)S(1)} collective-permute-done((bf16[4,6,768]{2,1,0:T(8,128)(2,1)S(1)}, bf16[4,6,768]{2,1,0:T(8,128)(2,1)S(1)}, u32[]{:S(2)}, u32[]{:S(2)}) %collective-permute-start.2) | collective-permute-done | bytes 36896 | tf_op jit(solution)/shard_map/ppermute | solution.py:20
  243.3 5.1 %fusion.5 = bf16[4,512,768]{2,1,0:T(8,128)(2,1)} fusion(f32[4,521,768]{2,1,0:T(8,128)} %get-tuple-element.28, bf16[4,3,768]{2,1,0:T(4,128)(2,1)S(1)} %collective-permute-done.3, bf16[4,6,768]{2,1,0:T(8,128)(2,1)S(1)} %collective-permute-done.2), kind=kLoop, calls=%fused_computation.26 | loop fusion | flops 7864320 | bytes 9492480 | tf_op jit(solution)/shard_map/convert_element_type | solution.py:123
  (20 shorter events, 0.3 us)
Async XLA Ops:
  1.4 23.5 %collective-permute-start.1 = (bf16[4,3,768]{2,1,0:T(4,128)(2,1)S(1)}, bf16[4,3,768]{2,1,0:T(4,128)(2,1)S(1)}, u32[]{:S(2)}, u32[]{:S(2)}) collective-permute-start(bf16[4,3,768]{2,1,0:T(4,128)(2,1)S(1)} %slice.91), channel_id=1, source_target_pairs={{1,0},{2,1},{3,2},{5,4},{6,5},{7,6},{9,8},{10,9},{11,10},{13,12},{... | collective-permute-start | bytes 55304 | tf_op jit(solution)/shard_map/ppermute | solution.py:20
  3.6 21.4 %collective-permute-start = (bf16[4,6,768]{2,1,0:T(8,128)(2,1)S(1)}, bf16[4,6,768]{2,1,0:T(8,128)(2,1)S(1)}, u32[]{:S(2)}, u32[]{:S(2)}) collective-permute-start(bf16[4,6,768]{2,1,0:T(8,128)(2,1)S(1)} %slice.90), channel_id=1, source_target_pairs={{0,1},{1,2},{2,3},{4,5},{5,6},{6,7},{8,9},{9,10},{10,11},{12,13},{... | collective-permute-start | bytes 110600 | tf_op jit(solution)/shard_map/ppermute | solution.py:20
  16.2 8.7 %copy-start.4 = (bf16[4,512,768]{2,1,0:T(8,128)(2,1)S(1)}, bf16[4,512,768]{2,1,0:T(8,128)(2,1)}, u32[]{:S(2)}) copy-start(bf16[4,512,768]{2,1,0:T(8,128)(2,1)} %param.6) | copy-start | bytes 9437188
  25.6 4.9 %copy-start = (f32[4,521,768]{2,1,0:T(8,128)}, f32[4,521,768]{2,1,0:T(8,128)S(1)}, u32[]{:S(2)}) copy-start(f32[4,521,768]{2,1,0:T(8,128)S(1)} %maximum_convert_fusion) | copy-start | bytes 19206148
  36.9 8.8 %copy-start.1 = (f32[1,4,512,768]{3,2,1,0:T(8,128)}, f32[1,4,512,768]{3,2,1,0:T(8,128)S(1)}, u32[]{:S(2)}) copy-start(f32[1,4,512,768]{3,2,1,0:T(8,128)S(1)} %get-tuple-element.62) | copy-start | bytes 18874372
  36.9 8.8 %copy-start.2 = (f32[1,4,512,768]{3,2,1,0:T(8,128)}, f32[1,4,512,768]{3,2,1,0:T(8,128)S(1)}, u32[]{:S(2)}) copy-start(f32[1,4,512,768]{3,2,1,0:T(8,128)S(1)} %get-tuple-element.63) | copy-start | bytes 18874372
  45.7 17.0 %copy-start.3 = (f32[1,4,512,768]{3,2,1,0:T(8,128)}, f32[1,4,512,768]{3,2,1,0:T(8,128)S(1)}, u32[]{:S(2)}) copy-start(f32[1,4,512,768]{3,2,1,0:T(8,128)S(1)} %get-tuple-element.60) | copy-start | bytes 18874372
  88.5 41.3 %slice-start = ((s8[6488064]{0:T(1024)(128)(4,1)}), s8[4194304]{0:T(1024)(128)(4,1)S(1)}, s32[]{:S(2)}) async-start(s8[6488064]{0:T(1024)(128)(4,1)} %bitcast.76), calls=%async_computation | async-start | bytes 8388608
  109.2 20.6 %slice-start.1 = ((s8[6488064]{0:T(1024)(128)(4,1)}), s8[2293760]{0:T(1024)(128)(4,1)S(1)}, s32[]{:S(2)}) async-start(s8[6488064]{0:T(1024)(128)(4,1)} %bitcast.76), calls=%async_computation.1 | async-start | bytes 4587520
  182.3 56.6 %copy-start.5 = (f32[6,768]{1,0:T(8,128)S(1)}, f32[6,768]{1,0:T(8,128)}, u32[]{:S(2)}) copy-start(f32[6,768]{1,0:T(8,128)} %param.8) | copy-start | bytes 55300
  182.3 56.6 %copy-start.6 = (f32[6,768]{1,0:T(8,128)S(1)}, f32[6,768]{1,0:T(8,128)}, u32[]{:S(2)}) copy-start(f32[6,768]{1,0:T(8,128)} %param.9) | copy-start | bytes 55300
  182.3 56.6 %copy-start.7 = (f32[6,768]{1,0:T(8,128)S(1)}, f32[6,768]{1,0:T(8,128)}, u32[]{:S(2)}) copy-start(f32[6,768]{1,0:T(8,128)} %param.10) | copy-start | bytes 55300
  236.3 3.3 %collective-permute-start.3 = (bf16[4,3,768]{2,1,0:T(4,128)(2,1)S(1)}, bf16[4,3,768]{2,1,0:T(4,128)(2,1)S(1)}, u32[]{:S(2)}, u32[]{:S(2)}) collective-permute-start(bf16[4,3,768]{2,1,0:T(4,128)(2,1)S(1)} %slice.128), channel_id=1, source_target_pairs={{0,1},{1,2},{2,3},{4,5},{5,6},{6,7},{8,9},{9,10},{10,11},{12,13},{... | collective-permute-start | bytes 55304 | tf_op jit(solution)/shard_map/ppermute | solution.py:20
  237.6 5.6 %collective-permute-start.2 = (bf16[4,6,768]{2,1,0:T(8,128)(2,1)S(1)}, bf16[4,6,768]{2,1,0:T(8,128)(2,1)S(1)}, u32[]{:S(2)}, u32[]{:S(2)}) collective-permute-start(bf16[4,6,768]{2,1,0:T(8,128)(2,1)S(1)} %slice.127), channel_id=1, source_target_pairs={{1,0},{2,1},{3,2},{5,4},{6,5},{7,6},{9,8},{10,9},{11,10},{13,12},{... | collective-permute-start | bytes 110600 | tf_op jit(solution)/shard_map/ppermute | solution.py:20
where the time goes:
time: 253 us; the launch traced here: 249 us
  other arithmetic  176 us (70%)
  blocking collectives  42.2 us (17%)
  local copies, waits for them, and re-layouts  17.9 us (7%)
  starting transfers between devices  6.91 us (3%)
  waiting for transfers between devices  3.67 us (1%)
  between operations  2.8 us (1%)
    psum x1, blocking collectives, per_device(): grad_params = lax.psum(grad_local, ('rows', 'group'))  42.2 us
    mul x2, other arithmetic, mix_window(): running = running + keep_mask * conv_out[3 + j:3 + j + span]  41.3 us
    reduce_sum x1, other arithmetic, mix_window(): keep_mask * weights[k] * padded[3 - k:3 - k + conv_rows]  36.3 us
    reduce_sum x1, other arithmetic, mix_window(): mixed = jnp.sum(shares[:, :, None] * stacked, axis=0)  17 us
    another operation x2, other arithmetic, mix_window(): stacked = jnp.stack(pooled)  15.2 us
    reduce_sum x1, other arithmetic, mix_window(): logits = jnp.sum(stacked * weights[5], axis=2)  14.1 us
    add_any x1, other arithmetic, mix_window(): logits = jnp.sum(stacked * weights[5], axis=2)  11.4 us
    reduce_sum x1, other arithmetic, mix_window(): return jnp.mean(mixed.reshape(span // 2, 2, padded.shape[1]), axis=1)  8.7 us
  transfers between devices with their start and end apart: 4, of which 1 were waited for; matrix products, arithmetic and copies ran while one was open for 8% of the time, Pallas kernels for 0%

commit v1 on v0

v1 whole, which is shorter than its diff:
```python
import functools

import jax
import jax.numpy as jnp
from jax import lax
from jax.experimental import pallas as pl
from jax.experimental.pallas import tpu as pltpu
from jax.sharding import PartitionSpec as P

STEP = 10


beta_one = 0.9
beta_two = 0.999
learn_rate = 0.2
decay_rate = 0.01
adam_eps = 1e-08
clip_limit = 1.0

TAPS = 4
SLOTS = 64
OWN = 56
LEAD = 4
WINDOW = 128
PAD = 16
F32 = jnp.float32
BF16 = jnp.bfloat16


def passed_along(value, axis, steps):
    count = lax.axis_size(axis)
    initial, last = (max(0, -steps), min(count, count - steps))
    return lax.ppermute(value, axis, [(source, source + steps) for source in range(initial, last)])


def rotate_rows(x, amount):
    for bit in (1, 2, 4):
        x = jnp.where((amount & bit) != 0, pltpu.roll(x, 8 - bit, x.ndim - 2), x)
    return x


def split(x):
    high = x.astype(BF16)
    return high, (x - high.astype(F32)).astype(BF16)


def kernel(
    shapes,
    base_ref,
    len_ref,
    x_hbm,
    g_ref,
    up_ref,
    down_ref,
    par_ref,
    out_ref,
    gin_hbm,
    grad_ref,
    xbuf,
    g32,
    gws,
    comp,
    gcs,
    cs,
    es,
    out32,
    ginbuf,
    carry_p,
    carry_o,
    acc,
    sems,
):
    rows, length, half, features, tiles = shapes
    count = rows * tiles
    pairs = count // 2
    chunks = features // 128
    base = base_ref[0]

    def iota(shape, dim):
        return lax.broadcasted_iota(jnp.int32, shape, dim)

    sub8 = iota((8, 128), 0)
    lane8 = iota((8, 128), 1)
    slot8 = lane8 % SLOTS
    first = [2 * slot8 - 3 - (2 * p + lane8 // SLOTS) for p in range(2)]
    group_of = [(f + ((sub8 - f) & 7)) >> 3 for f in first]
    turn = [f & 7 for f in first]
    first_e = 2 * slot8 - 3
    group_of_e = (first_e + ((sub8 - first_e) & 7)) >> 3
    turn_e = first_e & 7

    copy_x = pltpu.make_async_copy(x_hbm, xbuf.at[:, pl.ds(PAD, length), :], sems.at[0])
    copy_x.start()
    subd = iota((8, features), 0)
    for r in range(rows):
        xbuf[r, 0:PAD, :] = up_ref[r]
        xbuf[r, PAD + length : 2 * PAD + length, :] = down_ref[r]
        rest = xbuf.shape[1] - 2 * PAD - length
        if rest > 0:
            xbuf[r, 2 * PAD + length :, :] = jnp.zeros((rest, features), BF16)
        g32[r, PAD : PAD + half, :] = g_ref[r].astype(F32)
        head = pltpu.roll(up_ref[r].astype(F32)[0:8], 6, 0)
        g32[r, 8:16, :] = jnp.where(subd >= 6, head, 0.0)
        tail = pltpu.roll(down_ref[r].astype(F32)[8:16], 3, 0)
        g32[r, PAD + half : PAD + half + 8, :] = jnp.where(subd < 3, tail, 0.0)
        g32[r, PAD + half + 8 :, :] = jnp.zeros((g32.shape[1] - PAD - half - 8, features), F32)
    acc[...] = jnp.zeros_like(acc)
    copy_x.wait()

    def window(r, m):
        return xbuf[r, pl.ds(pl.multiple_of(2 * OWN * m, 16), WINDOW), :]

    def place(tile):
        return tile // tiles, tile % tiles

    def products(pair, _):
        bias_sums = []
        for side in range(2):
            tile = 2 * pair + side
            r, m = place(tile)
            start = pl.multiple_of(OWN * m + 8, 8)
            bias_sum = jnp.zeros((SLOTS, 128), F32)
            for c in range(chunks):
                lanes = slice(128 * c, 128 * c + 128)
                g = g32[r, pl.ds(start, SLOTS), lanes]
                scorer = jnp.broadcast_to(par_ref[5:6, lanes], (8, 128))
                g = jnp.concatenate([jnp.where(sub8 < 2, scorer, g[0:8]), g[8:]], axis=0)
                bias_sum = bias_sum + g * par_ref[4:5, lanes]
                for k in range(TAPS):
                    high, low = split(g * par_ref[k : k + 1, lanes])
                    gws[tile, SLOTS * k : SLOTS * (k + 1), lanes] = high
                    gws[tile, SLOTS * k : SLOTS * (k + 1), features + 128 * c : features + 128 * c + 128] = low
            bias_sums.append(
                jnp.broadcast_to(jnp.sum(bias_sum, axis=1, keepdims=True), (SLOTS, 128))
            )
            x = window(r, m)
            product = lax.dot_general(
                jnp.concatenate([x, x], axis=1),
                gws[tile],
                (((1,), (1,)), ((), ())),
                preferred_element_type=F32,
            )
            for p in range(2):
                banded = jnp.zeros((8, 128), F32)
                scored = jnp.zeros((8, 128), F32)
                for v in range(WINDOW // 8):
                    part = product[8 * v : 8 * v + 8, 128 * p : 128 * p + 128]
                    score = jnp.where(
                        lane8 < SLOTS,
                        jnp.broadcast_to(part[:, 0:1], (8, 128)),
                        jnp.broadcast_to(part[:, SLOTS : SLOTS + 1], (8, 128)),
                    )
                    here = group_of[p] == v
                    banded = jnp.where(here, part, banded)
                    scored = jnp.where(here, score, scored)
                comp[p, tile] = banded
                comp[2 + p, tile] = scored
        gcs[pair] = jnp.concatenate(bias_sums, axis=0).T[0:8]
        return 0

    lax.fori_loop(0, pairs, products, 0)

    left = lane8 < SLOTS
    starts = []
    for r in range(rows):
        first_end = len_ref[r, 0]
        second_end = first_end + len_ref[r, 1]
        third_end = second_end + len_ref[r, 2]
        starts.append((first_end, second_end, third_end, third_end + len_ref[r, 3]))

    def segment(at, r):
        one, two, three, last = starts[r]
        begin = jnp.where(at >= one, one, 0)
        begin = jnp.where(at >= two, two, begin)
        begin = jnp.where(at >= three, three, begin)
        end = jnp.where(at >= one, two, one)
        end = jnp.where(at >= two, three, end)
        end = jnp.where(at >= three, last, end)
        return begin, end

    def tile_start(m):
        return base + 2 * OWN * m - PAD

    bias_score = jnp.sum(par_ref[4:5, :] * par_ref[5:6, :])
    products_of, scores_of, keeps_of = [], [], []
    for tile in range(count):
        r, m = place(tile)
        at = tile_start(m) + 2 * slot8 + sub8 - 3
        offset = at - segment(at, r)[0]
        keeps = [(offset >= 2 * p + lane8 // SLOTS) & (at >= 0) for p in range(2)]
        keeps_of.append(keeps)
        sums = []
        for which in (0, 2):
            total = jnp.zeros((8, 128), F32)
            for p in range(2):
                total = total + jnp.where(keeps[p], rotate_rows(comp[which + p, tile], turn[p]), 0.0)
            sums.append(total + pltpu.roll(total, SLOTS, 1))
        products_of.append(sums[0])
        scores_of.append(sums[1])

    for pair in range(pairs):
        one, two = 2 * pair, 2 * pair + 1
        delta = sub8 - 3
        dots = jnp.where(left, products_of[one], products_of[two]) + gcs[pair]
        scores = jnp.where(left, scores_of[one], scores_of[two]) + bias_score
        coef = jnp.zeros((8, 128), F32)
        coef_e = jnp.zeros((8, 128), F32)
        for p in range(2):
            at = [tile_start(place(t)[1]) + 2 * slot8 + p for t in (one, two)]
            found = [segment(a, place(t)[0]) for a, t in zip(at, (one, two))]
            at = jnp.where(left, at[0], at[1])
            begin = jnp.where(left, found[0][0], found[1][0])
            end = jnp.where(left, found[0][1], found[1][1])
            offset = jnp.maximum(at - begin, 0)
            remain = end - at
            masks, inverses, logits, grads = [], [], [], []
            for b in range(1, TAPS + 1):
                if b == 3:
                    thirds = ((offset.astype(F32) + 0.5) * (1.0 / 3.0)).astype(jnp.int32)
                    within = offset - 3 * thirds
                else:
                    within = offset & (b - 1)
                upper = jnp.minimum(b - within, remain)
                mask = (delta >= p - within) & (delta < p + upper)
                inverse = 1.0 / jnp.maximum(within + upper, 1).astype(F32)
                masks.append(mask)
                inverses.append(inverse)
                logits.append(jnp.sum(jnp.where(mask, scores, 0.0), axis=0, keepdims=True) * inverse)
                grads.append(
                    jnp.sum(jnp.where(mask, dots, 0.0), axis=0, keepdims=True) * (0.5 * inverse)
                )
            largest = functools.reduce(jnp.maximum, logits)
            powers = [jnp.exp(logit - largest) for logit in logits]
            scale = 1.0 / sum(powers)
            shares = [power * scale for power in powers]
            mean = sum(share * grad for share, grad in zip(shares, grads))
            for mask, inverse, share, grad in zip(masks, inverses, shares, grads):
                coef = coef + jnp.where(mask, (0.5 * share) * inverse, 0.0)
                coef_e = coef_e + jnp.where(mask, share * (grad - mean) * inverse, 0.0)
        owned = (slot8 >= LEAD) & (slot8 < LEAD + OWN)
        coef = jnp.where(owned, coef, 0.0)
        coef_e = jnp.where(owned, coef_e, 0.0)
        es[pair] = rotate_rows(coef_e, (8 - turn_e) & 7)
        swapped = pltpu.roll(coef, SLOTS, 1)
        for side, tile in enumerate((one, two)):
            both = jnp.where(left, coef, swapped) if side == 0 else jnp.where(left, swapped, coef)
            for p in range(2):
                kept = jnp.where(keeps_of[tile][p], both, 0.0)
                cs[p, tile] = rotate_rows(kept, (8 - turn[p]) & 7)

    for r in range(rows):
        g32[r, 8:16, :] = jnp.zeros((8, features), F32)
        g32[r, PAD + half : PAD + half + 8, :] = jnp.zeros((8, features), F32)

    rows_e = iota((SLOTS, 128), 0)

    def apply(pair, _):
        spread = jnp.concatenate(
            [jnp.where(group_of_e == v, es[pair], 0.0) for v in range(WINDOW // 8)], axis=0
        ).T
        for side in range(2):
            tile = 2 * pair + side
            r, m = place(tile)
            from_row = OWN * m - 8
            part = spread[SLOTS * side : SLOTS * side + SLOTS]
            here = (from_row + rows_e >= 0) & (from_row + rows_e < half)
            own_e = jnp.sum(jnp.where(here, part, 0.0), axis=0, keepdims=True)
            far_e = jnp.sum(jnp.where(here, 0.0, part), axis=0, keepdims=True)
            at = tile_start(m) + lane8
            one, two, three = [len_ref[r, i] for i in range(3)]
            two = one + two
            three = two + three
            begin = jnp.where(at >= one, one, 0)
            begin = jnp.where(at >= two, two, begin)
            begin = jnp.where(at >= three, three, begin)
            offset = at - begin
            bands = []
            for p in range(2):
                bands.append(
                    jnp.concatenate(
                        [jnp.where(group_of[p] == v, cs[p, tile], 0.0) for v in range(WINDOW // 8)],
                        axis=0,
                    ).T
                )
            band = []
            for k in range(TAPS):
                kept = (offset >= k) & (at >= 0)
                rows_k = jnp.where(
                    sub8 == 0,
                    jnp.broadcast_to(own_e, (8, 128)),
                    jnp.broadcast_to(far_e, (8, 128)),
                )
                rows_k = jnp.where(kept, rows_k, 0.0)
                if k > 0:
                    rows_k = pltpu.roll(rows_k, 128 - k, 1)
                matrix = bands[k // 2][SLOTS * (k % 2) : SLOTS * (k % 2) + SLOTS]
                band.append(jnp.where(sub8 < 2, rows_k, matrix[0:8]))
                band.append(matrix[8:])
            matrix = jnp.concatenate(band, axis=0)
            total = jnp.sum(matrix[0:SLOTS], axis=1, keepdims=True)
            high, low = split(matrix)
            x = window(r, m)
            mixed = lax.dot_general(
                jnp.concatenate([high, low], axis=1),
                jnp.concatenate([x, x], axis=0),
                (((1,), (0,)), ((), ())),
                preferred_element_type=F32,
            )
            start = pl.multiple_of(OWN * m + 8, 8)
            for c in range(chunks):
                lanes = slice(128 * c, 128 * c + 128)
                g = g32[r, pl.ds(start, SLOTS), lanes]
                scorer = jnp.broadcast_to(par_ref[5:6, lanes], (8, 128))
                g = jnp.concatenate(
                    [jnp.where(sub8 == 0, scorer, jnp.where(sub8 < LEAD, 0.0, g[0:8])), g[8:]], axis=0
                )
                value = total * par_ref[4:5, lanes]
                for k in range(TAPS):
                    taken = mixed[SLOTS * k : SLOTS * (k + 1), lanes]
                    value = value + taken * par_ref[k : k + 1, lanes]
                    acc[k, :, lanes] += jnp.sum((taken * g).reshape(SLOTS // 8, 8, 128), axis=0)
                acc[4, :, lanes] += jnp.sum((total * g).reshape(SLOTS // 8, 8, 128), axis=0)
                acc[5, :, lanes] += jnp.where(sub8 == 0, value[0:8], 0.0)
                before = jnp.where(m > 0, carry_o[:, lanes], 0.0)
                out32[r, pl.ds(start, 8), lanes] = before + jnp.where(sub8 < LEAD, 0.0, value[0:8])
                out32[r, pl.ds(start + 8, OWN - 8), lanes] = value[8:OWN]
                carry_o[:, lanes] = value[OWN:]
            back = lax.dot_general(
                jnp.concatenate([high, high, low], axis=0),
                jnp.concatenate(
                    [gws[tile, :, :features], gws[tile, :, features:], gws[tile, :, :features]], axis=0
                ),
                (((0,), (0,)), ((), ())),
                preferred_element_type=F32,
            )
            to_row = pl.multiple_of(2 * OWN * m, 16)
            before = jnp.where(m > 0, carry_p[...], 0.0)
            ginbuf[r, pl.ds(to_row, 16), :] = (before + back[0:16]).astype(BF16)
            ginbuf[r, pl.ds(to_row + 16, 2 * OWN - 16), :] = back[16 : 2 * OWN].astype(BF16)
            carry_p[...] = back[2 * OWN :]
        return 0

    lax.fori_loop(0, pairs, apply, 0)

    copy_out = pltpu.make_async_copy(ginbuf.at[:, pl.ds(PAD, length), :], gin_hbm, sems.at[0])
    copy_out.start()
    for r in range(rows):
        out_ref[r] = out32[r, PAD : PAD + half, :].astype(BF16)
    for k in range(TAPS + 2):
        grad_ref[k : k + 1, :] = jnp.sum(acc[k], axis=0, keepdims=True)
    copy_out.wait()


def fused(base, lengths, inputs, cotangent, up, down, params):
    rows, length, features = inputs.shape
    half = cotangent.shape[1]
    tiles = -(-(half + 3 + LEAD) // OWN)
    count = rows * tiles
    x_rows = 2 * OWN * (tiles - 1) + WINDOW
    g_rows = -(-(OWN * (tiles - 1) + 8 + SLOTS) // 16) * 16
    shapes = (rows, length, half, features, tiles)
    whole = pl.BlockSpec(memory_space=pltpu.VMEM)
    return pl.pallas_call(
        functools.partial(kernel, shapes),
        out_shape=(
            jax.ShapeDtypeStruct((rows, half, features), BF16),
            jax.ShapeDtypeStruct((rows, length, features), BF16),
            jax.ShapeDtypeStruct((TAPS + 2, features), F32),
        ),
        in_specs=[
            pl.BlockSpec(memory_space=pltpu.SMEM),
            pl.BlockSpec(memory_space=pltpu.SMEM),
            pl.BlockSpec(memory_space=pl.ANY),
            whole,
            whole,
            whole,
            whole,
        ],
        out_specs=(whole, pl.BlockSpec(memory_space=pl.ANY), whole),
        scratch_shapes=[
            pltpu.VMEM((rows, x_rows, features), BF16),
            pltpu.VMEM((rows, g_rows, features), F32),
            pltpu.VMEM((count, TAPS * SLOTS, 2 * features), BF16),
            pltpu.VMEM((4, count, 8, 128), F32),
            pltpu.VMEM((count // 2, 8, 128), F32),
            pltpu.VMEM((2, count, 8, 128), F32),
            pltpu.VMEM((count // 2, 8, 128), F32),
            pltpu.VMEM((rows, g_rows, features), F32),
            pltpu.VMEM((rows, x_rows, features), BF16),
            pltpu.VMEM((16, features), F32),
            pltpu.VMEM((8, features), F32),
            pltpu.VMEM((TAPS + 2, 8, features), F32),
            pltpu.SemaphoreType.DMA((2,)),
        ],
        compiler_params=pltpu.CompilerParams(vmem_limit_bytes=60 * 1024 * 1024),
    )(base, lengths, inputs, cotangent, up, down, params)


def adam_update(grads, weights, first_old, second_old):
    first_new = beta_one * first_old + (1.0 - beta_one) * grads
    second_new = beta_two * second_old + (1.0 - beta_two) * grads * grads
    first_hat = first_new / (1.0 - beta_one**STEP)
    second_hat = second_new / (1.0 - beta_two**STEP)
    updated = weights - learn_rate * (
        first_hat / (jnp.sqrt(second_hat) + adam_eps) + decay_rate * weights
    )
    return (updated, first_new, second_new)


def total_over(value, axis):
    count = lax.axis_size(axis)
    if count & (count - 1):
        return lax.psum(value, axis)
    step = 1
    while step < count:
        value = value + lax.ppermute(value, axis, [(i, i ^ step) for i in range(count)])
        step *= 2
    return value


def per_device(inputs, lengths, params, first_moment, second_moment, cotangent):
    length_here = inputs.shape[1]
    half_here = cotangent.shape[1]
    send_up = jnp.concatenate(
        [cotangent[:, half_here - 2 :], inputs[:, length_here - (PAD - 2) :]], axis=1
    )
    send_down = jnp.concatenate([inputs[:, : PAD - 3], cotangent[:, :3]], axis=1)
    up = passed_along(send_up, "group", 1)
    down = passed_along(send_down, "group", -1)
    base = (lax.axis_index("group") * length_here).astype(jnp.int32).reshape(1)
    output, grad_inputs, grad_local = fused(base, lengths, inputs, cotangent, up, down, params)
    grad_params = total_over(total_over(grad_local, "group"), "rows")
    grad_norm = jnp.sqrt(jnp.sum(grad_params * grad_params))
    clip_scale = jnp.minimum(1.0, clip_limit / (grad_norm + 1e-06))
    new_params, new_first, new_second = adam_update(
        grad_params * clip_scale, params, first_moment, second_moment
    )
    return (output, grad_inputs, grad_norm, new_params, new_first, new_second)


def solution(mesh):
    in_specs = (P("rows", "group", None), P("rows", None), P(), P(), P(), P("rows", "group", None))
    out_specs = (P("rows", "group", None), P("rows", "group", None), P(), P(), P(), P())
    return jax.shard_map(
        per_device, mesh=mesh, in_specs=in_specs, out_specs=out_specs, check_vma=False
    )
```

time: 253 us -> 62.1 us (0.25); the launches traced: 249 us -> 61.7 us
  other arithmetic: 176 us -> 2.07 us
  blocking collectives: 42.2 us -> 0 us
  Pallas kernels: 0 us -> 26.4 us
  local copies, waits for them, and re-layouts: 17.9 us -> 4.12 us
  starting transfers between devices: 6.91 us -> 16 us
  waiting for transfers between devices: 3.67 us -> 10.4 us
    reduce_sum x8 -> x0, other arithmetic: 76.3 us -> none  [the longest x1 36.3 us: mix_window(): keep_mask * weights[k] * padded[3 - k:3 - k + conv_rows]]
    mul x3 -> x0, other arithmetic: 49 us -> none  [the longest x2 41.3 us: mix_window(): running = running + keep_mask * conv_out[3 + j:3 + j + span]]
    psum x1 -> x0, blocking collectives: 42.2 us -> none  [per_device(): grad_params = lax.psum(grad_local, ('rows', 'group'))]
    pallas_call x0 -> x1, Pallas kernels: none -> 26.4 us  [fused(): pl.pallas_call(functools.partial(kernel, shapes), out_shape=(jax.ShapeDty...]
    another operation x4 -> x0, other arithmetic: 22.8 us -> none  [the longest x2 15.2 us: mix_window(): stacked = jnp.stack(pooled)]
    ppermute x0 -> x5, starting transfers between devices: none -> 11.6 us  [total_over(): lax.ppermute(value, axis, [(i, i ^ step) for i in range(count)])]
    add_any x3 -> x0, other arithmetic: 11.4 us -> none  [the longest x1 11.4 us: mix_window(): logits = jnp.sum(stacked * weights[5], axis=2)]
    ppermute x0 -> x5, waiting for transfers between devices: none -> 9.55 us  [total_over(): lax.ppermute(value, axis, [(i, i ^ step) for i in range(count)])]
  transfers between devices with their start and end apart: 4 -> 7, of which waited for: 1 -> 6; matrix products, arithmetic and copies ran while one was open for 8% -> 3% of each run, Pallas kernels for 0% -> 0%
where the time goes in v1:
time: 62.1 us; the launch traced here: 61.7 us
  Pallas kernels  26.4 us (43%)
  starting transfers between devices  16 us (26%)
  waiting for transfers between devices  10.4 us (17%)
  local copies, waits for them, and re-layouts  4.12 us (7%)
  between operations  2.62 us (4%)
  other arithmetic  2.07 us (3%)
    pallas_call x1, Pallas kernels, fused(): pl.pallas_call(functools.partial(kernel, shapes), out_shape=(jax.ShapeDty...  26.4 us
    ppermute x5, starting transfers between devices, total_over(): lax.ppermute(value, axis, [(i, i ^ step) for i in range(count)])  11.6 us
    ppermute x5, waiting for transfers between devices, total_over(): lax.ppermute(value, axis, [(i, i ^ step) for i in range(count)])  9.55 us
    ppermute x2, starting transfers between devices, passed_along(): lax.ppermute(value, axis, [(source, source + steps) for source in range(i...  4.33 us
    slice x2, local copies, waits for them, and re-layouts, per_device(): send_down = jnp.concatenate([inputs[:, :PAD - 3], cotangent[:, :3]], axis=1)  1.73 us
  transfers between devices with their start and end apart: 7, of which 6 were waited for; matrix products, arithmetic and copies ran while one was open for 3% of the time, Pallas kernels for 0%

profile of v1, /device:TPU:0, one launch (start us, length us, event | category | flops | bytes accessed | tf_op | source)
XLA Modules:
  0.0 61.7 jit_solution(13038640688104090252)
XLA Ops:
  0.6 0.0 copy-start
  0.6 0.0 copy-start.4
  0.7 0.0 copy-start.3
  0.7 0.8 %slice.15 = bf16[4,3,768]{2,1,0:T(4,128)(2,1)S(1)} slice(bf16[4,256,768]{2,1,0:T(8,128)(2,1)} %g_ref.1), slice={[0:4], [0:3], [0:768]} | slice | bytes 36864 | tf_op jit(solution)/shard_map/slice | solution.py:427
  1.5 0.9 %slice.14 = bf16[4,13,768]{2,1,0:T(8,128)(2,1)S(1)} slice(bf16[4,512,768]{2,1,0:T(8,128)(2,1)} %x_hbm.1), slice={[0:4], [0:13], [0:768]} | slice | bytes 159744 | tf_op jit(solution)/shard_map/slice | solution.py:427
  2.4 1.3 %collective-permute-start.1 = (bf16[4,16,768]{2,1,0:T(8,128)(2,1)S(1)}, bf16[4,16,768]{2,1,0:T(8,128)(2,1)S(1)}, u32[]{:S(2)}, u32[]{:S(2)}) collective-permute-start(bf16[4,16,768]{2,1,0:T(8,128)(2,1)S(1)} %pad_maximum_fusion.1), channel_id=1, source_target_pairs={{1,0},{2,1},{3,2},{5,4},{6,5},{7,6},{9,8},{10,9},{11,10},{13,12},{... | collective-permute-start | bytes 294920 | tf_op jit(solution)/shard_map/ppermute | solution.py:33
  3.7 0.8 %slice.12 = bf16[4,2,768]{2,1,0:T(2,128)(2,1)S(1)} slice(bf16[4,256,768]{2,1,0:T(8,128)(2,1)} %g_ref.1), slice={[0:4], [254:256], [0:768]} | slice | bytes 24576 | tf_op jit(solution)/shard_map/slice | solution.py:425
  4.5 0.9 %slice.13 = bf16[4,14,768]{2,1,0:T(8,128)(2,1)S(1)} slice(bf16[4,512,768]{2,1,0:T(8,128)(2,1)} %x_hbm.1), slice={[0:4], [498:512], [0:768]} | slice | bytes 172032 | tf_op jit(solution)/shard_map/slice | solution.py:425
  5.5 3.0 %collective-permute-start = (bf16[4,16,768]{2,1,0:T(8,128)(2,1)S(1)}, bf16[4,16,768]{2,1,0:T(8,128)(2,1)S(1)}, u32[]{:S(2)}, u32[]{:S(2)}) collective-permute-start(bf16[4,16,768]{2,1,0:T(8,128)(2,1)S(1)} %pad_maximum_fusion), channel_id=1, source_target_pairs={{0,1},{1,2},{2,3},{4,5},{5,6},{6,7},{8,9},{9,10},{10,11},{12,13},{... | collective-permute-start | bytes 294920 | tf_op jit(solution)/shard_map/ppermute | solution.py:33
  8.6 0.0 collective-permute-done.1.down_ref
  8.6 0.0 copy-start.1
  8.6 0.9 %collective-permute-done.up_ref = bf16[4,16,768]{2,1,0:T(8,128)(2,1)S(1)} collective-permute-done((bf16[4,16,768]{2,1,0:T(8,128)(2,1)S(1)}, bf16[4,16,768]{2,1,0:T(8,128)(2,1)S(1)}, u32[]{:S(2)}, u32[]{:S(2)}) %collective-permute-start) | collective-permute-done | bytes 98336 | tf_op jit(solution)/shard_map/ppermute | solution.py:33
  9.5 0.0 copy-start.2
  9.5 0.0 copy-done.1
  9.5 0.6 %copy-done.2 = bf16[4,16,768]{2,1,0:T(8,128)(2,1)} copy-done((bf16[4,16,768]{2,1,0:T(8,128)(2,1)}, bf16[4,16,768]{2,1,0:T(8,128)(2,1)S(1)}, u32[]{:S(2)}) %copy-start.2) | copy-done | bytes 98328
  10.1 26.4 %shard_map.109 = (bf16[4,256,768]{2,1,0:T(8,128)(2,1)}, bf16[4,512,768]{2,1,0:T(8,128)(2,1)}, f32[6,768]{1,0:T(8,128)}) custom-call(s32[1]{0:T(128)} %bitcast.base_ref, s32[4,4]{1,0:T(4,128)} %len_ref.1, bf16[4,512,768]{2,1,0:T(8,128)(2,1)} %x_hbm.1, bf16[4,256,768]{2,1,0:T(8,128)(2,1)} %g_ref.1, bf16[4,16,768]{2,1,0:T(8,128)(2,1)} %copy-done.2, ...), custom_call_target="tpu_custom_call" | custom-call | tf_op jit(solution)/shard_map/pallas_call | solution.py:363
  36.6 3.3 %collective-permute-start.2 = (f32[6,768]{1,0:T(8,128)}, f32[6,768]{1,0:T(8,128)S(1)}, u32[]{:S(2)}, u32[]{:S(2)}) collective-permute-start(f32[6,768]{1,0:T(8,128)} %get-tuple-element.11), channel_id=1, source_target_pairs={{0,1},{1,0},{2,3},{3,2},{4,5},{5,4},{6,7},{7,6},{8,9},{9,8},{10,11... | collective-permute-start | bytes 55304 | tf_op jit(solution)/shard_map/ppermute | solution.py:416
  39.9 1.1 %collective-permute-done.2 = f32[6,768]{1,0:T(8,128)S(1)} collective-permute-done((f32[6,768]{1,0:T(8,128)}, f32[6,768]{1,0:T(8,128)S(1)}, u32[]{:S(2)}, u32[]{:S(2)}) %collective-permute-start.2) | collective-permute-done | bytes 18464 | tf_op jit(solution)/shard_map/ppermute | solution.py:416
  40.9 0.7 %add.33 = f32[6,768]{1,0:T(8,128)S(1)} add(f32[6,768]{1,0:T(8,128)} %get-tuple-element.11, f32[6,768]{1,0:T(8,128)S(1)} %collective-permute-done.2) | non-fusion elementwise | flops 4608 | bytes 55296 | tf_op jit(solution)/shard_map/add | solution.py:416
  41.7 2.6 %collective-permute-start.3 = (f32[6,768]{1,0:T(8,128)S(1)}, f32[6,768]{1,0:T(8,128)S(1)}, u32[]{:S(2)}, u32[]{:S(2)}) collective-permute-start(f32[6,768]{1,0:T(8,128)S(1)} %add.33), channel_id=1, source_target_pairs={{0,2},{1,3},{2,0},{3,1},{4,6},{5,7},{6,4},{7,5},{8,10},{9,11},{10,... | collective-permute-start | bytes 55304 | tf_op jit(solution)/shard_map/ppermute | solution.py:416
  44.3 1.8 %collective-permute-done.3 = f32[6,768]{1,0:T(8,128)S(1)} collective-permute-done((f32[6,768]{1,0:T(8,128)S(1)}, f32[6,768]{1,0:T(8,128)S(1)}, u32[]{:S(2)}, u32[]{:S(2)}) %collective-permute-start.3) | collective-permute-done | bytes 18464 | tf_op jit(solution)/shard_map/ppermute | solution.py:416
  46.1 1.5 %collective-permute-start.4 = (f32[6,768]{1,0:T(8,128)S(1)}, f32[6,768]{1,0:T(8,128)S(1)}, u32[]{:S(2)}, u32[]{:S(2)}) collective-permute-start(f32[6,768]{1,0:T(8,128)S(1)} %add.34), channel_id=1, source_target_pairs={{0,4},{4,0},{8,12},{12,8},{16,20},{20,16},{24,28},{28,24},{1,5},{5... | collective-permute-start | bytes 55304 | tf_op jit(solution)/shard_map/ppermute | solution.py:416
  47.6 2.3 %collective-permute-done.4 = f32[6,768]{1,0:T(8,128)S(1)} collective-permute-done((f32[6,768]{1,0:T(8,128)S(1)}, f32[6,768]{1,0:T(8,128)S(1)}, u32[]{:S(2)}, u32[]{:S(2)}) %collective-permute-start.4) | collective-permute-done | bytes 18464 | tf_op jit(solution)/shard_map/ppermute | solution.py:416
  50.0 1.6 %collective-permute-start.5 = (f32[6,768]{1,0:T(8,128)S(1)}, f32[6,768]{1,0:T(8,128)S(1)}, u32[]{:S(2)}, u32[]{:S(2)}) collective-permute-start(f32[6,768]{1,0:T(8,128)S(1)} %add.35), channel_id=1, source_target_pairs={{0,8},{4,12},{8,0},{12,4},{16,24},{20,28},{24,16},{28,20},{1,9},{5... | collective-permute-start | bytes 55304 | tf_op jit(solution)/shard_map/ppermute | solution.py:416
  51.5 2.2 %collective-permute-done.5 = f32[6,768]{1,0:T(8,128)S(1)} collective-permute-done((f32[6,768]{1,0:T(8,128)S(1)}, f32[6,768]{1,0:T(8,128)S(1)}, u32[]{:S(2)}, u32[]{:S(2)}) %collective-permute-start.5) | collective-permute-done | bytes 18464 | tf_op jit(solution)/shard_map/ppermute | solution.py:416
  53.8 2.6 %collective-permute-start.6 = (f32[6,768]{1,0:T(8,128)S(1)}, f32[6,768]{1,0:T(8,128)S(1)}, u32[]{:S(2)}, u32[]{:S(2)}) collective-permute-start(f32[6,768]{1,0:T(8,128)S(1)} %add.36), channel_id=1, source_target_pairs={{0,16},{4,20},{8,24},{12,28},{16,0},{20,4},{24,8},{28,12},{1,17},{... | collective-permute-start | bytes 55304 | tf_op jit(solution)/shard_map/ppermute | solution.py:416
  56.4 2.1 %collective-permute-done.6 = f32[6,768]{1,0:T(8,128)S(1)} collective-permute-done((f32[6,768]{1,0:T(8,128)S(1)}, f32[6,768]{1,0:T(8,128)S(1)}, u32[]{:S(2)}, u32[]{:S(2)}) %collective-permute-start.6) | collective-permute-done | bytes 18464 | tf_op jit(solution)/shard_map/ppermute | solution.py:416
  58.5 0.6 multiply_reduce_fusion
  59.9 0.0 copy-done
  59.9 0.0 copy-done.4
  59.9 0.0 copy-done.3
  59.9 0.6 %multiply_subtract_fusion = (f32[6,768]{1,0:T(8,128)}, f32[6,768]{1,0:T(8,128)}, f32[6,768]{1,0:T(8,128)}) fusion(f32[6,768]{1,0:T(8,128)S(1)} %copy-done, f32[6,768]{1,0:T(8,128)S(1)} %get-tuple-element.16, f32[]{:T(128)S(6)} %min.3, f32[6,768]{1,0:T(8,128)S(1)} %copy-done.3, f32[6,768]{1,0:T(8,128)S(1)} %copy-done.4), kind=kLoop, calls=%fused_computation.4 | loop fusion | flops 73728 | bytes 129028 | tf_op jit(solution)/shard_map/sub | solution.py:404
  (5 shorter events, 0.1 us)
Async XLA Ops:
  0.6 59.2 %copy-start = (f32[6,768]{1,0:T(8,128)S(1)}, f32[6,768]{1,0:T(8,128)}, u32[]{:S(2)}) copy-start(f32[6,768]{1,0:T(8,128)} %par_ref.1) | copy-start | bytes 55300
  0.6 59.2 %copy-start.4 = (f32[6,768]{1,0:T(8,128)S(1)}, f32[6,768]{1,0:T(8,128)}, u32[]{:S(2)}) copy-start(f32[6,768]{1,0:T(8,128)} %param.10) | copy-start | bytes 55300
  0.7 59.2 %copy-start.3 = (f32[6,768]{1,0:T(8,128)S(1)}, f32[6,768]{1,0:T(8,128)}, u32[]{:S(2)}) copy-start(f32[6,768]{1,0:T(8,128)} %param.9) | copy-start | bytes 55300
  2.4 6.1 %collective-permute-start.1 = (bf16[4,16,768]{2,1,0:T(8,128)(2,1)S(1)}, bf16[4,16,768]{2,1,0:T(8,128)(2,1)S(1)}, u32[]{:S(2)}, u32[]{:S(2)}) collective-permute-start(bf16[4,16,768]{2,1,0:T(8,128)(2,1)S(1)} %pad_maximum_fusion.1), channel_id=1, source_target_pairs={{1,0},{2,1},{3,2},{5,4},{6,5},{7,6},{9,8},{10,9},{11,10},{13,12},{... | collective-permute-start | bytes 294920 | tf_op jit(solution)/shard_map/ppermute | solution.py:33
  5.5 4.0 %collective-permute-start = (bf16[4,16,768]{2,1,0:T(8,128)(2,1)S(1)}, bf16[4,16,768]{2,1,0:T(8,128)(2,1)S(1)}, u32[]{:S(2)}, u32[]{:S(2)}) collective-permute-start(bf16[4,16,768]{2,1,0:T(8,128)(2,1)S(1)} %pad_maximum_fusion), channel_id=1, source_target_pairs={{0,1},{1,2},{2,3},{4,5},{5,6},{6,7},{8,9},{9,10},{10,11},{12,13},{... | collective-permute-start | bytes 294920 | tf_op jit(solution)/shard_map/ppermute | solution.py:33
  8.6 0.9 %copy-start.1 = (bf16[4,16,768]{2,1,0:T(8,128)(2,1)}, bf16[4,16,768]{2,1,0:T(8,128)(2,1)S(1)}, u32[]{:S(2)}) copy-start(bf16[4,16,768]{2,1,0:T(8,128)(2,1)S(1)} %collective-permute-done.1.down_ref) | copy-start | bytes 294916
  9.5 0.6 %copy-start.2 = (bf16[4,16,768]{2,1,0:T(8,128)(2,1)}, bf16[4,16,768]{2,1,0:T(8,128)(2,1)S(1)}, u32[]{:S(2)}) copy-start(bf16[4,16,768]{2,1,0:T(8,128)(2,1)S(1)} %collective-permute-done.up_ref) | copy-start | bytes 294916
  36.6 4.4 %collective-permute-start.2 = (f32[6,768]{1,0:T(8,128)}, f32[6,768]{1,0:T(8,128)S(1)}, u32[]{:S(2)}, u32[]{:S(2)}) collective-permute-start(f32[6,768]{1,0:T(8,128)} %get-tuple-element.11), channel_id=1, source_target_pairs={{0,1},{1,0},{2,3},{3,2},{4,5},{5,4},{6,7},{7,6},{8,9},{9,8},{10,11... | collective-permute-start | bytes 55304 | tf_op jit(solution)/shard_map/ppermute | solution.py:416
  41.7 4.4 %collective-permute-start.3 = (f32[6,768]{1,0:T(8,128)S(1)}, f32[6,768]{1,0:T(8,128)S(1)}, u32[]{:S(2)}, u32[]{:S(2)}) collective-permute-start(f32[6,768]{1,0:T(8,128)S(1)} %add.33), channel_id=1, source_target_pairs={{0,2},{1,3},{2,0},{3,1},{4,6},{5,7},{6,4},{7,5},{8,10},{9,11},{10,... | collective-permute-start | bytes 55304 | tf_op jit(solution)/shard_map/ppermute | solution.py:416
  46.1 3.8 %collective-permute-start.4 = (f32[6,768]{1,0:T(8,128)S(1)}, f32[6,768]{1,0:T(8,128)S(1)}, u32[]{:S(2)}, u32[]{:S(2)}) collective-permute-start(f32[6,768]{1,0:T(8,128)S(1)} %add.34), channel_id=1, source_target_pairs={{0,4},{4,0},{8,12},{12,8},{16,20},{20,16},{24,28},{28,24},{1,5},{5... | collective-permute-start | bytes 55304 | tf_op jit(solution)/shard_map/ppermute | solution.py:416
  50.0 3.8 %collective-permute-start.5 = (f32[6,768]{1,0:T(8,128)S(1)}, f32[6,768]{1,0:T(8,128)S(1)}, u32[]{:S(2)}, u32[]{:S(2)}) collective-permute-start(f32[6,768]{1,0:T(8,128)S(1)} %add.35), channel_id=1, source_target_pairs={{0,8},{4,12},{8,0},{12,4},{16,24},{20,28},{24,16},{28,20},{1,9},{5... | collective-permute-start | bytes 55304 | tf_op jit(solution)/shard_map/ppermute | solution.py:416
  53.8 4.7 %collective-permute-start.6 = (f32[6,768]{1,0:T(8,128)S(1)}, f32[6,768]{1,0:T(8,128)S(1)}, u32[]{:S(2)}, u32[]{:S(2)}) collective-permute-start(f32[6,768]{1,0:T(8,128)S(1)} %add.36), channel_id=1, source_target_pairs={{0,16},{4,20},{8,24},{12,28},{16,0},{20,4},{24,8},{28,12},{1,17},{... | collective-permute-start | bytes 55304 | tf_op jit(solution)/shard_map/ppermute | solution.py:416

commit v2 on v1

v2 whole, which is shorter than its diff:
```python
import functools

import jax
import jax.numpy as jnp
from jax import lax
from jax.experimental import pallas as pl
from jax.experimental.pallas import tpu as pltpu
from jax.sharding import PartitionSpec as P

STEP = 10


beta_one = 0.9
beta_two = 0.999
learn_rate = 0.2
decay_rate = 0.01
adam_eps = 1e-08
clip_limit = 1.0

TAPS = 4
SLOTS = 64
OWN = 56
LEAD = 4
WINDOW = 128
PAD = 16
F32 = jnp.float32
BF16 = jnp.bfloat16


def passed_along(value, axis, steps):
    count = lax.axis_size(axis)
    initial, last = (max(0, -steps), min(count, count - steps))
    return lax.ppermute(value, axis, [(source, source + steps) for source in range(initial, last)])


def rotate_rows(x, amount):
    for bit in (1, 2, 4):
        x = jnp.where((amount & bit) != 0, pltpu.roll(x, 8 - bit, x.ndim - 2), x)
    return x


def split(x):
    high = x.astype(BF16)
    return high, (x - high.astype(F32)).astype(BF16)


def iota(shape, dim):
    return lax.broadcasted_iota(jnp.int32, shape, dim)


def ends_of(len_ref, r):
    one = len_ref[r, 0]
    two = one + len_ref[r, 1]
    three = two + len_ref[r, 2]
    return one, two, three, three + len_ref[r, 3]


def begin_of(at, ends):
    begin = jnp.where(at >= ends[0], ends[0], 0)
    begin = jnp.where(at >= ends[1], ends[1], begin)
    return jnp.where(at >= ends[2], ends[2], begin)


def end_of(at, ends):
    end = jnp.where(at >= ends[0], ends[1], ends[0])
    end = jnp.where(at >= ends[1], ends[2], end)
    return jnp.where(at >= ends[2], ends[3], end)


def lanes_of(c):
    return slice(128 * c, 128 * c + 128)


def gather_rows(g_rows, up, down, half):
    sub = iota((8, up.shape[1]), 0)
    head = jnp.where(sub >= 6, pltpu.roll(up[0:8], 6, 0), 0.0)
    tail = jnp.where(sub < 3, pltpu.roll(down[8:16], 3, 0), 0.0)
    return head, tail


def forward_kernel(
    shapes,
    base_ref,
    len_ref,
    x_hbm,
    g_hbm,
    up_ref,
    down_ref,
    par_ref,
    out_hbm,
    mat_hbm,
    grad_ref,
    xb,
    gb,
    xf,
    g32,
    conv_high,
    conv_low,
    comp,
    cs,
    es,
    out32,
    outb,
    mat,
    carry_o,
    acc,
    sems,
):
    rows, length, half, features, tiles = shapes
    count = rows * tiles
    pairs = count // 2
    chunks = features // 128
    base = base_ref[0]
    padded = xb.shape[1]

    copies_x = [
        pltpu.make_async_copy(x_hbm.at[r], xb.at[r, pl.ds(PAD, length), :], sems.at[0, r])
        for r in range(rows)
    ]
    copies_g = [pltpu.make_async_copy(g_hbm.at[r], gb.at[r], sems.at[1, r]) for r in range(rows)]
    for r in range(rows):
        copies_x[r].start()
    for r in range(rows):
        copies_g[r].start()

    sub8 = iota((8, 128), 0)
    lane8 = iota((8, 128), 1)
    slot8 = lane8 % SLOTS
    left = lane8 < SLOTS
    first = [2 * slot8 - 3 - (2 * p + lane8 // SLOTS) for p in range(2)]
    group_of = [(f + ((sub8 - f) & 7)) >> 3 for f in first]
    turn = [f & 7 for f in first]
    first_e = 2 * slot8 - 3
    group_of_e = (first_e + ((sub8 - first_e) & 7)) >> 3
    turn_e = first_e & 7

    def place(tile):
        return tile // tiles, tile % tiles

    def tile_start(m):
        return base + 2 * OWN * m - PAD

    acc[...] = jnp.zeros_like(acc)

    for r in range(rows):
        xb[r, 0:PAD, :] = up_ref[r]
        xb[r, PAD + length : 2 * PAD + length, :] = down_ref[r]
        rest = padded - 2 * PAD - length
        if rest > 0:
            xb[r, 2 * PAD + length :, :] = jnp.zeros((rest, features), BF16)
    for c in range(chunks):
        xf[c, 0:8, :] = jnp.zeros((8, 128), F32)

    def convolve(r, _):
        pltpu.make_async_copy(x_hbm.at[r], xb.at[r, pl.ds(PAD, length), :], sems.at[0, r]).wait()
        ends = ends_of(len_ref, r)

        def widen(i, _):
            at = pl.multiple_of(i * 32, 32)
            for c in range(chunks):
                xf[c, pl.ds(at + 8, 32), :] = xb[r, pl.ds(at, 32), lanes_of(c)].astype(F32)
            return 0

        lax.fori_loop(0, padded // 32, widen, 0)

        def taps(i, _):
            at = pl.multiple_of(i * 16, 16)
            keeps = []
            for j in range(2):
                position = base - PAD + at + 8 * j + sub8
                offset = position - begin_of(position, ends)
                keeps.append([offset >= k for k in range(TAPS)])
            for c in range(chunks):
                parts = []
                for j in range(2):
                    value = par_ref[4:5, lanes_of(c)] + par_ref[0:1, lanes_of(c)] * xf[
                        c, pl.ds(at + 8 * j + 8, 8), :
                    ]
                    for k in range(1, TAPS):
                        shifted = xf[c, pl.ds(at + 8 * j + 8 - k, 8), :]
                        value = value + par_ref[k : k + 1, lanes_of(c)] * jnp.where(
                            keeps[j][k], shifted, 0.0
                        )
                    parts.append(value)
                high, low = split(jnp.concatenate(parts, axis=0))
                conv_high[r, c, pl.ds(at, 16), :] = high
                conv_low[r, c, pl.ds(at, 16), :] = low
            return 0

        lax.fori_loop(0, padded // 16, taps, 0)
        return 0

    lax.fori_loop(0, rows, convolve, 0)

    for r in range(rows):
        copies_g[r].wait()
        up = up_ref[r].astype(F32)
        down = down_ref[r].astype(F32)
        head, tail = gather_rows(None, up, down, half)
        after = g32.shape[2] - PAD - half - 8
        for c in range(chunks):
            g32[r, c, 8:16, :] = head[:, lanes_of(c)]
            g32[r, c, PAD + half : PAD + half + 8, :] = tail[:, lanes_of(c)]
            g32[r, c, PAD + half + 8 :, :] = jnp.zeros((after, 128), F32)

    def widen_g(i, _):
        r = i // (half // 32)
        at = pl.multiple_of((i % (half // 32)) * 32, 32)
        for c in range(chunks):
            g32[r, c, pl.ds(at + PAD, 32), :] = gb[r, pl.ds(at, 32), lanes_of(c)].astype(F32)
        return 0

    lax.fori_loop(0, rows * (half // 32), widen_g, 0)

    scorer_high = [par_ref[5:6, lanes_of(c)].astype(BF16).astype(F32) for c in range(chunks)]
    scorer_low = [par_ref[5:6, lanes_of(c)] - scorer_high[c] for c in range(chunks)]

    def products(pair, _):
        dots, scores = [], []
        for side in range(2):
            r, m = place(2 * pair + side)
            start = pl.multiple_of(OWN * m + 8, 8)
            at = pl.multiple_of(2 * OWN * m, 16)
            streamed, held = [], []
            for c in range(chunks):
                g = g32[r, c, pl.ds(start, SLOTS), :]
                top = jnp.where(sub8 == 0, scorer_high[c], jnp.where(sub8 == 1, scorer_low[c], g[0:8]))
                streamed.append(jnp.concatenate([top, g[8:]], axis=0).astype(BF16))
                held.append(
                    jnp.concatenate(
                        [
                            conv_high[r, c, pl.ds(at, WINDOW), :],
                            conv_low[r, c, pl.ds(at, WINDOW), :],
                        ],
                        axis=0,
                    )
                )
            product = lax.dot_general(
                jnp.concatenate(streamed, axis=1),
                jnp.concatenate(held, axis=1),
                (((1,), (1,)), ((), ())),
                preferred_element_type=F32,
            )
            product = product[:, :WINDOW] + product[:, WINDOW:]
            dots.append(product)
            scores.append(jnp.broadcast_to(product[0:1] + product[1:2], (SLOTS, WINDOW)))
        dots = jnp.concatenate(dots, axis=0).T
        scores = jnp.concatenate(scores, axis=0).T
        banded = jnp.zeros((8, 128), F32)
        scored = jnp.zeros((8, 128), F32)
        for v in range(WINDOW // 8):
            here = group_of_e == v
            banded = jnp.where(here, dots[8 * v : 8 * v + 8], banded)
            scored = jnp.where(here, scores[8 * v : 8 * v + 8], scored)
        comp[0, pair] = banded
        comp[1, pair] = scored
        return 0

    lax.fori_loop(0, pairs, products, 0)

    ends = [ends_of(len_ref, r) for r in range(rows)]
    delta = sub8 - 3
    for pair in range(pairs):
        both = (2 * pair, 2 * pair + 1)
        dots = rotate_rows(comp[0, pair], turn_e)
        scores = rotate_rows(comp[1, pair], turn_e)
        coef = jnp.zeros((8, 128), F32)
        coef_e = jnp.zeros((8, 128), F32)
        for p in range(2):
            at = [tile_start(place(t)[1]) + 2 * slot8 + p for t in both]
            begin = [begin_of(a, ends[place(t)[0]]) for a, t in zip(at, both)]
            end = [end_of(a, ends[place(t)[0]]) for a, t in zip(at, both)]
            offset = jnp.maximum(jnp.where(left, at[0] - begin[0], at[1] - begin[1]), 0)
            remain = jnp.where(left, end[0] - at[0], end[1] - at[1])
            masks, inverses, logits, grads = [], [], [], []
            for b in range(1, TAPS + 1):
                if b == 3:
                    thirds = ((offset.astype(F32) + 0.5) * (1.0 / 3.0)).astype(jnp.int32)
                    within = offset - 3 * thirds
                else:
                    within = offset & (b - 1)
                upper = jnp.minimum(b - within, remain)
                mask = (delta >= p - within) & (delta < p + upper)
                inverse = 1.0 / jnp.maximum(within + upper, 1).astype(F32)
                masks.append(mask)
                inverses.append(inverse)
                logits.append(jnp.sum(jnp.where(mask, scores, 0.0), axis=0, keepdims=True) * inverse)
                grads.append(
                    jnp.sum(jnp.where(mask, dots, 0.0), axis=0, keepdims=True) * (0.5 * inverse)
                )
            largest = functools.reduce(jnp.maximum, logits)
            powers = [jnp.exp(logit - largest) for logit in logits]
            scale = 1.0 / sum(powers)
            shares = [power * scale for power in powers]
            mean = sum(share * grad for share, grad in zip(shares, grads))
            for mask, inverse, share, grad in zip(masks, inverses, shares, grads):
                coef = coef + jnp.where(mask, (0.5 * share) * inverse, 0.0)
                coef_e = coef_e + jnp.where(mask, share * (grad - mean) * inverse, 0.0)
        owned = (slot8 >= LEAD) & (slot8 < LEAD + OWN)
        coef = jnp.where(owned, coef, 0.0)
        coef_e = jnp.where(owned, coef_e, 0.0)
        es[pair] = rotate_rows(coef_e, (8 - turn_e) & 7)
        swapped = pltpu.roll(coef, SLOTS, 1)
        for side, tile in enumerate(both):
            r, m = place(tile)
            at = tile_start(m) + 2 * slot8 + delta
            offset = at - begin_of(at, ends[r])
            alone = jnp.where(left, coef, swapped) if side == 0 else jnp.where(left, swapped, coef)
            for p in range(2):
                kept = jnp.where((offset >= 2 * p + lane8 // SLOTS) & (at >= 0), alone, 0.0)
                cs[p, tile] = rotate_rows(kept, (8 - turn[p]) & 7)

    for r in range(rows):
        for c in range(chunks):
            g32[r, c, 8:16, :] = jnp.zeros((8, 128), F32)
            g32[r, c, PAD + half : PAD + half + 8, :] = jnp.zeros((8, 128), F32)

    rows_e = iota((SLOTS, 128), 0)
    wide = 2 if chunks % 2 == 0 else 1

    def apply(pair, _):
        spread = jnp.concatenate(
            [jnp.where(group_of_e == v, es[pair], 0.0) for v in range(WINDOW // 8)], axis=0
        ).T
        for side in range(2):
            tile = 2 * pair + side
            r, m = place(tile)
            from_row = OWN * m - 8
            part = spread[SLOTS * side : SLOTS * side + SLOTS]
            here = (from_row + rows_e >= 0) & (from_row + rows_e < half)
            own_e = jnp.sum(jnp.where(here, part, 0.0), axis=0, keepdims=True)
            all_e = jnp.sum(part, axis=0, keepdims=True)
            at = tile_start(m) + lane8
            offset = at - begin_of(at, ends_of(len_ref, r))
            bands = []
            for p in range(2):
                bands.append(
                    jnp.concatenate(
                        [jnp.where(group_of[p] == v, cs[p, tile], 0.0) for v in range(WINDOW // 8)],
                        axis=0,
                    ).T
                )
            band = []
            for k in range(TAPS):
                row_k = jnp.where((offset >= k) & (at >= 0), jnp.broadcast_to(own_e, (8, 128)), 0.0)
                if k > 0:
                    row_k = pltpu.roll(row_k, 128 - k, 1)
                matrix = bands[k // 2][SLOTS * (k % 2) : SLOTS * (k % 2) + SLOTS]
                band.append(jnp.where(sub8 == 0, row_k, matrix[0:8]))
                band.append(matrix[8:])
            matrix = jnp.concatenate(band, axis=0)
            total = jnp.sum(matrix[0:SLOTS], axis=1, keepdims=True)
            high, low = split(matrix)
            back = jnp.concatenate(
                [jnp.where(sub8 < 2, jnp.broadcast_to(all_e, (8, 128)), matrix[0:8]), matrix[8:SLOTS]],
                axis=0,
            )
            back_high, back_low = split(back)
            mat[tile, :, 0:WINDOW] = back_high
            mat[tile, :, WINDOW:] = back_low
            factor = jnp.concatenate([high, low], axis=1)
            start = pl.multiple_of(OWN * m + 8, 8)
            window = pl.multiple_of(2 * OWN * m, 16)
            for w in range(chunks // wide):
                x = xb[r, pl.ds(window, WINDOW), 128 * wide * w : 128 * wide * (w + 1)]
                mixed = lax.dot_general(
                    factor,
                    jnp.concatenate([x, x], axis=0),
                    (((1,), (0,)), ((), ())),
                    preferred_element_type=F32,
                )
                for i in range(wide):
                    c = wide * w + i
                    lanes = lanes_of(c)
                    g = g32[r, c, pl.ds(start, SLOTS), :]
                    top = jnp.where(
                        sub8 == 0, par_ref[5:6, lanes], jnp.where(sub8 < LEAD, 0.0, g[0:8])
                    )
                    g = jnp.concatenate([top, g[8:]], axis=0)
                    value = total * par_ref[4:5, lanes]
                    for k in range(TAPS):
                        taken = mixed[SLOTS * k : SLOTS * (k + 1), lanes_of(i)]
                        value = value + taken * par_ref[k : k + 1, lanes]
                        acc[k, :, lanes] += jnp.sum((taken * g).reshape(SLOTS // 8, 8, 128), axis=0)
                    acc[4, :, lanes] += jnp.sum((total * g).reshape(SLOTS // 8, 8, 128), axis=0)
                    acc[5, :, lanes] += jnp.where(sub8 == 0, value[0:8], 0.0)
                    before = jnp.where(m > 0, carry_o[:, lanes], 0.0)
                    out32[c, pl.ds(start, 8), :] = before + jnp.where(sub8 < LEAD, 0.0, value[0:8])
                    out32[c, pl.ds(start + 8, OWN - 8), :] = value[8:OWN]
                    carry_o[:, lanes] = value[OWN:]

            @pl.when(m == tiles - 1)
            def _():
                for c in range(chunks):
                    outb[r, :, lanes_of(c)] = out32[c, PAD : PAD + half, :].astype(BF16)
                pltpu.make_async_copy(outb.at[r], out_hbm.at[r], sems.at[2, r]).start()

        return 0

    lax.fori_loop(0, pairs, apply, 0)

    copy_mat = pltpu.make_async_copy(mat, mat_hbm, sems.at[3, 0])
    copy_mat.start()
    for k in range(TAPS + 2):
        grad_ref[k : k + 1, :] = jnp.sum(acc[k], axis=0, keepdims=True)
    for r in range(rows):
        pltpu.make_async_copy(outb.at[r], out_hbm.at[r], sems.at[2, r]).wait()
    copy_mat.wait()


def backward_kernel(
    shapes,
    r,
    base_ref,
    len_ref,
    g_hbm,
    mat_hbm,
    up_ref,
    down_ref,
    par_ref,
    *refs,
):
    gin_hbm, gb, mat, g32, dc, ginb, sems = refs[-7:]
    rows, length, half, features, tiles = shapes
    chunks = features // 128
    base = base_ref[0]
    copy_g = pltpu.make_async_copy(g_hbm.at[r], gb, sems.at[0])
    copy_g.start()
    copy_mat = pltpu.make_async_copy(mat_hbm.at[pl.ds(r * tiles, tiles)], mat, sems.at[1])
    copy_mat.start()
    sub8 = iota((8, 128), 0)
    ends = ends_of(len_ref, r)
    head, tail = gather_rows(None, up_ref[r].astype(F32), down_ref[r].astype(F32), half)
    after = g32.shape[1] - PAD - half - 8
    for c in range(chunks):
        g32[c, 8:16, :] = head[:, lanes_of(c)]
        g32[c, PAD + half : PAD + half + 8, :] = tail[:, lanes_of(c)]
        g32[c, PAD + half + 8 :, :] = jnp.zeros((after, 128), F32)
    copy_g.wait()

    def widen_g(i, _):
        at = pl.multiple_of(i * 32, 32)
        for c in range(chunks):
            g32[c, pl.ds(at + PAD, 32), :] = gb[pl.ds(at, 32), lanes_of(c)].astype(F32)
        return 0

    lax.fori_loop(0, half // 32, widen_g, 0)
    copy_mat.wait()

    for m in range(tiles):
        streamed = jnp.concatenate(
            [mat[m, :, 0:WINDOW].T, mat[m, :, WINDOW:].T], axis=1
        )
        for c in range(chunks):
            scorer = par_ref[5:6, lanes_of(c)]
            scorer_high = scorer.astype(BF16).astype(F32)
            g = g32[c, OWN * m + 8 : OWN * m + 8 + SLOTS, :]
            top = jnp.where(sub8 == 0, scorer_high, jnp.where(sub8 == 1, scorer - scorer_high, g[0:8]))
            g = jnp.concatenate([top, g[8:]], axis=0).astype(BF16)
            part = lax.dot_general(
                streamed,
                jnp.concatenate([g, g], axis=0),
                (((1,), (0,)), ((), ())),
                preferred_element_type=F32,
            )
            at = 2 * OWN * m
            before = dc[c, at : at + PAD, :] if m > 0 else 0.0
            dc[c, at : at + PAD, :] = before + part[0:PAD]
            dc[c, at + PAD : at + WINDOW, :] = part[PAD:]

    def taps(i, _):
        at = pl.multiple_of(i * 16, 16)
        keeps = []
        for j in range(2):
            position = base + at + 8 * j + sub8
            remain = end_of(position, ends) - position
            keeps.append([remain > k for k in range(TAPS)])
        for c in range(chunks):
            parts = []
            for j in range(2):
                value = par_ref[0:1, lanes_of(c)] * dc[c, pl.ds(at + PAD + 8 * j, 8), :]
                for k in range(1, TAPS):
                    shifted = dc[c, pl.ds(at + PAD + 8 * j + k, 8), :]
                    value = value + par_ref[k : k + 1, lanes_of(c)] * jnp.where(keeps[j][k], shifted, 0.0)
                parts.append(value)
            ginb[pl.ds(at, 16), lanes_of(c)] = jnp.concatenate(parts, axis=0).astype(BF16)
        return 0

    lax.fori_loop(0, length // 16, taps, 0)
    copy_out = pltpu.make_async_copy(ginb, gin_hbm.at[r], sems.at[2])
    copy_out.start()
    copy_out.wait()


SMEM = pl.BlockSpec(memory_space=pltpu.SMEM)
VMEM = pl.BlockSpec(memory_space=pltpu.VMEM)
HBM = pl.BlockSpec(memory_space=pl.ANY)


def sizes_of(length, half):
    tiles = -(-(half + 3 + LEAD) // OWN)
    x_rows = -(-(2 * OWN * (tiles - 1) + WINDOW) // 32) * 32
    g_rows = -(-(OWN * (tiles - 1) + 8 + SLOTS) // 16) * 16
    return tiles, x_rows, g_rows


def forward(base, lengths, inputs, cotangent, up, down, params):
    rows, length, features = inputs.shape
    half = cotangent.shape[1]
    chunks = features // 128
    tiles, x_rows, g_rows = sizes_of(length, half)
    count = rows * tiles
    shapes = (rows, length, half, features, tiles)
    return pl.pallas_call(
        functools.partial(forward_kernel, shapes),
        out_shape=(
            jax.ShapeDtypeStruct((rows, half, features), BF16),
            jax.ShapeDtypeStruct((count, SLOTS, 2 * WINDOW), BF16),
            jax.ShapeDtypeStruct((TAPS + 2, features), F32),
        ),
        in_specs=[SMEM, SMEM, HBM, HBM, VMEM, VMEM, VMEM],
        out_specs=(HBM, HBM, VMEM),
        scratch_shapes=[
            pltpu.VMEM((rows, x_rows, features), BF16),
            pltpu.VMEM((rows, half, features), BF16),
            pltpu.VMEM((chunks, x_rows + 8, 128), F32),
            pltpu.VMEM((rows, chunks, g_rows, 128), F32),
            pltpu.VMEM((rows, chunks, x_rows, 128), BF16),
            pltpu.VMEM((rows, chunks, x_rows, 128), BF16),
            pltpu.VMEM((2, count // 2, 8, 128), F32),
            pltpu.VMEM((2, count, 8, 128), F32),
            pltpu.VMEM((count // 2, 8, 128), F32),
            pltpu.VMEM((chunks, g_rows, 128), F32),
            pltpu.VMEM((rows, half, features), BF16),
            pltpu.VMEM((count, SLOTS, 2 * WINDOW), BF16),
            pltpu.VMEM((8, features), F32),
            pltpu.VMEM((TAPS + 2, 8, features), F32),
            pltpu.SemaphoreType.DMA((4, rows)),
        ],
        compiler_params=pltpu.CompilerParams(vmem_limit_bytes=40 * 1024 * 1024),
        cost_estimate=pl.CostEstimate(
            flops=2 * count * SLOTS * WINDOW * features * 12,
            bytes_accessed=8 * inputs.size,
            transcendentals=0,
        ),
    )(base, lengths, inputs, cotangent, up, down, params)


def backward(r, base, lengths, cotangent, matrices, up, down, params, grown):
    rows, half, features = cotangent.shape
    length = 2 * half
    chunks = features // 128
    tiles, x_rows, g_rows = sizes_of(length, half)
    shapes = (rows, length, half, features, tiles)
    operands = [base, lengths, cotangent, matrices, up, down, params]
    in_specs = [SMEM, SMEM, HBM, HBM, VMEM, VMEM, VMEM]
    if grown is not None:
        operands.append(grown)
        in_specs.append(HBM)
    return pl.pallas_call(
        functools.partial(backward_kernel, shapes, r),
        out_shape=jax.ShapeDtypeStruct((rows, length, features), BF16),
        in_specs=in_specs,
        out_specs=HBM,
        scratch_shapes=[
            pltpu.VMEM((half, features), BF16),
            pltpu.VMEM((tiles, SLOTS, 2 * WINDOW), BF16),
            pltpu.VMEM((chunks, g_rows, 128), F32),
            pltpu.VMEM((chunks, x_rows, 128), F32),
            pltpu.VMEM((length, features), BF16),
            pltpu.SemaphoreType.DMA((3,)),
        ],
        input_output_aliases={} if grown is None else {7: 0},
        compiler_params=pltpu.CompilerParams(vmem_limit_bytes=16 * 1024 * 1024),
        cost_estimate=pl.CostEstimate(
            flops=2 * tiles * SLOTS * WINDOW * features * 4,
            bytes_accessed=4 * length * features,
            transcendentals=0,
        ),
    )(*operands)


def adam_update(grads, weights, first_old, second_old):
    first_new = beta_one * first_old + (1.0 - beta_one) * grads
    second_new = beta_two * second_old + (1.0 - beta_two) * grads * grads
    first_hat = first_new / (1.0 - beta_one**STEP)
    second_hat = second_new / (1.0 - beta_two**STEP)
    updated = weights - learn_rate * (
        first_hat / (jnp.sqrt(second_hat) + adam_eps) + decay_rate * weights
    )
    return (updated, first_new, second_new)


def rounds_of(axes):
    rounds = []
    for axis in axes:
        count = lax.axis_size(axis)
        step = 1
        while step < count:
            rounds.append((axis, [(i, i ^ step) for i in range(count)]))
            step *= 2
    return rounds


def per_device(inputs, lengths, params, first_moment, second_moment, cotangent):
    rows_here, length_here, features = inputs.shape
    half_here = cotangent.shape[1]
    send_up = jnp.concatenate(
        [cotangent[:, half_here - 2 :], inputs[:, length_here - (PAD - 2) :]], axis=1
    )
    send_down = jnp.concatenate([inputs[:, : PAD - 3], cotangent[:, :3]], axis=1)
    up = passed_along(send_up, "group", 1)
    down = passed_along(send_down, "group", -1)
    base = (lax.axis_index("group") * length_here).astype(jnp.int32).reshape(1)
    output, matrices, grad_params = forward(base, lengths, inputs, cotangent, up, down, params)
    grad_inputs = None
    row = 0
    for axis, exchange in rounds_of(("group", "rows")):
        received = lax.ppermute(grad_params, axis, exchange)
        if row < rows_here:
            matrices, grad_params = lax.optimization_barrier((matrices, grad_params))
            grad_inputs = backward(
                row, base, lengths, cotangent, matrices, up, down, params, grad_inputs
            )
            row += 1
            received, grad_inputs = lax.optimization_barrier((received, grad_inputs))
        grad_params = grad_params + received
    while row < rows_here:
        grad_inputs = backward(row, base, lengths, cotangent, matrices, up, down, params, grad_inputs)
        row += 1
    grad_norm = jnp.sqrt(jnp.sum(grad_params * grad_params))
    clip_scale = jnp.minimum(1.0, clip_limit / (grad_norm + 1e-06))
    new_params, new_first, new_second = adam_update(
        grad_params * clip_scale, params, first_moment, second_moment
    )
    return (output, grad_inputs, grad_norm, new_params, new_first, new_second)


def solution(mesh):
    in_specs = (P("rows", "group", None), P("rows", None), P(), P(), P(), P("rows", "group", None))
    out_specs = (P("rows", "group", None), P("rows", "group", None), P(), P(), P(), P())
    return jax.shard_map(
        per_device, mesh=mesh, in_specs=in_specs, out_specs=out_specs, check_vma=False
    )
```

time: 62.1 us -> 69 us (1.11)
  Pallas kernels: 26.4 us -> 37.2 us
  waiting for transfers between devices: 10.4 us -> 3.21 us
  local copies, waits for them, and re-layouts: 4.12 us -> 8.19 us
  other arithmetic: 2.07 us -> 1.35 us
    pallas_call x1 -> x5, Pallas kernels: 26.4 us -> 37.2 us  [the longest x1 22.7 us: forward(): pl.pallas_call(functools.partial(forward_kernel, shapes), out_shape=(jax....]
    ppermute x5, waiting for transfers between devices: 9.55 us -> 2.3 us  [per_device(): received = lax.ppermute(grad_params, axis, exchange)]
    unnamed x10 -> x14, local copies, waits for them, and re-layouts: 0.65 us -> 4.73 us
    add x4, other arithmetic: 0.76 us -> 0.03 us  [per_device(): grad_params = grad_params + received]
  transfers between devices with their start and end apart: 7 -> 7, of which waited for: 6 -> 2; matrix products, arithmetic and copies ran while one was open for 3% -> 3% of each run, Pallas kernels for 0% -> 21%
where the time goes in v2:
time: 69 us; the launch traced here: 68.5 us
  Pallas kernels  37.2 us (54%)
  starting transfers between devices  15.9 us (23%)
  local copies, waits for them, and re-layouts  8.19 us (12%)
  waiting for transfers between devices  3.21 us (5%)
  between operations  2.7 us (4%)
  other arithmetic  1.35 us (2%)
    pallas_call x1, Pallas kernels, forward(): pl.pallas_call(functools.partial(forward_kernel, shapes), out_shape=(jax....  22.7 us
    pallas_call x4, Pallas kernels, backward(): pl.pallas_call(functools.partial(backward_kernel, shapes, r), out_shape=j...  14.5 us
    ppermute x5, starting transfers between devices, per_device(): received = lax.ppermute(grad_params, axis, exchange)  11.6 us
    unnamed x14, local copies, waits for them, and re-layouts  4.73 us
    ppermute x2, starting transfers between devices, passed_along(): lax.ppermute(value, axis, [(source, source + steps) for source in range(i...  4.33 us
    ppermute x5, waiting for transfers between devices, per_device(): received = lax.ppermute(grad_params, axis, exchange)  2.3 us
    slice x2, local copies, waits for them, and re-layouts, per_device(): send_down = jnp.concatenate([inputs[:, :PAD - 3], cotangent[:, :3]], axis=1)  1.71 us
  transfers between devices with their start and end apart: 7, of which 2 were waited for; matrix products, arithmetic and copies ran while one was open for 3% of the time, Pallas kernels for 21%

profile of v2, /device:TPU:0, one launch (start us, length us, event | category | flops | bytes accessed | tf_op | source)
XLA Modules:
  0.0 68.5 jit_solution(14871590471438803341)
XLA Ops:
  0.6 0.8 %slice.15 = bf16[4,3,768]{2,1,0:T(4,128)(2,1)S(1)} slice(bf16[4,256,768]{2,1,0:T(8,128)(2,1)} %g_hbm.9), slice={[0:4], [0:3], [0:768]} | slice | bytes 36864 | tf_op jit(solution)/shard_map/slice | solution.py:611
  1.4 0.9 %slice.14 = bf16[4,13,768]{2,1,0:T(8,128)(2,1)S(1)} slice(bf16[4,512,768]{2,1,0:T(8,128)(2,1)} %x_hbm.1), slice={[0:4], [0:13], [0:768]} | slice | bytes 159744 | tf_op jit(solution)/shard_map/slice | solution.py:611
  2.4 1.3 %collective-permute-start.1 = (bf16[4,16,768]{2,1,0:T(8,128)(2,1)S(1)}, bf16[4,16,768]{2,1,0:T(8,128)(2,1)S(1)}, u32[]{:S(2)}, u32[]{:S(2)}) collective-permute-start(bf16[4,16,768]{2,1,0:T(8,128)(2,1)S(1)} %pad_maximum_fusion.1), channel_id=1, source_target_pairs={{1,0},{2,1},{3,2},{5,4},{6,5},{7,6},{9,8},{10,9},{11,10},{13,12},{... | collective-permute-start | bytes 294920 | tf_op jit(solution)/shard_map/ppermute | solution.py:33
  3.7 0.8 %slice.12 = bf16[4,2,768]{2,1,0:T(2,128)(2,1)S(1)} slice(bf16[4,256,768]{2,1,0:T(8,128)(2,1)} %g_hbm.9), slice={[0:4], [254:256], [0:768]} | slice | bytes 24576 | tf_op jit(solution)/shard_map/slice | solution.py:609
  4.5 0.9 %slice.13 = bf16[4,14,768]{2,1,0:T(8,128)(2,1)S(1)} slice(bf16[4,512,768]{2,1,0:T(8,128)(2,1)} %x_hbm.1), slice={[0:4], [498:512], [0:768]} | slice | bytes 172032 | tf_op jit(solution)/shard_map/slice | solution.py:609
  5.5 3.0 %collective-permute-start = (bf16[4,16,768]{2,1,0:T(8,128)(2,1)S(1)}, bf16[4,16,768]{2,1,0:T(8,128)(2,1)S(1)}, u32[]{:S(2)}, u32[]{:S(2)}) collective-permute-start(bf16[4,16,768]{2,1,0:T(8,128)(2,1)S(1)} %pad_maximum_fusion), channel_id=1, source_target_pairs={{0,1},{1,2},{2,3},{4,5},{5,6},{6,7},{8,9},{9,10},{10,11},{12,13},{... | collective-permute-start | bytes 294920 | tf_op jit(solution)/shard_map/ppermute | solution.py:33
  8.5 0.0 collective-permute-done.1.down_ref
  8.5 0.9 %collective-permute-done.up_ref = bf16[4,16,768]{2,1,0:T(8,128)(2,1)S(1)} collective-permute-done((bf16[4,16,768]{2,1,0:T(8,128)(2,1)S(1)}, bf16[4,16,768]{2,1,0:T(8,128)(2,1)S(1)}, u32[]{:S(2)}, u32[]{:S(2)}) %collective-permute-start) | collective-permute-done | bytes 98336 | tf_op jit(solution)/shard_map/ppermute | solution.py:33
  9.4 0.0 copy-start
  9.4 1.4 %copy-done = bf16[4,256,768]{2,1,0:T(8,128)(2,1)S(1)} copy-done((bf16[4,256,768]{2,1,0:T(8,128)(2,1)S(1)}, bf16[4,256,768]{2,1,0:T(8,128)(2,1)}, u32[]{:S(2)}) %copy-start) | copy-done | bytes 1572888
  10.8 0.0 copy-start.1
  10.9 0.7 %copy-done.1 = f32[6,768]{1,0:T(8,128)S(1)} copy-done((f32[6,768]{1,0:T(8,128)S(1)}, f32[6,768]{1,0:T(8,128)}, u32[]{:S(2)}) %copy-start.1) | copy-done | bytes 18456
  11.6 0.0 copy-start.3
  11.6 0.7 copy-done.3
  12.3 0.0 copy-start.4
  12.3 1.9 %copy-done.4 = bf16[4,512,768]{2,1,0:T(8,128)(2,1)S(1)} copy-done((bf16[4,512,768]{2,1,0:T(8,128)(2,1)S(1)}, bf16[4,512,768]{2,1,0:T(8,128)(2,1)}, u32[]{:S(2)}) %copy-start.4) | copy-done | bytes 3145752
  14.2 22.7 %shard_map.109 = (bf16[4,256,768]{2,1,0:T(8,128)(2,1)}, bf16[20,64,256]{2,1,0:T(8,128)(2,1)S(1)}, f32[6,768]{1,0:T(8,128)S(1)}) custom-call(s32[1]{0:T(128)} %bitcast.base_ref, s32[4,4]{1,0:T(4,128)S(1)} %copy-done.3, bf16[4,512,768]{2,1,0:T(8,128)(2,1)S(1)} %copy-done.4, bf16[4,256,768]{2,1,0:T(8,128)(2,1)S(1)} %copy-done, ...), custom_call_target="tpu_custom_call" | custom-call | flops 3019898880 | bytes 12582912 | tf_op jit(solution)/shard_map/pallas_call | solution.py:514
  36.9 3.3 %collective-permute-start.2 = (f32[6,768]{1,0:T(8,128)S(1)}, f32[6,768]{1,0:T(8,128)S(1)}, u32[]{:S(2)}, u32[]{:S(2)}) collective-permute-start(f32[6,768]{1,0:T(8,128)S(1)} %get-tuple-element.29), channel_id=1, source_target_pairs={{0,1},{1,0},{2,3},{3,2},{4,5},{5,4},{6,7},{7,6},{8,9},{9,8},{10,11... | collective-permute-start | bytes 55304 | tf_op jit(solution)/shard_map/ppermute | solution.py:619
  40.2 3.6 %shard_map.110.refs_0_ = bf16[4,512,768]{2,1,0:T(8,128)(2,1)} custom-call(s32[1]{0:T(128)} %bitcast.base_ref, s32[4,4]{1,0:T(4,128)S(1)} %copy-done.3, bf16[4,256,768]{2,1,0:T(8,128)(2,1)S(1)} %copy-done, bf16[20,64,256]{2,1,0:T(8,128)(2,1)S(1)} %get-tuple-element.39.mat_hbm, bf16[4,16,768]{2,1,0:T(8,128)(2,1)S(1)} %collective-permute-done.up_ref, ...), custom_call_target="tpu_custom_call" | custom-call | flops 251658240 | bytes 1572864 | tf_op jit(solution)/shard_map/pallas_call | solution.py:560
  43.8 0.0 collective-permute-done.2
  43.8 2.4 %collective-permute-start.3 = (f32[6,768]{1,0:T(8,128)S(1)}, f32[6,768]{1,0:T(8,128)S(1)}, u32[]{:S(2)}, u32[]{:S(2)}) collective-permute-start(f32[6,768]{1,0:T(8,128)S(1)} %add.33), channel_id=1, source_target_pairs={{0,2},{1,3},{2,0},{3,1},{4,6},{5,7},{6,4},{7,5},{8,10},{9,11},{10,... | collective-permute-start | bytes 55304 | tf_op jit(solution)/shard_map/ppermute | solution.py:619
  46.2 3.6 %shard_map.111.refs_0_ = bf16[4,512,768]{2,1,0:T(8,128)(2,1)} custom-call(s32[1]{0:T(128)} %bitcast.base_ref, s32[4,4]{1,0:T(4,128)S(1)} %copy-done.3, bf16[4,256,768]{2,1,0:T(8,128)(2,1)S(1)} %copy-done, bf16[20,64,256]{2,1,0:T(8,128)(2,1)S(1)} %get-tuple-element.39.mat_hbm, ...), custom_call_target="tpu_custom_call", output_to_operand_aliasing={{}: (7, {})} | custom-call | flops 251658240 | bytes 1572864 | tf_op jit(solution)/shard_map/pallas_call | solution.py:560
  49.8 0.0 collective-permute-done.3
  49.9 1.6 %collective-permute-start.4 = (f32[6,768]{1,0:T(8,128)S(1)}, f32[6,768]{1,0:T(8,128)S(1)}, u32[]{:S(2)}, u32[]{:S(2)}) collective-permute-start(f32[6,768]{1,0:T(8,128)S(1)} %add.34), channel_id=1, source_target_pairs={{0,4},{4,0},{8,12},{12,8},{16,20},{20,16},{24,28},{28,24},{1,5},{5... | collective-permute-start | bytes 55304 | tf_op jit(solution)/shard_map/ppermute | solution.py:619
  51.4 3.6 %shard_map.112.refs_0_ = bf16[4,512,768]{2,1,0:T(8,128)(2,1)} custom-call(s32[1]{0:T(128)} %bitcast.base_ref, s32[4,4]{1,0:T(4,128)S(1)} %copy-done.3, bf16[4,256,768]{2,1,0:T(8,128)(2,1)S(1)} %copy-done, bf16[20,64,256]{2,1,0:T(8,128)(2,1)S(1)} %get-tuple-element.39.mat_hbm, ...), custom_call_target="tpu_custom_call", output_to_operand_aliasing={{}: (7, {})} | custom-call | flops 251658240 | bytes 1572864 | tf_op jit(solution)/shard_map/pallas_call | solution.py:560
  55.1 0.0 collective-permute-done.4
  55.1 0.0 copy-start.2
  55.1 0.0 copy-start.5
  55.1 0.0 copy-start.6
  55.1 1.6 %collective-permute-start.5 = (f32[6,768]{1,0:T(8,128)S(1)}, f32[6,768]{1,0:T(8,128)S(1)}, u32[]{:S(2)}, u32[]{:S(2)}) collective-permute-start(f32[6,768]{1,0:T(8,128)S(1)} %add.35), channel_id=1, source_target_pairs={{0,8},{4,12},{8,0},{12,4},{16,24},{20,28},{24,16},{28,20},{1,9},{5... | collective-permute-start | bytes 55304 | tf_op jit(solution)/shard_map/ppermute | solution.py:619
  56.8 3.6 %shard_map.113 = bf16[4,512,768]{2,1,0:T(8,128)(2,1)} custom-call(s32[1]{0:T(128)} %bitcast.base_ref, s32[4,4]{1,0:T(4,128)S(1)} %copy-done.3, bf16[4,256,768]{2,1,0:T(8,128)(2,1)S(1)} %copy-done, bf16[20,64,256]{2,1,0:T(8,128)(2,1)S(1)} %get-tuple-element.39.mat_hbm, ...), custom_call_target="tpu_custom_call", output_to_operand_aliasing={{}: (7, {})} | custom-call | flops 251658240 | bytes 1572864 | tf_op jit(solution)/shard_map/pallas_call | solution.py:560
  60.4 0.0 collective-permute-done.5
  60.4 2.7 %collective-permute-start.6 = (f32[6,768]{1,0:T(8,128)S(1)}, f32[6,768]{1,0:T(8,128)S(1)}, u32[]{:S(2)}, u32[]{:S(2)}) collective-permute-start(f32[6,768]{1,0:T(8,128)S(1)} %add.36), channel_id=1, source_target_pairs={{0,16},{4,20},{8,24},{12,28},{16,0},{20,4},{24,8},{28,12},{1,17},{... | collective-permute-start | bytes 55304 | tf_op jit(solution)/shard_map/ppermute | solution.py:619
  63.1 2.3 %collective-permute-done.6 = f32[6,768]{1,0:T(8,128)S(1)} collective-permute-done((f32[6,768]{1,0:T(8,128)S(1)}, f32[6,768]{1,0:T(8,128)S(1)}, u32[]{:S(2)}, u32[]{:S(2)}) %collective-permute-start.6) | collective-permute-done | bytes 18464 | tf_op jit(solution)/shard_map/ppermute | solution.py:619
  65.4 0.6 multiply_reduce_fusion
  66.7 0.0 copy-done.2
  66.7 0.0 copy-done.5
  66.7 0.0 copy-done.6
  66.7 0.6 multiply_subtract_fusion
  (6 shorter events, 0.1 us)
Async XLA Ops:
  2.4 6.1 %collective-permute-start.1 = (bf16[4,16,768]{2,1,0:T(8,128)(2,1)S(1)}, bf16[4,16,768]{2,1,0:T(8,128)(2,1)S(1)}, u32[]{:S(2)}, u32[]{:S(2)}) collective-permute-start(bf16[4,16,768]{2,1,0:T(8,128)(2,1)S(1)} %pad_maximum_fusion.1), channel_id=1, source_target_pairs={{1,0},{2,1},{3,2},{5,4},{6,5},{7,6},{9,8},{10,9},{11,10},{13,12},{... | collective-permute-start | bytes 294920 | tf_op jit(solution)/shard_map/ppermute | solution.py:33
  5.5 4.0 %collective-permute-start = (bf16[4,16,768]{2,1,0:T(8,128)(2,1)S(1)}, bf16[4,16,768]{2,1,0:T(8,128)(2,1)S(1)}, u32[]{:S(2)}, u32[]{:S(2)}) collective-permute-start(bf16[4,16,768]{2,1,0:T(8,128)(2,1)S(1)} %pad_maximum_fusion), channel_id=1, source_target_pairs={{0,1},{1,2},{2,3},{4,5},{5,6},{6,7},{8,9},{9,10},{10,11},{12,13},{... | collective-permute-start | bytes 294920 | tf_op jit(solution)/shard_map/ppermute | solution.py:33
  9.4 1.4 %copy-start = (bf16[4,256,768]{2,1,0:T(8,128)(2,1)S(1)}, bf16[4,256,768]{2,1,0:T(8,128)(2,1)}, u32[]{:S(2)}) copy-start(bf16[4,256,768]{2,1,0:T(8,128)(2,1)} %g_hbm.9) | copy-start | bytes 4718596
  10.8 0.7 %copy-start.1 = (f32[6,768]{1,0:T(8,128)S(1)}, f32[6,768]{1,0:T(8,128)}, u32[]{:S(2)}) copy-start(f32[6,768]{1,0:T(8,128)} %par_ref.9) | copy-start | bytes 55300
  11.6 0.7 copy-start.3
  12.3 1.9 %copy-start.4 = (bf16[4,512,768]{2,1,0:T(8,128)(2,1)S(1)}, bf16[4,512,768]{2,1,0:T(8,128)(2,1)}, u32[]{:S(2)}) copy-start(bf16[4,512,768]{2,1,0:T(8,128)(2,1)} %x_hbm.1) | copy-start | bytes 9437188
  36.9 6.9 %collective-permute-start.2 = (f32[6,768]{1,0:T(8,128)S(1)}, f32[6,768]{1,0:T(8,128)S(1)}, u32[]{:S(2)}, u32[]{:S(2)}) collective-permute-start(f32[6,768]{1,0:T(8,128)S(1)} %get-tuple-element.29), channel_id=1, source_target_pairs={{0,1},{1,0},{2,3},{3,2},{4,5},{5,4},{6,7},{7,6},{8,9},{9,8},{10,11... | collective-permute-start | bytes 55304 | tf_op jit(solution)/shard_map/ppermute | solution.py:619
  43.8 6.0 %collective-permute-start.3 = (f32[6,768]{1,0:T(8,128)S(1)}, f32[6,768]{1,0:T(8,128)S(1)}, u32[]{:S(2)}, u32[]{:S(2)}) collective-permute-start(f32[6,768]{1,0:T(8,128)S(1)} %add.33), channel_id=1, source_target_pairs={{0,2},{1,3},{2,0},{3,1},{4,6},{5,7},{6,4},{7,5},{8,10},{9,11},{10,... | collective-permute-start | bytes 55304 | tf_op jit(solution)/shard_map/ppermute | solution.py:619
  49.9 5.2 %collective-permute-start.4 = (f32[6,768]{1,0:T(8,128)S(1)}, f32[6,768]{1,0:T(8,128)S(1)}, u32[]{:S(2)}, u32[]{:S(2)}) collective-permute-start(f32[6,768]{1,0:T(8,128)S(1)} %add.34), channel_id=1, source_target_pairs={{0,4},{4,0},{8,12},{12,8},{16,20},{20,16},{24,28},{28,24},{1,5},{5... | collective-permute-start | bytes 55304 | tf_op jit(solution)/shard_map/ppermute | solution.py:619
  55.1 11.6 %copy-start.2 = (f32[6,768]{1,0:T(8,128)S(1)}, f32[6,768]{1,0:T(8,128)}, u32[]{:S(2)}) copy-start(f32[6,768]{1,0:T(8,128)} %par_ref.9) | copy-start | bytes 55300
  55.1 11.6 %copy-start.5 = (f32[6,768]{1,0:T(8,128)S(1)}, f32[6,768]{1,0:T(8,128)}, u32[]{:S(2)}) copy-start(f32[6,768]{1,0:T(8,128)} %param.9) | copy-start | bytes 55300
  55.1 11.6 %copy-start.6 = (f32[6,768]{1,0:T(8,128)S(1)}, f32[6,768]{1,0:T(8,128)}, u32[]{:S(2)}) copy-start(f32[6,768]{1,0:T(8,128)} %param.10) | copy-start | bytes 55300
  55.1 5.3 %collective-permute-start.5 = (f32[6,768]{1,0:T(8,128)S(1)}, f32[6,768]{1,0:T(8,128)S(1)}, u32[]{:S(2)}, u32[]{:S(2)}) collective-permute-start(f32[6,768]{1,0:T(8,128)S(1)} %add.35), channel_id=1, source_target_pairs={{0,8},{4,12},{8,0},{12,4},{16,24},{20,28},{24,16},{28,20},{1,9},{5... | collective-permute-start | bytes 55304 | tf_op jit(solution)/shard_map/ppermute | solution.py:619
  60.4 5.0 %collective-permute-start.6 = (f32[6,768]{1,0:T(8,128)S(1)}, f32[6,768]{1,0:T(8,128)S(1)}, u32[]{:S(2)}, u32[]{:S(2)}) collective-permute-start(f32[6,768]{1,0:T(8,128)S(1)} %add.36), channel_id=1, source_target_pairs={{0,16},{4,20},{8,24},{12,28},{16,0},{20,4},{24,8},{28,12},{1,17},{... | collective-permute-start | bytes 55304 | tf_op jit(solution)/shard_map/ppermute | solution.py:619

commit v3 on v2

v3 whole, which is shorter than its diff:
```python
import functools

import jax
import jax.numpy as jnp
from jax import lax
from jax.experimental import pallas as pl
from jax.experimental.pallas import tpu as pltpu
from jax.sharding import PartitionSpec as P

STEP = 10


beta_one = 0.9
beta_two = 0.999
learn_rate = 0.2
decay_rate = 0.01
adam_eps = 1e-08
clip_limit = 1.0

TAPS = 4
SLOTS = 64
OWN = 56
LEAD = 4
WINDOW = 128
PAD = 16
F32 = jnp.float32
BF16 = jnp.bfloat16


def passed_along(value, axis, steps):
    count = lax.axis_size(axis)
    initial, last = (max(0, -steps), min(count, count - steps))
    return lax.ppermute(value, axis, [(source, source + steps) for source in range(initial, last)])


def rotate_rows(x, amount):
    for bit in (1, 2, 4):
        x = jnp.where((amount & bit) != 0, pltpu.roll(x, 8 - bit, x.ndim - 2), x)
    return x


def split(x):
    high = x.astype(BF16)
    return high, (x - high.astype(F32)).astype(BF16)


def iota(shape, dim):
    return lax.broadcasted_iota(jnp.int32, shape, dim)


def ends_of(len_ref, r):
    one = len_ref[r, 0]
    two = one + len_ref[r, 1]
    three = two + len_ref[r, 2]
    return one, two, three, three + len_ref[r, 3]


def begin_of(at, ends):
    begin = jnp.where(at >= ends[0], ends[0], 0)
    begin = jnp.where(at >= ends[1], ends[1], begin)
    return jnp.where(at >= ends[2], ends[2], begin)


def end_of(at, ends):
    end = jnp.where(at >= ends[0], ends[1], ends[0])
    end = jnp.where(at >= ends[1], ends[2], end)
    return jnp.where(at >= ends[2], ends[3], end)


def lanes_of(c):
    return slice(128 * c, 128 * c + 128)


def pack_kernel(x_hbm, g_hbm, up_ref, down_ref, x_first, x_last, g_first, g_last, sems):
    rows, length, features = x_hbm.shape
    half = g_hbm.shape[1]
    copies = [
        pltpu.make_async_copy(x_hbm.at[:, pl.ds(length - PAD, PAD), :], x_last, sems.at[0]),
        pltpu.make_async_copy(g_hbm.at[:, pl.ds(half - PAD, PAD), :], g_last, sems.at[1]),
        pltpu.make_async_copy(x_hbm.at[:, pl.ds(0, PAD), :], x_first, sems.at[2]),
        pltpu.make_async_copy(g_hbm.at[:, pl.ds(0, PAD), :], g_first, sems.at[3]),
    ]
    for copy in copies:
        copy.start()
    sub = iota((PAD, features), 0)
    for copy in copies:
        copy.wait()
    for r in range(rows):
        moved = pltpu.roll(g_last[r].astype(F32), 2, 0)
        up_ref[r] = jnp.where(sub < 2, moved, x_last[r].astype(F32)).astype(BF16)
        moved = pltpu.roll(g_first[r].astype(F32), PAD - 3, 0)
        down_ref[r] = jnp.where(sub < PAD - 3, x_first[r].astype(F32), moved).astype(BF16)


def forward_kernel(
    shapes,
    base_ref,
    len_ref,
    x_ref,
    g_ref,
    up_ref,
    down_ref,
    par_ref,
    out_hbm,
    mat,
    g32,
    grad_ref,
    xb,
    xf,
    conv_high,
    conv_low,
    dots_ref,
    comp,
    cs,
    es,
    fac_a,
    fac_b,
    tot,
    rows_e_ref,
    out32,
    outb,
    carry_o,
    acc,
    sems,
):
    rows, length, half, features, tiles = shapes
    count = rows * tiles
    pairs = count // 2
    chunks = features // 128
    base = base_ref[0]
    padded = xb.shape[1]

    def copy_out(r):
        return pltpu.make_async_copy(outb.at[r], out_hbm.at[r], sems.at[r])

    sub8 = iota((8, 128), 0)
    lane8 = iota((8, 128), 1)
    slot8 = lane8 % SLOTS
    left = lane8 < SLOTS
    delta = sub8 - 3
    first = [2 * slot8 - 3 - (2 * p + lane8 // SLOTS) for p in range(2)]
    group_of = [(f + ((sub8 - f) & 7)) >> 3 for f in first]
    turn = [f & 7 for f in first]
    first_e = 2 * slot8 - 3
    group_of_e = (first_e + ((sub8 - first_e) & 7)) >> 3
    turn_e = first_e & 7

    def place(tile):
        return tile // tiles, tile % tiles

    def tile_start(m):
        return base + 2 * OWN * m - PAD

    acc[...] = jnp.zeros_like(acc)
    carry_o[...] = jnp.zeros_like(carry_o)

    def convolve(r, at, side, where, ends):
        keeps = []
        for j in range(2):
            position = base - PAD + at + 8 * j + sub8
            offset = position - begin_of(position, ends)
            keeps.append([offset >= k for k in range(TAPS)])
        for c in range(chunks):
            parts = []
            for j in range(2):
                row = where + 8 * j
                value = par_ref[4:5, lanes_of(c)] + par_ref[0:1, lanes_of(c)] * xf[side, c, row : row + 8, :]
                for k in range(1, TAPS):
                    shifted = xf[side, c, row - k : row - k + 8, :]
                    value = value + par_ref[k : k + 1, lanes_of(c)] * jnp.where(keeps[j][k], shifted, 0.0)
                parts.append(value)
            high, low = split(jnp.concatenate(parts, axis=0))
            conv_high[r, c, pl.ds(at, 16), :] = high
            conv_low[r, c, pl.ds(at, 16), :] = low

    subd = iota((8, features), 0)
    for r in range(rows):
        up = up_ref[r]
        down = down_ref[r]
        xb[r, 0:PAD, :] = up
        xb[r, PAD + length : 2 * PAD + length, :] = down
        rest = padded - 2 * PAD - length
        if rest > 0:
            xb[r, 2 * PAD + length :, :] = jnp.zeros((rest, features), BF16)
        xb[r, PAD : PAD + length, :] = x_ref[r]
        before = jnp.where(subd >= 6, pltpu.roll(up.astype(F32)[0:8], 6, 0), 0.0)
        after = jnp.where(subd < 3, pltpu.roll(down.astype(F32)[8:16], 3, 0), 0.0)
        rest = g32.shape[2] - PAD - half - 8
        for c in range(chunks):
            g32[r, c, 8:16, :] = before[:, lanes_of(c)]
            g32[r, c, PAD : PAD + half, :] = g_ref[r, :, lanes_of(c)].astype(F32)
            g32[r, c, PAD + half : PAD + half + 8, :] = after[:, lanes_of(c)]
            g32[r, c, PAD + half + 8 :, :] = jnp.zeros((rest, 128), F32)
        for c in range(chunks):
            xf[r % 2, c, 0:8, :] = jnp.zeros((8, 128), F32)
            xf[r % 2, c, 8:24, :] = up[:, lanes_of(c)].astype(F32)
        convolve(r, 0, r % 2, 8, ends_of(len_ref, r))

    scorer_high = [par_ref[5:6, lanes_of(c)].astype(BF16).astype(F32) for c in range(chunks)]
    scorer_low = [par_ref[5:6, lanes_of(c)] - scorer_high[c] for c in range(chunks)]

    def convolve_pair(pair):
        for side in range(2):
            r, m = place(2 * pair + side)
            ends = ends_of(len_ref, r)
            at = pl.multiple_of(2 * OWN * m, 16)
            for c in range(chunks):
                xf[side, c, 8 : 8 + WINDOW, :] = xb[r, pl.ds(at, WINDOW), lanes_of(c)].astype(F32)
            for b in range(1, WINDOW // 16):
                convolve(r, pl.multiple_of(at + 16 * b, 16), side, 8 + 16 * b, ends)

    def multiply_pair(pair):
        for side in range(2):
            r, m = place(2 * pair + side)
            start = pl.multiple_of(OWN * m + 8, 8)
            at = pl.multiple_of(2 * OWN * m, 16)
            streamed, held = [], []
            for c in range(chunks):
                g = g32[r, c, pl.ds(start, SLOTS), :]
                top = jnp.where(sub8 == 0, scorer_high[c], jnp.where(sub8 == 1, scorer_low[c], g[0:8]))
                streamed.append(jnp.concatenate([top, g[8:]], axis=0).astype(BF16))
                held.append(
                    jnp.concatenate(
                        [
                            conv_high[r, c, pl.ds(at, WINDOW), :],
                            conv_low[r, c, pl.ds(at, WINDOW), :],
                        ],
                        axis=0,
                    )
                )
            product = lax.dot_general(
                jnp.concatenate(streamed, axis=1),
                jnp.concatenate(held, axis=1),
                (((1,), (1,)), ((), ())),
                preferred_element_type=F32,
            )
            dots_ref[SLOTS * side : SLOTS * side + SLOTS, :] = product[:, :WINDOW] + product[:, WINDOW:]

    def extract_pair(pair):
        dots = dots_ref[...]
        scores = jnp.concatenate(
            [
                jnp.broadcast_to(dots[i : i + 1] + dots[i + 1 : i + 2], (SLOTS, WINDOW))
                for i in (0, SLOTS)
            ],
            axis=0,
        ).T
        dots = dots.T
        banded = jnp.zeros((8, 128), F32)
        scored = jnp.zeros((8, 128), F32)
        for v in range(WINDOW // 8):
            here = group_of_e == v
            banded = jnp.where(here, dots[8 * v : 8 * v + 8], banded)
            scored = jnp.where(here, scores[8 * v : 8 * v + 8], scored)
        comp[0, pair] = banded
        comp[1, pair] = scored

    convolve_pair(0)
    multiply_pair(0)
    convolve_pair(1)

    def first_loop(i, _):
        extract_pair(i - 1)
        multiply_pair(i)
        convolve_pair(i + 1)
        return 0

    lax.fori_loop(1, pairs - 1, first_loop, 0)
    extract_pair(pairs - 2)
    multiply_pair(pairs - 1)
    extract_pair(pairs - 1)

    ends = [ends_of(len_ref, r) for r in range(rows)]
    for pair in range(pairs):
        both = (2 * pair, 2 * pair + 1)
        dots = rotate_rows(comp[0, pair], turn_e)
        scores = rotate_rows(comp[1, pair], turn_e)
        coef = jnp.zeros((8, 128), F32)
        coef_e = jnp.zeros((8, 128), F32)
        for p in range(2):
            at = [tile_start(place(t)[1]) + 2 * slot8 + p for t in both]
            begin = [begin_of(a, ends[place(t)[0]]) for a, t in zip(at, both)]
            end = [end_of(a, ends[place(t)[0]]) for a, t in zip(at, both)]
            offset = jnp.maximum(jnp.where(left, at[0] - begin[0], at[1] - begin[1]), 0)
            remain = jnp.where(left, end[0] - at[0], end[1] - at[1])
            masks, inverses, logits, grads = [], [], [], []
            for b in range(1, TAPS + 1):
                if b == 3:
                    thirds = ((offset.astype(F32) + 0.5) * (1.0 / 3.0)).astype(jnp.int32)
                    within = offset - 3 * thirds
                else:
                    within = offset & (b - 1)
                upper = jnp.minimum(b - within, remain)
                mask = (delta >= p - within) & (delta < p + upper)
                inverse = 1.0 / jnp.maximum(within + upper, 1).astype(F32)
                masks.append(mask)
                inverses.append(inverse)
                logits.append(jnp.sum(jnp.where(mask, scores, 0.0), axis=0, keepdims=True) * inverse)
                grads.append(
                    jnp.sum(jnp.where(mask, dots, 0.0), axis=0, keepdims=True) * (0.5 * inverse)
                )
            largest = functools.reduce(jnp.maximum, logits)
            powers = [jnp.exp(logit - largest) for logit in logits]
            scale = 1.0 / sum(powers)
            shares = [power * scale for power in powers]
            mean = sum(share * grad for share, grad in zip(shares, grads))
            for mask, inverse, share, grad in zip(masks, inverses, shares, grads):
                coef = coef + jnp.where(mask, (0.5 * share) * inverse, 0.0)
                coef_e = coef_e + jnp.where(mask, share * (grad - mean) * inverse, 0.0)
        owned = (slot8 >= LEAD) & (slot8 < LEAD + OWN)
        coef = jnp.where(owned, coef, 0.0)
        coef_e = jnp.where(owned, coef_e, 0.0)
        es[pair] = rotate_rows(coef_e, (8 - turn_e) & 7)
        swapped = pltpu.roll(coef, SLOTS, 1)
        for side, tile in enumerate(both):
            r, m = place(tile)
            at = tile_start(m) + 2 * slot8 + delta
            offset = at - begin_of(at, ends[r])
            alone = jnp.where(left, coef, swapped) if side == 0 else jnp.where(left, swapped, coef)
            for p in range(2):
                kept = jnp.where((offset >= 2 * p + lane8 // SLOTS) & (at >= 0), alone, 0.0)
                cs[p, tile] = rotate_rows(kept, (8 - turn[p]) & 7)

    slots_down = iota((SLOTS, 128), 0)
    wide = 2 if chunks % 2 == 0 else 1
    factors = (fac_a, fac_b)

    def spread_pair(pair):
        spread = jnp.concatenate(
            [jnp.where(group_of_e == v, es[pair], 0.0) for v in range(WINDOW // 8)], axis=0
        ).T
        for side in range(2):
            _, m = place(2 * pair + side)
            from_row = OWN * m - 8
            part = spread[SLOTS * side : SLOTS * side + SLOTS]
            here = (from_row + slots_down >= 0) & (from_row + slots_down < half)
            own_e = jnp.sum(jnp.where(here, part, 0.0), axis=0, keepdims=True)
            all_e = jnp.sum(part, axis=0, keepdims=True)
            rows_e_ref[side, 0] = jnp.broadcast_to(own_e, (8, 128))
            rows_e_ref[side, 1] = jnp.broadcast_to(all_e, (8, 128))

    def build(pair, side):
        tile = 2 * pair + side
        r, m = place(tile)
        own_e = rows_e_ref[side, 0]
        all_e = rows_e_ref[side, 1]
        at = tile_start(m) + lane8
        offset = at - begin_of(at, ends_of(len_ref, r))
        bands = []
        for p in range(2):
            bands.append(
                jnp.concatenate(
                    [jnp.where(group_of[p] == v, cs[p, tile], 0.0) for v in range(WINDOW // 8)], axis=0
                ).T
            )
        for k in range(TAPS):
            row_k = jnp.where((offset >= k) & (at >= 0), own_e, 0.0)
            if k > 0:
                row_k = pltpu.roll(row_k, 128 - k, 1)
            matrix = bands[k // 2][SLOTS * (k % 2) : SLOTS * (k % 2) + SLOTS]
            if k == 0:
                back = jnp.concatenate([jnp.where(sub8 < 2, all_e, matrix[0:8]), matrix[8:]], axis=0)
                high, low = split(back)
                mat[tile, :, 0:WINDOW] = high
                mat[tile, :, WINDOW:] = low
            matrix = jnp.concatenate([jnp.where(sub8 == 0, row_k, matrix[0:8]), matrix[8:]], axis=0)
            if k == 0:
                total = jnp.sum(matrix, axis=1, keepdims=True)
                tot[side] = jnp.broadcast_to(total, (SLOTS, 128))
            high, low = split(matrix)
            factors[side][SLOTS * k : SLOTS * (k + 1), 0:WINDOW] = high
            factors[side][SLOTS * k : SLOTS * (k + 1), WINDOW:] = low

    def apply(pair, side):
        tile = 2 * pair + side
        r, m = place(tile)
        start = pl.multiple_of(OWN * m + 8, 8)
        window = pl.multiple_of(2 * OWN * m, 16)
        factor = factors[side][...]
        total = tot[side]
        from_row = OWN * m - 8
        mine = [from_row + 8 * i + sub8 < half for i in range(SLOTS // 8)]
        for w in range(chunks // wide):
            x = xb[r, pl.ds(window, WINDOW), 128 * wide * w : 128 * wide * (w + 1)]
            mixed = lax.dot_general(
                factor,
                jnp.concatenate([x, x], axis=0),
                (((1,), (0,)), ((), ())),
                preferred_element_type=F32,
            )
            for i in range(wide):
                c = wide * w + i
                lanes = lanes_of(c)
                g = g32[r, c, pl.ds(start, SLOTS), :]
                parts = [
                    jnp.where(
                        sub8 == 0,
                        par_ref[5:6, lanes],
                        jnp.where((sub8 >= LEAD) & (from_row + sub8 >= 0), g[0:8], 0.0),
                    )
                ]
                for j in range(1, SLOTS // 8):
                    parts.append(jnp.where(mine[j], g[8 * j : 8 * j + 8], 0.0))
                g = jnp.concatenate(parts, axis=0)
                value = total * par_ref[4:5, lanes]
                for k in range(TAPS):
                    taken = mixed[SLOTS * k : SLOTS * (k + 1), lanes_of(i)]
                    value = value + taken * par_ref[k : k + 1, lanes]
                    acc[k, :, lanes] += jnp.sum((taken * g).reshape(SLOTS // 8, 8, 128), axis=0)
                acc[4, :, lanes] += jnp.sum((total * g).reshape(SLOTS // 8, 8, 128), axis=0)
                acc[5, :, lanes] += jnp.where(sub8 == 0, value[0:8], 0.0)
                top = carry_o[:, lanes] + jnp.where(sub8 < LEAD, 0.0, value[0:8])
                out32[r % 2, c, pl.ds(start, 8), :] = top
                out32[r % 2, c, pl.ds(start + 8, OWN - 8), :] = value[8:OWN]
                carry_o[:, lanes] = jnp.where(m < tiles - 1, value[OWN:], 0.0)

    def finish(r):
        for c in range(chunks):
            outb[r, :, lanes_of(c)] = out32[r % 2, c, PAD : PAD + half, :].astype(BF16)
        copy_out(r).start()

    spread_pair(0)
    build(0, 0)
    build(0, 1)

    def second_loop(i, _):
        for side in range(2):
            r, m = place(2 * i - 1 + side)

            @pl.when((m == 0) & (i > 0))
            def _():
                finish(r - 1)

        spread_pair(i + 1)
        for side in range(2):
            apply(i, side)
            build(i + 1, side)
        return 0

    lax.fori_loop(0, pairs - 1, second_loop, 0)
    apply(pairs - 1, 0)
    apply(pairs - 1, 1)
    for r in range(rows):
        if r * tiles > 2 * (pairs - 2):
            finish(r - 1)
    finish(rows - 1)
    for k in range(TAPS + 2):
        grad_ref[k : k + 1, :] = jnp.sum(acc[k], axis=0, keepdims=True)
    for r in range(rows):
        copy_out(r).wait()


def backward_kernel(shapes, r, base_ref, len_ref, mat, g32, par_ref, *refs):
    gin_hbm, dc, ginb, sems = refs[-4:]
    rows, length, half, features, tiles = shapes
    chunks = features // 128
    wide = 2 if chunks % 2 == 0 else 1
    base = base_ref[0]
    sub8 = iota((8, 128), 0)
    ends = ends_of(len_ref, r)

    for m in range(tiles):
        tile = r * tiles + m
        streamed = jnp.concatenate([mat[tile, :, 0:WINDOW].T, mat[tile, :, WINDOW:].T], axis=1)
        at = 2 * OWN * m
        for w in range(chunks // wide):
            held = []
            for i in range(wide):
                lanes = lanes_of(wide * w + i)
                scorer = par_ref[5:6, lanes]
                scorer_high = scorer.astype(BF16).astype(F32)
                g = g32[r, wide * w + i, OWN * m + 8 : OWN * m + 8 + SLOTS, :]
                top = jnp.where(
                    sub8 == 0, scorer_high, jnp.where(sub8 == 1, scorer - scorer_high, g[0:8])
                )
                held.append(jnp.concatenate([top, g[8:]], axis=0).astype(BF16))
            held = jnp.concatenate(held, axis=1)
            part = lax.dot_general(
                streamed,
                jnp.concatenate([held, held], axis=0),
                (((1,), (0,)), ((), ())),
                preferred_element_type=F32,
            )
            for i in range(wide):
                c = wide * w + i
                before = dc[c, at : at + PAD, :] if m > 0 else 0.0
                dc[c, at : at + PAD, :] = before + part[0:PAD, lanes_of(i)]
                dc[c, at + PAD : at + WINDOW, :] = part[PAD:, lanes_of(i)]

    def taps(i, _):
        at = pl.multiple_of(i * 16, 16)
        keeps = []
        for j in range(2):
            position = base + at + 8 * j + sub8
            remain = end_of(position, ends) - position
            keeps.append([remain > k for k in range(TAPS)])
        for c in range(chunks):
            parts = []
            for j in range(2):
                value = par_ref[0:1, lanes_of(c)] * dc[c, pl.ds(at + PAD + 8 * j, 8), :]
                for k in range(1, TAPS):
                    shifted = dc[c, pl.ds(at + PAD + 8 * j + k, 8), :]
                    value = value + par_ref[k : k + 1, lanes_of(c)] * jnp.where(keeps[j][k], shifted, 0.0)
                parts.append(value)
            ginb[pl.ds(at, 16), lanes_of(c)] = jnp.concatenate(parts, axis=0).astype(BF16)
        return 0

    pieces = 2
    copies = []
    for piece in range(pieces):
        size = length // pieces
        lax.fori_loop(piece * size // 16, (piece + 1) * size // 16, taps, 0)
        copies.append(
            pltpu.make_async_copy(
                ginb.at[pl.ds(piece * size, size), :],
                gin_hbm.at[r, pl.ds(piece * size, size), :],
                sems.at[piece],
            )
        )
        copies[-1].start()
    for copy in copies:
        copy.wait()


SMEM = pl.BlockSpec(memory_space=pltpu.SMEM)
VMEM = pl.BlockSpec(memory_space=pltpu.VMEM)
HBM = pl.BlockSpec(memory_space=pltpu.HBM)


def sizes_of(length, half):
    tiles = -(-(half + 3 + LEAD) // OWN)
    x_rows = 2 * OWN * (tiles - 1) + WINDOW
    g_rows = -(-(OWN * (tiles - 1) + 8 + SLOTS) // 16) * 16
    return tiles, x_rows, g_rows


def packed(inputs, cotangent):
    rows, _, features = inputs.shape
    part = jax.ShapeDtypeStruct((rows, PAD, features), BF16)
    return pl.pallas_call(
        pack_kernel,
        out_shape=(part, part),
        in_specs=[HBM, HBM],
        out_specs=(VMEM, VMEM),
        scratch_shapes=[pltpu.VMEM((rows, PAD, features), BF16)] * 4 + [pltpu.SemaphoreType.DMA((4,))],
        compiler_params=pltpu.CompilerParams(vmem_limit_bytes=60 * 1024 * 1024),
    )(inputs, cotangent)


def forward(base, lengths, inputs, cotangent, up, down, params):
    rows, length, features = inputs.shape
    half = cotangent.shape[1]
    chunks = features // 128
    tiles, x_rows, g_rows = sizes_of(length, half)
    count = rows * tiles
    shapes = (rows, length, half, features, tiles)
    return pl.pallas_call(
        functools.partial(forward_kernel, shapes),
        out_shape=(
            jax.ShapeDtypeStruct((rows, half, features), BF16),
            jax.ShapeDtypeStruct((count, SLOTS, 2 * WINDOW), BF16),
            jax.ShapeDtypeStruct((rows, chunks, g_rows, 128), F32),
            jax.ShapeDtypeStruct((TAPS + 2, features), F32),
        ),
        in_specs=[SMEM, SMEM, VMEM, VMEM, VMEM, VMEM, VMEM],
        out_specs=(HBM, VMEM, VMEM, VMEM),
        scratch_shapes=[
            pltpu.VMEM((rows, x_rows, features), BF16),
            pltpu.VMEM((2, chunks, WINDOW + 8, 128), F32),
            pltpu.VMEM((rows, chunks, x_rows, 128), BF16),
            pltpu.VMEM((rows, chunks, x_rows, 128), BF16),
            pltpu.VMEM((2 * SLOTS, WINDOW), F32),
            pltpu.VMEM((2, count // 2, 8, 128), F32),
            pltpu.VMEM((2, count, 8, 128), F32),
            pltpu.VMEM((count // 2, 8, 128), F32),
            pltpu.VMEM((TAPS * SLOTS, 2 * WINDOW), BF16),
            pltpu.VMEM((TAPS * SLOTS, 2 * WINDOW), BF16),
            pltpu.VMEM((2, SLOTS, 128), F32),
            pltpu.VMEM((2, 2, 8, 128), F32),
            pltpu.VMEM((2, chunks, g_rows, 128), F32),
            pltpu.VMEM((rows, half, features), BF16),
            pltpu.VMEM((8, features), F32),
            pltpu.VMEM((TAPS + 2, 8, features), F32),
            pltpu.SemaphoreType.DMA((rows,)),
        ],
        compiler_params=pltpu.CompilerParams(vmem_limit_bytes=40 * 1024 * 1024),
        cost_estimate=pl.CostEstimate(
            flops=2 * count * SLOTS * WINDOW * features * 12,
            bytes_accessed=8 * inputs.size,
            transcendentals=0,
        ),
    )(base, lengths, inputs, cotangent, up, down, params)


def backward(r, base, lengths, shape, matrices, padded, params, grown):
    rows, length, features = shape
    half = length // 2
    chunks = features // 128
    tiles, x_rows, g_rows = sizes_of(length, half)
    shapes = (rows, length, half, features, tiles)
    operands = [base, lengths, matrices, padded, params]
    in_specs = [SMEM, SMEM, VMEM, VMEM, VMEM]
    if grown is not None:
        operands.append(grown)
        in_specs.append(HBM)
    return pl.pallas_call(
        functools.partial(backward_kernel, shapes, r),
        out_shape=jax.ShapeDtypeStruct(shape, BF16),
        in_specs=in_specs,
        out_specs=HBM,
        scratch_shapes=[
            pltpu.VMEM((chunks, x_rows, 128), F32),
            pltpu.VMEM((length, features), BF16),
            pltpu.SemaphoreType.DMA((2,)),
        ],
        input_output_aliases={} if grown is None else {5: 0},
        compiler_params=pltpu.CompilerParams(vmem_limit_bytes=12 * 1024 * 1024),
        cost_estimate=pl.CostEstimate(
            flops=2 * tiles * SLOTS * WINDOW * features * 4,
            bytes_accessed=4 * length * features,
            transcendentals=0,
        ),
    )(*operands)


def adam_update(grads, weights, first_old, second_old):
    first_new = beta_one * first_old + (1.0 - beta_one) * grads
    second_new = beta_two * second_old + (1.0 - beta_two) * grads * grads
    first_hat = first_new / (1.0 - beta_one**STEP)
    second_hat = second_new / (1.0 - beta_two**STEP)
    updated = weights - learn_rate * (
        first_hat / (jnp.sqrt(second_hat) + adam_eps) + decay_rate * weights
    )
    return (updated, first_new, second_new)


def rounds_of(axes):
    rounds = []
    for axis in axes:
        count = lax.axis_size(axis)
        step = 1
        while step < count:
            rounds.append((axis, [(i, i ^ step) for i in range(count)]))
            step *= 2
    return rounds


def per_device(inputs, lengths, params, first_moment, second_moment, cotangent):
    rows_here, length_here, _ = inputs.shape
    send_up, send_down = packed(inputs, cotangent)
    up = passed_along(send_up, "group", 1)
    down = passed_along(send_down, "group", -1)
    base = (lax.axis_index("group") * length_here).astype(jnp.int32).reshape(1)
    output, matrices, padded, grad_params = forward(
        base, lengths, inputs, cotangent, up, down, params
    )

    def backward_row(row, matrices, grown):
        return backward(row, base, lengths, inputs.shape, matrices, padded, params, grown)

    grad_inputs = None
    row = 0
    for axis, exchange in rounds_of(("group", "rows")):
        received = lax.ppermute(grad_params, axis, exchange)
        if row < rows_here:
            matrices, grad_params = lax.optimization_barrier((matrices, grad_params))
            grad_inputs = backward_row(row, matrices, grad_inputs)
            row += 1
            received, grad_inputs = lax.optimization_barrier((received, grad_inputs))
        grad_params = grad_params + received
    while row < rows_here:
        grad_inputs = backward_row(row, matrices, grad_inputs)
        row += 1
    grad_norm = jnp.sqrt(jnp.sum(grad_params * grad_params))
    clip_scale = jnp.minimum(1.0, clip_limit / (grad_norm + 1e-06))
    new_params, new_first, new_second = adam_update(
        grad_params * clip_scale, params, first_moment, second_moment
    )
    return (output, grad_inputs, grad_norm, new_params, new_first, new_second)


def solution(mesh):
    in_specs = (P("rows", "group", None), P("rows", None), P(), P(), P(), P("rows", "group", None))
    out_specs = (P("rows", "group", None), P("rows", "group", None), P(), P(), P(), P())
    return jax.shard_map(
        per_device, mesh=mesh, in_specs=in_specs, out_specs=out_specs, check_vma=False
    )
```

time: 69 us -> 54.7 us (0.79)
  Pallas kernels: 37.2 us -> 29.1 us
  local copies, waits for them, and re-layouts: 8.19 us -> 1.43 us
  waiting for transfers between devices: 3.21 us -> 7.25 us
  starting transfers between devices: 15.9 us -> 12.8 us
    pallas_call x1, Pallas kernels: 22.7 us -> 15.5 us  [forward(): pl.pallas_call(functools.partial(forward_kernel, shapes), out_shape=(jax....]
    slice x4 -> x0, local copies, waits for them, and re-layouts: 3.46 us -> none  [the longest x2 1.71 us: per_device(): send_down = jnp.concatenate([inputs[:, :PAD - 3], cotangent[:, :3]], axis=1)]
    unnamed x14 -> x12, local copies, waits for them, and re-layouts: 4.73 us -> 1.43 us
    ppermute x2, waiting for transfers between devices: 0.91 us -> 4.19 us  [passed_along(): lax.ppermute(value, axis, [(source, source + steps) for source in range(i...]
    pallas_call x4, Pallas kernels: 14.5 us -> 11.6 us  [backward(): pl.pallas_call(functools.partial(backward_kernel, shapes, r), out_shape=j...]
    ppermute x5, starting transfers between devices: 11.6 us -> 9.18 us  [per_device(): received = lax.ppermute(grad_params, axis, exchange)]
    pallas_call x0 -> x1, Pallas kernels: none -> 1.94 us  [packed(): pl.pallas_call(pack_kernel, out_shape=(part, part), in_specs=[HBM, HBM],...]
    ppermute x5, waiting for transfers between devices: 2.3 us -> 3.05 us  [per_device(): received = lax.ppermute(grad_params, axis, exchange)]
  transfers between devices with their start and end apart: 7 -> 7, of which waited for: 2 -> 3; matrix products, arithmetic and copies ran while one was open for 3% -> 0% of each run, Pallas kernels for 21% -> 21%
where the time goes in v3:
time: 54.7 us; the launch traced here: 54.5 us
  Pallas kernels  29.1 us (53%)
  starting transfers between devices  12.8 us (23%)
  waiting for transfers between devices  7.25 us (13%)
  between operations  2.7 us (5%)
  local copies, waits for them, and re-layouts  1.43 us (3%)
  other arithmetic  1.27 us (2%)
    pallas_call x1, Pallas kernels, forward(): pl.pallas_call(functools.partial(forward_kernel, shapes), out_shape=(jax....  15.5 us
    pallas_call x4, Pallas kernels, backward(): pl.pallas_call(functools.partial(backward_kernel, shapes, r), out_shape=j...  11.6 us
    ppermute x5, starting transfers between devices, per_device(): received = lax.ppermute(grad_params, axis, exchange)  9.18 us
    ppermute x2, waiting for transfers between devices, passed_along(): lax.ppermute(value, axis, [(source, source + steps) for source in range(i...  4.19 us
    ppermute x2, starting transfers between devices, passed_along(): lax.ppermute(value, axis, [(source, source + steps) for source in range(i...  3.65 us
    ppermute x5, waiting for transfers between devices, per_device(): received = lax.ppermute(grad_params, axis, exchange)  3.05 us
    pallas_call x1, Pallas kernels, packed(): pl.pallas_call(pack_kernel, out_shape=(part, part), in_specs=[HBM, HBM],...  1.94 us
    unnamed x12, local copies, waits for them, and re-layouts  1.43 us
  transfers between devices with their start and end apart: 7, of which 3 were waited for; matrix products, arithmetic and copies ran while one was open for 0% of the time, Pallas kernels for 21%

profile of v3, /device:TPU:0, one launch (start us, length us, event | category | flops | bytes accessed | tf_op | source)
XLA Modules:
  0.0 54.5 jit_solution(15516740926949797367)
XLA Ops:
  0.6 0.0 copy-start
  0.6 0.0 copy-start.2
  0.7 0.0 copy-start.3
  0.7 1.9 %shard_map.109 = (bf16[4,16,768]{2,1,0:T(8,128)(2,1)}, bf16[4,16,768]{2,1,0:T(8,128)(2,1)}) custom-call(bf16[4,512,768]{2,1,0:T(8,128)(2,1)} %x_ref.1, bf16[4,256,768]{2,1,0:T(8,128)(2,1)} %g_ref.1), custom_call_target="tpu_custom_call" | custom-call | tf_op jit(solution)/shard_map/pallas_call | solution.py:540
  2.6 2.4 %collective-permute-start = (bf16[4,16,768]{2,1,0:T(8,128)(2,1)}, bf16[4,16,768]{2,1,0:T(8,128)(2,1)S(1)}, u32[]{:S(2)}, u32[]{:S(2)}) collective-permute-start(bf16[4,16,768]{2,1,0:T(8,128)(2,1)} %get-tuple-element.28), channel_id=1, source_target_pairs={{0,1},{1,2},{2,3},{4,5},{5,6},{6,7},{8,9},{9,10},{10,11},{12,13},{... | collective-permute-start | bytes 294920 | tf_op jit(solution)/shard_map/ppermute | solution.py:33
  5.0 1.3 %collective-permute-start.1 = (bf16[4,16,768]{2,1,0:T(8,128)(2,1)}, bf16[4,16,768]{2,1,0:T(8,128)(2,1)S(1)}, u32[]{:S(2)}, u32[]{:S(2)}) collective-permute-start(bf16[4,16,768]{2,1,0:T(8,128)(2,1)} %get-tuple-element.29), channel_id=1, source_target_pairs={{1,0},{2,1},{3,2},{5,4},{6,5},{7,6},{9,8},{10,9},{11,10},{13,12},{... | collective-permute-start | bytes 294920 | tf_op jit(solution)/shard_map/ppermute | solution.py:33
  6.3 0.0 collective-permute-done.up_ref
  6.3 4.2 %collective-permute-done.1.down_ref = bf16[4,16,768]{2,1,0:T(8,128)(2,1)S(1)} collective-permute-done((bf16[4,16,768]{2,1,0:T(8,128)(2,1)}, bf16[4,16,768]{2,1,0:T(8,128)(2,1)S(1)}, u32[]{:S(2)}, u32[]{:S(2)}) %collective-permute-start.1) | collective-permute-done | bytes 98336 | tf_op jit(solution)/shard_map/ppermute | solution.py:33
  10.5 0.0 copy-done
  10.5 0.0 copy-done.2
  10.5 0.0 copy-done.3
  10.5 0.0 copy-start.1
  10.5 1.4 %copy-done.1 = bf16[4,256,768]{2,1,0:T(8,128)(2,1)S(1)} copy-done((bf16[4,256,768]{2,1,0:T(8,128)(2,1)S(1)}, bf16[4,256,768]{2,1,0:T(8,128)(2,1)}, u32[]{:S(2)}) %copy-start.1) | copy-done | bytes 1572888
  11.9 15.5 %shard_map.110 = (bf16[4,256,768]{2,1,0:T(8,128)(2,1)}, bf16[20,64,256]{2,1,0:T(8,128)(2,1)S(1)}, f32[4,6,304,128]{3,2,1,0:T(8,128)S(1)}, f32[6,768]{1,0:T(8,128)S(1)}) custom-call(s32[1]{0:T(128)} %bitcast.base_ref, s32[4,4]{1,0:T(4,128)S(1)} %copy-done.3, bf16[4,512,768]{2,1,0:T(8,128)(2,1)S(1)} %copy-done, bf16[4,256,768]{2,1,0:T(8,128)(2,1)S(1)} %copy-done.1, ...), custom_call_target="tpu_custom_call" | custom-call | flops 3019898880 | bytes 12582912 | tf_op jit(solution)/shard_map/pallas_call | solution.py:557
  27.4 3.3 %collective-permute-start.2 = (f32[6,768]{1,0:T(8,128)S(1)}, f32[6,768]{1,0:T(8,128)S(1)}, u32[]{:S(2)}, u32[]{:S(2)}) collective-permute-start(f32[6,768]{1,0:T(8,128)S(1)} %get-tuple-element.34), channel_id=1, source_target_pairs={{0,1},{1,0},{2,3},{3,2},{4,5},{5,4},{6,7},{7,6},{8,9},{9,8},{10,11... | collective-permute-start | bytes 55304 | tf_op jit(solution)/shard_map/ppermute | solution.py:664
  30.7 2.9 %shard_map.111.refs_0_ = bf16[4,512,768]{2,1,0:T(8,128)(2,1)} custom-call(s32[1]{0:T(128)} %bitcast.base_ref, s32[4,4]{1,0:T(4,128)S(1)} %copy-done.3, bf16[20,64,256]{2,1,0:T(8,128)(2,1)S(1)} %get-tuple-element.45.mat, f32[4,6,304,128]{3,2,1,0:T(8,128)S(1)} %get-tuple-element.35.g32, f32[6,768]{1,0:T(8,128)S(1)} %copy-done.2), custom_call_target="tpu_custom_call" | custom-call | flops 251658240 | bytes 1572864 | tf_op jit(solution)/shard_map/pallas_call | solution.py:606
  33.7 0.0 collective-permute-done.2
  33.7 0.1 collective-permute-start.3
  33.8 2.9 %shard_map.112.refs_0_ = bf16[4,512,768]{2,1,0:T(8,128)(2,1)} custom-call(s32[1]{0:T(128)} %bitcast.base_ref, s32[4,4]{1,0:T(4,128)S(1)} %copy-done.3, bf16[20,64,256]{2,1,0:T(8,128)(2,1)S(1)} %get-tuple-element.45.mat, f32[4,6,304,128]{3,2,1,0:T(8,128)S(1)} %get-tuple-element.35.g32, f32[6,768]{1,0:T(8,128)S(1)} %copy-done.2, ...), custom_call_target="tpu_custom_call", output_to_operand_aliasing={{}: (5, {})} | custom-call | flops 251658240 | bytes 1572864 | tf_op jit(solution)/shard_map/pallas_call | solution.py:606
  36.7 0.9 %collective-permute-done.3 = f32[6,768]{1,0:T(8,128)S(1)} collective-permute-done((f32[6,768]{1,0:T(8,128)S(1)}, f32[6,768]{1,0:T(8,128)S(1)}, u32[]{:S(2)}, u32[]{:S(2)}) %collective-permute-start.3) | collective-permute-done | bytes 18464 | tf_op jit(solution)/shard_map/ppermute | solution.py:664
  37.6 1.5 %collective-permute-start.4 = (f32[6,768]{1,0:T(8,128)S(1)}, f32[6,768]{1,0:T(8,128)S(1)}, u32[]{:S(2)}, u32[]{:S(2)}) collective-permute-start(f32[6,768]{1,0:T(8,128)S(1)} %add.34), channel_id=1, source_target_pairs={{0,4},{4,0},{8,12},{12,8},{16,20},{20,16},{24,28},{28,24},{1,5},{5... | collective-permute-start | bytes 55304 | tf_op jit(solution)/shard_map/ppermute | solution.py:664
  39.1 2.9 %shard_map.113.refs_0_ = bf16[4,512,768]{2,1,0:T(8,128)(2,1)} custom-call(s32[1]{0:T(128)} %bitcast.base_ref, s32[4,4]{1,0:T(4,128)S(1)} %copy-done.3, bf16[20,64,256]{2,1,0:T(8,128)(2,1)S(1)} %get-tuple-element.45.mat, f32[4,6,304,128]{3,2,1,0:T(8,128)S(1)} %get-tuple-element.35.g32, f32[6,768]{1,0:T(8,128)S(1)} %copy-done.2, ...), custom_call_target="tpu_custom_call", output_to_operand_aliasing={{}: (5, {})} | custom-call | flops 251658240 | bytes 1572864 | tf_op jit(solution)/shard_map/pallas_call | solution.py:606
  42.0 0.0 collective-permute-done.4
  42.0 0.0 copy-start.4
  42.0 0.0 copy-start.5
  42.0 1.6 %collective-permute-start.5 = (f32[6,768]{1,0:T(8,128)S(1)}, f32[6,768]{1,0:T(8,128)S(1)}, u32[]{:S(2)}, u32[]{:S(2)}) collective-permute-start(f32[6,768]{1,0:T(8,128)S(1)} %add.35), channel_id=1, source_target_pairs={{0,8},{4,12},{8,0},{12,4},{16,24},{20,28},{24,16},{28,20},{1,9},{5... | collective-permute-start | bytes 55304 | tf_op jit(solution)/shard_map/ppermute | solution.py:664
  43.7 2.9 %shard_map.114 = bf16[4,512,768]{2,1,0:T(8,128)(2,1)} custom-call(s32[1]{0:T(128)} %bitcast.base_ref, s32[4,4]{1,0:T(4,128)S(1)} %copy-done.3, bf16[20,64,256]{2,1,0:T(8,128)(2,1)S(1)} %get-tuple-element.45.mat, f32[4,6,304,128]{3,2,1,0:T(8,128)S(1)} %get-tuple-element.35.g32, f32[6,768]{1,0:T(8,128)S(1)} %copy-done.2, ...), custom_call_target="tpu_custom_call", output_to_operand_aliasing={{}: (5, {})} | custom-call | flops 251658240 | bytes 1572864 | tf_op jit(solution)/shard_map/pallas_call | solution.py:606
  46.6 0.0 collective-permute-done.5
  46.6 2.6 %collective-permute-start.6 = (f32[6,768]{1,0:T(8,128)S(1)}, f32[6,768]{1,0:T(8,128)S(1)}, u32[]{:S(2)}, u32[]{:S(2)}) collective-permute-start(f32[6,768]{1,0:T(8,128)S(1)} %add.36), channel_id=1, source_target_pairs={{0,16},{4,20},{8,24},{12,28},{16,0},{20,4},{24,8},{28,12},{1,17},{... | collective-permute-start | bytes 55304 | tf_op jit(solution)/shard_map/ppermute | solution.py:664
  49.3 2.1 %collective-permute-done.6 = f32[6,768]{1,0:T(8,128)S(1)} collective-permute-done((f32[6,768]{1,0:T(8,128)S(1)}, f32[6,768]{1,0:T(8,128)S(1)}, u32[]{:S(2)}, u32[]{:S(2)}) %collective-permute-start.6) | collective-permute-done | bytes 18464 | tf_op jit(solution)/shard_map/ppermute | solution.py:664
  51.4 0.6 %multiply_reduce_fusion = (f32[]{:T(128)}, f32[6,768]{1,0:T(8,128)S(1)}) fusion(f32[6,768]{1,0:T(8,128)S(1)} %add.36, f32[6,768]{1,0:T(8,128)S(1)} %collective-permute-done.6), kind=kLoop, calls=%fused_computation.4 | loop fusion | flops 13823 | bytes 55300 | tf_op jit(solution)/shard_map/reduce_sum | solution.py:674
  52.8 0.0 copy-done.4
  52.8 0.0 copy-done.5
  52.8 0.6 %multiply_subtract_fusion = (f32[6,768]{1,0:T(8,128)}, f32[6,768]{1,0:T(8,128)}, f32[6,768]{1,0:T(8,128)}) fusion(f32[6,768]{1,0:T(8,128)S(1)} %copy-done.2, f32[6,768]{1,0:T(8,128)S(1)} %get-tuple-element.54, f32[]{:T(128)S(6)} %min.3, f32[6,768]{1,0:T(8,128)S(1)} %copy-done.4, f32[6,768]{1,0:T(8,128)S(1)} %copy-done.5), kind=kLoop, calls=%fused_computation.2 | loop fusion | flops 73728 | bytes 129028 | tf_op jit(solution)/shard_map/sub | solution.py:631
  (4 shorter events, 0.0 us)
Async XLA Ops:
  0.6 9.9 %copy-start = (bf16[4,512,768]{2,1,0:T(8,128)(2,1)S(1)}, bf16[4,512,768]{2,1,0:T(8,128)(2,1)}, u32[]{:S(2)}) copy-start(bf16[4,512,768]{2,1,0:T(8,128)(2,1)} %x_ref.1) | copy-start | bytes 9437188
  0.6 9.9 %copy-start.2 = (f32[6,768]{1,0:T(8,128)S(1)}, f32[6,768]{1,0:T(8,128)}, u32[]{:S(2)}) copy-start(f32[6,768]{1,0:T(8,128)} %par_ref.9) | copy-start | bytes 55300
  0.7 9.8 %copy-start.3 = (s32[4,4]{1,0:T(4,128)S(1)}, s32[4,4]{1,0:T(4,128)}, u32[]{:S(2)}) copy-start(s32[4,4]{1,0:T(4,128)} %len_ref.9) | copy-start | bytes 196
  2.6 3.7 %collective-permute-start = (bf16[4,16,768]{2,1,0:T(8,128)(2,1)}, bf16[4,16,768]{2,1,0:T(8,128)(2,1)S(1)}, u32[]{:S(2)}, u32[]{:S(2)}) collective-permute-start(bf16[4,16,768]{2,1,0:T(8,128)(2,1)} %get-tuple-element.28), channel_id=1, source_target_pairs={{0,1},{1,2},{2,3},{4,5},{5,6},{6,7},{8,9},{9,10},{10,11},{12,13},{... | collective-permute-start | bytes 294920 | tf_op jit(solution)/shard_map/ppermute | solution.py:33
  5.0 5.5 %collective-permute-start.1 = (bf16[4,16,768]{2,1,0:T(8,128)(2,1)}, bf16[4,16,768]{2,1,0:T(8,128)(2,1)S(1)}, u32[]{:S(2)}, u32[]{:S(2)}) collective-permute-start(bf16[4,16,768]{2,1,0:T(8,128)(2,1)} %get-tuple-element.29), channel_id=1, source_target_pairs={{1,0},{2,1},{3,2},{5,4},{6,5},{7,6},{9,8},{10,9},{11,10},{13,12},{... | collective-permute-start | bytes 294920 | tf_op jit(solution)/shard_map/ppermute | solution.py:33
  10.5 1.4 %copy-start.1 = (bf16[4,256,768]{2,1,0:T(8,128)(2,1)S(1)}, bf16[4,256,768]{2,1,0:T(8,128)(2,1)}, u32[]{:S(2)}) copy-start(bf16[4,256,768]{2,1,0:T(8,128)(2,1)} %g_ref.1) | copy-start | bytes 4718596
  27.4 6.2 %collective-permute-start.2 = (f32[6,768]{1,0:T(8,128)S(1)}, f32[6,768]{1,0:T(8,128)S(1)}, u32[]{:S(2)}, u32[]{:S(2)}) collective-permute-start(f32[6,768]{1,0:T(8,128)S(1)} %get-tuple-element.34), channel_id=1, source_target_pairs={{0,1},{1,0},{2,3},{3,2},{4,5},{5,4},{6,7},{7,6},{8,9},{9,8},{10,11... | collective-permute-start | bytes 55304 | tf_op jit(solution)/shard_map/ppermute | solution.py:664
  33.7 3.9 %collective-permute-start.3 = (f32[6,768]{1,0:T(8,128)S(1)}, f32[6,768]{1,0:T(8,128)S(1)}, u32[]{:S(2)}, u32[]{:S(2)}) collective-permute-start(f32[6,768]{1,0:T(8,128)S(1)} %add.33), channel_id=1, source_target_pairs={{0,2},{1,3},{2,0},{3,1},{4,6},{5,7},{6,4},{7,5},{8,10},{9,11},{10,... | collective-permute-start | bytes 55304 | tf_op jit(solution)/shard_map/ppermute | solution.py:664
  37.6 4.4 %collective-permute-start.4 = (f32[6,768]{1,0:T(8,128)S(1)}, f32[6,768]{1,0:T(8,128)S(1)}, u32[]{:S(2)}, u32[]{:S(2)}) collective-permute-start(f32[6,768]{1,0:T(8,128)S(1)} %add.34), channel_id=1, source_target_pairs={{0,4},{4,0},{8,12},{12,8},{16,20},{20,16},{24,28},{28,24},{1,5},{5... | collective-permute-start | bytes 55304 | tf_op jit(solution)/shard_map/ppermute | solution.py:664
  42.0 10.7 %copy-start.4 = (f32[6,768]{1,0:T(8,128)S(1)}, f32[6,768]{1,0:T(8,128)}, u32[]{:S(2)}) copy-start(f32[6,768]{1,0:T(8,128)} %param.9) | copy-start | bytes 55300
  42.0 10.7 %copy-start.5 = (f32[6,768]{1,0:T(8,128)S(1)}, f32[6,768]{1,0:T(8,128)}, u32[]{:S(2)}) copy-start(f32[6,768]{1,0:T(8,128)} %param.10) | copy-start | bytes 55300
  42.0 4.5 %collective-permute-start.5 = (f32[6,768]{1,0:T(8,128)S(1)}, f32[6,768]{1,0:T(8,128)S(1)}, u32[]{:S(2)}, u32[]{:S(2)}) collective-permute-start(f32[6,768]{1,0:T(8,128)S(1)} %add.35), channel_id=1, source_target_pairs={{0,8},{4,12},{8,0},{12,4},{16,24},{20,28},{24,16},{28,20},{1,9},{5... | collective-permute-start | bytes 55304 | tf_op jit(solution)/shard_map/ppermute | solution.py:664
  46.6 4.8 %collective-permute-start.6 = (f32[6,768]{1,0:T(8,128)S(1)}, f32[6,768]{1,0:T(8,128)S(1)}, u32[]{:S(2)}, u32[]{:S(2)}) collective-permute-start(f32[6,768]{1,0:T(8,128)S(1)} %add.36), channel_id=1, source_target_pairs={{0,16},{4,20},{8,24},{12,28},{16,0},{20,4},{24,8},{28,12},{1,17},{... | collective-permute-start | bytes 55304 | tf_op jit(solution)/shard_map/ppermute | solution.py:664

commit v4 on v3

--- a/solution.py
+++ b/solution.py
@@ -19,6 +19,7 @@
 
 TAPS = 4
 SLOTS = 64
+PACK_LIMIT = 50 * 1024 * 1024
 OWN = 56
 LEAD = 4
 WINDOW = 128
@@ -27,10 +28,10 @@
 BF16 = jnp.bfloat16
 
 
-def passed_along(value, axis, steps):
+def pairs_of(axis, first):
     count = lax.axis_size(axis)
-    initial, last = (max(0, -steps), min(count, count - steps))
-    return lax.ppermute(value, axis, [(source, source + steps) for source in range(initial, last)])
+    pairs = [(i, i + 1) for i in range(first, count - 1, 2)]
+    return pairs + [(j, i) for i, j in pairs]
 
 
 def rotate_rows(x, amount):
@@ -71,7 +72,7 @@
     return slice(128 * c, 128 * c + 128)
 
 
-def pack_kernel(x_hbm, g_hbm, up_ref, down_ref, x_first, x_last, g_first, g_last, sems):
+def pack_kernel(base_ref, x_hbm, g_hbm, near_ref, far_ref, x_first, x_last, g_first, g_last, sems):
     rows, length, features = x_hbm.shape
     half = g_hbm.shape[1]
     copies = [
@@ -82,14 +83,17 @@
     ]
     for copy in copies:
         copy.start()
+    even = (base_ref[0] // length) % 2 == 0
     sub = iota((PAD, features), 0)
     for copy in copies:
         copy.wait()
     for r in range(rows):
         moved = pltpu.roll(g_last[r].astype(F32), 2, 0)
-        up_ref[r] = jnp.where(sub < 2, moved, x_last[r].astype(F32)).astype(BF16)
+        last = jnp.where(sub < 2, moved, x_last[r].astype(F32))
         moved = pltpu.roll(g_first[r].astype(F32), PAD - 3, 0)
-        down_ref[r] = jnp.where(sub < PAD - 3, x_first[r].astype(F32), moved).astype(BF16)
+        first = jnp.where(sub < PAD - 3, x_first[r].astype(F32), moved)
+        near_ref[r] = jnp.where(even, last, first).astype(BF16)
+        far_ref[r] = jnp.where(even, first, last).astype(BF16)
 
 
 def forward_kernel(
@@ -98,8 +102,8 @@
     len_ref,
     x_ref,
     g_ref,
-    up_ref,
-    down_ref,
+    near_ref,
+    far_ref,
     par_ref,
     out_hbm,
     mat,
@@ -107,9 +111,13 @@
     grad_ref,
     xb,
     xf,
-    conv_high,
-    conv_low,
-    dots_ref,
+    conv_aa,
+    conv_ab,
+    conv_ba,
+    conv_bb,
+    edge,
+    dots_a,
+    dots_b,
     comp,
     cs,
     es,
@@ -128,7 +136,6 @@
     pairs = count // 2
     chunks = features // 128
     base = base_ref[0]
-    padded = xb.shape[1]
 
     def copy_out(r):
         return pltpu.make_async_copy(outb.at[r], out_hbm.at[r], sems.at[r])
@@ -154,7 +161,7 @@
     acc[...] = jnp.zeros_like(acc)
     carry_o[...] = jnp.zeros_like(carry_o)
 
-    def convolve(r, at, side, where, ends):
+    def convolve(r, at, side, where, ends, place_high, place_low):
         keeps = []
         for j in range(2):
             position = base - PAD + at + 8 * j + sub8
@@ -170,21 +177,26 @@
                     value = value + par_ref[k : k + 1, lanes_of(c)] * jnp.where(keeps[j][k], shifted, 0.0)
                 parts.append(value)
             high, low = split(jnp.concatenate(parts, axis=0))
-            conv_high[r, c, pl.ds(at, 16), :] = high
-            conv_low[r, c, pl.ds(at, 16), :] = low
+            for ref, *index in place_high(c):
+                ref[(*index, slice(None))] = high
+            for ref, *index in place_low(c):
+                ref[(*index, slice(None))] = low
 
     subd = iota((8, features), 0)
+    even = (base // length) % 2 == 0
     for r in range(rows):
-        up = up_ref[r]
-        down = down_ref[r]
-        xb[r, 0:PAD, :] = up
-        xb[r, PAD + length : 2 * PAD + length, :] = down
-        rest = padded - 2 * PAD - length
+        near = near_ref[r].astype(F32)
+        far = far_ref[r].astype(F32)
+        up = jnp.where(even, far, near)
+        down = jnp.where(even, near, far)
+        xb[r, 0:PAD, :] = up.astype(BF16)
+        xb[r, PAD + length : 2 * PAD + length, :] = down.astype(BF16)
+        rest = xb.shape[1] - 2 * PAD - length
         if rest > 0:
             xb[r, 2 * PAD + length :, :] = jnp.zeros((rest, features), BF16)
         xb[r, PAD : PAD + length, :] = x_ref[r]
-        before = jnp.where(subd >= 6, pltpu.roll(up.astype(F32)[0:8], 6, 0), 0.0)
-        after = jnp.where(subd < 3, pltpu.roll(down.astype(F32)[8:16], 3, 0), 0.0)
+        before = jnp.where(subd >= 6, pltpu.roll(up[0:8], 6, 0), 0.0)
+        after = jnp.where(subd < 3, pltpu.roll(down[8:16], 3, 0), 0.0)
         rest = g32.shape[2] - PAD - half - 8
         for c in range(chunks):
             g32[r, c, 8:16, :] = before[:, lanes_of(c)]
@@ -193,51 +205,71 @@
             g32[r, c, PAD + half + 8 :, :] = jnp.zeros((rest, 128), F32)
         for c in range(chunks):
             xf[r % 2, c, 0:8, :] = jnp.zeros((8, 128), F32)
-            xf[r % 2, c, 8:24, :] = up[:, lanes_of(c)].astype(F32)
-        convolve(r, 0, r % 2, 8, ends_of(len_ref, r))
+            xf[r % 2, c, 8:24, :] = up[:, lanes_of(c)]
+        convolve(
+            r,
+            0,
+            r % 2,
+            8,
+            ends_of(len_ref, r),
+            lambda c: [(edge, count + r, c, slice(0, 16))],
+            lambda c: [(edge, count + r, c, slice(16, 32))],
+        )
 
     scorer_high = [par_ref[5:6, lanes_of(c)].astype(BF16).astype(F32) for c in range(chunks)]
     scorer_low = [par_ref[5:6, lanes_of(c)] - scorer_high[c] for c in range(chunks)]
 
-    def convolve_pair(pair):
+    convs = ((conv_aa, conv_ab), (conv_ba, conv_bb))
+    dots_refs = (dots_a, dots_b)
+
+    def convolve_pair(pair, parity):
         for side in range(2):
-            r, m = place(2 * pair + side)
+            tile = 2 * pair + side
+            r, m = place(tile)
             ends = ends_of(len_ref, r)
             at = pl.multiple_of(2 * OWN * m, 16)
+            conv = convs[parity][side]
+            source = jnp.where(m == 0, count + r, tile - 1)
             for c in range(chunks):
-                xf[side, c, 8 : 8 + WINDOW, :] = xb[r, pl.ds(at, WINDOW), lanes_of(c)].astype(F32)
+                conv[c, 0:16, :] = edge[source, c, 0:16, :]
+                conv[c, WINDOW : WINDOW + 16, :] = edge[source, c, 16:32, :]
+                xf[2 * parity + side, c, 8 : 8 + WINDOW, :] = xb[r, pl.ds(at, WINDOW), lanes_of(c)].astype(F32)
             for b in range(1, WINDOW // 16):
-                convolve(r, pl.multiple_of(at + 16 * b, 16), side, 8 + 16 * b, ends)
-
-    def multiply_pair(pair):
+                last = b == WINDOW // 16 - 1
+                convolve(
+                    r,
+                    at + 16 * b,
+                    2 * parity + side,
+                    8 + 16 * b,
+                    ends,
+                    lambda c: [(conv, c, slice(16 * b, 16 * b + 16))]
+                    + ([(edge, tile, c, slice(0, 16))] if last else []),
+                    lambda c: [(conv, c, slice(WINDOW + 16 * b, WINDOW + 16 * b + 16))]
+                    + ([(edge, tile, c, slice(16, 32))] if last else []),
+                )
+
+    def multiply_pair(pair, parity):
         for side in range(2):
             r, m = place(2 * pair + side)
             start = pl.multiple_of(OWN * m + 8, 8)
-            at = pl.multiple_of(2 * OWN * m, 16)
             streamed, held = [], []
             for c in range(chunks):
                 g = g32[r, c, pl.ds(start, SLOTS), :]
                 top = jnp.where(sub8 == 0, scorer_high[c], jnp.where(sub8 == 1, scorer_low[c], g[0:8]))
                 streamed.append(jnp.concatenate([top, g[8:]], axis=0).astype(BF16))
-                held.append(
-                    jnp.concatenate(
-                        [
-                            conv_high[r, c, pl.ds(at, WINDOW), :],
-                            conv_low[r, c, pl.ds(at, WINDOW), :],
-                        ],
-                        axis=0,
-                    )
-                )
+                held.append(convs[parity][side][c])
             product = lax.dot_general(
                 jnp.concatenate(streamed, axis=1),
                 jnp.concatenate(held, axis=1),
                 (((1,), (1,)), ((), ())),
                 preferred_element_type=F32,
             )
-            dots_ref[SLOTS * side : SLOTS * side + SLOTS, :] = product[:, :WINDOW] + product[:, WINDOW:]
-
-    def extract_pair(pair):
-        dots = dots_ref[...]
+            dots_refs[parity][SLOTS * side : SLOTS * side + SLOTS, :] = (
+                product[:, :WINDOW] + product[:, WINDOW:]
+            )
+
+    def extract_pair(pair, parity):
+        dots = dots_refs[parity][...]
         scores = jnp.concatenate(
             [
                 jnp.broadcast_to(dots[i : i + 1] + dots[i + 1 : i + 2], (SLOTS, WINDOW))
@@ -255,20 +287,20 @@
         comp[0, pair] = banded
         comp[1, pair] = scored
 
-    convolve_pair(0)
-    multiply_pair(0)
-    convolve_pair(1)
+    dots_b[...] = jnp.zeros_like(dots_b)
+    convolve_pair(0, 0)
 
     def first_loop(i, _):
-        extract_pair(i - 1)
-        multiply_pair(i)
-        convolve_pair(i + 1)
+        extract_pair(jnp.maximum(2 * i - 1, 0), 1)
+        multiply_pair(2 * i, 0)
+        convolve_pair(2 * i + 1, 1)
+        extract_pair(2 * i, 0)
+        multiply_pair(2 * i + 1, 1)
+        convolve_pair(jnp.minimum(2 * i + 2, pairs - 1), 0)
         return 0
 
-    lax.fori_loop(1, pairs - 1, first_loop, 0)
-    extract_pair(pairs - 2)
-    multiply_pair(pairs - 1)
-    extract_pair(pairs - 1)
+    lax.fori_loop(0, pairs // 2, first_loop, 0)
+    extract_pair(pairs - 1, 1)
 
     ends = [ends_of(len_ref, r) for r in range(rows)]
     for pair in range(pairs):
@@ -487,29 +519,45 @@
                 dc[c, at : at + PAD, :] = before + part[0:PAD, lanes_of(i)]
                 dc[c, at + PAD : at + WINDOW, :] = part[PAD:, lanes_of(i)]
 
-    def taps(i, _):
-        at = pl.multiple_of(i * 16, 16)
+    def taps_at(at, masked):
         keeps = []
-        for j in range(2):
-            position = base + at + 8 * j + sub8
-            remain = end_of(position, ends) - position
-            keeps.append([remain > k for k in range(TAPS)])
+        if masked:
+            for j in range(4):
+                position = base + at + 8 * j + sub8
+                remain = end_of(position, ends) - position
+                keeps.append([remain > k for k in range(TAPS)])
         for c in range(chunks):
             parts = []
-            for j in range(2):
+            for j in range(4):
                 value = par_ref[0:1, lanes_of(c)] * dc[c, pl.ds(at + PAD + 8 * j, 8), :]
                 for k in range(1, TAPS):
                     shifted = dc[c, pl.ds(at + PAD + 8 * j + k, 8), :]
-                    value = value + par_ref[k : k + 1, lanes_of(c)] * jnp.where(keeps[j][k], shifted, 0.0)
+                    if masked:
+                        shifted = jnp.where(keeps[j][k], shifted, 0.0)
+                    value = value + par_ref[k : k + 1, lanes_of(c)] * shifted
                 parts.append(value)
-            ginb[pl.ds(at, 16), lanes_of(c)] = jnp.concatenate(parts, axis=0).astype(BF16)
+            ginb[pl.ds(at, 32), lanes_of(c)] = jnp.concatenate(parts, axis=0).astype(BF16)
+
+    def taps(i, _):
+        at = pl.multiple_of(i * 32, 32)
+        reach = [(end > base + at) & (end <= base + at + 32 + TAPS - 2) for end in ends]
+        crosses = functools.reduce(jnp.logical_or, reach)
+
+        @pl.when(crosses)
+        def _():
+            taps_at(at, True)
+
+        @pl.when(jnp.logical_not(crosses))
+        def _():
+            taps_at(at, False)
+
         return 0
 
     pieces = 2
     copies = []
     for piece in range(pieces):
         size = length // pieces
-        lax.fori_loop(piece * size // 16, (piece + 1) * size // 16, taps, 0)
+        lax.fori_loop(piece * size // 32, (piece + 1) * size // 32, taps, 0)
         copies.append(
             pltpu.make_async_copy(
                 ginb.at[pl.ds(piece * size, size), :],
@@ -534,22 +582,22 @@
     return tiles, x_rows, g_rows
 
 
-def packed(inputs, cotangent):
+def packed(base, inputs, cotangent):
     rows, _, features = inputs.shape
     part = jax.ShapeDtypeStruct((rows, PAD, features), BF16)
     return pl.pallas_call(
         pack_kernel,
         out_shape=(part, part),
-        in_specs=[HBM, HBM],
+        in_specs=[SMEM, HBM, HBM],
         out_specs=(VMEM, VMEM),
         scratch_shapes=[pltpu.VMEM((rows, PAD, features), BF16)] * 4 + [pltpu.SemaphoreType.DMA((4,))],
-        compiler_params=pltpu.CompilerParams(vmem_limit_bytes=60 * 1024 * 1024),
-    )(inputs, cotangent)
-
-
-def forward(base, lengths, inputs, cotangent, up, down, params):
-    rows, length, features = inputs.shape
-    half = cotangent.shape[1]
+        compiler_params=pltpu.CompilerParams(vmem_limit_bytes=PACK_LIMIT),
+    )(base, inputs, cotangent)
+
+
+def forward(base, lengths, inputs, cotangent, near, far, params):
+    rows, half, features = cotangent.shape
+    length = 2 * half
     chunks = features // 128
     tiles, x_rows, g_rows = sizes_of(length, half)
     count = rows * tiles
@@ -566,9 +614,13 @@
         out_specs=(HBM, VMEM, VMEM, VMEM),
         scratch_shapes=[
             pltpu.VMEM((rows, x_rows, features), BF16),
-            pltpu.VMEM((2, chunks, WINDOW + 8, 128), F32),
-            pltpu.VMEM((rows, chunks, x_rows, 128), BF16),
-            pltpu.VMEM((rows, chunks, x_rows, 128), BF16),
+            pltpu.VMEM((4, chunks, WINDOW + 8, 128), F32),
+            pltpu.VMEM((chunks, 2 * WINDOW, 128), BF16),
+            pltpu.VMEM((chunks, 2 * WINDOW, 128), BF16),
+            pltpu.VMEM((chunks, 2 * WINDOW, 128), BF16),
+            pltpu.VMEM((chunks, 2 * WINDOW, 128), BF16),
+            pltpu.VMEM((count + rows, chunks, 32, 128), BF16),
+            pltpu.VMEM((2 * SLOTS, WINDOW), F32),
             pltpu.VMEM((2 * SLOTS, WINDOW), F32),
             pltpu.VMEM((2, count // 2, 8, 128), F32),
             pltpu.VMEM((2, count, 8, 128), F32),
@@ -589,7 +641,7 @@
             bytes_accessed=8 * inputs.size,
             transcendentals=0,
         ),
-    )(base, lengths, inputs, cotangent, up, down, params)
+    )(base, lengths, inputs, cotangent, near, far, params)
 
 
 def backward(r, base, lengths, shape, matrices, padded, params, grown):
@@ -647,12 +699,12 @@
 
 def per_device(inputs, lengths, params, first_moment, second_moment, cotangent):
     rows_here, length_here, _ = inputs.shape
-    send_up, send_down = packed(inputs, cotangent)
-    up = passed_along(send_up, "group", 1)
-    down = passed_along(send_down, "group", -1)
     base = (lax.axis_index("group") * length_here).astype(jnp.int32).reshape(1)
+    near, far = packed(base, inputs, cotangent)
+    far = lax.ppermute(far, "group", pairs_of("group", 1))
+    near = lax.ppermute(near, "group", pairs_of("group", 0))
     output, matrices, padded, grad_params = forward(
-        base, lengths, inputs, cotangent, up, down, params
+        base, lengths, inputs, cotangent, near, far, params
     )
 
     def backward_row(row, matrices, grown):

time: 54.7 us -> 49.5 us (0.905)
  waiting for transfers between devices: 7.25 us -> 2.44 us
  Pallas kernels: 29.1 us -> 26.6 us
  starting transfers between devices: 12.8 us -> 14.7 us
    ppermute x5, starting transfers between devices: 9.18 us -> 13.5 us  [per_device(): received = lax.ppermute(grad_params, axis, exchange)]
    ppermute x2, waiting for transfers between devices: 4.19 us -> 0.28 us  [the longest x1 0.28 us: per_device(): near = lax.ppermute(near, 'group', pairs_of('group', 0))]
    ppermute x2, starting transfers between devices: 3.65 us -> 1.17 us  [the longest x1 0.65 us: per_device(): far = lax.ppermute(far, 'group', pairs_of('group', 1))]
    ppermute x5, waiting for transfers between devices: 3.05 us -> 2.15 us  [per_device(): received = lax.ppermute(grad_params, axis, exchange)]
    pallas_call x1, Pallas kernels: 1.94 us -> 1.08 us  [packed(): pl.pallas_call(pack_kernel, out_shape=(part, part), in_specs=[SMEM, HBM,...]
    pallas_call x4, Pallas kernels: 11.6 us -> 10.8 us  [backward(): pl.pallas_call(functools.partial(backward_kernel, shapes, r), out_shape=j...]
    pallas_call x1, Pallas kernels: 15.5 us -> 14.8 us  [forward(): pl.pallas_call(functools.partial(forward_kernel, shapes), out_shape=(jax....]
  transfers between devices with their start and end apart: 7 -> 7, of which waited for: 3 -> 2; matrix products, arithmetic and copies ran while one was open for 0% -> 0% of each run, Pallas kernels for 21% -> 22%
where the time goes in v4:
time: 49.5 us; the launch traced here: 49.3 us
  Pallas kernels  26.6 us (54%)
  starting transfers between devices  14.7 us (30%)
  between operations  2.68 us (5%)
  waiting for transfers between devices  2.44 us (5%)
  local copies, waits for them, and re-layouts  1.58 us (3%)
  other arithmetic  1.27 us (3%)
    pallas_call x1, Pallas kernels, forward(): pl.pallas_call(functools.partial(forward_kernel, shapes), out_shape=(jax....  14.8 us
    ppermute x5, starting transfers between devices, per_device(): received = lax.ppermute(grad_params, axis, exchange)  13.5 us
    pallas_call x4, Pallas kernels, backward(): pl.pallas_call(functools.partial(backward_kernel, shapes, r), out_shape=j...  10.8 us
    ppermute x5, waiting for transfers between devices, per_device(): received = lax.ppermute(grad_params, axis, exchange)  2.15 us
    unnamed x12, local copies, waits for them, and re-layouts  1.58 us
    pallas_call x1, Pallas kernels, packed(): pl.pallas_call(pack_kernel, out_shape=(part, part), in_specs=[SMEM, HBM,...  1.08 us
  transfers between devices with their start and end apart: 7, of which 2 were waited for; matrix products, arithmetic and copies ran while one was open for 0% of the time, Pallas kernels for 22%

profile of v4, /device:TPU:0, one launch (start us, length us, event | category | flops | bytes accessed | tf_op | source)
XLA Modules:
  0.0 49.3 jit_solution(14341545578318658373)
XLA Ops:
  0.6 0.0 copy-start
  0.6 0.0 copy-start.1
  0.7 1.5 %copy-done.1 = bf16[4,256,768]{2,1,0:T(8,128)(2,1)S(1)} copy-done((bf16[4,256,768]{2,1,0:T(8,128)(2,1)S(1)}, bf16[4,256,768]{2,1,0:T(8,128)(2,1)}, u32[]{:S(2)}) %copy-start.1) | copy-done | bytes 1572888
  2.2 0.0 copy-start.2
  2.2 0.0 copy-start.3
  2.2 1.1 %shard_map.109 = (bf16[4,16,768]{2,1,0:T(8,128)(2,1)S(1)}, bf16[4,16,768]{2,1,0:T(8,128)(2,1)S(1)}) custom-call(s32[1]{0:T(128)} %bitcast.base_ref, bf16[4,512,768]{2,1,0:T(8,128)(2,1)} %x_ref.1, bf16[4,256,768]{2,1,0:T(8,128)(2,1)S(1)} %copy-done.1), custom_call_target="tpu_custom_call" | custom-call | tf_op jit(solution)/shard_map/pallas_call | solution.py:588
  3.3 0.5 %collective-permute-start = (bf16[4,16,768]{2,1,0:T(8,128)(2,1)S(1)}, bf16[4,16,768]{2,1,0:T(8,128)(2,1)S(1)}, u32[]{:S(2)}, u32[]{:S(2)}) collective-permute-start(bf16[4,16,768]{2,1,0:T(8,128)(2,1)S(1)} %get-tuple-element.28), channel_id=1, source_target_pairs={{0,1},{2,3},{1,0},{3,2},{4,5},{6,7},{5,4},{7,6},{8,9},{10,11},{9,8... | collective-permute-start | bytes 294920 | tf_op jit(solution)/shard_map/ppermute | solution.py:705
  3.8 0.7 %collective-permute-start.1 = (bf16[4,16,768]{2,1,0:T(8,128)(2,1)S(1)}, bf16[4,16,768]{2,1,0:T(8,128)(2,1)S(1)}, u32[]{:S(2)}, u32[]{:S(2)}) collective-permute-start(bf16[4,16,768]{2,1,0:T(8,128)(2,1)S(1)} %get-tuple-element.29), channel_id=1, source_target_pairs={{1,2},{2,1},{5,6},{6,5},{9,10},{10,9},{13,14},{14,13},{17,18},{18,... | collective-permute-start | bytes 294920 | tf_op jit(solution)/shard_map/ppermute | solution.py:704
  4.5 0.3 collective-permute-done.near_ref
  4.8 0.0 collective-permute-done.1.far_ref
  4.8 0.0 copy-done
  4.8 0.0 copy-done.2
  4.8 0.0 copy-done.3
  4.8 14.8 %shard_map.110 = (bf16[4,256,768]{2,1,0:T(8,128)(2,1)}, bf16[20,64,256]{2,1,0:T(8,128)(2,1)S(1)}, f32[4,6,304,128]{3,2,1,0:T(8,128)S(1)}, f32[6,768]{1,0:T(8,128)S(1)}) custom-call(s32[1]{0:T(128)} %bitcast.base_ref, s32[4,4]{1,0:T(4,128)S(1)} %copy-done.3, bf16[4,512,768]{2,1,0:T(8,128)(2,1)S(1)} %copy-done, bf16[4,256,768]{2,1,0:T(8,128)(2,1)S(1)} %copy-done.1, ...), custom_call_target="tpu_custom_call" | custom-call | flops 3019898880 | bytes 12582912 | tf_op jit(solution)/shard_map/pallas_call | solution.py:605
  19.6 5.9 %collective-permute-start.2 = (f32[6,768]{1,0:T(8,128)S(1)}, f32[6,768]{1,0:T(8,128)S(1)}, u32[]{:S(2)}, u32[]{:S(2)}) collective-permute-start(f32[6,768]{1,0:T(8,128)S(1)} %get-tuple-element.34), channel_id=1, source_target_pairs={{0,1},{1,0},{2,3},{3,2},{4,5},{5,4},{6,7},{7,6},{8,9},{9,8},{10,11... | collective-permute-start | bytes 55304 | tf_op jit(solution)/shard_map/ppermute | solution.py:716
  25.5 2.7 %shard_map.111.refs_0_ = bf16[4,512,768]{2,1,0:T(8,128)(2,1)} custom-call(s32[1]{0:T(128)} %bitcast.base_ref, s32[4,4]{1,0:T(4,128)S(1)} %copy-done.3, bf16[20,64,256]{2,1,0:T(8,128)(2,1)S(1)} %get-tuple-element.45.mat, f32[4,6,304,128]{3,2,1,0:T(8,128)S(1)} %get-tuple-element.35.g32, f32[6,768]{1,0:T(8,128)S(1)} %copy-done.2), custom_call_target="tpu_custom_call" | custom-call | flops 251658240 | bytes 1572864 | tf_op jit(solution)/shard_map/pallas_call | solution.py:658
  28.2 0.0 collective-permute-done.2
  28.2 1.7 %collective-permute-start.3 = (f32[6,768]{1,0:T(8,128)S(1)}, f32[6,768]{1,0:T(8,128)S(1)}, u32[]{:S(2)}, u32[]{:S(2)}) collective-permute-start(f32[6,768]{1,0:T(8,128)S(1)} %add.33), channel_id=1, source_target_pairs={{0,2},{1,3},{2,0},{3,1},{4,6},{5,7},{6,4},{7,5},{8,10},{9,11},{10,... | collective-permute-start | bytes 55304 | tf_op jit(solution)/shard_map/ppermute | solution.py:716
  29.9 2.7 %shard_map.112.refs_0_ = bf16[4,512,768]{2,1,0:T(8,128)(2,1)} custom-call(s32[1]{0:T(128)} %bitcast.base_ref, s32[4,4]{1,0:T(4,128)S(1)} %copy-done.3, bf16[20,64,256]{2,1,0:T(8,128)(2,1)S(1)} %get-tuple-element.45.mat, f32[4,6,304,128]{3,2,1,0:T(8,128)S(1)} %get-tuple-element.35.g32, f32[6,768]{1,0:T(8,128)S(1)} %copy-done.2, ...), custom_call_target="tpu_custom_call", output_to_operand_aliasing={{}: (5, {})} | custom-call | flops 251658240 | bytes 1572864 | tf_op jit(solution)/shard_map/pallas_call | solution.py:658
  32.6 0.0 collective-permute-done.3
  32.6 1.6 %collective-permute-start.4 = (f32[6,768]{1,0:T(8,128)S(1)}, f32[6,768]{1,0:T(8,128)S(1)}, u32[]{:S(2)}, u32[]{:S(2)}) collective-permute-start(f32[6,768]{1,0:T(8,128)S(1)} %add.34), channel_id=1, source_target_pairs={{0,4},{4,0},{8,12},{12,8},{16,20},{20,16},{24,28},{28,24},{1,5},{5... | collective-permute-start | bytes 55304 | tf_op jit(solution)/shard_map/ppermute | solution.py:716
  34.3 2.7 %shard_map.113.refs_0_ = bf16[4,512,768]{2,1,0:T(8,128)(2,1)} custom-call(s32[1]{0:T(128)} %bitcast.base_ref, s32[4,4]{1,0:T(4,128)S(1)} %copy-done.3, bf16[20,64,256]{2,1,0:T(8,128)(2,1)S(1)} %get-tuple-element.45.mat, f32[4,6,304,128]{3,2,1,0:T(8,128)S(1)} %get-tuple-element.35.g32, f32[6,768]{1,0:T(8,128)S(1)} %copy-done.2, ...), custom_call_target="tpu_custom_call", output_to_operand_aliasing={{}: (5, {})} | custom-call | flops 251658240 | bytes 1572864 | tf_op jit(solution)/shard_map/pallas_call | solution.py:658
  37.0 0.0 collective-permute-done.4
  37.0 0.0 copy-start.4
  37.0 0.0 copy-start.5
  37.0 1.6 %collective-permute-start.5 = (f32[6,768]{1,0:T(8,128)S(1)}, f32[6,768]{1,0:T(8,128)S(1)}, u32[]{:S(2)}, u32[]{:S(2)}) collective-permute-start(f32[6,768]{1,0:T(8,128)S(1)} %add.35), channel_id=1, source_target_pairs={{0,8},{4,12},{8,0},{12,4},{16,24},{20,28},{24,16},{28,20},{1,9},{5... | collective-permute-start | bytes 55304 | tf_op jit(solution)/shard_map/ppermute | solution.py:716
  38.7 2.7 %shard_map.114 = bf16[4,512,768]{2,1,0:T(8,128)(2,1)} custom-call(s32[1]{0:T(128)} %bitcast.base_ref, s32[4,4]{1,0:T(4,128)S(1)} %copy-done.3, bf16[20,64,256]{2,1,0:T(8,128)(2,1)S(1)} %get-tuple-element.45.mat, f32[4,6,304,128]{3,2,1,0:T(8,128)S(1)} %get-tuple-element.35.g32, f32[6,768]{1,0:T(8,128)S(1)} %copy-done.2, ...), custom_call_target="tpu_custom_call", output_to_operand_aliasing={{}: (5, {})} | custom-call | flops 251658240 | bytes 1572864 | tf_op jit(solution)/shard_map/pallas_call | solution.py:658
  41.4 0.0 collective-permute-done.5
  41.4 2.6 %collective-permute-start.6 = (f32[6,768]{1,0:T(8,128)S(1)}, f32[6,768]{1,0:T(8,128)S(1)}, u32[]{:S(2)}, u32[]{:S(2)}) collective-permute-start(f32[6,768]{1,0:T(8,128)S(1)} %add.36), channel_id=1, source_target_pairs={{0,16},{4,20},{8,24},{12,28},{16,0},{20,4},{24,8},{28,12},{1,17},{... | collective-permute-start | bytes 55304 | tf_op jit(solution)/shard_map/ppermute | solution.py:716
  44.0 2.1 %collective-permute-done.6 = f32[6,768]{1,0:T(8,128)S(1)} collective-permute-done((f32[6,768]{1,0:T(8,128)S(1)}, f32[6,768]{1,0:T(8,128)S(1)}, u32[]{:S(2)}, u32[]{:S(2)}) %collective-permute-start.6) | collective-permute-done | bytes 18464 | tf_op jit(solution)/shard_map/ppermute | solution.py:716
  46.2 0.6 %multiply_reduce_fusion = (f32[]{:T(128)}, f32[6,768]{1,0:T(8,128)S(1)}) fusion(f32[6,768]{1,0:T(8,128)S(1)} %add.36, f32[6,768]{1,0:T(8,128)S(1)} %collective-permute-done.6), kind=kLoop, calls=%fused_computation.4 | loop fusion | flops 13823 | bytes 55300 | tf_op jit(solution)/shard_map/reduce_sum | solution.py:726
  47.5 0.0 copy-done.4
  47.5 0.0 copy-done.5
  47.5 0.6 %multiply_subtract_fusion = (f32[6,768]{1,0:T(8,128)}, f32[6,768]{1,0:T(8,128)}, f32[6,768]{1,0:T(8,128)}) fusion(f32[6,768]{1,0:T(8,128)S(1)} %copy-done.2, f32[6,768]{1,0:T(8,128)S(1)} %get-tuple-element.54, f32[]{:T(128)S(6)} %min.3, f32[6,768]{1,0:T(8,128)S(1)} %copy-done.4, f32[6,768]{1,0:T(8,128)S(1)} %copy-done.5), kind=kLoop, calls=%fused_computation.2 | loop fusion | flops 73728 | bytes 129028 | tf_op jit(solution)/shard_map/sub | solution.py:683
  (4 shorter events, 0.0 us)
Async XLA Ops:
  0.6 4.1 %copy-start = (bf16[4,512,768]{2,1,0:T(8,128)(2,1)S(1)}, bf16[4,512,768]{2,1,0:T(8,128)(2,1)}, u32[]{:S(2)}) copy-start(bf16[4,512,768]{2,1,0:T(8,128)(2,1)} %x_ref.1) | copy-start | bytes 9437188
  0.6 1.6 %copy-start.1 = (bf16[4,256,768]{2,1,0:T(8,128)(2,1)S(1)}, bf16[4,256,768]{2,1,0:T(8,128)(2,1)}, u32[]{:S(2)}) copy-start(bf16[4,256,768]{2,1,0:T(8,128)(2,1)} %g_ref.1) | copy-start | bytes 4718596
  2.2 2.6 %copy-start.2 = (f32[6,768]{1,0:T(8,128)S(1)}, f32[6,768]{1,0:T(8,128)}, u32[]{:S(2)}) copy-start(f32[6,768]{1,0:T(8,128)} %par_ref.9) | copy-start | bytes 55300
  2.2 2.6 %copy-start.3 = (s32[4,4]{1,0:T(4,128)S(1)}, s32[4,4]{1,0:T(4,128)}, u32[]{:S(2)}) copy-start(s32[4,4]{1,0:T(4,128)} %len_ref.9) | copy-start | bytes 196
  3.3 1.5 %collective-permute-start = (bf16[4,16,768]{2,1,0:T(8,128)(2,1)S(1)}, bf16[4,16,768]{2,1,0:T(8,128)(2,1)S(1)}, u32[]{:S(2)}, u32[]{:S(2)}) collective-permute-start(bf16[4,16,768]{2,1,0:T(8,128)(2,1)S(1)} %get-tuple-element.28), channel_id=1, source_target_pairs={{0,1},{2,3},{1,0},{3,2},{4,5},{6,7},{5,4},{7,6},{8,9},{10,11},{9,8... | collective-permute-start | bytes 294920 | tf_op jit(solution)/shard_map/ppermute | solution.py:705
  3.8 0.9 %collective-permute-start.1 = (bf16[4,16,768]{2,1,0:T(8,128)(2,1)S(1)}, bf16[4,16,768]{2,1,0:T(8,128)(2,1)S(1)}, u32[]{:S(2)}, u32[]{:S(2)}) collective-permute-start(bf16[4,16,768]{2,1,0:T(8,128)(2,1)S(1)} %get-tuple-element.29), channel_id=1, source_target_pairs={{1,2},{2,1},{5,6},{6,5},{9,10},{10,9},{13,14},{14,13},{17,18},{18,... | collective-permute-start | bytes 294920 | tf_op jit(solution)/shard_map/ppermute | solution.py:704
  19.6 8.6 %collective-permute-start.2 = (f32[6,768]{1,0:T(8,128)S(1)}, f32[6,768]{1,0:T(8,128)S(1)}, u32[]{:S(2)}, u32[]{:S(2)}) collective-permute-start(f32[6,768]{1,0:T(8,128)S(1)} %get-tuple-element.34), channel_id=1, source_target_pairs={{0,1},{1,0},{2,3},{3,2},{4,5},{5,4},{6,7},{7,6},{8,9},{9,8},{10,11... | collective-permute-start | bytes 55304 | tf_op jit(solution)/shard_map/ppermute | solution.py:716
  28.2 4.4 %collective-permute-start.3 = (f32[6,768]{1,0:T(8,128)S(1)}, f32[6,768]{1,0:T(8,128)S(1)}, u32[]{:S(2)}, u32[]{:S(2)}) collective-permute-start(f32[6,768]{1,0:T(8,128)S(1)} %add.33), channel_id=1, source_target_pairs={{0,2},{1,3},{2,0},{3,1},{4,6},{5,7},{6,4},{7,5},{8,10},{9,11},{10,... | collective-permute-start | bytes 55304 | tf_op jit(solution)/shard_map/ppermute | solution.py:716
  32.6 4.3 %collective-permute-start.4 = (f32[6,768]{1,0:T(8,128)S(1)}, f32[6,768]{1,0:T(8,128)S(1)}, u32[]{:S(2)}, u32[]{:S(2)}) collective-permute-start(f32[6,768]{1,0:T(8,128)S(1)} %add.34), channel_id=1, source_target_pairs={{0,4},{4,0},{8,12},{12,8},{16,20},{20,16},{24,28},{28,24},{1,5},{5... | collective-permute-start | bytes 55304 | tf_op jit(solution)/shard_map/ppermute | solution.py:716
  37.0 10.5 %copy-start.4 = (f32[6,768]{1,0:T(8,128)S(1)}, f32[6,768]{1,0:T(8,128)}, u32[]{:S(2)}) copy-start(f32[6,768]{1,0:T(8,128)} %param.9) | copy-start | bytes 55300
  37.0 10.5 %copy-start.5 = (f32[6,768]{1,0:T(8,128)S(1)}, f32[6,768]{1,0:T(8,128)}, u32[]{:S(2)}) copy-start(f32[6,768]{1,0:T(8,128)} %param.10) | copy-start | bytes 55300
  37.0 4.3 %collective-permute-start.5 = (f32[6,768]{1,0:T(8,128)S(1)}, f32[6,768]{1,0:T(8,128)S(1)}, u32[]{:S(2)}, u32[]{:S(2)}) collective-permute-start(f32[6,768]{1,0:T(8,128)S(1)} %add.35), channel_id=1, source_target_pairs={{0,8},{4,12},{8,0},{12,4},{16,24},{20,28},{24,16},{28,20},{1,9},{5... | collective-permute-start | bytes 55304 | tf_op jit(solution)/shard_map/ppermute | solution.py:716
  41.4 4.8 %collective-permute-start.6 = (f32[6,768]{1,0:T(8,128)S(1)}, f32[6,768]{1,0:T(8,128)S(1)}, u32[]{:S(2)}, u32[]{:S(2)}) collective-permute-start(f32[6,768]{1,0:T(8,128)S(1)} %add.36), channel_id=1, source_target_pairs={{0,16},{4,20},{8,24},{12,28},{16,0},{20,4},{24,8},{28,12},{1,17},{... | collective-permute-start | bytes 55304 | tf_op jit(solution)/shard_map/ppermute | solution.py:716

commit v5 on v4

--- a/solution.py
+++ b/solution.py
@@ -96,12 +96,92 @@
         far_ref[r] = jnp.where(even, first, last).astype(BF16)
 
 
+def convolve_block(base, ends, par_ref, load, at, place_high, place_low):
+    chunks = par_ref.shape[1] // 128
+    sub8 = iota((8, 128), 0)
+    keeps = []
+    for j in range(2):
+        position = base - PAD + at + 8 * j + sub8
+        offset = position - begin_of(position, ends)
+        keeps.append([offset >= k for k in range(TAPS)])
+    for c in range(chunks):
+        lanes = lanes_of(c)
+        parts = []
+        for j in range(2):
+            value = par_ref[4:5, lanes] + par_ref[0:1, lanes] * load(c, 8 * j)
+            for k in range(1, TAPS):
+                shifted = jnp.where(keeps[j][k], load(c, 8 * j - k), 0.0)
+                value = value + par_ref[k : k + 1, lanes] * shifted
+            parts.append(value)
+        high, low = split(jnp.concatenate(parts, axis=0))
+        place_high(c, high)
+        place_low(c, low)
+
+
+def conv_kernel(shapes, base_ref, len_ref, x_ref, par_ref, conv_ref, xf):
+    rows, length, half, features, tiles = shapes
+    chunks = features // 128
+    base = base_ref[0]
+    blocks = 2 * OWN // 16
+    for c in range(chunks):
+        xf[c, 0 : 8 + PAD, :] = jnp.zeros((8 + PAD, 128), F32)
+        rest = xf.shape[1] - 8 - PAD - length
+        xf[c, 8 + PAD + length :, :] = jnp.zeros((rest, 128), F32)
+
+    def one_row(r, _):
+        ends = ends_of(len_ref, r)
+
+        def widen(i, _):
+            at = pl.multiple_of(i * 32, 32)
+            for c in range(chunks):
+                xf[c, pl.ds(at + 8 + PAD, 32), :] = x_ref[r, pl.ds(at, 32), lanes_of(c)].astype(F32)
+            return 0
+
+        lax.fori_loop(0, length // 32, widen, 0)
+
+        def one_tile(m, _):
+            tile = r * tiles + m
+            before = jnp.maximum(tile - 1, 0)
+            for b in range(blocks):
+                at = pl.multiple_of(2 * OWN * m + 16 * b, 16)
+
+                def put(first):
+                    def store(c, value):
+                        conv_ref[tile, c, first + 16 * b : first + 16 * b + 16, :] = value
+                        if b == 0:
+                            conv_ref[before, c, first + WINDOW - 16 : first + WINDOW, :] = value
+
+                    return store
+
+                convolve_block(
+                    base,
+                    ends,
+                    par_ref,
+                    lambda c, shift: xf[c, pl.ds(at + 8 + shift, 8), :],
+                    at,
+                    put(0),
+                    put(WINDOW),
+                )
+            return 0
+
+        lax.fori_loop(0, tiles, one_tile, 0)
+        return 0
+
+    lax.fori_loop(0, rows, one_row, 0)
+    for r in range(rows):
+        last = r * tiles + tiles - 1
+        for c in range(chunks):
+            for first in (0, WINDOW):
+                conv_ref[last, c, first + WINDOW - 16 : first + WINDOW, :] = jnp.zeros((16, 128), BF16)
+
+
 def forward_kernel(
     shapes,
     base_ref,
     len_ref,
     x_ref,
     g_ref,
+    conv_ref,
     near_ref,
     far_ref,
     par_ref,
@@ -111,13 +191,7 @@
     grad_ref,
     xb,
     xf,
-    conv_aa,
-    conv_ab,
-    conv_ba,
-    conv_bb,
     edge,
-    dots_a,
-    dots_b,
     comp,
     cs,
     es,
@@ -132,8 +206,7 @@
     sems,
 ):
     rows, length, half, features, tiles = shapes
-    count = rows * tiles
-    pairs = count // 2
+    pairs = rows * tiles // 2
     chunks = features // 128
     base = base_ref[0]
 
@@ -152,35 +225,15 @@
     group_of_e = (first_e + ((sub8 - first_e) & 7)) >> 3
     turn_e = first_e & 7
 
-    def place(tile):
-        return tile // tiles, tile % tiles
+    def place(pair, side):
+        r, m = 2 * (pair // tiles) + side, pair % tiles
+        return r, m, r * tiles + m
 
     def tile_start(m):
         return base + 2 * OWN * m - PAD
 
     acc[...] = jnp.zeros_like(acc)
     carry_o[...] = jnp.zeros_like(carry_o)
-
-    def convolve(r, at, side, where, ends, place_high, place_low):
-        keeps = []
-        for j in range(2):
-            position = base - PAD + at + 8 * j + sub8
-            offset = position - begin_of(position, ends)
-            keeps.append([offset >= k for k in range(TAPS)])
-        for c in range(chunks):
-            parts = []
-            for j in range(2):
-                row = where + 8 * j
-                value = par_ref[4:5, lanes_of(c)] + par_ref[0:1, lanes_of(c)] * xf[side, c, row : row + 8, :]
-                for k in range(1, TAPS):
-                    shifted = xf[side, c, row - k : row - k + 8, :]
-                    value = value + par_ref[k : k + 1, lanes_of(c)] * jnp.where(keeps[j][k], shifted, 0.0)
-                parts.append(value)
-            high, low = split(jnp.concatenate(parts, axis=0))
-            for ref, *index in place_high(c):
-                ref[(*index, slice(None))] = high
-            for ref, *index in place_low(c):
-                ref[(*index, slice(None))] = low
 
     subd = iota((8, features), 0)
     even = (base // length) % 2 == 0
@@ -204,80 +257,73 @@
             g32[r, c, PAD + half : PAD + half + 8, :] = after[:, lanes_of(c)]
             g32[r, c, PAD + half + 8 :, :] = jnp.zeros((rest, 128), F32)
         for c in range(chunks):
-            xf[r % 2, c, 0:8, :] = jnp.zeros((8, 128), F32)
-            xf[r % 2, c, 8:24, :] = up[:, lanes_of(c)]
-        convolve(
-            r,
-            0,
-            r % 2,
-            8,
-            ends_of(len_ref, r),
-            lambda c: [(edge, count + r, c, slice(0, 16))],
-            lambda c: [(edge, count + r, c, slice(16, 32))],
-        )
+            lanes = lanes_of(c)
+            xf[c, 0:8, :] = jnp.zeros((8, 128), F32)
+            xf[c, 8:24, :] = up[:, lanes]
+            xf[c, 24:40, :] = x_ref[r, 0:16, lanes].astype(F32)
+            xf[c, 40:56, :] = x_ref[r, length - 16 : length, lanes].astype(F32)
+            xf[c, 56:72, :] = down[:, lanes]
+        ends = ends_of(len_ref, r)
+        for at, where, slot in ((0, 8, 0), (PAD, 24, 16), (PAD + length, 56, 32)):
+
+            def put(first):
+                def store(c, value):
+                    edge[r, c, first : first + 16, :] = value
+
+                return store
+
+            convolve_block(
+                base,
+                ends,
+                par_ref,
+                lambda c, shift: xf[c, where + shift : where + shift + 8, :],
+                at,
+                put(slot),
+                put(48 + slot),
+            )
 
     scorer_high = [par_ref[5:6, lanes_of(c)].astype(BF16).astype(F32) for c in range(chunks)]
     scorer_low = [par_ref[5:6, lanes_of(c)] - scorer_high[c] for c in range(chunks)]
 
-    convs = ((conv_aa, conv_ab), (conv_ba, conv_bb))
-    dots_refs = (dots_a, dots_b)
-
-    def convolve_pair(pair, parity):
+    def held_rows(r, m, c):
+        tile = r * tiles + m
+        parts = []
+        for first, own in ((0, 0), (WINDOW, 48)):
+            begin = 0
+            if m == 0:
+                parts.append(edge[r, c, own : own + 32, :])
+                begin = 32
+            if m == tiles - 1:
+                end = PAD + length - 2 * OWN * m
+                parts.append(conv_ref[tile, c, first + begin : first + end, :])
+                parts.append(edge[r, c, own + 32 : own + 48, :])
+                begin = end + 16
+            if begin < WINDOW:
+                parts.append(conv_ref[tile, c, first + begin : first + WINDOW, :])
+        return jnp.concatenate(parts, axis=0)
+
+    for pair in range(pairs):
+        dots, scores = [], []
         for side in range(2):
-            tile = 2 * pair + side
-            r, m = place(tile)
-            ends = ends_of(len_ref, r)
-            at = pl.multiple_of(2 * OWN * m, 16)
-            conv = convs[parity][side]
-            source = jnp.where(m == 0, count + r, tile - 1)
-            for c in range(chunks):
-                conv[c, 0:16, :] = edge[source, c, 0:16, :]
-                conv[c, WINDOW : WINDOW + 16, :] = edge[source, c, 16:32, :]
-                xf[2 * parity + side, c, 8 : 8 + WINDOW, :] = xb[r, pl.ds(at, WINDOW), lanes_of(c)].astype(F32)
-            for b in range(1, WINDOW // 16):
-                last = b == WINDOW // 16 - 1
-                convolve(
-                    r,
-                    at + 16 * b,
-                    2 * parity + side,
-                    8 + 16 * b,
-                    ends,
-                    lambda c: [(conv, c, slice(16 * b, 16 * b + 16))]
-                    + ([(edge, tile, c, slice(0, 16))] if last else []),
-                    lambda c: [(conv, c, slice(WINDOW + 16 * b, WINDOW + 16 * b + 16))]
-                    + ([(edge, tile, c, slice(16, 32))] if last else []),
-                )
-
-    def multiply_pair(pair, parity):
-        for side in range(2):
-            r, m = place(2 * pair + side)
-            start = pl.multiple_of(OWN * m + 8, 8)
+            r, m, _ = place(pair, side)
+            start = OWN * m + 8
             streamed, held = [], []
             for c in range(chunks):
-                g = g32[r, c, pl.ds(start, SLOTS), :]
+                g = g32[r, c, start : start + SLOTS, :]
                 top = jnp.where(sub8 == 0, scorer_high[c], jnp.where(sub8 == 1, scorer_low[c], g[0:8]))
                 streamed.append(jnp.concatenate([top, g[8:]], axis=0).astype(BF16))
-                held.append(convs[parity][side][c])
+                held.append(held_rows(r, m, c))
             product = lax.dot_general(
                 jnp.concatenate(streamed, axis=1),
                 jnp.concatenate(held, axis=1),
                 (((1,), (1,)), ((), ())),
                 preferred_element_type=F32,
             )
-            dots_refs[parity][SLOTS * side : SLOTS * side + SLOTS, :] = (
-                product[:, :WINDOW] + product[:, WINDOW:]
-            )
-
-    def extract_pair(pair, parity):
-        dots = dots_refs[parity][...]
-        scores = jnp.concatenate(
-            [
-                jnp.broadcast_to(dots[i : i + 1] + dots[i + 1 : i + 2], (SLOTS, WINDOW))
-                for i in (0, SLOTS)
-            ],
-            axis=0,
-        ).T
-        dots = dots.T
+            product = product[:, :WINDOW] + product[:, WINDOW:]
+            dots.append(product)
+            scores.append(jnp.broadcast_to(product[0:1] + product[1:2], (SLOTS, WINDOW)))
+        dots = jnp.concatenate(dots, axis=0).T
+        scores = jnp.concatenate(scores, axis=0).T
         banded = jnp.zeros((8, 128), F32)
         scored = jnp.zeros((8, 128), F32)
         for v in range(WINDOW // 8):
@@ -287,34 +333,19 @@
         comp[0, pair] = banded
         comp[1, pair] = scored
 
-    dots_b[...] = jnp.zeros_like(dots_b)
-    convolve_pair(0, 0)
-
-    def first_loop(i, _):
-        extract_pair(jnp.maximum(2 * i - 1, 0), 1)
-        multiply_pair(2 * i, 0)
-        convolve_pair(2 * i + 1, 1)
-        extract_pair(2 * i, 0)
-        multiply_pair(2 * i + 1, 1)
-        convolve_pair(jnp.minimum(2 * i + 2, pairs - 1), 0)
-        return 0
-
-    lax.fori_loop(0, pairs // 2, first_loop, 0)
-    extract_pair(pairs - 1, 1)
-
     ends = [ends_of(len_ref, r) for r in range(rows)]
     for pair in range(pairs):
-        both = (2 * pair, 2 * pair + 1)
+        both = [place(pair, side) for side in range(2)]
         dots = rotate_rows(comp[0, pair], turn_e)
         scores = rotate_rows(comp[1, pair], turn_e)
         coef = jnp.zeros((8, 128), F32)
         coef_e = jnp.zeros((8, 128), F32)
         for p in range(2):
-            at = [tile_start(place(t)[1]) + 2 * slot8 + p for t in both]
-            begin = [begin_of(a, ends[place(t)[0]]) for a, t in zip(at, both)]
-            end = [end_of(a, ends[place(t)[0]]) for a, t in zip(at, both)]
-            offset = jnp.maximum(jnp.where(left, at[0] - begin[0], at[1] - begin[1]), 0)
-            remain = jnp.where(left, end[0] - at[0], end[1] - at[1])
+            at = tile_start(both[0][1]) + 2 * slot8 + p
+            begin = [begin_of(at, ends[r]) for r, _, _ in both]
+            end = [end_of(at, ends[r]) for r, _, _ in both]
+            offset = jnp.maximum(at - jnp.where(left, begin[0], begin[1]), 0)
+            remain = jnp.where(left, end[0], end[1]) - at
             masks, inverses, logits, grads = [], [], [], []
             for b in range(1, TAPS + 1):
                 if b == 3:
@@ -344,8 +375,7 @@
         coef_e = jnp.where(owned, coef_e, 0.0)
         es[pair] = rotate_rows(coef_e, (8 - turn_e) & 7)
         swapped = pltpu.roll(coef, SLOTS, 1)
-        for side, tile in enumerate(both):
-            r, m = place(tile)
+        for side, (r, m, tile) in enumerate(both):
             at = tile_start(m) + 2 * slot8 + delta
             offset = at - begin_of(at, ends[r])
             alone = jnp.where(left, coef, swapped) if side == 0 else jnp.where(left, swapped, coef)
@@ -362,7 +392,7 @@
             [jnp.where(group_of_e == v, es[pair], 0.0) for v in range(WINDOW // 8)], axis=0
         ).T
         for side in range(2):
-            _, m = place(2 * pair + side)
+            _, m, _ = place(pair, side)
             from_row = OWN * m - 8
             part = spread[SLOTS * side : SLOTS * side + SLOTS]
             here = (from_row + slots_down >= 0) & (from_row + slots_down < half)
@@ -372,8 +402,7 @@
             rows_e_ref[side, 1] = jnp.broadcast_to(all_e, (8, 128))
 
     def build(pair, side):
-        tile = 2 * pair + side
-        r, m = place(tile)
+        r, m, tile = place(pair, side)
         own_e = rows_e_ref[side, 0]
         all_e = rows_e_ref[side, 1]
         at = tile_start(m) + lane8
@@ -404,8 +433,7 @@
             factors[side][SLOTS * k : SLOTS * (k + 1), WINDOW:] = low
 
     def apply(pair, side):
-        tile = 2 * pair + side
-        r, m = place(tile)
+        r, m, _ = place(pair, side)
         start = pl.multiple_of(OWN * m + 8, 8)
         window = pl.multiple_of(2 * OWN * m, 16)
         factor = factors[side][...]
@@ -441,14 +469,14 @@
                     acc[k, :, lanes] += jnp.sum((taken * g).reshape(SLOTS // 8, 8, 128), axis=0)
                 acc[4, :, lanes] += jnp.sum((total * g).reshape(SLOTS // 8, 8, 128), axis=0)
                 acc[5, :, lanes] += jnp.where(sub8 == 0, value[0:8], 0.0)
-                top = carry_o[:, lanes] + jnp.where(sub8 < LEAD, 0.0, value[0:8])
-                out32[r % 2, c, pl.ds(start, 8), :] = top
-                out32[r % 2, c, pl.ds(start + 8, OWN - 8), :] = value[8:OWN]
-                carry_o[:, lanes] = jnp.where(m < tiles - 1, value[OWN:], 0.0)
-
-    def finish(r):
+                top = carry_o[side, :, lanes] + jnp.where(sub8 < LEAD, 0.0, value[0:8])
+                out32[side, c, pl.ds(start, 8), :] = top
+                out32[side, c, pl.ds(start + 8, OWN - 8), :] = value[8:OWN]
+                carry_o[side, :, lanes] = jnp.where(m < tiles - 1, value[OWN:], 0.0)
+
+    def finish(r, side):
         for c in range(chunks):
-            outb[r, :, lanes_of(c)] = out32[r % 2, c, PAD : PAD + half, :].astype(BF16)
+            outb[r, :, lanes_of(c)] = out32[side, c, PAD : PAD + half, :].astype(BF16)
         copy_out(r).start()
 
     spread_pair(0)
@@ -456,12 +484,10 @@
     build(0, 1)
 
     def second_loop(i, _):
-        for side in range(2):
-            r, m = place(2 * i - 1 + side)
-
-            @pl.when((m == 0) & (i > 0))
-            def _():
-                finish(r - 1)
+        @pl.when((i % tiles == 0) & (i > 0))
+        def _():
+            for side in range(2):
+                finish(2 * (i // tiles) - 2 + side, side)
 
         spread_pair(i + 1)
         for side in range(2):
@@ -472,10 +498,8 @@
     lax.fori_loop(0, pairs - 1, second_loop, 0)
     apply(pairs - 1, 0)
     apply(pairs - 1, 1)
-    for r in range(rows):
-        if r * tiles > 2 * (pairs - 2):
-            finish(r - 1)
-    finish(rows - 1)
+    for side in range(2):
+        finish(rows - 2 + side, side)
     for k in range(TAPS + 2):
         grad_ref[k : k + 1, :] = jnp.sum(acc[k], axis=0, keepdims=True)
     for r in range(rows):
@@ -595,7 +619,26 @@
     )(base, inputs, cotangent)
 
 
-def forward(base, lengths, inputs, cotangent, near, far, params):
+def convolved(base, lengths, inputs, params):
+    rows, length, features = inputs.shape
+    half = length // 2
+    chunks = features // 128
+    tiles, x_rows, _ = sizes_of(length, half)
+    shapes = (rows, length, half, features, tiles)
+    return pl.pallas_call(
+        functools.partial(conv_kernel, shapes),
+        out_shape=jax.ShapeDtypeStruct((rows * tiles, chunks, 2 * WINDOW, 128), BF16),
+        in_specs=[SMEM, SMEM, VMEM, VMEM],
+        out_specs=VMEM,
+        scratch_shapes=[pltpu.VMEM((chunks, 8 + x_rows, 128), F32)],
+        compiler_params=pltpu.CompilerParams(vmem_limit_bytes=24 * 1024 * 1024),
+        cost_estimate=pl.CostEstimate(
+            flops=24 * inputs.size, bytes_accessed=8 * inputs.size, transcendentals=0
+        ),
+    )(base, lengths, inputs, params)
+
+
+def forward(base, lengths, inputs, cotangent, conv, near, far, params):
     rows, half, features = cotangent.shape
     length = 2 * half
     chunks = features // 128
@@ -610,18 +653,12 @@
             jax.ShapeDtypeStruct((rows, chunks, g_rows, 128), F32),
             jax.ShapeDtypeStruct((TAPS + 2, features), F32),
         ),
-        in_specs=[SMEM, SMEM, VMEM, VMEM, VMEM, VMEM, VMEM],
+        in_specs=[SMEM, SMEM, VMEM, VMEM, VMEM, VMEM, VMEM, VMEM],
         out_specs=(HBM, VMEM, VMEM, VMEM),
         scratch_shapes=[
             pltpu.VMEM((rows, x_rows, features), BF16),
-            pltpu.VMEM((4, chunks, WINDOW + 8, 128), F32),
-            pltpu.VMEM((chunks, 2 * WINDOW, 128), BF16),
-            pltpu.VMEM((chunks, 2 * WINDOW, 128), BF16),
-            pltpu.VMEM((chunks, 2 * WINDOW, 128), BF16),
-            pltpu.VMEM((chunks, 2 * WINDOW, 128), BF16),
-            pltpu.VMEM((count + rows, chunks, 32, 128), BF16),
-            pltpu.VMEM((2 * SLOTS, WINDOW), F32),
-            pltpu.VMEM((2 * SLOTS, WINDOW), F32),
+            pltpu.VMEM((chunks, 72, 128), F32),
+            pltpu.VMEM((rows, chunks, 96, 128), BF16),
             pltpu.VMEM((2, count // 2, 8, 128), F32),
             pltpu.VMEM((2, count, 8, 128), F32),
             pltpu.VMEM((count // 2, 8, 128), F32),
@@ -631,17 +668,17 @@
             pltpu.VMEM((2, 2, 8, 128), F32),
             pltpu.VMEM((2, chunks, g_rows, 128), F32),
             pltpu.VMEM((rows, half, features), BF16),
-            pltpu.VMEM((8, features), F32),
+            pltpu.VMEM((2, 8, features), F32),
             pltpu.VMEM((TAPS + 2, 8, features), F32),
             pltpu.SemaphoreType.DMA((rows,)),
         ],
-        compiler_params=pltpu.CompilerParams(vmem_limit_bytes=40 * 1024 * 1024),
+        compiler_params=pltpu.CompilerParams(vmem_limit_bytes=28 * 1024 * 1024),
         cost_estimate=pl.CostEstimate(
             flops=2 * count * SLOTS * WINDOW * features * 12,
             bytes_accessed=8 * inputs.size,
             transcendentals=0,
         ),
-    )(base, lengths, inputs, cotangent, near, far, params)
+    )(base, lengths, inputs, cotangent, conv, near, far, params)
 
 
 def backward(r, base, lengths, shape, matrices, padded, params, grown):
@@ -703,8 +740,9 @@
     near, far = packed(base, inputs, cotangent)
     far = lax.ppermute(far, "group", pairs_of("group", 1))
     near = lax.ppermute(near, "group", pairs_of("group", 0))
+    conv = convolved(base, lengths, inputs, params)
     output, matrices, padded, grad_params = forward(
-        base, lengths, inputs, cotangent, near, far, params
+        base, lengths, inputs, cotangent, conv, near, far, params
     )
 
     def backward_row(row, matrices, grown):

time: 49.5 us -> 47.1 us (0.952)
  starting transfers between devices: 14.7 us -> 11 us
  waiting for transfers between devices: 2.44 us -> 3.2 us
  Pallas kernels: 26.6 us -> 27.2 us
    pallas_call x0 -> x1, Pallas kernels: none -> 5.65 us  [convolved(): pl.pallas_call(functools.partial(conv_kernel, shapes), out_shape=jax.Shap...]
    pallas_call x1, Pallas kernels: 14.8 us -> 9.63 us  [forward(): pl.pallas_call(functools.partial(forward_kernel, shapes), out_shape=(jax....]
    ppermute x5, starting transfers between devices: 13.5 us -> 9.86 us  [per_device(): received = lax.ppermute(grad_params, axis, exchange)]
    ppermute x5, waiting for transfers between devices: 2.15 us -> 3.19 us  [per_device(): received = lax.ppermute(grad_params, axis, exchange)]
  transfers between devices with their start and end apart: 7 -> 7, of which waited for: 2 -> 2; matrix products, arithmetic and copies ran while one was open for 0% -> 0% of each run, Pallas kernels for 22% -> 35%
where the time goes in v5:
time: 47.1 us; the launch traced here: 46.9 us
  Pallas kernels  27.2 us (58%)
  starting transfers between devices  11 us (23%)
  waiting for transfers between devices  3.2 us (7%)
  between operations  2.71 us (6%)
  local copies, waits for them, and re-layouts  1.58 us (3%)
  other arithmetic  1.27 us (3%)
    pallas_call x4, Pallas kernels, backward(): pl.pallas_call(functools.partial(backward_kernel, shapes, r), out_shape=j...  10.8 us
    ppermute x5, starting transfers between devices, per_device(): received = lax.ppermute(grad_params, axis, exchange)  9.86 us
    pallas_call x1, Pallas kernels, forward(): pl.pallas_call(functools.partial(forward_kernel, shapes), out_shape=(jax....  9.63 us
    pallas_call x1, Pallas kernels, convolved(): pl.pallas_call(functools.partial(conv_kernel, shapes), out_shape=jax.Shap...  5.65 us
    ppermute x5, waiting for transfers between devices, per_device(): received = lax.ppermute(grad_params, axis, exchange)  3.19 us
    unnamed x12, local copies, waits for them, and re-layouts  1.58 us
    pallas_call x1, Pallas kernels, packed(): pl.pallas_call(pack_kernel, out_shape=(part, part), in_specs=[SMEM, HBM,...  1.08 us
  transfers between devices with their start and end apart: 7, of which 2 were waited for; matrix products, arithmetic and copies ran while one was open for 0% of the time, Pallas kernels for 35%

profile of v5, /device:TPU:0, one launch (start us, length us, event | category | flops | bytes accessed | tf_op | source)
XLA Modules:
  0.0 46.9 jit_solution(5609684787271082720)
XLA Ops:
  0.6 0.0 copy-start
  0.6 0.0 copy-start.1
  0.7 1.5 %copy-done.1 = bf16[4,256,768]{2,1,0:T(8,128)(2,1)S(1)} copy-done((bf16[4,256,768]{2,1,0:T(8,128)(2,1)S(1)}, bf16[4,256,768]{2,1,0:T(8,128)(2,1)}, u32[]{:S(2)}) %copy-start.1) | copy-done | bytes 1572888
  2.2 0.0 copy-start.2
  2.2 0.0 copy-start.3
  2.2 1.1 %shard_map.110 = (bf16[4,16,768]{2,1,0:T(8,128)(2,1)S(1)}, bf16[4,16,768]{2,1,0:T(8,128)(2,1)S(1)}) custom-call(s32[1]{0:T(128)} %bitcast.base_ref, bf16[4,512,768]{2,1,0:T(8,128)(2,1)} %x_ref.3, bf16[4,256,768]{2,1,0:T(8,128)(2,1)S(1)} %copy-done.1), custom_call_target="tpu_custom_call" | custom-call | tf_op jit(solution)/shard_map/pallas_call | solution.py:612
  3.3 0.5 %collective-permute-start = (bf16[4,16,768]{2,1,0:T(8,128)(2,1)S(1)}, bf16[4,16,768]{2,1,0:T(8,128)(2,1)S(1)}, u32[]{:S(2)}, u32[]{:S(2)}) collective-permute-start(bf16[4,16,768]{2,1,0:T(8,128)(2,1)S(1)} %get-tuple-element.28), channel_id=1, source_target_pairs={{0,1},{2,3},{1,0},{3,2},{4,5},{6,7},{5,4},{7,6},{8,9},{10,11},{9,8... | collective-permute-start | bytes 294920 | tf_op jit(solution)/shard_map/ppermute | solution.py:742
  3.8 0.7 %collective-permute-start.1 = (bf16[4,16,768]{2,1,0:T(8,128)(2,1)S(1)}, bf16[4,16,768]{2,1,0:T(8,128)(2,1)S(1)}, u32[]{:S(2)}, u32[]{:S(2)}) collective-permute-start(bf16[4,16,768]{2,1,0:T(8,128)(2,1)S(1)} %get-tuple-element.29), channel_id=1, source_target_pairs={{1,2},{2,1},{5,6},{6,5},{9,10},{10,9},{13,14},{14,13},{17,18},{18,... | collective-permute-start | bytes 294920 | tf_op jit(solution)/shard_map/ppermute | solution.py:741
  4.5 0.0 copy-done
  4.5 0.0 copy-done.2
  4.5 0.0 copy-done.3
  4.5 5.7 %shard_map.109.conv_ref = bf16[20,6,256,128]{3,2,1,0:T(8,128)(2,1)S(1)} custom-call(s32[1]{0:T(128)} %bitcast.base_ref, s32[4,4]{1,0:T(4,128)S(1)} %copy-done.3, bf16[4,512,768]{2,1,0:T(8,128)(2,1)S(1)} %copy-done, f32[6,768]{1,0:T(8,128)S(1)} %copy-done.2), custom_call_target="tpu_custom_call" | custom-call | flops 37748736 | bytes 12582912 | tf_op jit(solution)/shard_map/pallas_call | solution.py:628
  10.2 0.0 collective-permute-done.near_ref
  10.2 0.0 collective-permute-done.1.far_ref
  10.2 9.6 %shard_map.111 = (bf16[4,256,768]{2,1,0:T(8,128)(2,1)}, bf16[20,64,256]{2,1,0:T(8,128)(2,1)S(1)}, f32[4,6,304,128]{3,2,1,0:T(8,128)S(1)}, f32[6,768]{1,0:T(8,128)S(1)}) custom-call(s32[1]{0:T(128)} %bitcast.base_ref, s32[4,4]{1,0:T(4,128)S(1)} %copy-done.3, bf16[4,512,768]{2,1,0:T(8,128)(2,1)S(1)} %copy-done, bf16[4,256,768]{2,1,0:T(8,128)(2,1)S(1)} %copy-done.1, ...), custom_call_target="tpu_custom_call" | custom-call | flops 3019898880 | bytes 12582912 | tf_op jit(solution)/shard_map/pallas_call | solution.py:648
  19.8 3.9 %collective-permute-start.2 = (f32[6,768]{1,0:T(8,128)S(1)}, f32[6,768]{1,0:T(8,128)S(1)}, u32[]{:S(2)}, u32[]{:S(2)}) collective-permute-start(f32[6,768]{1,0:T(8,128)S(1)} %get-tuple-element.34), channel_id=1, source_target_pairs={{0,1},{1,0},{2,3},{3,2},{4,5},{5,4},{6,7},{7,6},{8,9},{9,8},{10,11... | collective-permute-start | bytes 55304 | tf_op jit(solution)/shard_map/ppermute | solution.py:754
  23.8 2.7 %shard_map.112.refs_0_ = bf16[4,512,768]{2,1,0:T(8,128)(2,1)} custom-call(s32[1]{0:T(128)} %bitcast.base_ref, s32[4,4]{1,0:T(4,128)S(1)} %copy-done.3, bf16[20,64,256]{2,1,0:T(8,128)(2,1)S(1)} %get-tuple-element.45.mat, f32[4,6,304,128]{3,2,1,0:T(8,128)S(1)} %get-tuple-element.35.g32, f32[6,768]{1,0:T(8,128)S(1)} %copy-done.2), custom_call_target="tpu_custom_call" | custom-call | flops 251658240 | bytes 1572864 | tf_op jit(solution)/shard_map/pallas_call | solution.py:695
  26.5 0.0 collective-permute-done.2
  26.5 0.1 collective-permute-start.3
  26.6 2.7 %shard_map.113.refs_0_ = bf16[4,512,768]{2,1,0:T(8,128)(2,1)} custom-call(s32[1]{0:T(128)} %bitcast.base_ref, s32[4,4]{1,0:T(4,128)S(1)} %copy-done.3, bf16[20,64,256]{2,1,0:T(8,128)(2,1)S(1)} %get-tuple-element.45.mat, f32[4,6,304,128]{3,2,1,0:T(8,128)S(1)} %get-tuple-element.35.g32, f32[6,768]{1,0:T(8,128)S(1)} %copy-done.2, ...), custom_call_target="tpu_custom_call", output_to_operand_aliasing={{}: (5, {})} | custom-call | flops 251658240 | bytes 1572864 | tf_op jit(solution)/shard_map/pallas_call | solution.py:695
  29.3 1.1 %collective-permute-done.3 = f32[6,768]{1,0:T(8,128)S(1)} collective-permute-done((f32[6,768]{1,0:T(8,128)S(1)}, f32[6,768]{1,0:T(8,128)S(1)}, u32[]{:S(2)}, u32[]{:S(2)}) %collective-permute-start.3) | collective-permute-done | bytes 18464 | tf_op jit(solution)/shard_map/ppermute | solution.py:754
  30.4 1.5 %collective-permute-start.4 = (f32[6,768]{1,0:T(8,128)S(1)}, f32[6,768]{1,0:T(8,128)S(1)}, u32[]{:S(2)}, u32[]{:S(2)}) collective-permute-start(f32[6,768]{1,0:T(8,128)S(1)} %add.34), channel_id=1, source_target_pairs={{0,4},{4,0},{8,12},{12,8},{16,20},{20,16},{24,28},{28,24},{1,5},{5... | collective-permute-start | bytes 55304 | tf_op jit(solution)/shard_map/ppermute | solution.py:754
  31.9 2.7 %shard_map.114.refs_0_ = bf16[4,512,768]{2,1,0:T(8,128)(2,1)} custom-call(s32[1]{0:T(128)} %bitcast.base_ref, s32[4,4]{1,0:T(4,128)S(1)} %copy-done.3, bf16[20,64,256]{2,1,0:T(8,128)(2,1)S(1)} %get-tuple-element.45.mat, f32[4,6,304,128]{3,2,1,0:T(8,128)S(1)} %get-tuple-element.35.g32, f32[6,768]{1,0:T(8,128)S(1)} %copy-done.2, ...), custom_call_target="tpu_custom_call", output_to_operand_aliasing={{}: (5, {})} | custom-call | flops 251658240 | bytes 1572864 | tf_op jit(solution)/shard_map/pallas_call | solution.py:695
  34.6 0.0 collective-permute-done.4
  34.6 0.0 copy-start.4
  34.6 0.0 copy-start.5
  34.6 1.7 %collective-permute-start.5 = (f32[6,768]{1,0:T(8,128)S(1)}, f32[6,768]{1,0:T(8,128)S(1)}, u32[]{:S(2)}, u32[]{:S(2)}) collective-permute-start(f32[6,768]{1,0:T(8,128)S(1)} %add.35), channel_id=1, source_target_pairs={{0,8},{4,12},{8,0},{12,4},{16,24},{20,28},{24,16},{28,20},{1,9},{5... | collective-permute-start | bytes 55304 | tf_op jit(solution)/shard_map/ppermute | solution.py:754
  36.3 2.7 %shard_map.115 = bf16[4,512,768]{2,1,0:T(8,128)(2,1)} custom-call(s32[1]{0:T(128)} %bitcast.base_ref, s32[4,4]{1,0:T(4,128)S(1)} %copy-done.3, bf16[20,64,256]{2,1,0:T(8,128)(2,1)S(1)} %get-tuple-element.45.mat, f32[4,6,304,128]{3,2,1,0:T(8,128)S(1)} %get-tuple-element.35.g32, f32[6,768]{1,0:T(8,128)S(1)} %copy-done.2, ...), custom_call_target="tpu_custom_call", output_to_operand_aliasing={{}: (5, {})} | custom-call | flops 251658240 | bytes 1572864 | tf_op jit(solution)/shard_map/pallas_call | solution.py:695
  39.0 0.0 collective-permute-done.5
  39.0 2.7 %collective-permute-start.6 = (f32[6,768]{1,0:T(8,128)S(1)}, f32[6,768]{1,0:T(8,128)S(1)}, u32[]{:S(2)}, u32[]{:S(2)}) collective-permute-start(f32[6,768]{1,0:T(8,128)S(1)} %add.36), channel_id=1, source_target_pairs={{0,16},{4,20},{8,24},{12,28},{16,0},{20,4},{24,8},{28,12},{1,17},{... | collective-permute-start | bytes 55304 | tf_op jit(solution)/shard_map/ppermute | solution.py:754
  41.7 2.1 %collective-permute-done.6 = f32[6,768]{1,0:T(8,128)S(1)} collective-permute-done((f32[6,768]{1,0:T(8,128)S(1)}, f32[6,768]{1,0:T(8,128)S(1)}, u32[]{:S(2)}, u32[]{:S(2)}) %collective-permute-start.6) | collective-permute-done | bytes 18464 | tf_op jit(solution)/shard_map/ppermute | solution.py:754
  43.8 0.6 %multiply_reduce_fusion = (f32[]{:T(128)}, f32[6,768]{1,0:T(8,128)S(1)}) fusion(f32[6,768]{1,0:T(8,128)S(1)} %add.36, f32[6,768]{1,0:T(8,128)S(1)} %collective-permute-done.6), kind=kLoop, calls=%fused_computation.4 | loop fusion | flops 13823 | bytes 55300 | tf_op jit(solution)/shard_map/reduce_sum | solution.py:764
  45.2 0.0 copy-done.4
  45.2 0.0 copy-done.5
  45.2 0.6 %multiply_subtract_fusion = (f32[6,768]{1,0:T(8,128)}, f32[6,768]{1,0:T(8,128)}, f32[6,768]{1,0:T(8,128)}) fusion(f32[6,768]{1,0:T(8,128)S(1)} %copy-done.2, f32[6,768]{1,0:T(8,128)S(1)} %get-tuple-element.54, f32[]{:T(128)S(6)} %min.3, f32[6,768]{1,0:T(8,128)S(1)} %copy-done.4, f32[6,768]{1,0:T(8,128)S(1)} %copy-done.5), kind=kLoop, calls=%fused_computation.2 | loop fusion | flops 73728 | bytes 129028 | tf_op jit(solution)/shard_map/sub | solution.py:720
  (4 shorter events, 0.0 us)
Async XLA Ops:
  0.6 3.8 %copy-start = (bf16[4,512,768]{2,1,0:T(8,128)(2,1)S(1)}, bf16[4,512,768]{2,1,0:T(8,128)(2,1)}, u32[]{:S(2)}) copy-start(bf16[4,512,768]{2,1,0:T(8,128)(2,1)} %x_ref.3) | copy-start | bytes 9437188
  0.6 1.6 %copy-start.1 = (bf16[4,256,768]{2,1,0:T(8,128)(2,1)S(1)}, bf16[4,256,768]{2,1,0:T(8,128)(2,1)}, u32[]{:S(2)}) copy-start(bf16[4,256,768]{2,1,0:T(8,128)(2,1)} %g_ref.1) | copy-start | bytes 4718596
  2.2 2.3 %copy-start.2 = (f32[6,768]{1,0:T(8,128)S(1)}, f32[6,768]{1,0:T(8,128)}, u32[]{:S(2)}) copy-start(f32[6,768]{1,0:T(8,128)} %par_ref.11) | copy-start | bytes 55300
  2.2 2.3 %copy-start.3 = (s32[4,4]{1,0:T(4,128)S(1)}, s32[4,4]{1,0:T(4,128)}, u32[]{:S(2)}) copy-start(s32[4,4]{1,0:T(4,128)} %len_ref.11) | copy-start | bytes 196
  3.3 6.9 %collective-permute-start = (bf16[4,16,768]{2,1,0:T(8,128)(2,1)S(1)}, bf16[4,16,768]{2,1,0:T(8,128)(2,1)S(1)}, u32[]{:S(2)}, u32[]{:S(2)}) collective-permute-start(bf16[4,16,768]{2,1,0:T(8,128)(2,1)S(1)} %get-tuple-element.28), channel_id=1, source_target_pairs={{0,1},{2,3},{1,0},{3,2},{4,5},{6,7},{5,4},{7,6},{8,9},{10,11},{9,8... | collective-permute-start | bytes 294920 | tf_op jit(solution)/shard_map/ppermute | solution.py:742
  3.8 6.4 %collective-permute-start.1 = (bf16[4,16,768]{2,1,0:T(8,128)(2,1)S(1)}, bf16[4,16,768]{2,1,0:T(8,128)(2,1)S(1)}, u32[]{:S(2)}, u32[]{:S(2)}) collective-permute-start(bf16[4,16,768]{2,1,0:T(8,128)(2,1)S(1)} %get-tuple-element.29), channel_id=1, source_target_pairs={{1,2},{2,1},{5,6},{6,5},{9,10},{10,9},{13,14},{14,13},{17,18},{18,... | collective-permute-start | bytes 294920 | tf_op jit(solution)/shard_map/ppermute | solution.py:741
  19.8 6.6 %collective-permute-start.2 = (f32[6,768]{1,0:T(8,128)S(1)}, f32[6,768]{1,0:T(8,128)S(1)}, u32[]{:S(2)}, u32[]{:S(2)}) collective-permute-start(f32[6,768]{1,0:T(8,128)S(1)} %get-tuple-element.34), channel_id=1, source_target_pairs={{0,1},{1,0},{2,3},{3,2},{4,5},{5,4},{6,7},{7,6},{8,9},{9,8},{10,11... | collective-permute-start | bytes 55304 | tf_op jit(solution)/shard_map/ppermute | solution.py:754
  26.5 3.9 %collective-permute-start.3 = (f32[6,768]{1,0:T(8,128)S(1)}, f32[6,768]{1,0:T(8,128)S(1)}, u32[]{:S(2)}, u32[]{:S(2)}) collective-permute-start(f32[6,768]{1,0:T(8,128)S(1)} %add.33), channel_id=1, source_target_pairs={{0,2},{1,3},{2,0},{3,1},{4,6},{5,7},{6,4},{7,5},{8,10},{9,11},{10,... | collective-permute-start | bytes 55304 | tf_op jit(solution)/shard_map/ppermute | solution.py:754
  30.4 4.2 %collective-permute-start.4 = (f32[6,768]{1,0:T(8,128)S(1)}, f32[6,768]{1,0:T(8,128)S(1)}, u32[]{:S(2)}, u32[]{:S(2)}) collective-permute-start(f32[6,768]{1,0:T(8,128)S(1)} %add.34), channel_id=1, source_target_pairs={{0,4},{4,0},{8,12},{12,8},{16,20},{20,16},{24,28},{28,24},{1,5},{5... | collective-permute-start | bytes 55304 | tf_op jit(solution)/shard_map/ppermute | solution.py:754
  34.6 10.5 %copy-start.4 = (f32[6,768]{1,0:T(8,128)S(1)}, f32[6,768]{1,0:T(8,128)}, u32[]{:S(2)}) copy-start(f32[6,768]{1,0:T(8,128)} %param.9) | copy-start | bytes 55300
  34.6 10.5 %copy-start.5 = (f32[6,768]{1,0:T(8,128)S(1)}, f32[6,768]{1,0:T(8,128)}, u32[]{:S(2)}) copy-start(f32[6,768]{1,0:T(8,128)} %param.10) | copy-start | bytes 55300
  34.6 4.4 %collective-permute-start.5 = (f32[6,768]{1,0:T(8,128)S(1)}, f32[6,768]{1,0:T(8,128)S(1)}, u32[]{:S(2)}, u32[]{:S(2)}) collective-permute-start(f32[6,768]{1,0:T(8,128)S(1)} %add.35), channel_id=1, source_target_pairs={{0,8},{4,12},{8,0},{12,4},{16,24},{20,28},{24,16},{28,20},{1,9},{5... | collective-permute-start | bytes 55304 | tf_op jit(solution)/shard_map/ppermute | solution.py:754
  39.0 4.8 %collective-permute-start.6 = (f32[6,768]{1,0:T(8,128)S(1)}, f32[6,768]{1,0:T(8,128)S(1)}, u32[]{:S(2)}, u32[]{:S(2)}) collective-permute-start(f32[6,768]{1,0:T(8,128)S(1)} %add.36), channel_id=1, source_target_pairs={{0,16},{4,20},{8,24},{12,28},{16,0},{20,4},{24,8},{28,12},{1,17},{... | collective-permute-start | bytes 55304 | tf_op jit(solution)/shard_map/ppermute | solution.py:754

commit v6 on v5

--- a/solution.py
+++ b/solution.py
@@ -19,7 +19,7 @@
 
 TAPS = 4
 SLOTS = 64
-PACK_LIMIT = 50 * 1024 * 1024
+PACK_LIMIT = 53 * 1024 * 1024
 OWN = 56
 LEAD = 4
 WINDOW = 128
@@ -96,11 +96,11 @@
         far_ref[r] = jnp.where(even, first, last).astype(BF16)
 
 
-def convolve_block(base, ends, par_ref, load, at, place_high, place_low):
+def convolve_block(base, ends, par_ref, load, at, place_high, place_low, masked=True):
     chunks = par_ref.shape[1] // 128
     sub8 = iota((8, 128), 0)
     keeps = []
-    for j in range(2):
+    for j in range(2 if masked else 0):
         position = base - PAD + at + 8 * j + sub8
         offset = position - begin_of(position, ends)
         keeps.append([offset >= k for k in range(TAPS)])
@@ -110,7 +110,9 @@
         for j in range(2):
             value = par_ref[4:5, lanes] + par_ref[0:1, lanes] * load(c, 8 * j)
             for k in range(1, TAPS):
-                shifted = jnp.where(keeps[j][k], load(c, 8 * j - k), 0.0)
+                shifted = load(c, 8 * j - k)
+                if masked:
+                    shifted = jnp.where(keeps[j][k], shifted, 0.0)
                 value = value + par_ref[k : k + 1, lanes] * shifted
             parts.append(value)
         high, low = split(jnp.concatenate(parts, axis=0))
@@ -118,38 +120,37 @@
         place_low(c, low)
 
 
-def conv_kernel(shapes, base_ref, len_ref, x_ref, par_ref, conv_ref, xf):
+def conv_kernel(shapes, base_ref, len_ref, x_ref, par_ref, high_ref, low_ref, xf):
     rows, length, half, features, tiles = shapes
     chunks = features // 128
     base = base_ref[0]
-    blocks = 2 * OWN // 16
+    step = 64
     for c in range(chunks):
-        xf[c, 0 : 8 + PAD, :] = jnp.zeros((8 + PAD, 128), F32)
-        rest = xf.shape[1] - 8 - PAD - length
-        xf[c, 8 + PAD + length :, :] = jnp.zeros((rest, 128), F32)
+        xf[c, 0:8, :] = jnp.zeros((8, 128), F32)
+    rest = high_ref.shape[2] - PAD - length
+    for r in range(rows):
+        for c in range(chunks):
+            for ref in (high_ref, low_ref):
+                ref[r, c, 0:PAD, :] = jnp.zeros((PAD, 128), BF16)
+                ref[r, c, PAD + length :, :] = jnp.zeros((rest, 128), BF16)
 
     def one_row(r, _):
         ends = ends_of(len_ref, r)
 
         def widen(i, _):
-            at = pl.multiple_of(i * 32, 32)
+            at = pl.multiple_of(i * step, step)
             for c in range(chunks):
-                xf[c, pl.ds(at + 8 + PAD, 32), :] = x_ref[r, pl.ds(at, 32), lanes_of(c)].astype(F32)
+                xf[c, pl.ds(at + 8, step), :] = x_ref[r, pl.ds(at, step), lanes_of(c)].astype(F32)
             return 0
 
-        lax.fori_loop(0, length // 32, widen, 0)
-
-        def one_tile(m, _):
-            tile = r * tiles + m
-            before = jnp.maximum(tile - 1, 0)
-            for b in range(blocks):
-                at = pl.multiple_of(2 * OWN * m + 16 * b, 16)
-
-                def put(first):
+        lax.fori_loop(0, length // step, widen, 0)
+
+        def blocks(at, masked):
+            for b in range(step // 16):
+
+                def put(ref):
                     def store(c, value):
-                        conv_ref[tile, c, first + 16 * b : first + 16 * b + 16, :] = value
-                        if b == 0:
-                            conv_ref[before, c, first + WINDOW - 16 : first + WINDOW, :] = value
+                        ref[r, c, pl.ds(at + PAD + 16 * b, 16), :] = value
 
                     return store
 
@@ -157,22 +158,32 @@
                     base,
                     ends,
                     par_ref,
-                    lambda c, shift: xf[c, pl.ds(at + 8 + shift, 8), :],
-                    at,
-                    put(0),
-                    put(WINDOW),
+                    lambda c, shift: xf[c, pl.ds(at + 8 + 16 * b + shift, 8), :],
+                    at + PAD + 16 * b,
+                    put(high_ref),
+                    put(low_ref),
+                    masked,
                 )
+
+        def one_step(i, _):
+            at = pl.multiple_of(i * step, step)
+            reach = [(end > base + at - TAPS + 1) & (end < base + at + step) for end in ends]
+            starts = functools.reduce(jnp.logical_or, reach)
+
+            @pl.when(starts)
+            def _():
+                blocks(at, True)
+
+            @pl.when(jnp.logical_not(starts))
+            def _():
+                blocks(at, False)
+
             return 0
 
-        lax.fori_loop(0, tiles, one_tile, 0)
+        lax.fori_loop(0, length // step, one_step, 0)
         return 0
 
     lax.fori_loop(0, rows, one_row, 0)
-    for r in range(rows):
-        last = r * tiles + tiles - 1
-        for c in range(chunks):
-            for first in (0, WINDOW):
-                conv_ref[last, c, first + WINDOW - 16 : first + WINDOW, :] = jnp.zeros((16, 128), BF16)
 
 
 def forward_kernel(
@@ -181,7 +192,8 @@
     len_ref,
     x_ref,
     g_ref,
-    conv_ref,
+    high_ref,
+    low_ref,
     near_ref,
     far_ref,
     par_ref,
@@ -286,20 +298,20 @@
     scorer_low = [par_ref[5:6, lanes_of(c)] - scorer_high[c] for c in range(chunks)]
 
     def held_rows(r, m, c):
-        tile = r * tiles + m
         parts = []
-        for first, own in ((0, 0), (WINDOW, 48)):
+        at = 2 * OWN * m
+        for ref, own in ((high_ref, 0), (low_ref, 48)):
             begin = 0
             if m == 0:
                 parts.append(edge[r, c, own : own + 32, :])
                 begin = 32
             if m == tiles - 1:
-                end = PAD + length - 2 * OWN * m
-                parts.append(conv_ref[tile, c, first + begin : first + end, :])
+                end = PAD + length - at
+                parts.append(ref[r, c, at + begin : at + end, :])
                 parts.append(edge[r, c, own + 32 : own + 48, :])
                 begin = end + 16
             if begin < WINDOW:
-                parts.append(conv_ref[tile, c, first + begin : first + WINDOW, :])
+                parts.append(ref[r, c, at + begin : at + WINDOW, :])
         return jnp.concatenate(parts, axis=0)
 
     for pair in range(pairs):
@@ -625,12 +637,13 @@
     chunks = features // 128
     tiles, x_rows, _ = sizes_of(length, half)
     shapes = (rows, length, half, features, tiles)
+    part = jax.ShapeDtypeStruct((rows, chunks, x_rows, 128), BF16)
     return pl.pallas_call(
         functools.partial(conv_kernel, shapes),
-        out_shape=jax.ShapeDtypeStruct((rows * tiles, chunks, 2 * WINDOW, 128), BF16),
+        out_shape=(part, part),
         in_specs=[SMEM, SMEM, VMEM, VMEM],
-        out_specs=VMEM,
-        scratch_shapes=[pltpu.VMEM((chunks, 8 + x_rows, 128), F32)],
+        out_specs=(VMEM, VMEM),
+        scratch_shapes=[pltpu.VMEM((chunks, 8 + length, 128), F32)],
         compiler_params=pltpu.CompilerParams(vmem_limit_bytes=24 * 1024 * 1024),
         cost_estimate=pl.CostEstimate(
             flops=24 * inputs.size, bytes_accessed=8 * inputs.size, transcendentals=0
@@ -638,7 +651,7 @@
     )(base, lengths, inputs, params)
 
 
-def forward(base, lengths, inputs, cotangent, conv, near, far, params):
+def forward(base, lengths, inputs, cotangent, high, low, near, far, params):
     rows, half, features = cotangent.shape
     length = 2 * half
     chunks = features // 128
@@ -653,7 +666,7 @@
             jax.ShapeDtypeStruct((rows, chunks, g_rows, 128), F32),
             jax.ShapeDtypeStruct((TAPS + 2, features), F32),
         ),
-        in_specs=[SMEM, SMEM, VMEM, VMEM, VMEM, VMEM, VMEM, VMEM],
+        in_specs=[SMEM, SMEM, VMEM, VMEM, VMEM, VMEM, VMEM, VMEM, VMEM],
         out_specs=(HBM, VMEM, VMEM, VMEM),
         scratch_shapes=[
             pltpu.VMEM((rows, x_rows, features), BF16),
@@ -678,7 +691,7 @@
             bytes_accessed=8 * inputs.size,
             transcendentals=0,
         ),
-    )(base, lengths, inputs, cotangent, conv, near, far, params)
+    )(base, lengths, inputs, cotangent, high, low, near, far, params)
 
 
 def backward(r, base, lengths, shape, matrices, padded, params, grown):
@@ -712,15 +725,34 @@
     )(*operands)
 
 
-def adam_update(grads, weights, first_old, second_old):
-    first_new = beta_one * first_old + (1.0 - beta_one) * grads
-    second_new = beta_two * second_old + (1.0 - beta_two) * grads * grads
+def update_kernel(
+    grad_ref, other_ref, par_ref, first_ref, second_ref, norm_ref, new_ref, new_first_ref, new_second_ref
+):
+    grads = grad_ref[...] + other_ref[...]
+    norm = jnp.sqrt(jnp.sum(grads * grads, keepdims=True))
+    norm_ref[...] = norm
+    grads = grads * jnp.minimum(1.0, clip_limit / (norm + 1e-06))
+    weights = par_ref[...]
+    first_new = beta_one * first_ref[...] + (1.0 - beta_one) * grads
+    second_new = beta_two * second_ref[...] + (1.0 - beta_two) * grads * grads
     first_hat = first_new / (1.0 - beta_one**STEP)
     second_hat = second_new / (1.0 - beta_two**STEP)
-    updated = weights - learn_rate * (
+    new_ref[...] = weights - learn_rate * (
         first_hat / (jnp.sqrt(second_hat) + adam_eps) + decay_rate * weights
     )
-    return (updated, first_new, second_new)
+    new_first_ref[...] = first_new
+    new_second_ref[...] = second_new
+
+
+def update(grads, other, weights, first_old, second_old):
+    like = jax.ShapeDtypeStruct(weights.shape, F32)
+    return pl.pallas_call(
+        update_kernel,
+        out_shape=(jax.ShapeDtypeStruct((1, 1), F32), like, like, like),
+        in_specs=[VMEM] * 5,
+        out_specs=(VMEM,) * 4,
+        compiler_params=pltpu.CompilerParams(vmem_limit_bytes=4 * 1024 * 1024),
+    )(grads, other, weights, first_old, second_old)
 
 
 def rounds_of(axes):
@@ -740,9 +772,9 @@
     near, far = packed(base, inputs, cotangent)
     far = lax.ppermute(far, "group", pairs_of("group", 1))
     near = lax.ppermute(near, "group", pairs_of("group", 0))
-    conv = convolved(base, lengths, inputs, params)
+    high, low = convolved(base, lengths, inputs, params)
     output, matrices, padded, grad_params = forward(
-        base, lengths, inputs, cotangent, conv, near, far, params
+        base, lengths, inputs, cotangent, high, low, near, far, params
     )
 
     def backward_row(row, matrices, grown):
@@ -750,22 +782,23 @@
 
     grad_inputs = None
     row = 0
+    received = jnp.zeros_like(grad_params)
     for axis, exchange in rounds_of(("group", "rows")):
+        if row > 0:
+            grad_params = grad_params + received
         received = lax.ppermute(grad_params, axis, exchange)
         if row < rows_here:
             matrices, grad_params = lax.optimization_barrier((matrices, grad_params))
             grad_inputs = backward_row(row, matrices, grad_inputs)
-            row += 1
             received, grad_inputs = lax.optimization_barrier((received, grad_inputs))
-        grad_params = grad_params + received
+        row += 1
     while row < rows_here:
         grad_inputs = backward_row(row, matrices, grad_inputs)
         row += 1
-    grad_norm = jnp.sqrt(jnp.sum(grad_params * grad_params))
-    clip_scale = jnp.minimum(1.0, clip_limit / (grad_norm + 1e-06))
-    new_params, new_first, new_second = adam_update(
-        grad_params * clip_scale, params, first_moment, second_moment
+    grad_norm, new_params, new_first, new_second = update(
+        grad_params, received, params, first_moment, second_moment
     )
+    grad_norm = grad_norm.reshape(())
     return (output, grad_inputs, grad_norm, new_params, new_first, new_second)
 
 

time: 47.1 us -> 42.4 us (0.900)
  between operations: 2.71 us -> 0.86 us
  local copies, waits for them, and re-layouts: 1.58 us -> 0.03 us
  other arithmetic: 1.27 us -> 0.02 us
    unnamed x12, local copies, waits for them, and re-layouts: 1.58 us -> 0.03 us
    sub x1 -> x0, other arithmetic: 0.64 us -> none  [adam_update(): weights - learn_rate * (first_hat / (jnp.sqrt(second_hat) + adam_eps) + d...]
    reduce_sum x1 -> x0, other arithmetic: 0.61 us -> none  [per_device(): grad_norm = jnp.sqrt(jnp.sum(grad_params * grad_params))]
    pallas_call x1 -> x2, Pallas kernels: 5.65 us -> 5.16 us  [the longest x1 4.37 us: convolved(): pl.pallas_call(functools.partial(conv_kernel, shapes), out_shape=(part, p...]
  transfers between devices with their start and end apart: 7 -> 7, of which waited for: 2 -> 2; matrix products, arithmetic and copies ran while one was open for 0% -> 0% of each run, Pallas kernels for 35% -> 36%
where the time goes in v6:
time: 42.4 us; the launch traced here: 42.3 us
  Pallas kernels  26.9 us (63%)
  starting transfers between devices  11.1 us (26%)
  waiting for transfers between devices  3.41 us (8%)
  between operations  0.86 us (2%)
    pallas_call x4, Pallas kernels, backward(): pl.pallas_call(functools.partial(backward_kernel, shapes, r), out_shape=j...  10.8 us
    ppermute x5, starting transfers between devices, per_device(): received = lax.ppermute(grad_params, axis, exchange)  9.93 us
    pallas_call x1, Pallas kernels, forward(): pl.pallas_call(functools.partial(forward_kernel, shapes), out_shape=(jax....  9.64 us
    pallas_call x1, Pallas kernels, convolved(): pl.pallas_call(functools.partial(conv_kernel, shapes), out_shape=(part, p...  4.37 us
    ppermute x5, waiting for transfers between devices, per_device(): received = lax.ppermute(grad_params, axis, exchange)  3.4 us
    pallas_call x1, Pallas kernels, packed(): pl.pallas_call(pack_kernel, out_shape=(part, part), in_specs=[SMEM, HBM,...  1.29 us
  transfers between devices with their start and end apart: 7, of which 2 were waited for; matrix products, arithmetic and copies ran while one was open for 0% of the time, Pallas kernels for 36%

profile of v6, /device:TPU:0, one launch (start us, length us, event | category | flops | bytes accessed | tf_op | source)
XLA Modules:
  0.0 42.3 jit_solution(4951340455151450554)
XLA Ops:
  0.6 0.0 copy-start
  0.6 0.0 copy-start.2
  0.7 0.0 copy-start.3
  0.7 0.0 copy-start.1
  0.7 1.3 %shard_map.110 = (bf16[4,16,768]{2,1,0:T(8,128)(2,1)S(1)}, bf16[4,16,768]{2,1,0:T(8,128)(2,1)S(1)}) custom-call(s32[1]{0:T(128)} %bitcast.base_ref, bf16[4,512,768]{2,1,0:T(8,128)(2,1)} %x_ref.3, bf16[4,256,768]{2,1,0:T(8,128)(2,1)} %g_ref.1), custom_call_target="tpu_custom_call" | custom-call | tf_op jit(solution)/shard_map/pallas_call | solution.py:624
  2.0 0.5 %collective-permute-start = (bf16[4,16,768]{2,1,0:T(8,128)(2,1)S(1)}, bf16[4,16,768]{2,1,0:T(8,128)(2,1)S(1)}, u32[]{:S(2)}, u32[]{:S(2)}) collective-permute-start(bf16[4,16,768]{2,1,0:T(8,128)(2,1)S(1)} %get-tuple-element.36), channel_id=1, source_target_pairs={{0,1},{2,3},{1,0},{3,2},{4,5},{6,7},{5,4},{7,6},{8,9},{10,11},{9,8... | collective-permute-start | bytes 294920 | tf_op jit(solution)/shard_map/ppermute | solution.py:774
  2.5 0.7 %collective-permute-start.1 = (bf16[4,16,768]{2,1,0:T(8,128)(2,1)S(1)}, bf16[4,16,768]{2,1,0:T(8,128)(2,1)S(1)}, u32[]{:S(2)}, u32[]{:S(2)}) collective-permute-start(bf16[4,16,768]{2,1,0:T(8,128)(2,1)S(1)} %get-tuple-element.37), channel_id=1, source_target_pairs={{1,2},{2,1},{5,6},{6,5},{9,10},{10,9},{13,14},{14,13},{17,18},{18,... | collective-permute-start | bytes 294920 | tf_op jit(solution)/shard_map/ppermute | solution.py:773
  3.2 0.0 copy-done
  3.2 0.0 copy-done.2
  3.2 0.0 copy-done.3
  3.2 4.4 %shard_map.109 = (bf16[4,6,576,128]{3,2,1,0:T(8,128)(2,1)S(1)}, bf16[4,6,576,128]{3,2,1,0:T(8,128)(2,1)S(1)}) custom-call(s32[1]{0:T(128)} %bitcast.base_ref, s32[4,4]{1,0:T(4,128)S(1)} %copy-done.3, bf16[4,512,768]{2,1,0:T(8,128)(2,1)S(1)} %copy-done, f32[6,768]{1,0:T(8,128)S(1)} %copy-done.2), custom_call_target="tpu_custom_call" | custom-call | flops 37748736 | bytes 12582912 | tf_op jit(solution)/shard_map/pallas_call | solution.py:641
  7.6 0.0 collective-permute-done.near_ref
  7.6 0.0 collective-permute-done.1.far_ref
  7.6 0.0 copy-done.1
  7.6 9.6 %shard_map.111 = (bf16[4,256,768]{2,1,0:T(8,128)(2,1)}, bf16[20,64,256]{2,1,0:T(8,128)(2,1)S(1)}, f32[4,6,304,128]{3,2,1,0:T(8,128)S(1)}, f32[6,768]{1,0:T(8,128)S(1)}) custom-call(s32[1]{0:T(128)} %bitcast.base_ref, s32[4,4]{1,0:T(4,128)S(1)} %copy-done.3, bf16[4,512,768]{2,1,0:T(8,128)(2,1)S(1)} %copy-done, bf16[4,256,768]{2,1,0:T(8,128)(2,1)S(1)} %copy-done.1, ...), custom_call_target="tpu_custom_call" | custom-call | flops 3019898880 | bytes 12582912 | tf_op jit(solution)/shard_map/pallas_call | solution.py:661
  17.2 4.1 %collective-permute-start.2 = (f32[6,768]{1,0:T(8,128)S(1)}, f32[6,768]{1,0:T(8,128)S(1)}, u32[]{:S(2)}, u32[]{:S(2)}) collective-permute-start(f32[6,768]{1,0:T(8,128)S(1)} %get-tuple-element.42), channel_id=1, source_target_pairs={{0,1},{1,0},{2,3},{3,2},{4,5},{5,4},{6,7},{7,6},{8,9},{9,8},{10,11... | collective-permute-start | bytes 55304 | tf_op jit(solution)/shard_map/ppermute | solution.py:789
  21.4 2.7 %shard_map.112.refs_0_ = bf16[4,512,768]{2,1,0:T(8,128)(2,1)} custom-call(s32[1]{0:T(128)} %bitcast.base_ref, s32[4,4]{1,0:T(4,128)S(1)} %copy-done.3, bf16[20,64,256]{2,1,0:T(8,128)(2,1)S(1)} %get-tuple-element.53.mat, f32[4,6,304,128]{3,2,1,0:T(8,128)S(1)} %get-tuple-element.43.g32, f32[6,768]{1,0:T(8,128)S(1)} %copy-done.2), custom_call_target="tpu_custom_call" | custom-call | flops 251658240 | bytes 1572864 | tf_op jit(solution)/shard_map/pallas_call | solution.py:708
  24.1 0.0 collective-permute-done.2
  24.1 0.1 collective-permute-start.3
  24.2 2.7 %shard_map.113.refs_0_ = bf16[4,512,768]{2,1,0:T(8,128)(2,1)} custom-call(s32[1]{0:T(128)} %bitcast.base_ref, s32[4,4]{1,0:T(4,128)S(1)} %copy-done.3, bf16[20,64,256]{2,1,0:T(8,128)(2,1)S(1)} %get-tuple-element.53.mat, f32[4,6,304,128]{3,2,1,0:T(8,128)S(1)} %get-tuple-element.43.g32, f32[6,768]{1,0:T(8,128)S(1)} %copy-done.2, ...), custom_call_target="tpu_custom_call", output_to_operand_aliasing={{}: (5, {})} | custom-call | flops 251658240 | bytes 1572864 | tf_op jit(solution)/shard_map/pallas_call | solution.py:708
  26.9 1.1 %collective-permute-done.3 = f32[6,768]{1,0:T(8,128)S(1)} collective-permute-done((f32[6,768]{1,0:T(8,128)S(1)}, f32[6,768]{1,0:T(8,128)S(1)}, u32[]{:S(2)}, u32[]{:S(2)}) %collective-permute-start.3) | collective-permute-done | bytes 18464 | tf_op jit(solution)/shard_map/ppermute | solution.py:789
  28.0 1.4 %collective-permute-start.4 = (f32[6,768]{1,0:T(8,128)S(1)}, f32[6,768]{1,0:T(8,128)S(1)}, u32[]{:S(2)}, u32[]{:S(2)}) collective-permute-start(f32[6,768]{1,0:T(8,128)S(1)} %add.13), channel_id=1, source_target_pairs={{0,4},{4,0},{8,12},{12,8},{16,20},{20,16},{24,28},{28,24},{1,5},{5... | collective-permute-start | bytes 55304 | tf_op jit(solution)/shard_map/ppermute | solution.py:789
  29.4 2.7 %shard_map.114.refs_0_ = bf16[4,512,768]{2,1,0:T(8,128)(2,1)} custom-call(s32[1]{0:T(128)} %bitcast.base_ref, s32[4,4]{1,0:T(4,128)S(1)} %copy-done.3, bf16[20,64,256]{2,1,0:T(8,128)(2,1)S(1)} %get-tuple-element.53.mat, f32[4,6,304,128]{3,2,1,0:T(8,128)S(1)} %get-tuple-element.43.g32, f32[6,768]{1,0:T(8,128)S(1)} %copy-done.2, ...), custom_call_target="tpu_custom_call", output_to_operand_aliasing={{}: (5, {})} | custom-call | flops 251658240 | bytes 1572864 | tf_op jit(solution)/shard_map/pallas_call | solution.py:708
  32.1 0.0 collective-permute-done.4
  32.1 0.0 copy-start.4
  32.2 0.0 copy-start.5
  32.2 1.8 %collective-permute-start.5 = (f32[6,768]{1,0:T(8,128)S(1)}, f32[6,768]{1,0:T(8,128)S(1)}, u32[]{:S(2)}, u32[]{:S(2)}) collective-permute-start(f32[6,768]{1,0:T(8,128)S(1)} %add.14), channel_id=1, source_target_pairs={{0,8},{4,12},{8,0},{12,4},{16,24},{20,28},{24,16},{28,20},{1,9},{5... | collective-permute-start | bytes 55304 | tf_op jit(solution)/shard_map/ppermute | solution.py:789
  34.0 2.7 %shard_map.115 = bf16[4,512,768]{2,1,0:T(8,128)(2,1)} custom-call(s32[1]{0:T(128)} %bitcast.base_ref, s32[4,4]{1,0:T(4,128)S(1)} %copy-done.3, bf16[20,64,256]{2,1,0:T(8,128)(2,1)S(1)} %get-tuple-element.53.mat, f32[4,6,304,128]{3,2,1,0:T(8,128)S(1)} %get-tuple-element.43.g32, f32[6,768]{1,0:T(8,128)S(1)} %copy-done.2, ...), custom_call_target="tpu_custom_call", output_to_operand_aliasing={{}: (5, {})} | custom-call | flops 251658240 | bytes 1572864 | tf_op jit(solution)/shard_map/pallas_call | solution.py:708
  36.7 0.0 collective-permute-done.5
  36.7 2.5 %collective-permute-start.6 = (f32[6,768]{1,0:T(8,128)S(1)}, f32[6,768]{1,0:T(8,128)S(1)}, u32[]{:S(2)}, u32[]{:S(2)}) collective-permute-start(f32[6,768]{1,0:T(8,128)S(1)} %add.15.grad_ref), channel_id=1, source_target_pairs={{0,16},{4,20},{8,24},{12,28},{16,0},{20,4},{24,8},{28,12},{1,17},{... | collective-permute-start | bytes 55304 | tf_op jit(solution)/shard_map/ppermute | solution.py:789
  39.2 2.3 %collective-permute-done.6.other_ref = f32[6,768]{1,0:T(8,128)S(1)} collective-permute-done((f32[6,768]{1,0:T(8,128)S(1)}, f32[6,768]{1,0:T(8,128)S(1)}, u32[]{:S(2)}, u32[]{:S(2)}) %collective-permute-start.6) | collective-permute-done | bytes 18464 | tf_op jit(solution)/shard_map/ppermute | solution.py:789
  41.5 0.0 copy-done.4
  41.5 0.0 copy-done.5
  41.5 0.8 %shard_map.116 = (f32[1,1]{1,0:T(1,128)}, f32[6,768]{1,0:T(8,128)}, f32[6,768]{1,0:T(8,128)}, f32[6,768]{1,0:T(8,128)}) custom-call(f32[6,768]{1,0:T(8,128)S(1)} %add.15.grad_ref, f32[6,768]{1,0:T(8,128)S(1)} %collective-permute-done.6.other_ref, f32[6,768]{1,0:T(8,128)S(1)} %copy-done.2, f32[6,768]{1,0:T(8,128)S(1)} %copy-done.4, f32[6,768]{1,0:T(8,128)S(1)} %copy-done.5), custom_call_target="tpu_custom_call" | custom-call | tf_op jit(solution)/shard_map/pallas_call | solution.py:749
  (4 shorter events, 0.0 us)
Async XLA Ops:
  0.6 2.5 %copy-start = (bf16[4,512,768]{2,1,0:T(8,128)(2,1)S(1)}, bf16[4,512,768]{2,1,0:T(8,128)(2,1)}, u32[]{:S(2)}) copy-start(bf16[4,512,768]{2,1,0:T(8,128)(2,1)} %x_ref.3) | copy-start | bytes 9437188
  0.6 2.5 %copy-start.2 = (f32[6,768]{1,0:T(8,128)S(1)}, f32[6,768]{1,0:T(8,128)}, u32[]{:S(2)}) copy-start(f32[6,768]{1,0:T(8,128)} %par_ref.13) | copy-start | bytes 55300
  0.7 2.5 %copy-start.3 = (s32[4,4]{1,0:T(4,128)S(1)}, s32[4,4]{1,0:T(4,128)}, u32[]{:S(2)}) copy-start(s32[4,4]{1,0:T(4,128)} %len_ref.11) | copy-start | bytes 196
  0.7 6.9 %copy-start.1 = (bf16[4,256,768]{2,1,0:T(8,128)(2,1)S(1)}, bf16[4,256,768]{2,1,0:T(8,128)(2,1)}, u32[]{:S(2)}) copy-start(bf16[4,256,768]{2,1,0:T(8,128)(2,1)} %g_ref.1) | copy-start | bytes 4718596
  2.0 5.6 %collective-permute-start = (bf16[4,16,768]{2,1,0:T(8,128)(2,1)S(1)}, bf16[4,16,768]{2,1,0:T(8,128)(2,1)S(1)}, u32[]{:S(2)}, u32[]{:S(2)}) collective-permute-start(bf16[4,16,768]{2,1,0:T(8,128)(2,1)S(1)} %get-tuple-element.36), channel_id=1, source_target_pairs={{0,1},{2,3},{1,0},{3,2},{4,5},{6,7},{5,4},{7,6},{8,9},{10,11},{9,8... | collective-permute-start | bytes 294920 | tf_op jit(solution)/shard_map/ppermute | solution.py:774
  2.5 5.1 %collective-permute-start.1 = (bf16[4,16,768]{2,1,0:T(8,128)(2,1)S(1)}, bf16[4,16,768]{2,1,0:T(8,128)(2,1)S(1)}, u32[]{:S(2)}, u32[]{:S(2)}) collective-permute-start(bf16[4,16,768]{2,1,0:T(8,128)(2,1)S(1)} %get-tuple-element.37), channel_id=1, source_target_pairs={{1,2},{2,1},{5,6},{6,5},{9,10},{10,9},{13,14},{14,13},{17,18},{18,... | collective-permute-start | bytes 294920 | tf_op jit(solution)/shard_map/ppermute | solution.py:773
  17.2 6.8 %collective-permute-start.2 = (f32[6,768]{1,0:T(8,128)S(1)}, f32[6,768]{1,0:T(8,128)S(1)}, u32[]{:S(2)}, u32[]{:S(2)}) collective-permute-start(f32[6,768]{1,0:T(8,128)S(1)} %get-tuple-element.42), channel_id=1, source_target_pairs={{0,1},{1,0},{2,3},{3,2},{4,5},{5,4},{6,7},{7,6},{8,9},{9,8},{10,11... | collective-permute-start | bytes 55304 | tf_op jit(solution)/shard_map/ppermute | solution.py:789
  24.1 3.9 %collective-permute-start.3 = (f32[6,768]{1,0:T(8,128)S(1)}, f32[6,768]{1,0:T(8,128)S(1)}, u32[]{:S(2)}, u32[]{:S(2)}) collective-permute-start(f32[6,768]{1,0:T(8,128)S(1)} %add.12), channel_id=1, source_target_pairs={{0,2},{1,3},{2,0},{3,1},{4,6},{5,7},{6,4},{7,5},{8,10},{9,11},{10,... | collective-permute-start | bytes 55304 | tf_op jit(solution)/shard_map/ppermute | solution.py:789
  28.0 4.1 %collective-permute-start.4 = (f32[6,768]{1,0:T(8,128)S(1)}, f32[6,768]{1,0:T(8,128)S(1)}, u32[]{:S(2)}, u32[]{:S(2)}) collective-permute-start(f32[6,768]{1,0:T(8,128)S(1)} %add.13), channel_id=1, source_target_pairs={{0,4},{4,0},{8,12},{12,8},{16,20},{20,16},{24,28},{28,24},{1,5},{5... | collective-permute-start | bytes 55304 | tf_op jit(solution)/shard_map/ppermute | solution.py:789
  32.1 9.4 %copy-start.4 = (f32[6,768]{1,0:T(8,128)S(1)}, f32[6,768]{1,0:T(8,128)}, u32[]{:S(2)}) copy-start(f32[6,768]{1,0:T(8,128)} %first_ref.1) | copy-start | bytes 55300
  32.2 9.3 %copy-start.5 = (f32[6,768]{1,0:T(8,128)S(1)}, f32[6,768]{1,0:T(8,128)}, u32[]{:S(2)}) copy-start(f32[6,768]{1,0:T(8,128)} %second_ref.1) | copy-start | bytes 55300
  32.2 4.5 %collective-permute-start.5 = (f32[6,768]{1,0:T(8,128)S(1)}, f32[6,768]{1,0:T(8,128)S(1)}, u32[]{:S(2)}, u32[]{:S(2)}) collective-permute-start(f32[6,768]{1,0:T(8,128)S(1)} %add.14), channel_id=1, source_target_pairs={{0,8},{4,12},{8,0},{12,4},{16,24},{20,28},{24,16},{28,20},{1,9},{5... | collective-permute-start | bytes 55304 | tf_op jit(solution)/shard_map/ppermute | solution.py:789
  36.7 4.8 %collective-permute-start.6 = (f32[6,768]{1,0:T(8,128)S(1)}, f32[6,768]{1,0:T(8,128)S(1)}, u32[]{:S(2)}, u32[]{:S(2)}) collective-permute-start(f32[6,768]{1,0:T(8,128)S(1)} %add.15.grad_ref), channel_id=1, source_target_pairs={{0,16},{4,20},{8,24},{12,28},{16,0},{20,4},{24,8},{28,12},{1,17},{... | collective-permute-start | bytes 55304 | tf_op jit(solution)/shard_map/ppermute | solution.py:789

commit v7 on v6

--- a/solution.py
+++ b/solution.py
@@ -782,16 +782,18 @@
 
     grad_inputs = None
     row = 0
-    received = jnp.zeros_like(grad_params)
+    received = None
     for axis, exchange in rounds_of(("group", "rows")):
-        if row > 0:
+        if received is not None:
             grad_params = grad_params + received
+            if row < rows_here:
+                matrices, grad_params = lax.optimization_barrier((matrices, grad_params))
+                grown = backward_row(row, matrices, grad_inputs)
+                received = lax.ppermute(grad_params, axis, exchange)
+                received, grad_inputs = lax.optimization_barrier((received, grown))
+                row += 1
+                continue
         received = lax.ppermute(grad_params, axis, exchange)
-        if row < rows_here:
-            matrices, grad_params = lax.optimization_barrier((matrices, grad_params))
-            grad_inputs = backward_row(row, matrices, grad_inputs)
-            received, grad_inputs = lax.optimization_barrier((received, grad_inputs))
-        row += 1
     while row < rows_here:
         grad_inputs = backward_row(row, matrices, grad_inputs)
         row += 1

time: 42.4 us -> 41 us (0.967)
  waiting for transfers between devices: 3.41 us -> 1.74 us
    ppermute x5, waiting for transfers between devices: 3.4 us -> 1.74 us  [per_device(): received = lax.ppermute(grad_params, axis, exchange)]
  transfers between devices with their start and end apart: 7 -> 7, of which waited for: 2 -> 2; matrix products, arithmetic and copies ran while one was open for 0% -> 0% of each run, Pallas kernels for 36% -> 37%
where the time goes in v7:
time: 41 us; the launch traced here: 40.8 us
  Pallas kernels  26.9 us (66%)
  starting transfers between devices  11.3 us (28%)
  waiting for transfers between devices  1.74 us (4%)
  between operations  0.86 us (2%)
    pallas_call x4, Pallas kernels, backward(): pl.pallas_call(functools.partial(backward_kernel, shapes, r), out_shape=j...  10.8 us
    ppermute x5, starting transfers between devices, per_device(): received = lax.ppermute(grad_params, axis, exchange)  10.1 us
    pallas_call x1, Pallas kernels, forward(): pl.pallas_call(functools.partial(forward_kernel, shapes), out_shape=(jax....  9.64 us
    pallas_call x1, Pallas kernels, convolved(): pl.pallas_call(functools.partial(conv_kernel, shapes), out_shape=(part, p...  4.37 us
    ppermute x5, waiting for transfers between devices, per_device(): received = lax.ppermute(grad_params, axis, exchange)  1.74 us
    pallas_call x1, Pallas kernels, packed(): pl.pallas_call(pack_kernel, out_shape=(part, part), in_specs=[SMEM, HBM,...  1.29 us
  transfers between devices with their start and end apart: 7, of which 2 were waited for; matrix products, arithmetic and copies ran while one was open for 0% of the time, Pallas kernels for 37%

profile of v7, /device:TPU:0, one launch (start us, length us, event | category | flops | bytes accessed | tf_op | source)
XLA Modules:
  0.0 40.8 jit_solution(9338196751641250048)
XLA Ops:
  0.6 0.0 copy-start
  0.6 0.0 copy-start.2
  0.7 0.0 copy-start.3
  0.7 0.0 copy-start.1
  0.7 1.3 %shard_map.110 = (bf16[4,16,768]{2,1,0:T(8,128)(2,1)S(1)}, bf16[4,16,768]{2,1,0:T(8,128)(2,1)S(1)}) custom-call(s32[1]{0:T(128)} %bitcast.base_ref, bf16[4,512,768]{2,1,0:T(8,128)(2,1)} %x_ref.3, bf16[4,256,768]{2,1,0:T(8,128)(2,1)} %g_ref.1), custom_call_target="tpu_custom_call" | custom-call | tf_op jit(solution)/shard_map/pallas_call | solution.py:624
  2.0 0.5 %collective-permute-start = (bf16[4,16,768]{2,1,0:T(8,128)(2,1)S(1)}, bf16[4,16,768]{2,1,0:T(8,128)(2,1)S(1)}, u32[]{:S(2)}, u32[]{:S(2)}) collective-permute-start(bf16[4,16,768]{2,1,0:T(8,128)(2,1)S(1)} %get-tuple-element.36), channel_id=1, source_target_pairs={{0,1},{2,3},{1,0},{3,2},{4,5},{6,7},{5,4},{7,6},{8,9},{10,11},{9,8... | collective-permute-start | bytes 294920 | tf_op jit(solution)/shard_map/ppermute | solution.py:774
  2.5 0.7 %collective-permute-start.1 = (bf16[4,16,768]{2,1,0:T(8,128)(2,1)S(1)}, bf16[4,16,768]{2,1,0:T(8,128)(2,1)S(1)}, u32[]{:S(2)}, u32[]{:S(2)}) collective-permute-start(bf16[4,16,768]{2,1,0:T(8,128)(2,1)S(1)} %get-tuple-element.37), channel_id=1, source_target_pairs={{1,2},{2,1},{5,6},{6,5},{9,10},{10,9},{13,14},{14,13},{17,18},{18,... | collective-permute-start | bytes 294920 | tf_op jit(solution)/shard_map/ppermute | solution.py:773
  3.2 0.0 copy-done
  3.2 0.0 copy-done.2
  3.2 0.0 copy-done.3
  3.2 4.4 %shard_map.109 = (bf16[4,6,576,128]{3,2,1,0:T(8,128)(2,1)S(1)}, bf16[4,6,576,128]{3,2,1,0:T(8,128)(2,1)S(1)}) custom-call(s32[1]{0:T(128)} %bitcast.base_ref, s32[4,4]{1,0:T(4,128)S(1)} %copy-done.3, bf16[4,512,768]{2,1,0:T(8,128)(2,1)S(1)} %copy-done, f32[6,768]{1,0:T(8,128)S(1)} %copy-done.2), custom_call_target="tpu_custom_call" | custom-call | flops 37748736 | bytes 12582912 | tf_op jit(solution)/shard_map/pallas_call | solution.py:641
  7.6 0.0 collective-permute-done.near_ref
  7.6 0.0 collective-permute-done.1.far_ref
  7.6 0.0 copy-done.1
  7.6 9.6 %shard_map.111 = (bf16[4,256,768]{2,1,0:T(8,128)(2,1)}, bf16[20,64,256]{2,1,0:T(8,128)(2,1)S(1)}, f32[4,6,304,128]{3,2,1,0:T(8,128)S(1)}, f32[6,768]{1,0:T(8,128)S(1)}) custom-call(s32[1]{0:T(128)} %bitcast.base_ref, s32[4,4]{1,0:T(4,128)S(1)} %copy-done.3, bf16[4,512,768]{2,1,0:T(8,128)(2,1)S(1)} %copy-done, bf16[4,256,768]{2,1,0:T(8,128)(2,1)S(1)} %copy-done.1, ...), custom_call_target="tpu_custom_call" | custom-call | flops 3019898880 | bytes 12582912 | tf_op jit(solution)/shard_map/pallas_call | solution.py:661
  17.2 4.1 %collective-permute-start.2 = (f32[6,768]{1,0:T(8,128)S(1)}, f32[6,768]{1,0:T(8,128)S(1)}, u32[]{:S(2)}, u32[]{:S(2)}) collective-permute-start(f32[6,768]{1,0:T(8,128)S(1)} %get-tuple-element.40), channel_id=1, source_target_pairs={{0,1},{1,0},{2,3},{3,2},{4,5},{5,4},{6,7},{7,6},{8,9},{9,8},{10,11... | collective-permute-start | bytes 55304 | tf_op jit(solution)/shard_map/ppermute | solution.py:796
  21.4 0.8 %collective-permute-done.2 = f32[6,768]{1,0:T(8,128)S(1)} collective-permute-done((f32[6,768]{1,0:T(8,128)S(1)}, f32[6,768]{1,0:T(8,128)S(1)}, u32[]{:S(2)}, u32[]{:S(2)}) %collective-permute-start.2) | collective-permute-done | bytes 18464 | tf_op jit(solution)/shard_map/ppermute | solution.py:796
  22.2 0.2 collective-permute-start.3
  22.5 2.7 %shard_map.112.refs_0_ = bf16[4,512,768]{2,1,0:T(8,128)(2,1)} custom-call(s32[1]{0:T(128)} %bitcast.base_ref, s32[4,4]{1,0:T(4,128)S(1)} %copy-done.3, bf16[20,64,256]{2,1,0:T(8,128)(2,1)S(1)} %get-tuple-element.54.mat, f32[4,6,304,128]{3,2,1,0:T(8,128)S(1)} %get-tuple-element.43.g32, f32[6,768]{1,0:T(8,128)S(1)} %copy-done.2), custom_call_target="tpu_custom_call" | custom-call | flops 251658240 | bytes 1572864 | tf_op jit(solution)/shard_map/pallas_call | solution.py:708
  25.2 0.9 %collective-permute-done.3 = f32[6,768]{1,0:T(8,128)S(1)} collective-permute-done((f32[6,768]{1,0:T(8,128)S(1)}, f32[6,768]{1,0:T(8,128)S(1)}, u32[]{:S(2)}, u32[]{:S(2)}) %collective-permute-start.3) | collective-permute-done | bytes 18464 | tf_op jit(solution)/shard_map/ppermute | solution.py:792
  26.1 1.5 %collective-permute-start.4 = (f32[6,768]{1,0:T(8,128)S(1)}, f32[6,768]{1,0:T(8,128)S(1)}, u32[]{:S(2)}, u32[]{:S(2)}) collective-permute-start(f32[6,768]{1,0:T(8,128)S(1)} %add.13), channel_id=1, source_target_pairs={{0,4},{4,0},{8,12},{12,8},{16,20},{20,16},{24,28},{28,24},{1,5},{5... | collective-permute-start | bytes 55304 | tf_op jit(solution)/shard_map/ppermute | solution.py:792
  27.6 2.7 %shard_map.113.refs_0_ = bf16[4,512,768]{2,1,0:T(8,128)(2,1)} custom-call(s32[1]{0:T(128)} %bitcast.base_ref, s32[4,4]{1,0:T(4,128)S(1)} %copy-done.3, bf16[20,64,256]{2,1,0:T(8,128)(2,1)S(1)} %get-tuple-element.54.mat, f32[4,6,304,128]{3,2,1,0:T(8,128)S(1)} %get-tuple-element.43.g32, f32[6,768]{1,0:T(8,128)S(1)} %copy-done.2, ...), custom_call_target="tpu_custom_call", output_to_operand_aliasing={{}: (5, {})} | custom-call | flops 251658240 | bytes 1572864 | tf_op jit(solution)/shard_map/pallas_call | solution.py:708
  30.3 0.0 collective-permute-done.4
  30.3 1.6 %collective-permute-start.5 = (f32[6,768]{1,0:T(8,128)S(1)}, f32[6,768]{1,0:T(8,128)S(1)}, u32[]{:S(2)}, u32[]{:S(2)}) collective-permute-start(f32[6,768]{1,0:T(8,128)S(1)} %add.14), channel_id=1, source_target_pairs={{0,8},{4,12},{8,0},{12,4},{16,24},{20,28},{24,16},{28,20},{1,9},{5... | collective-permute-start | bytes 55304 | tf_op jit(solution)/shard_map/ppermute | solution.py:792
  31.9 2.7 %shard_map.114.refs_0_ = bf16[4,512,768]{2,1,0:T(8,128)(2,1)} custom-call(s32[1]{0:T(128)} %bitcast.base_ref, s32[4,4]{1,0:T(4,128)S(1)} %copy-done.3, bf16[20,64,256]{2,1,0:T(8,128)(2,1)S(1)} %get-tuple-element.54.mat, f32[4,6,304,128]{3,2,1,0:T(8,128)S(1)} %get-tuple-element.43.g32, f32[6,768]{1,0:T(8,128)S(1)} %copy-done.2, ...), custom_call_target="tpu_custom_call", output_to_operand_aliasing={{}: (5, {})} | custom-call | flops 251658240 | bytes 1572864 | tf_op jit(solution)/shard_map/pallas_call | solution.py:708
  34.6 0.0 collective-permute-done.5
  34.6 0.0 copy-start.4
  34.6 0.0 copy-start.5
  34.7 2.6 %collective-permute-start.6 = (f32[6,768]{1,0:T(8,128)S(1)}, f32[6,768]{1,0:T(8,128)S(1)}, u32[]{:S(2)}, u32[]{:S(2)}) collective-permute-start(f32[6,768]{1,0:T(8,128)S(1)} %add.15.grad_ref), channel_id=1, source_target_pairs={{0,16},{4,20},{8,24},{12,28},{16,0},{20,4},{24,8},{28,12},{1,17},{... | collective-permute-start | bytes 55304 | tf_op jit(solution)/shard_map/ppermute | solution.py:792
  37.3 2.7 %shard_map.115 = bf16[4,512,768]{2,1,0:T(8,128)(2,1)} custom-call(s32[1]{0:T(128)} %bitcast.base_ref, s32[4,4]{1,0:T(4,128)S(1)} %copy-done.3, bf16[20,64,256]{2,1,0:T(8,128)(2,1)S(1)} %get-tuple-element.54.mat, f32[4,6,304,128]{3,2,1,0:T(8,128)S(1)} %get-tuple-element.43.g32, f32[6,768]{1,0:T(8,128)S(1)} %copy-done.2, ...), custom_call_target="tpu_custom_call", output_to_operand_aliasing={{}: (5, {})} | custom-call | flops 251658240 | bytes 1572864 | tf_op jit(solution)/shard_map/pallas_call | solution.py:708
  40.0 0.0 collective-permute-done.6.other_ref
  40.0 0.0 copy-done.4
  40.0 0.0 copy-done.5
  40.0 0.8 %shard_map.116 = (f32[1,1]{1,0:T(1,128)}, f32[6,768]{1,0:T(8,128)}, f32[6,768]{1,0:T(8,128)}, f32[6,768]{1,0:T(8,128)}) custom-call(f32[6,768]{1,0:T(8,128)S(1)} %add.15.grad_ref, f32[6,768]{1,0:T(8,128)S(1)} %collective-permute-done.6.other_ref, f32[6,768]{1,0:T(8,128)S(1)} %copy-done.2, f32[6,768]{1,0:T(8,128)S(1)} %copy-done.4, f32[6,768]{1,0:T(8,128)S(1)} %copy-done.5), custom_call_target="tpu_custom_call" | custom-call | tf_op jit(solution)/shard_map/pallas_call | solution.py:749
  (4 shorter events, 0.0 us)
Async XLA Ops:
  0.6 2.5 %copy-start = (bf16[4,512,768]{2,1,0:T(8,128)(2,1)S(1)}, bf16[4,512,768]{2,1,0:T(8,128)(2,1)}, u32[]{:S(2)}) copy-start(bf16[4,512,768]{2,1,0:T(8,128)(2,1)} %x_ref.3) | copy-start | bytes 9437188
  0.6 2.5 %copy-start.2 = (f32[6,768]{1,0:T(8,128)S(1)}, f32[6,768]{1,0:T(8,128)}, u32[]{:S(2)}) copy-start(f32[6,768]{1,0:T(8,128)} %par_ref.13) | copy-start | bytes 55300
  0.7 2.5 %copy-start.3 = (s32[4,4]{1,0:T(4,128)S(1)}, s32[4,4]{1,0:T(4,128)}, u32[]{:S(2)}) copy-start(s32[4,4]{1,0:T(4,128)} %len_ref.11) | copy-start | bytes 196
  0.7 6.9 %copy-start.1 = (bf16[4,256,768]{2,1,0:T(8,128)(2,1)S(1)}, bf16[4,256,768]{2,1,0:T(8,128)(2,1)}, u32[]{:S(2)}) copy-start(bf16[4,256,768]{2,1,0:T(8,128)(2,1)} %g_ref.1) | copy-start | bytes 4718596
  2.0 5.6 %collective-permute-start = (bf16[4,16,768]{2,1,0:T(8,128)(2,1)S(1)}, bf16[4,16,768]{2,1,0:T(8,128)(2,1)S(1)}, u32[]{:S(2)}, u32[]{:S(2)}) collective-permute-start(bf16[4,16,768]{2,1,0:T(8,128)(2,1)S(1)} %get-tuple-element.36), channel_id=1, source_target_pairs={{0,1},{2,3},{1,0},{3,2},{4,5},{6,7},{5,4},{7,6},{8,9},{10,11},{9,8... | collective-permute-start | bytes 294920 | tf_op jit(solution)/shard_map/ppermute | solution.py:774
  2.5 5.1 %collective-permute-start.1 = (bf16[4,16,768]{2,1,0:T(8,128)(2,1)S(1)}, bf16[4,16,768]{2,1,0:T(8,128)(2,1)S(1)}, u32[]{:S(2)}, u32[]{:S(2)}) collective-permute-start(bf16[4,16,768]{2,1,0:T(8,128)(2,1)S(1)} %get-tuple-element.37), channel_id=1, source_target_pairs={{1,2},{2,1},{5,6},{6,5},{9,10},{10,9},{13,14},{14,13},{17,18},{18,... | collective-permute-start | bytes 294920 | tf_op jit(solution)/shard_map/ppermute | solution.py:773
  17.2 5.0 %collective-permute-start.2 = (f32[6,768]{1,0:T(8,128)S(1)}, f32[6,768]{1,0:T(8,128)S(1)}, u32[]{:S(2)}, u32[]{:S(2)}) collective-permute-start(f32[6,768]{1,0:T(8,128)S(1)} %get-tuple-element.40), channel_id=1, source_target_pairs={{0,1},{1,0},{2,3},{3,2},{4,5},{5,4},{6,7},{7,6},{8,9},{9,8},{10,11... | collective-permute-start | bytes 55304 | tf_op jit(solution)/shard_map/ppermute | solution.py:796
  22.2 3.8 %collective-permute-start.3 = (f32[6,768]{1,0:T(8,128)S(1)}, f32[6,768]{1,0:T(8,128)S(1)}, u32[]{:S(2)}, u32[]{:S(2)}) collective-permute-start(f32[6,768]{1,0:T(8,128)S(1)} %add.12), channel_id=1, source_target_pairs={{0,2},{1,3},{2,0},{3,1},{4,6},{5,7},{6,4},{7,5},{8,10},{9,11},{10,... | collective-permute-start | bytes 55304 | tf_op jit(solution)/shard_map/ppermute | solution.py:792
  26.1 4.2 %collective-permute-start.4 = (f32[6,768]{1,0:T(8,128)S(1)}, f32[6,768]{1,0:T(8,128)S(1)}, u32[]{:S(2)}, u32[]{:S(2)}) collective-permute-start(f32[6,768]{1,0:T(8,128)S(1)} %add.13), channel_id=1, source_target_pairs={{0,4},{4,0},{8,12},{12,8},{16,20},{20,16},{24,28},{28,24},{1,5},{5... | collective-permute-start | bytes 55304 | tf_op jit(solution)/shard_map/ppermute | solution.py:792
  30.3 4.3 %collective-permute-start.5 = (f32[6,768]{1,0:T(8,128)S(1)}, f32[6,768]{1,0:T(8,128)S(1)}, u32[]{:S(2)}, u32[]{:S(2)}) collective-permute-start(f32[6,768]{1,0:T(8,128)S(1)} %add.14), channel_id=1, source_target_pairs={{0,8},{4,12},{8,0},{12,4},{16,24},{20,28},{24,16},{28,20},{1,9},{5... | collective-permute-start | bytes 55304 | tf_op jit(solution)/shard_map/ppermute | solution.py:792
  34.6 5.4 %copy-start.4 = (f32[6,768]{1,0:T(8,128)S(1)}, f32[6,768]{1,0:T(8,128)}, u32[]{:S(2)}) copy-start(f32[6,768]{1,0:T(8,128)} %first_ref.1) | copy-start | bytes 55300
  34.6 5.4 %copy-start.5 = (f32[6,768]{1,0:T(8,128)S(1)}, f32[6,768]{1,0:T(8,128)}, u32[]{:S(2)}) copy-start(f32[6,768]{1,0:T(8,128)} %second_ref.1) | copy-start | bytes 55300
  34.7 5.3 %collective-permute-start.6 = (f32[6,768]{1,0:T(8,128)S(1)}, f32[6,768]{1,0:T(8,128)S(1)}, u32[]{:S(2)}, u32[]{:S(2)}) collective-permute-start(f32[6,768]{1,0:T(8,128)S(1)} %add.15.grad_ref), channel_id=1, source_target_pairs={{0,16},{4,20},{8,24},{12,28},{16,0},{20,4},{24,8},{28,12},{1,17},{... | collective-permute-start | bytes 55304 | tf_op jit(solution)/shard_map/ppermute | solution.py:792

commit v8 on v7

--- a/solution.py
+++ b/solution.py
@@ -120,30 +120,34 @@
         place_low(c, low)
 
 
-def conv_kernel(shapes, base_ref, len_ref, x_ref, par_ref, high_ref, low_ref, xf):
+def conv_kernel(shapes, base_ref, len_hbm, x_ref, par_ref, high_ref, low_ref, xf, len_ref, sem):
     rows, length, half, features, tiles = shapes
     chunks = features // 128
     base = base_ref[0]
     step = 64
-    for c in range(chunks):
-        xf[c, 0:8, :] = jnp.zeros((8, 128), F32)
-    rest = high_ref.shape[2] - PAD - length
+    copy_len = pltpu.make_async_copy(len_hbm, len_ref, sem.at[0])
+    copy_len.start()
+    begin = 2 * PAD + length
+    rest = high_ref.shape[2] - begin
     for r in range(rows):
         for c in range(chunks):
-            for ref in (high_ref, low_ref):
-                ref[r, c, 0:PAD, :] = jnp.zeros((PAD, 128), BF16)
-                ref[r, c, PAD + length :, :] = jnp.zeros((rest, 128), BF16)
+            xf[r, c, 0:8, :] = jnp.zeros((8, 128), F32)
+            if rest > 0:
+                for ref in (high_ref, low_ref):
+                    ref[r, c, begin:, :] = jnp.zeros((rest, 128), BF16)
+
+    def widen(i, _):
+        r = i // (length // step)
+        at = pl.multiple_of((i % (length // step)) * step, step)
+        for c in range(chunks):
+            xf[r, c, pl.ds(at + 8, step), :] = x_ref[r, pl.ds(at, step), lanes_of(c)].astype(F32)
+        return 0
+
+    lax.fori_loop(0, rows * (length // step), widen, 0)
+    copy_len.wait()
 
     def one_row(r, _):
         ends = ends_of(len_ref, r)
-
-        def widen(i, _):
-            at = pl.multiple_of(i * step, step)
-            for c in range(chunks):
-                xf[c, pl.ds(at + 8, step), :] = x_ref[r, pl.ds(at, step), lanes_of(c)].astype(F32)
-            return 0
-
-        lax.fori_loop(0, length // step, widen, 0)
 
         def blocks(at, masked):
             for b in range(step // 16):
@@ -158,7 +162,7 @@
                     base,
                     ends,
                     par_ref,
-                    lambda c, shift: xf[c, pl.ds(at + 8 + 16 * b + shift, 8), :],
+                    lambda c, shift: xf[r, c, pl.ds(at + 8 + 16 * b + shift, 8), :],
                     at + PAD + 16 * b,
                     put(high_ref),
                     put(low_ref),
@@ -197,7 +201,7 @@
     near_ref,
     far_ref,
     par_ref,
-    out_hbm,
+    out32,
     mat,
     g32,
     grad_ref,
@@ -211,19 +215,13 @@
     fac_b,
     tot,
     rows_e_ref,
-    out32,
-    outb,
     carry_o,
     acc,
-    sems,
 ):
     rows, length, half, features, tiles = shapes
     pairs = rows * tiles // 2
     chunks = features // 128
     base = base_ref[0]
-
-    def copy_out(r):
-        return pltpu.make_async_copy(outb.at[r], out_hbm.at[r], sems.at[r])
 
     sub8 = iota((8, 128), 0)
     lane8 = iota((8, 128), 1)
@@ -417,6 +415,10 @@
         r, m, tile = place(pair, side)
         own_e = rows_e_ref[side, 0]
         all_e = rows_e_ref[side, 1]
+        from_row = OWN * m - 8
+        mine = [
+            (from_row + 8 * i + sub8 >= 0) & (from_row + 8 * i + sub8 < half) for i in range(SLOTS // 8)
+        ]
         at = tile_start(m) + lane8
         offset = at - begin_of(at, ends_of(len_ref, r))
         bands = []
@@ -436,7 +438,9 @@
                 high, low = split(back)
                 mat[tile, :, 0:WINDOW] = high
                 mat[tile, :, WINDOW:] = low
-            matrix = jnp.concatenate([jnp.where(sub8 == 0, row_k, matrix[0:8]), matrix[8:]], axis=0)
+            parts = [jnp.where(mine[i], matrix[8 * i : 8 * i + 8], 0.0) for i in range(SLOTS // 8)]
+            parts[0] = jnp.where(sub8 == 0, row_k, parts[0])
+            matrix = jnp.concatenate(parts, axis=0)
             if k == 0:
                 total = jnp.sum(matrix, axis=1, keepdims=True)
                 tot[side] = jnp.broadcast_to(total, (SLOTS, 128))
@@ -450,8 +454,6 @@
         window = pl.multiple_of(2 * OWN * m, 16)
         factor = factors[side][...]
         total = tot[side]
-        from_row = OWN * m - 8
-        mine = [from_row + 8 * i + sub8 < half for i in range(SLOTS // 8)]
         for w in range(chunks // wide):
             x = xb[r, pl.ds(window, WINDOW), 128 * wide * w : 128 * wide * (w + 1)]
             mixed = lax.dot_general(
@@ -464,16 +466,7 @@
                 c = wide * w + i
                 lanes = lanes_of(c)
                 g = g32[r, c, pl.ds(start, SLOTS), :]
-                parts = [
-                    jnp.where(
-                        sub8 == 0,
-                        par_ref[5:6, lanes],
-                        jnp.where((sub8 >= LEAD) & (from_row + sub8 >= 0), g[0:8], 0.0),
-                    )
-                ]
-                for j in range(1, SLOTS // 8):
-                    parts.append(jnp.where(mine[j], g[8 * j : 8 * j + 8], 0.0))
-                g = jnp.concatenate(parts, axis=0)
+                g = jnp.concatenate([jnp.where(sub8 == 0, par_ref[5:6, lanes], g[0:8]), g[8:]], axis=0)
                 value = total * par_ref[4:5, lanes]
                 for k in range(TAPS):
                     taken = mixed[SLOTS * k : SLOTS * (k + 1), lanes_of(i)]
@@ -482,25 +475,15 @@
                 acc[4, :, lanes] += jnp.sum((total * g).reshape(SLOTS // 8, 8, 128), axis=0)
                 acc[5, :, lanes] += jnp.where(sub8 == 0, value[0:8], 0.0)
                 top = carry_o[side, :, lanes] + jnp.where(sub8 < LEAD, 0.0, value[0:8])
-                out32[side, c, pl.ds(start, 8), :] = top
-                out32[side, c, pl.ds(start + 8, OWN - 8), :] = value[8:OWN]
+                out32[r, c, pl.ds(start, 8), :] = top
+                out32[r, c, pl.ds(start + 8, OWN - 8), :] = value[8:OWN]
                 carry_o[side, :, lanes] = jnp.where(m < tiles - 1, value[OWN:], 0.0)
-
-    def finish(r, side):
-        for c in range(chunks):
-            outb[r, :, lanes_of(c)] = out32[side, c, PAD : PAD + half, :].astype(BF16)
-        copy_out(r).start()
 
     spread_pair(0)
     build(0, 0)
     build(0, 1)
 
     def second_loop(i, _):
-        @pl.when((i % tiles == 0) & (i > 0))
-        def _():
-            for side in range(2):
-                finish(2 * (i // tiles) - 2 + side, side)
-
         spread_pair(i + 1)
         for side in range(2):
             apply(i, side)
@@ -510,22 +493,22 @@
     lax.fori_loop(0, pairs - 1, second_loop, 0)
     apply(pairs - 1, 0)
     apply(pairs - 1, 1)
-    for side in range(2):
-        finish(rows - 2 + side, side)
     for k in range(TAPS + 2):
         grad_ref[k : k + 1, :] = jnp.sum(acc[k], axis=0, keepdims=True)
-    for r in range(rows):
-        copy_out(r).wait()
-
-
-def backward_kernel(shapes, r, base_ref, len_ref, mat, g32, par_ref, *refs):
-    gin_hbm, dc, ginb, sems = refs[-4:]
+
+
+def backward_kernel(shapes, r, base_ref, len_ref, mat, g32, out32, par_ref, *refs):
+    out_hbm, gin_hbm, outb, dc, ginb, sems = refs[-6:]
     rows, length, half, features, tiles = shapes
     chunks = features // 128
     wide = 2 if chunks % 2 == 0 else 1
     base = base_ref[0]
     sub8 = iota((8, 128), 0)
     ends = ends_of(len_ref, r)
+    for c in range(chunks):
+        outb[:, lanes_of(c)] = out32[r, c, PAD : PAD + half, :].astype(BF16)
+    copies = [pltpu.make_async_copy(outb, out_hbm.at[r], sems.at[2])]
+    copies[0].start()
 
     for m in range(tiles):
         tile = r * tiles + m
@@ -590,7 +573,6 @@
         return 0
 
     pieces = 2
-    copies = []
     for piece in range(pieces):
         size = length // pieces
         lax.fori_loop(piece * size // 32, (piece + 1) * size // 32, taps, 0)
@@ -641,9 +623,13 @@
     return pl.pallas_call(
         functools.partial(conv_kernel, shapes),
         out_shape=(part, part),
-        in_specs=[SMEM, SMEM, VMEM, VMEM],
+        in_specs=[SMEM, HBM, VMEM, VMEM],
         out_specs=(VMEM, VMEM),
-        scratch_shapes=[pltpu.VMEM((chunks, 8 + length, 128), F32)],
+        scratch_shapes=[
+            pltpu.VMEM((rows, chunks, 8 + length, 128), F32),
+            pltpu.SMEM(lengths.shape, jnp.int32),
+            pltpu.SemaphoreType.DMA((1,)),
+        ],
         compiler_params=pltpu.CompilerParams(vmem_limit_bytes=24 * 1024 * 1024),
         cost_estimate=pl.CostEstimate(
             flops=24 * inputs.size, bytes_accessed=8 * inputs.size, transcendentals=0
@@ -661,13 +647,13 @@
     return pl.pallas_call(
         functools.partial(forward_kernel, shapes),
         out_shape=(
-            jax.ShapeDtypeStruct((rows, half, features), BF16),
+            jax.ShapeDtypeStruct((rows, chunks, g_rows, 128), F32),
             jax.ShapeDtypeStruct((count, SLOTS, 2 * WINDOW), BF16),
             jax.ShapeDtypeStruct((rows, chunks, g_rows, 128), F32),
             jax.ShapeDtypeStruct((TAPS + 2, features), F32),
         ),
         in_specs=[SMEM, SMEM, VMEM, VMEM, VMEM, VMEM, VMEM, VMEM, VMEM],
-        out_specs=(HBM, VMEM, VMEM, VMEM),
+        out_specs=(VMEM, VMEM, VMEM, VMEM),
         scratch_shapes=[
             pltpu.VMEM((rows, x_rows, features), BF16),
             pltpu.VMEM((chunks, 72, 128), F32),
@@ -679,11 +665,8 @@
             pltpu.VMEM((TAPS * SLOTS, 2 * WINDOW), BF16),
             pltpu.VMEM((2, SLOTS, 128), F32),
             pltpu.VMEM((2, 2, 8, 128), F32),
-            pltpu.VMEM((2, chunks, g_rows, 128), F32),
-            pltpu.VMEM((rows, half, features), BF16),
             pltpu.VMEM((2, 8, features), F32),
             pltpu.VMEM((TAPS + 2, 8, features), F32),
-            pltpu.SemaphoreType.DMA((rows,)),
         ],
         compiler_params=pltpu.CompilerParams(vmem_limit_bytes=28 * 1024 * 1024),
         cost_estimate=pl.CostEstimate(
@@ -694,28 +677,32 @@
     )(base, lengths, inputs, cotangent, high, low, near, far, params)
 
 
-def backward(r, base, lengths, shape, matrices, padded, params, grown):
+def backward(r, base, lengths, shape, matrices, padded, outputs, params, grown):
     rows, length, features = shape
     half = length // 2
     chunks = features // 128
     tiles, x_rows, g_rows = sizes_of(length, half)
     shapes = (rows, length, half, features, tiles)
-    operands = [base, lengths, matrices, padded, params]
-    in_specs = [SMEM, SMEM, VMEM, VMEM, VMEM]
+    operands = [base, lengths, matrices, padded, outputs, params]
+    in_specs = [SMEM, SMEM, VMEM, VMEM, VMEM, VMEM]
     if grown is not None:
-        operands.append(grown)
-        in_specs.append(HBM)
+        operands.extend(grown)
+        in_specs.extend([HBM, HBM])
     return pl.pallas_call(
         functools.partial(backward_kernel, shapes, r),
-        out_shape=jax.ShapeDtypeStruct(shape, BF16),
+        out_shape=(
+            jax.ShapeDtypeStruct((rows, half, features), BF16),
+            jax.ShapeDtypeStruct(shape, BF16),
+        ),
         in_specs=in_specs,
-        out_specs=HBM,
+        out_specs=(HBM, HBM),
         scratch_shapes=[
+            pltpu.VMEM((half, features), BF16),
             pltpu.VMEM((chunks, x_rows, 128), F32),
             pltpu.VMEM((length, features), BF16),
-            pltpu.SemaphoreType.DMA((2,)),
+            pltpu.SemaphoreType.DMA((3,)),
         ],
-        input_output_aliases={} if grown is None else {5: 0},
+        input_output_aliases={} if grown is None else {6: 0, 7: 1},
         compiler_params=pltpu.CompilerParams(vmem_limit_bytes=12 * 1024 * 1024),
         cost_estimate=pl.CostEstimate(
             flops=2 * tiles * SLOTS * WINDOW * features * 4,
@@ -773,14 +760,14 @@
     far = lax.ppermute(far, "group", pairs_of("group", 1))
     near = lax.ppermute(near, "group", pairs_of("group", 0))
     high, low = convolved(base, lengths, inputs, params)
-    output, matrices, padded, grad_params = forward(
+    outputs, matrices, padded, grad_params = forward(
         base, lengths, inputs, cotangent, high, low, near, far, params
     )
 
     def backward_row(row, matrices, grown):
-        return backward(row, base, lengths, inputs.shape, matrices, padded, params, grown)
-
-    grad_inputs = None
+        return backward(row, base, lengths, inputs.shape, matrices, padded, outputs, params, grown)
+
+    grown = None
     row = 0
     received = None
     for axis, exchange in rounds_of(("group", "rows")):
@@ -788,15 +775,16 @@
             grad_params = grad_params + received
             if row < rows_here:
                 matrices, grad_params = lax.optimization_barrier((matrices, grad_params))
-                grown = backward_row(row, matrices, grad_inputs)
+                grown = backward_row(row, matrices, grown)
                 received = lax.ppermute(grad_params, axis, exchange)
-                received, grad_inputs = lax.optimization_barrier((received, grown))
+                received, grown = lax.optimization_barrier((received, grown))
                 row += 1
                 continue
         received = lax.ppermute(grad_params, axis, exchange)
     while row < rows_here:
-        grad_inputs = backward_row(row, matrices, grad_inputs)
+        grown = backward_row(row, matrices, grown)
         row += 1
+    output, grad_inputs = grown
     grad_norm, new_params, new_first, new_second = update(
         grad_params, received, params, first_moment, second_moment
     )

time: 41 us -> 39.8 us (0.971)
  Pallas kernels: 26.9 us -> 25.8 us
    pallas_call x1, Pallas kernels: 9.64 us -> 8.81 us  [forward(): pl.pallas_call(functools.partial(forward_kernel, shapes), out_shape=(jax....]
  transfers between devices with their start and end apart: 7 -> 7, of which waited for: 2 -> 2; matrix products, arithmetic and copies ran while one was open for 0% -> 0% of each run, Pallas kernels for 37% -> 38%
where the time goes in v8:
time: 39.8 us; the launch traced here: 39.6 us
  Pallas kernels  25.8 us (65%)
  starting transfers between devices  11.2 us (28%)
  waiting for transfers between devices  1.78 us (4%)
  between operations  0.85 us (2%)
    pallas_call x4, Pallas kernels, backward(): pl.pallas_call(functools.partial(backward_kernel, shapes, r), out_shape=(...  10.9 us
    ppermute x5, starting transfers between devices, per_device(): received = lax.ppermute(grad_params, axis, exchange)  9.98 us
    pallas_call x1, Pallas kernels, forward(): pl.pallas_call(functools.partial(forward_kernel, shapes), out_shape=(jax....  8.81 us
    pallas_call x1, Pallas kernels, convolved(): pl.pallas_call(functools.partial(conv_kernel, shapes), out_shape=(part, p...  4.05 us
    ppermute x5, waiting for transfers between devices, per_device(): received = lax.ppermute(grad_params, axis, exchange)  1.78 us
    pallas_call x1, Pallas kernels, packed(): pl.pallas_call(pack_kernel, out_shape=(part, part), in_specs=[SMEM, HBM,...  1.29 us
  transfers between devices with their start and end apart: 7, of which 2 were waited for; matrix products, arithmetic and copies ran while one was open for 0% of the time, Pallas kernels for 38%

profile of v8, /device:TPU:0, one launch (start us, length us, event | category | flops | bytes accessed | tf_op | source)
XLA Modules:
  0.0 39.6 jit_solution(14536210465099675855)
XLA Ops:
  0.6 0.0 copy-start
  0.6 0.0 copy-start.2
  0.7 0.0 copy-start.3
  0.7 0.0 copy-start.1
  0.7 1.3 %shard_map.110 = (bf16[4,16,768]{2,1,0:T(8,128)(2,1)S(1)}, bf16[4,16,768]{2,1,0:T(8,128)(2,1)S(1)}) custom-call(s32[1]{0:T(128)} %bitcast.base_ref, bf16[4,512,768]{2,1,0:T(8,128)(2,1)} %x_ref.3, bf16[4,256,768]{2,1,0:T(8,128)(2,1)} %g_ref.1), custom_call_target="tpu_custom_call" | custom-call | tf_op jit(solution)/shard_map/pallas_call | solution.py:606
  2.0 0.5 %collective-permute-start = (bf16[4,16,768]{2,1,0:T(8,128)(2,1)S(1)}, bf16[4,16,768]{2,1,0:T(8,128)(2,1)S(1)}, u32[]{:S(2)}, u32[]{:S(2)}) collective-permute-start(bf16[4,16,768]{2,1,0:T(8,128)(2,1)S(1)} %get-tuple-element.48), channel_id=1, source_target_pairs={{0,1},{2,3},{1,0},{3,2},{4,5},{6,7},{5,4},{7,6},{8,9},{10,11},{9,8... | collective-permute-start | bytes 294920 | tf_op jit(solution)/shard_map/ppermute | solution.py:761
  2.5 0.7 %collective-permute-start.1 = (bf16[4,16,768]{2,1,0:T(8,128)(2,1)S(1)}, bf16[4,16,768]{2,1,0:T(8,128)(2,1)S(1)}, u32[]{:S(2)}, u32[]{:S(2)}) collective-permute-start(bf16[4,16,768]{2,1,0:T(8,128)(2,1)S(1)} %get-tuple-element.49), channel_id=1, source_target_pairs={{1,2},{2,1},{5,6},{6,5},{9,10},{10,9},{13,14},{14,13},{17,18},{18,... | collective-permute-start | bytes 294920 | tf_op jit(solution)/shard_map/ppermute | solution.py:760
  3.2 0.0 copy-done
  3.2 0.0 copy-done.2
  3.2 0.0 copy-done.3
  3.2 4.1 %shard_map.109 = (bf16[4,6,576,128]{3,2,1,0:T(8,128)(2,1)S(1)}, bf16[4,6,576,128]{3,2,1,0:T(8,128)(2,1)S(1)}) custom-call(s32[1]{0:T(128)} %bitcast.base_ref, s32[4,4]{1,0:T(4,128)S(1)} %copy-done.3, bf16[4,512,768]{2,1,0:T(8,128)(2,1)S(1)} %copy-done, f32[6,768]{1,0:T(8,128)S(1)} %copy-done.2), custom_call_target="tpu_custom_call" | custom-call | flops 37748736 | bytes 12582912 | tf_op jit(solution)/shard_map/pallas_call | solution.py:623
  7.3 0.0 collective-permute-done.near_ref
  7.3 0.0 collective-permute-done.1.far_ref
  7.3 0.0 copy-done.1
  7.3 8.8 %shard_map.111 = (f32[4,6,304,128]{3,2,1,0:T(8,128)S(1)}, bf16[20,64,256]{2,1,0:T(8,128)(2,1)S(1)}, f32[4,6,304,128]{3,2,1,0:T(8,128)S(1)}, f32[6,768]{1,0:T(8,128)S(1)}) custom-call(s32[1]{0:T(128)} %bitcast.base_ref, s32[4,4]{1,0:T(4,128)S(1)} %copy-done.3, bf16[4,512,768]{2,1,0:T(8,128)(2,1)S(1)} %copy-done, bf16[4,256,768]{2,1,0:T(8,128)(2,1)S(1)} %copy-done.1, ...), custom_call_target="tpu_custom_call" | custom-call | flops 3019898880 | bytes 12582912 | tf_op jit(solution)/shard_map/pallas_call | solution.py:647
  16.1 4.0 %collective-permute-start.2 = (f32[6,768]{1,0:T(8,128)S(1)}, f32[6,768]{1,0:T(8,128)S(1)}, u32[]{:S(2)}, u32[]{:S(2)}) collective-permute-start(f32[6,768]{1,0:T(8,128)S(1)} %get-tuple-element.51), channel_id=1, source_target_pairs={{0,1},{1,0},{2,3},{3,2},{4,5},{5,4},{6,7},{7,6},{8,9},{9,8},{10,11... | collective-permute-start | bytes 55304 | tf_op jit(solution)/shard_map/ppermute | solution.py:783
  20.1 0.8 %collective-permute-done.2 = f32[6,768]{1,0:T(8,128)S(1)} collective-permute-done((f32[6,768]{1,0:T(8,128)S(1)}, f32[6,768]{1,0:T(8,128)S(1)}, u32[]{:S(2)}, u32[]{:S(2)}) %collective-permute-start.2) | collective-permute-done | bytes 18464 | tf_op jit(solution)/shard_map/ppermute | solution.py:783
  21.0 0.2 collective-permute-start.3
  21.2 2.7 %shard_map.112 = (bf16[4,256,768]{2,1,0:T(8,128)(2,1)}, bf16[4,512,768]{2,1,0:T(8,128)(2,1)}) custom-call(s32[1]{0:T(128)} %bitcast.base_ref, s32[4,4]{1,0:T(4,128)S(1)} %copy-done.3, bf16[20,64,256]{2,1,0:T(8,128)(2,1)S(1)} %get-tuple-element.74.mat, f32[4,6,304,128]{3,2,1,0:T(8,128)S(1)} %get-tuple-element.54.g32, ...), custom_call_target="tpu_custom_call" | custom-call | flops 251658240 | bytes 1572864 | tf_op jit(solution)/shard_map/pallas_call | solution.py:691
  23.9 0.9 %collective-permute-done.3 = f32[6,768]{1,0:T(8,128)S(1)} collective-permute-done((f32[6,768]{1,0:T(8,128)S(1)}, f32[6,768]{1,0:T(8,128)S(1)}, u32[]{:S(2)}, u32[]{:S(2)}) %collective-permute-start.3) | collective-permute-done | bytes 18464 | tf_op jit(solution)/shard_map/ppermute | solution.py:779
  24.8 1.4 %collective-permute-start.4 = (f32[6,768]{1,0:T(8,128)S(1)}, f32[6,768]{1,0:T(8,128)S(1)}, u32[]{:S(2)}, u32[]{:S(2)}) collective-permute-start(f32[6,768]{1,0:T(8,128)S(1)} %add.13), channel_id=1, source_target_pairs={{0,4},{4,0},{8,12},{12,8},{16,20},{20,16},{24,28},{28,24},{1,5},{5... | collective-permute-start | bytes 55304 | tf_op jit(solution)/shard_map/ppermute | solution.py:779
  26.3 2.7 %shard_map.113 = (bf16[4,256,768]{2,1,0:T(8,128)(2,1)}, bf16[4,512,768]{2,1,0:T(8,128)(2,1)}) custom-call(s32[1]{0:T(128)} %bitcast.base_ref, s32[4,4]{1,0:T(4,128)S(1)} %copy-done.3, bf16[20,64,256]{2,1,0:T(8,128)(2,1)S(1)} %get-tuple-element.74.mat, f32[4,6,304,128]{3,2,1,0:T(8,128)S(1)} %get-tuple-element.54.g32, ...), custom_call_target="tpu_custom_call", output_to_operand_aliasing={{0}: (6, {}), {1}: (7, {})} | custom-call | flops 251658240 | bytes 1572864 | tf_op jit(solution)/shard_map/pallas_call | solution.py:691
  29.0 0.0 collective-permute-done.4
  29.0 1.7 %collective-permute-start.5 = (f32[6,768]{1,0:T(8,128)S(1)}, f32[6,768]{1,0:T(8,128)S(1)}, u32[]{:S(2)}, u32[]{:S(2)}) collective-permute-start(f32[6,768]{1,0:T(8,128)S(1)} %add.14), channel_id=1, source_target_pairs={{0,8},{4,12},{8,0},{12,4},{16,24},{20,28},{24,16},{28,20},{1,9},{5... | collective-permute-start | bytes 55304 | tf_op jit(solution)/shard_map/ppermute | solution.py:779
  30.7 2.7 %shard_map.114 = (bf16[4,256,768]{2,1,0:T(8,128)(2,1)}, bf16[4,512,768]{2,1,0:T(8,128)(2,1)}) custom-call(s32[1]{0:T(128)} %bitcast.base_ref, s32[4,4]{1,0:T(4,128)S(1)} %copy-done.3, bf16[20,64,256]{2,1,0:T(8,128)(2,1)S(1)} %get-tuple-element.74.mat, f32[4,6,304,128]{3,2,1,0:T(8,128)S(1)} %get-tuple-element.54.g32, ...), custom_call_target="tpu_custom_call", output_to_operand_aliasing={{0}: (6, {}), {1}: (7, {})} | custom-call | flops 251658240 | bytes 1572864 | tf_op jit(solution)/shard_map/pallas_call | solution.py:691
  33.4 0.0 collective-permute-done.5
  33.4 0.0 copy-start.4
  33.4 0.0 copy-start.5
  33.4 2.7 %collective-permute-start.6 = (f32[6,768]{1,0:T(8,128)S(1)}, f32[6,768]{1,0:T(8,128)S(1)}, u32[]{:S(2)}, u32[]{:S(2)}) collective-permute-start(f32[6,768]{1,0:T(8,128)S(1)} %add.15.grad_ref), channel_id=1, source_target_pairs={{0,16},{4,20},{8,24},{12,28},{16,0},{20,4},{24,8},{28,12},{1,17},{... | collective-permute-start | bytes 55304 | tf_op jit(solution)/shard_map/ppermute | solution.py:779
  36.1 2.7 %shard_map.115 = (bf16[4,256,768]{2,1,0:T(8,128)(2,1)}, bf16[4,512,768]{2,1,0:T(8,128)(2,1)}) custom-call(s32[1]{0:T(128)} %bitcast.base_ref, s32[4,4]{1,0:T(4,128)S(1)} %copy-done.3, bf16[20,64,256]{2,1,0:T(8,128)(2,1)S(1)} %get-tuple-element.74.mat, f32[4,6,304,128]{3,2,1,0:T(8,128)S(1)} %get-tuple-element.54.g32, ...), custom_call_target="tpu_custom_call", output_to_operand_aliasing={{0}: (6, {}), {1}: (7, {})} | custom-call | flops 251658240 | bytes 1572864 | tf_op jit(solution)/shard_map/pallas_call | solution.py:691
  38.8 0.0 collective-permute-done.6.other_ref
  38.8 0.0 copy-done.4
  38.8 0.0 copy-done.5
  38.9 0.8 %shard_map.116 = (f32[1,1]{1,0:T(1,128)}, f32[6,768]{1,0:T(8,128)}, f32[6,768]{1,0:T(8,128)}, f32[6,768]{1,0:T(8,128)}) custom-call(f32[6,768]{1,0:T(8,128)S(1)} %add.15.grad_ref, f32[6,768]{1,0:T(8,128)S(1)} %collective-permute-done.6.other_ref, f32[6,768]{1,0:T(8,128)S(1)} %copy-done.2, f32[6,768]{1,0:T(8,128)S(1)} %copy-done.4, f32[6,768]{1,0:T(8,128)S(1)} %copy-done.5), custom_call_target="tpu_custom_call" | custom-call | tf_op jit(solution)/shard_map/pallas_call | solution.py:736
  (4 shorter events, 0.0 us)
Async XLA Ops:
  0.6 2.5 %copy-start = (bf16[4,512,768]{2,1,0:T(8,128)(2,1)S(1)}, bf16[4,512,768]{2,1,0:T(8,128)(2,1)}, u32[]{:S(2)}) copy-start(bf16[4,512,768]{2,1,0:T(8,128)(2,1)} %x_ref.3) | copy-start | bytes 9437188
  0.6 2.5 %copy-start.2 = (f32[6,768]{1,0:T(8,128)S(1)}, f32[6,768]{1,0:T(8,128)}, u32[]{:S(2)}) copy-start(f32[6,768]{1,0:T(8,128)} %par_ref.13) | copy-start | bytes 55300
  0.7 2.5 %copy-start.3 = (s32[4,4]{1,0:T(4,128)S(1)}, s32[4,4]{1,0:T(4,128)}, u32[]{:S(2)}) copy-start(s32[4,4]{1,0:T(4,128)} %len_ref.9) | copy-start | bytes 196
  0.7 6.6 %copy-start.1 = (bf16[4,256,768]{2,1,0:T(8,128)(2,1)S(1)}, bf16[4,256,768]{2,1,0:T(8,128)(2,1)}, u32[]{:S(2)}) copy-start(bf16[4,256,768]{2,1,0:T(8,128)(2,1)} %g_ref.1) | copy-start | bytes 4718596
  2.0 5.3 %collective-permute-start = (bf16[4,16,768]{2,1,0:T(8,128)(2,1)S(1)}, bf16[4,16,768]{2,1,0:T(8,128)(2,1)S(1)}, u32[]{:S(2)}, u32[]{:S(2)}) collective-permute-start(bf16[4,16,768]{2,1,0:T(8,128)(2,1)S(1)} %get-tuple-element.48), channel_id=1, source_target_pairs={{0,1},{2,3},{1,0},{3,2},{4,5},{6,7},{5,4},{7,6},{8,9},{10,11},{9,8... | collective-permute-start | bytes 294920 | tf_op jit(solution)/shard_map/ppermute | solution.py:761
  2.5 4.8 %collective-permute-start.1 = (bf16[4,16,768]{2,1,0:T(8,128)(2,1)S(1)}, bf16[4,16,768]{2,1,0:T(8,128)(2,1)S(1)}, u32[]{:S(2)}, u32[]{:S(2)}) collective-permute-start(bf16[4,16,768]{2,1,0:T(8,128)(2,1)S(1)} %get-tuple-element.49), channel_id=1, source_target_pairs={{1,2},{2,1},{5,6},{6,5},{9,10},{10,9},{13,14},{14,13},{17,18},{18,... | collective-permute-start | bytes 294920 | tf_op jit(solution)/shard_map/ppermute | solution.py:760
  16.1 4.9 %collective-permute-start.2 = (f32[6,768]{1,0:T(8,128)S(1)}, f32[6,768]{1,0:T(8,128)S(1)}, u32[]{:S(2)}, u32[]{:S(2)}) collective-permute-start(f32[6,768]{1,0:T(8,128)S(1)} %get-tuple-element.51), channel_id=1, source_target_pairs={{0,1},{1,0},{2,3},{3,2},{4,5},{5,4},{6,7},{7,6},{8,9},{9,8},{10,11... | collective-permute-start | bytes 55304 | tf_op jit(solution)/shard_map/ppermute | solution.py:783
  21.0 3.8 %collective-permute-start.3 = (f32[6,768]{1,0:T(8,128)S(1)}, f32[6,768]{1,0:T(8,128)S(1)}, u32[]{:S(2)}, u32[]{:S(2)}) collective-permute-start(f32[6,768]{1,0:T(8,128)S(1)} %add.12), channel_id=1, source_target_pairs={{0,2},{1,3},{2,0},{3,1},{4,6},{5,7},{6,4},{7,5},{8,10},{9,11},{10,... | collective-permute-start | bytes 55304 | tf_op jit(solution)/shard_map/ppermute | solution.py:779
  24.8 4.1 %collective-permute-start.4 = (f32[6,768]{1,0:T(8,128)S(1)}, f32[6,768]{1,0:T(8,128)S(1)}, u32[]{:S(2)}, u32[]{:S(2)}) collective-permute-start(f32[6,768]{1,0:T(8,128)S(1)} %add.13), channel_id=1, source_target_pairs={{0,4},{4,0},{8,12},{12,8},{16,20},{20,16},{24,28},{28,24},{1,5},{5... | collective-permute-start | bytes 55304 | tf_op jit(solution)/shard_map/ppermute | solution.py:779
  29.0 4.4 %collective-permute-start.5 = (f32[6,768]{1,0:T(8,128)S(1)}, f32[6,768]{1,0:T(8,128)S(1)}, u32[]{:S(2)}, u32[]{:S(2)}) collective-permute-start(f32[6,768]{1,0:T(8,128)S(1)} %add.14), channel_id=1, source_target_pairs={{0,8},{4,12},{8,0},{12,4},{16,24},{20,28},{24,16},{28,20},{1,9},{5... | collective-permute-start | bytes 55304 | tf_op jit(solution)/shard_map/ppermute | solution.py:779
  33.4 5.4 %copy-start.4 = (f32[6,768]{1,0:T(8,128)S(1)}, f32[6,768]{1,0:T(8,128)}, u32[]{:S(2)}) copy-start(f32[6,768]{1,0:T(8,128)} %first_ref.1) | copy-start | bytes 55300
  33.4 5.4 %copy-start.5 = (f32[6,768]{1,0:T(8,128)S(1)}, f32[6,768]{1,0:T(8,128)}, u32[]{:S(2)}) copy-start(f32[6,768]{1,0:T(8,128)} %second_ref.1) | copy-start | bytes 55300
  33.4 5.4 %collective-permute-start.6 = (f32[6,768]{1,0:T(8,128)S(1)}, f32[6,768]{1,0:T(8,128)S(1)}, u32[]{:S(2)}, u32[]{:S(2)}) collective-permute-start(f32[6,768]{1,0:T(8,128)S(1)} %add.15.grad_ref), channel_id=1, source_target_pairs={{0,16},{4,20},{8,24},{12,28},{16,0},{20,4},{24,8},{28,12},{1,17},{... | collective-permute-start | bytes 55304 | tf_op jit(solution)/shard_map/ppermute | solution.py:779

commit v9 on v8

--- a/solution.py
+++ b/solution.py
@@ -193,7 +193,7 @@
 def forward_kernel(
     shapes,
     base_ref,
-    len_ref,
+    len_hbm,
     x_ref,
     g_ref,
     high_ref,
@@ -217,11 +217,15 @@
     rows_e_ref,
     carry_o,
     acc,
+    len_ref,
+    sem,
 ):
     rows, length, half, features, tiles = shapes
     pairs = rows * tiles // 2
     chunks = features // 128
     base = base_ref[0]
+    copy_len = pltpu.make_async_copy(len_hbm, len_ref, sem.at[0])
+    copy_len.start()
 
     sub8 = iota((8, 128), 0)
     lane8 = iota((8, 128), 1)
@@ -245,52 +249,9 @@
     acc[...] = jnp.zeros_like(acc)
     carry_o[...] = jnp.zeros_like(carry_o)
 
-    subd = iota((8, features), 0)
-    even = (base // length) % 2 == 0
     for r in range(rows):
-        near = near_ref[r].astype(F32)
-        far = far_ref[r].astype(F32)
-        up = jnp.where(even, far, near)
-        down = jnp.where(even, near, far)
-        xb[r, 0:PAD, :] = up.astype(BF16)
-        xb[r, PAD + length : 2 * PAD + length, :] = down.astype(BF16)
-        rest = xb.shape[1] - 2 * PAD - length
-        if rest > 0:
-            xb[r, 2 * PAD + length :, :] = jnp.zeros((rest, features), BF16)
-        xb[r, PAD : PAD + length, :] = x_ref[r]
-        before = jnp.where(subd >= 6, pltpu.roll(up[0:8], 6, 0), 0.0)
-        after = jnp.where(subd < 3, pltpu.roll(down[8:16], 3, 0), 0.0)
-        rest = g32.shape[2] - PAD - half - 8
         for c in range(chunks):
-            g32[r, c, 8:16, :] = before[:, lanes_of(c)]
             g32[r, c, PAD : PAD + half, :] = g_ref[r, :, lanes_of(c)].astype(F32)
-            g32[r, c, PAD + half : PAD + half + 8, :] = after[:, lanes_of(c)]
-            g32[r, c, PAD + half + 8 :, :] = jnp.zeros((rest, 128), F32)
-        for c in range(chunks):
-            lanes = lanes_of(c)
-            xf[c, 0:8, :] = jnp.zeros((8, 128), F32)
-            xf[c, 8:24, :] = up[:, lanes]
-            xf[c, 24:40, :] = x_ref[r, 0:16, lanes].astype(F32)
-            xf[c, 40:56, :] = x_ref[r, length - 16 : length, lanes].astype(F32)
-            xf[c, 56:72, :] = down[:, lanes]
-        ends = ends_of(len_ref, r)
-        for at, where, slot in ((0, 8, 0), (PAD, 24, 16), (PAD + length, 56, 32)):
-
-            def put(first):
-                def store(c, value):
-                    edge[r, c, first : first + 16, :] = value
-
-                return store
-
-            convolve_block(
-                base,
-                ends,
-                par_ref,
-                lambda c, shift: xf[c, where + shift : where + shift + 8, :],
-                at,
-                put(slot),
-                put(48 + slot),
-            )
 
     scorer_high = [par_ref[5:6, lanes_of(c)].astype(BF16).astype(F32) for c in range(chunks)]
     scorer_low = [par_ref[5:6, lanes_of(c)] - scorer_high[c] for c in range(chunks)]
@@ -312,7 +273,7 @@
                 parts.append(ref[r, c, at + begin : at + WINDOW, :])
         return jnp.concatenate(parts, axis=0)
 
-    for pair in range(pairs):
+    def multiply(pair):
         dots, scores = [], []
         for side in range(2):
             r, m, _ = place(pair, side)
@@ -342,6 +303,61 @@
             scored = jnp.where(here, scores[8 * v : 8 * v + 8], scored)
         comp[0, pair] = banded
         comp[1, pair] = scored
+
+    inner = [pair for pair in range(pairs) if 0 < pair % tiles < tiles - 1]
+    for pair in inner:
+        multiply(pair)
+
+    copy_len.wait()
+    subd = iota((8, features), 0)
+    even = (base // length) % 2 == 0
+    for r in range(rows):
+        near = near_ref[r].astype(F32)
+        far = far_ref[r].astype(F32)
+        up = jnp.where(even, far, near)
+        down = jnp.where(even, near, far)
+        xb[r, 0:PAD, :] = up.astype(BF16)
+        xb[r, PAD + length : 2 * PAD + length, :] = down.astype(BF16)
+        rest = xb.shape[1] - 2 * PAD - length
+        if rest > 0:
+            xb[r, 2 * PAD + length :, :] = jnp.zeros((rest, features), BF16)
+        xb[r, PAD : PAD + length, :] = x_ref[r]
+        before = jnp.where(subd >= 6, pltpu.roll(up[0:8], 6, 0), 0.0)
+        after = jnp.where(subd < 3, pltpu.roll(down[8:16], 3, 0), 0.0)
+        rest = g32.shape[2] - PAD - half - 8
+        for c in range(chunks):
+            g32[r, c, 8:16, :] = before[:, lanes_of(c)]
+            g32[r, c, PAD + half : PAD + half + 8, :] = after[:, lanes_of(c)]
+            g32[r, c, PAD + half + 8 :, :] = jnp.zeros((rest, 128), F32)
+        for c in range(chunks):
+            lanes = lanes_of(c)
+            xf[c, 0:8, :] = jnp.zeros((8, 128), F32)
+            xf[c, 8:24, :] = up[:, lanes]
+            xf[c, 24:40, :] = x_ref[r, 0:16, lanes].astype(F32)
+            xf[c, 40:56, :] = x_ref[r, length - 16 : length, lanes].astype(F32)
+            xf[c, 56:72, :] = down[:, lanes]
+        ends = ends_of(len_ref, r)
+        for at, where, slot in ((0, 8, 0), (PAD, 24, 16), (PAD + length, 56, 32)):
+
+            def put(first):
+                def store(c, value):
+                    edge[r, c, first : first + 16, :] = value
+
+                return store
+
+            convolve_block(
+                base,
+                ends,
+                par_ref,
+                lambda c, shift: xf[c, where + shift : where + shift + 8, :],
+                at,
+                put(slot),
+                put(48 + slot),
+            )
+
+    for pair in range(pairs):
+        if pair not in inner:
+            multiply(pair)
 
     ends = [ends_of(len_ref, r) for r in range(rows)]
     for pair in range(pairs):
@@ -483,14 +499,22 @@
     build(0, 0)
     build(0, 1)
 
+    def one_pair(pair):
+        spread_pair(pair + 1)
+        for side in range(2):
+            apply(pair, side)
+            build(pair + 1, side)
+
+    together = 2
+
     def second_loop(i, _):
-        spread_pair(i + 1)
-        for side in range(2):
-            apply(i, side)
-            build(i + 1, side)
+        for j in range(together):
+            one_pair(together * i + j)
         return 0
 
-    lax.fori_loop(0, pairs - 1, second_loop, 0)
+    lax.fori_loop(0, (pairs - 1) // together, second_loop, 0)
+    for pair in range((pairs - 1) // together * together, pairs - 1):
+        one_pair(pair)
     apply(pairs - 1, 0)
     apply(pairs - 1, 1)
     for k in range(TAPS + 2):
@@ -652,7 +676,7 @@
             jax.ShapeDtypeStruct((rows, chunks, g_rows, 128), F32),
             jax.ShapeDtypeStruct((TAPS + 2, features), F32),
         ),
-        in_specs=[SMEM, SMEM, VMEM, VMEM, VMEM, VMEM, VMEM, VMEM, VMEM],
+        in_specs=[SMEM, HBM, VMEM, VMEM, VMEM, VMEM, VMEM, VMEM, VMEM],
         out_specs=(VMEM, VMEM, VMEM, VMEM),
         scratch_shapes=[
             pltpu.VMEM((rows, x_rows, features), BF16),
@@ -667,6 +691,8 @@
             pltpu.VMEM((2, 2, 8, 128), F32),
             pltpu.VMEM((2, 8, features), F32),
             pltpu.VMEM((TAPS + 2, 8, features), F32),
+            pltpu.SMEM(lengths.shape, jnp.int32),
+            pltpu.SemaphoreType.DMA((1,)),
         ],
         compiler_params=pltpu.CompilerParams(vmem_limit_bytes=28 * 1024 * 1024),
         cost_estimate=pl.CostEstimate(

time: 39.8 us -> 39.3 us (0.987)
  Pallas kernels: 25.8 us -> 25.4 us
    pallas_call x1, Pallas kernels: 8.81 us -> 8.29 us  [forward(): pl.pallas_call(functools.partial(forward_kernel, shapes), out_shape=(jax....]
where the time goes in v9:
time: 39.3 us; the launch traced here: 39.1 us
  Pallas kernels  25.4 us (65%)
  starting transfers between devices  11.3 us (29%)
  waiting for transfers between devices  1.59 us (4%)
  between operations  0.86 us (2%)
    pallas_call x4, Pallas kernels, backward(): pl.pallas_call(functools.partial(backward_kernel, shapes, r), out_shape=(...  10.9 us
    ppermute x5, starting transfers between devices, per_device(): received = lax.ppermute(grad_params, axis, exchange)  10.1 us
    pallas_call x1, Pallas kernels, forward(): pl.pallas_call(functools.partial(forward_kernel, shapes), out_shape=(jax....  8.29 us
    pallas_call x1, Pallas kernels, convolved(): pl.pallas_call(functools.partial(conv_kernel, shapes), out_shape=(part, p...  4.12 us
    ppermute x5, waiting for transfers between devices, per_device(): received = lax.ppermute(grad_params, axis, exchange)  1.59 us
    pallas_call x1, Pallas kernels, packed(): pl.pallas_call(pack_kernel, out_shape=(part, part), in_specs=[SMEM, HBM,...  1.29 us
    pallas_call x1, Pallas kernels, update(): pl.pallas_call(update_kernel, out_shape=(jax.ShapeDtypeStruct((1, 1), F32...  0.79 us
  transfers between devices with their start and end apart: 7, of which 2 were waited for; matrix products, arithmetic and copies ran while one was open for 0% of the time, Pallas kernels for 38%

profile of v9, /device:TPU:0, one launch (start us, length us, event | category | flops | bytes accessed | tf_op | source)
XLA Modules:
  0.0 39.1 jit_solution(12165190514841008438)
XLA Ops:
  0.6 0.0 copy-start
  0.6 0.0 copy-start.2
  0.7 0.0 copy-start.3
  0.7 0.0 copy-start.1
  0.7 1.3 %shard_map.110 = (bf16[4,16,768]{2,1,0:T(8,128)(2,1)S(1)}, bf16[4,16,768]{2,1,0:T(8,128)(2,1)S(1)}) custom-call(s32[1]{0:T(128)} %bitcast.base_ref, bf16[4,512,768]{2,1,0:T(8,128)(2,1)} %x_ref.3, bf16[4,256,768]{2,1,0:T(8,128)(2,1)} %g_ref.1), custom_call_target="tpu_custom_call" | custom-call | tf_op jit(solution)/shard_map/pallas_call | solution.py:630
  2.0 0.5 %collective-permute-start = (bf16[4,16,768]{2,1,0:T(8,128)(2,1)S(1)}, bf16[4,16,768]{2,1,0:T(8,128)(2,1)S(1)}, u32[]{:S(2)}, u32[]{:S(2)}) collective-permute-start(bf16[4,16,768]{2,1,0:T(8,128)(2,1)S(1)} %get-tuple-element.48), channel_id=1, source_target_pairs={{0,1},{2,3},{1,0},{3,2},{4,5},{6,7},{5,4},{7,6},{8,9},{10,11},{9,8... | collective-permute-start | bytes 294920 | tf_op jit(solution)/shard_map/ppermute | solution.py:787
  2.5 0.7 %collective-permute-start.1 = (bf16[4,16,768]{2,1,0:T(8,128)(2,1)S(1)}, bf16[4,16,768]{2,1,0:T(8,128)(2,1)S(1)}, u32[]{:S(2)}, u32[]{:S(2)}) collective-permute-start(bf16[4,16,768]{2,1,0:T(8,128)(2,1)S(1)} %get-tuple-element.49), channel_id=1, source_target_pairs={{1,2},{2,1},{5,6},{6,5},{9,10},{10,9},{13,14},{14,13},{17,18},{18,... | collective-permute-start | bytes 294920 | tf_op jit(solution)/shard_map/ppermute | solution.py:786
  3.2 0.0 copy-done
  3.2 0.0 copy-done.2
  3.2 0.0 copy-done.3
  3.2 4.1 %shard_map.109 = (bf16[4,6,576,128]{3,2,1,0:T(8,128)(2,1)S(1)}, bf16[4,6,576,128]{3,2,1,0:T(8,128)(2,1)S(1)}) custom-call(s32[1]{0:T(128)} %bitcast.base_ref, s32[4,4]{1,0:T(4,128)S(1)} %copy-done.3, bf16[4,512,768]{2,1,0:T(8,128)(2,1)S(1)} %copy-done, f32[6,768]{1,0:T(8,128)S(1)} %copy-done.2), custom_call_target="tpu_custom_call" | custom-call | flops 37748736 | bytes 12582912 | tf_op jit(solution)/shard_map/pallas_call | solution.py:647
  7.3 0.0 collective-permute-done.near_ref
  7.3 0.0 collective-permute-done.1.far_ref
  7.3 0.0 copy-done.1
  7.3 8.3 %shard_map.111 = (f32[4,6,304,128]{3,2,1,0:T(8,128)S(1)}, bf16[20,64,256]{2,1,0:T(8,128)(2,1)S(1)}, f32[4,6,304,128]{3,2,1,0:T(8,128)S(1)}, f32[6,768]{1,0:T(8,128)S(1)}) custom-call(s32[1]{0:T(128)} %bitcast.base_ref, s32[4,4]{1,0:T(4,128)S(1)} %copy-done.3, bf16[4,512,768]{2,1,0:T(8,128)(2,1)S(1)} %copy-done, bf16[4,256,768]{2,1,0:T(8,128)(2,1)S(1)} %copy-done.1, ...), custom_call_target="tpu_custom_call" | custom-call | flops 3019898880 | bytes 12582912 | tf_op jit(solution)/shard_map/pallas_call | solution.py:671
  15.6 4.0 %collective-permute-start.2 = (f32[6,768]{1,0:T(8,128)S(1)}, f32[6,768]{1,0:T(8,128)S(1)}, u32[]{:S(2)}, u32[]{:S(2)}) collective-permute-start(f32[6,768]{1,0:T(8,128)S(1)} %get-tuple-element.51), channel_id=1, source_target_pairs={{0,1},{1,0},{2,3},{3,2},{4,5},{5,4},{6,7},{7,6},{8,9},{9,8},{10,11... | collective-permute-start | bytes 55304 | tf_op jit(solution)/shard_map/ppermute | solution.py:809
  19.6 0.8 %collective-permute-done.2 = f32[6,768]{1,0:T(8,128)S(1)} collective-permute-done((f32[6,768]{1,0:T(8,128)S(1)}, f32[6,768]{1,0:T(8,128)S(1)}, u32[]{:S(2)}, u32[]{:S(2)}) %collective-permute-start.2) | collective-permute-done | bytes 18464 | tf_op jit(solution)/shard_map/ppermute | solution.py:809
  20.5 0.4 collective-permute-start.3
  20.8 2.7 %shard_map.112 = (bf16[4,256,768]{2,1,0:T(8,128)(2,1)}, bf16[4,512,768]{2,1,0:T(8,128)(2,1)}) custom-call(s32[1]{0:T(128)} %bitcast.base_ref, s32[4,4]{1,0:T(4,128)S(1)} %copy-done.3, bf16[20,64,256]{2,1,0:T(8,128)(2,1)S(1)} %get-tuple-element.74.mat, f32[4,6,304,128]{3,2,1,0:T(8,128)S(1)} %get-tuple-element.54.g32, ...), custom_call_target="tpu_custom_call" | custom-call | flops 251658240 | bytes 1572864 | tf_op jit(solution)/shard_map/pallas_call | solution.py:717
  23.6 0.7 %collective-permute-done.3 = f32[6,768]{1,0:T(8,128)S(1)} collective-permute-done((f32[6,768]{1,0:T(8,128)S(1)}, f32[6,768]{1,0:T(8,128)S(1)}, u32[]{:S(2)}, u32[]{:S(2)}) %collective-permute-start.3) | collective-permute-done | bytes 18464 | tf_op jit(solution)/shard_map/ppermute | solution.py:805
  24.3 1.5 %collective-permute-start.4 = (f32[6,768]{1,0:T(8,128)S(1)}, f32[6,768]{1,0:T(8,128)S(1)}, u32[]{:S(2)}, u32[]{:S(2)}) collective-permute-start(f32[6,768]{1,0:T(8,128)S(1)} %add.13), channel_id=1, source_target_pairs={{0,4},{4,0},{8,12},{12,8},{16,20},{20,16},{24,28},{28,24},{1,5},{5... | collective-permute-start | bytes 55304 | tf_op jit(solution)/shard_map/ppermute | solution.py:805
  25.8 2.7 %shard_map.113 = (bf16[4,256,768]{2,1,0:T(8,128)(2,1)}, bf16[4,512,768]{2,1,0:T(8,128)(2,1)}) custom-call(s32[1]{0:T(128)} %bitcast.base_ref, s32[4,4]{1,0:T(4,128)S(1)} %copy-done.3, bf16[20,64,256]{2,1,0:T(8,128)(2,1)S(1)} %get-tuple-element.74.mat, f32[4,6,304,128]{3,2,1,0:T(8,128)S(1)} %get-tuple-element.54.g32, ...), custom_call_target="tpu_custom_call", output_to_operand_aliasing={{0}: (6, {}), {1}: (7, {})} | custom-call | flops 251658240 | bytes 1572864 | tf_op jit(solution)/shard_map/pallas_call | solution.py:717
  28.5 0.0 collective-permute-done.4
  28.5 1.7 %collective-permute-start.5 = (f32[6,768]{1,0:T(8,128)S(1)}, f32[6,768]{1,0:T(8,128)S(1)}, u32[]{:S(2)}, u32[]{:S(2)}) collective-permute-start(f32[6,768]{1,0:T(8,128)S(1)} %add.14), channel_id=1, source_target_pairs={{0,8},{4,12},{8,0},{12,4},{16,24},{20,28},{24,16},{28,20},{1,9},{5... | collective-permute-start | bytes 55304 | tf_op jit(solution)/shard_map/ppermute | solution.py:805
  30.2 2.7 %shard_map.114 = (bf16[4,256,768]{2,1,0:T(8,128)(2,1)}, bf16[4,512,768]{2,1,0:T(8,128)(2,1)}) custom-call(s32[1]{0:T(128)} %bitcast.base_ref, s32[4,4]{1,0:T(4,128)S(1)} %copy-done.3, bf16[20,64,256]{2,1,0:T(8,128)(2,1)S(1)} %get-tuple-element.74.mat, f32[4,6,304,128]{3,2,1,0:T(8,128)S(1)} %get-tuple-element.54.g32, ...), custom_call_target="tpu_custom_call", output_to_operand_aliasing={{0}: (6, {}), {1}: (7, {})} | custom-call | flops 251658240 | bytes 1572864 | tf_op jit(solution)/shard_map/pallas_call | solution.py:717
  32.9 0.0 collective-permute-done.5
  33.0 0.0 copy-start.4
  33.0 0.0 copy-start.5
  33.0 2.6 %collective-permute-start.6 = (f32[6,768]{1,0:T(8,128)S(1)}, f32[6,768]{1,0:T(8,128)S(1)}, u32[]{:S(2)}, u32[]{:S(2)}) collective-permute-start(f32[6,768]{1,0:T(8,128)S(1)} %add.15.grad_ref), channel_id=1, source_target_pairs={{0,16},{4,20},{8,24},{12,28},{16,0},{20,4},{24,8},{28,12},{1,17},{... | collective-permute-start | bytes 55304 | tf_op jit(solution)/shard_map/ppermute | solution.py:805
  35.6 2.7 %shard_map.115 = (bf16[4,256,768]{2,1,0:T(8,128)(2,1)}, bf16[4,512,768]{2,1,0:T(8,128)(2,1)}) custom-call(s32[1]{0:T(128)} %bitcast.base_ref, s32[4,4]{1,0:T(4,128)S(1)} %copy-done.3, bf16[20,64,256]{2,1,0:T(8,128)(2,1)S(1)} %get-tuple-element.74.mat, f32[4,6,304,128]{3,2,1,0:T(8,128)S(1)} %get-tuple-element.54.g32, ...), custom_call_target="tpu_custom_call", output_to_operand_aliasing={{0}: (6, {}), {1}: (7, {})} | custom-call | flops 251658240 | bytes 1572864 | tf_op jit(solution)/shard_map/pallas_call | solution.py:717
  38.3 0.0 collective-permute-done.6.other_ref
  38.3 0.0 copy-done.4
  38.3 0.0 copy-done.5
  38.4 0.8 %shard_map.116 = (f32[1,1]{1,0:T(1,128)}, f32[6,768]{1,0:T(8,128)}, f32[6,768]{1,0:T(8,128)}, f32[6,768]{1,0:T(8,128)}) custom-call(f32[6,768]{1,0:T(8,128)S(1)} %add.15.grad_ref, f32[6,768]{1,0:T(8,128)S(1)} %collective-permute-done.6.other_ref, f32[6,768]{1,0:T(8,128)S(1)} %copy-done.2, f32[6,768]{1,0:T(8,128)S(1)} %copy-done.4, f32[6,768]{1,0:T(8,128)S(1)} %copy-done.5), custom_call_target="tpu_custom_call" | custom-call | tf_op jit(solution)/shard_map/pallas_call | solution.py:762
  (4 shorter events, 0.0 us)
Async XLA Ops:
  0.6 2.5 %copy-start = (bf16[4,512,768]{2,1,0:T(8,128)(2,1)S(1)}, bf16[4,512,768]{2,1,0:T(8,128)(2,1)}, u32[]{:S(2)}) copy-start(bf16[4,512,768]{2,1,0:T(8,128)(2,1)} %x_ref.3) | copy-start | bytes 9437188
  0.6 2.5 %copy-start.2 = (f32[6,768]{1,0:T(8,128)S(1)}, f32[6,768]{1,0:T(8,128)}, u32[]{:S(2)}) copy-start(f32[6,768]{1,0:T(8,128)} %par_ref.13) | copy-start | bytes 55300
  0.7 2.5 %copy-start.3 = (s32[4,4]{1,0:T(4,128)S(1)}, s32[4,4]{1,0:T(4,128)}, u32[]{:S(2)}) copy-start(s32[4,4]{1,0:T(4,128)} %len_ref.7) | copy-start | bytes 196
  0.7 6.7 %copy-start.1 = (bf16[4,256,768]{2,1,0:T(8,128)(2,1)S(1)}, bf16[4,256,768]{2,1,0:T(8,128)(2,1)}, u32[]{:S(2)}) copy-start(bf16[4,256,768]{2,1,0:T(8,128)(2,1)} %g_ref.1) | copy-start | bytes 4718596
  2.0 5.3 %collective-permute-start = (bf16[4,16,768]{2,1,0:T(8,128)(2,1)S(1)}, bf16[4,16,768]{2,1,0:T(8,128)(2,1)S(1)}, u32[]{:S(2)}, u32[]{:S(2)}) collective-permute-start(bf16[4,16,768]{2,1,0:T(8,128)(2,1)S(1)} %get-tuple-element.48), channel_id=1, source_target_pairs={{0,1},{2,3},{1,0},{3,2},{4,5},{6,7},{5,4},{7,6},{8,9},{10,11},{9,8... | collective-permute-start | bytes 294920 | tf_op jit(solution)/shard_map/ppermute | solution.py:787
  2.5 4.8 %collective-permute-start.1 = (bf16[4,16,768]{2,1,0:T(8,128)(2,1)S(1)}, bf16[4,16,768]{2,1,0:T(8,128)(2,1)S(1)}, u32[]{:S(2)}, u32[]{:S(2)}) collective-permute-start(bf16[4,16,768]{2,1,0:T(8,128)(2,1)S(1)} %get-tuple-element.49), channel_id=1, source_target_pairs={{1,2},{2,1},{5,6},{6,5},{9,10},{10,9},{13,14},{14,13},{17,18},{18,... | collective-permute-start | bytes 294920 | tf_op jit(solution)/shard_map/ppermute | solution.py:786
  15.6 4.8 %collective-permute-start.2 = (f32[6,768]{1,0:T(8,128)S(1)}, f32[6,768]{1,0:T(8,128)S(1)}, u32[]{:S(2)}, u32[]{:S(2)}) collective-permute-start(f32[6,768]{1,0:T(8,128)S(1)} %get-tuple-element.51), channel_id=1, source_target_pairs={{0,1},{1,0},{2,3},{3,2},{4,5},{5,4},{6,7},{7,6},{8,9},{9,8},{10,11... | collective-permute-start | bytes 55304 | tf_op jit(solution)/shard_map/ppermute | solution.py:809
  20.5 3.8 %collective-permute-start.3 = (f32[6,768]{1,0:T(8,128)S(1)}, f32[6,768]{1,0:T(8,128)S(1)}, u32[]{:S(2)}, u32[]{:S(2)}) collective-permute-start(f32[6,768]{1,0:T(8,128)S(1)} %add.12), channel_id=1, source_target_pairs={{0,2},{1,3},{2,0},{3,1},{4,6},{5,7},{6,4},{7,5},{8,10},{9,11},{10,... | collective-permute-start | bytes 55304 | tf_op jit(solution)/shard_map/ppermute | solution.py:805
  24.3 4.2 %collective-permute-start.4 = (f32[6,768]{1,0:T(8,128)S(1)}, f32[6,768]{1,0:T(8,128)S(1)}, u32[]{:S(2)}, u32[]{:S(2)}) collective-permute-start(f32[6,768]{1,0:T(8,128)S(1)} %add.13), channel_id=1, source_target_pairs={{0,4},{4,0},{8,12},{12,8},{16,20},{20,16},{24,28},{28,24},{1,5},{5... | collective-permute-start | bytes 55304 | tf_op jit(solution)/shard_map/ppermute | solution.py:805
  28.5 4.4 %collective-permute-start.5 = (f32[6,768]{1,0:T(8,128)S(1)}, f32[6,768]{1,0:T(8,128)S(1)}, u32[]{:S(2)}, u32[]{:S(2)}) collective-permute-start(f32[6,768]{1,0:T(8,128)S(1)} %add.14), channel_id=1, source_target_pairs={{0,8},{4,12},{8,0},{12,4},{16,24},{20,28},{24,16},{28,20},{1,9},{5... | collective-permute-start | bytes 55304 | tf_op jit(solution)/shard_map/ppermute | solution.py:805
  33.0 5.4 %copy-start.4 = (f32[6,768]{1,0:T(8,128)S(1)}, f32[6,768]{1,0:T(8,128)}, u32[]{:S(2)}) copy-start(f32[6,768]{1,0:T(8,128)} %first_ref.1) | copy-start | bytes 55300
  33.0 5.4 %copy-start.5 = (f32[6,768]{1,0:T(8,128)S(1)}, f32[6,768]{1,0:T(8,128)}, u32[]{:S(2)}) copy-start(f32[6,768]{1,0:T(8,128)} %second_ref.1) | copy-start | bytes 55300
  33.0 5.3 %collective-permute-start.6 = (f32[6,768]{1,0:T(8,128)S(1)}, f32[6,768]{1,0:T(8,128)S(1)}, u32[]{:S(2)}, u32[]{:S(2)}) collective-permute-start(f32[6,768]{1,0:T(8,128)S(1)} %add.15.grad_ref), channel_id=1, source_target_pairs={{0,16},{4,20},{8,24},{12,28},{16,0},{20,4},{24,8},{28,12},{1,17},{... | collective-permute-start | bytes 55304 | tf_op jit(solution)/shard_map/ppermute | solution.py:805

commit v10 on v9

--- a/solution.py
+++ b/solution.py
@@ -108,7 +108,7 @@
         lanes = lanes_of(c)
         parts = []
         for j in range(2):
-            value = par_ref[4:5, lanes] + par_ref[0:1, lanes] * load(c, 8 * j)
+            value = par_ref[0:1, lanes] * load(c, 8 * j)
             for k in range(1, TAPS):
                 shifted = load(c, 8 * j - k)
                 if masked:
@@ -209,6 +209,7 @@
     xf,
     edge,
     comp,
+    biases,
     cs,
     es,
     fac_a,
@@ -274,13 +275,15 @@
         return jnp.concatenate(parts, axis=0)
 
     def multiply(pair):
-        dots, scores = [], []
+        dots, scores, added = [], [], []
         for side in range(2):
             r, m, _ = place(pair, side)
             start = OWN * m + 8
             streamed, held = [], []
+            biased = jnp.zeros((SLOTS, 128), F32)
             for c in range(chunks):
                 g = g32[r, c, start : start + SLOTS, :]
+                biased = biased + g * par_ref[4:5, lanes_of(c)]
                 top = jnp.where(sub8 == 0, scorer_high[c], jnp.where(sub8 == 1, scorer_low[c], g[0:8]))
                 streamed.append(jnp.concatenate([top, g[8:]], axis=0).astype(BF16))
                 held.append(held_rows(r, m, c))
@@ -291,6 +294,7 @@
                 preferred_element_type=F32,
             )
             product = product[:, :WINDOW] + product[:, WINDOW:]
+            added.append(jnp.broadcast_to(jnp.sum(biased, axis=1, keepdims=True), (SLOTS, 128)))
             dots.append(product)
             scores.append(jnp.broadcast_to(product[0:1] + product[1:2], (SLOTS, WINDOW)))
         dots = jnp.concatenate(dots, axis=0).T
@@ -303,6 +307,7 @@
             scored = jnp.where(here, scores[8 * v : 8 * v + 8], scored)
         comp[0, pair] = banded
         comp[1, pair] = scored
+        biases[pair] = jnp.concatenate(added, axis=0).T[0:8]
 
     inner = [pair for pair in range(pairs) if 0 < pair % tiles < tiles - 1]
     for pair in inner:
@@ -359,11 +364,13 @@
         if pair not in inner:
             multiply(pair)
 
+    bias_score = jnp.sum(par_ref[4:5, :] * par_ref[5:6, :])
+
     ends = [ends_of(len_ref, r) for r in range(rows)]
     for pair in range(pairs):
         both = [place(pair, side) for side in range(2)]
-        dots = rotate_rows(comp[0, pair], turn_e)
-        scores = rotate_rows(comp[1, pair], turn_e)
+        dots = rotate_rows(comp[0, pair], turn_e) + biases[pair]
+        scores = rotate_rows(comp[1, pair], turn_e) + bias_score
         coef = jnp.zeros((8, 128), F32)
         coef_e = jnp.zeros((8, 128), F32)
         for p in range(2):
@@ -683,6 +690,7 @@
             pltpu.VMEM((chunks, 72, 128), F32),
             pltpu.VMEM((rows, chunks, 96, 128), BF16),
             pltpu.VMEM((2, count // 2, 8, 128), F32),
+            pltpu.VMEM((count // 2, 8, 128), F32),
             pltpu.VMEM((2, count, 8, 128), F32),
             pltpu.VMEM((count // 2, 8, 128), F32),
             pltpu.VMEM((TAPS * SLOTS, 2 * WINDOW), BF16),

time: 39.3 us -> 39.2 us (level)
  no operation moved by 1% of the time
where the time goes in v10:
time: 39.2 us; the launch traced here: 39.1 us
  Pallas kernels  25.2 us (64%)
  starting transfers between devices  11.5 us (29%)
  waiting for transfers between devices  1.49 us (4%)
  between operations  0.86 us (2%)
    pallas_call x4, Pallas kernels, backward(): pl.pallas_call(functools.partial(backward_kernel, shapes, r), out_shape=(...  10.9 us
    ppermute x5, starting transfers between devices, per_device(): received = lax.ppermute(grad_params, axis, exchange)  10.3 us
    pallas_call x1, Pallas kernels, forward(): pl.pallas_call(functools.partial(forward_kernel, shapes), out_shape=(jax....  8.38 us
    pallas_call x1, Pallas kernels, convolved(): pl.pallas_call(functools.partial(conv_kernel, shapes), out_shape=(part, p...  3.84 us
    ppermute x5, waiting for transfers between devices, per_device(): received = lax.ppermute(grad_params, axis, exchange)  1.48 us
    pallas_call x1, Pallas kernels, packed(): pl.pallas_call(pack_kernel, out_shape=(part, part), in_specs=[SMEM, HBM,...  1.29 us
    pallas_call x1, Pallas kernels, update(): pl.pallas_call(update_kernel, out_shape=(jax.ShapeDtypeStruct((1, 1), F32...  0.79 us
  transfers between devices with their start and end apart: 7, of which 2 were waited for; matrix products, arithmetic and copies ran while one was open for 0% of the time, Pallas kernels for 38%

profile of v10, /device:TPU:0, one launch (start us, length us, event | category | flops | bytes accessed | tf_op | source)
XLA Modules:
  0.0 39.1 jit_solution(14821611175349284854)
XLA Ops:
  0.6 0.0 copy-start
  0.6 0.0 copy-start.2
  0.7 0.0 copy-start.3
  0.7 0.0 copy-start.1
  0.7 1.3 %shard_map.110 = (bf16[4,16,768]{2,1,0:T(8,128)(2,1)S(1)}, bf16[4,16,768]{2,1,0:T(8,128)(2,1)S(1)}) custom-call(s32[1]{0:T(128)} %bitcast.base_ref, bf16[4,512,768]{2,1,0:T(8,128)(2,1)} %x_ref.3, bf16[4,256,768]{2,1,0:T(8,128)(2,1)} %g_ref.1), custom_call_target="tpu_custom_call" | custom-call | tf_op jit(solution)/shard_map/pallas_call | solution.py:637
  2.0 0.5 %collective-permute-start = (bf16[4,16,768]{2,1,0:T(8,128)(2,1)S(1)}, bf16[4,16,768]{2,1,0:T(8,128)(2,1)S(1)}, u32[]{:S(2)}, u32[]{:S(2)}) collective-permute-start(bf16[4,16,768]{2,1,0:T(8,128)(2,1)S(1)} %get-tuple-element.48), channel_id=1, source_target_pairs={{0,1},{2,3},{1,0},{3,2},{4,5},{6,7},{5,4},{7,6},{8,9},{10,11},{9,8... | collective-permute-start | bytes 294920 | tf_op jit(solution)/shard_map/ppermute | solution.py:795
  2.5 0.7 %collective-permute-start.1 = (bf16[4,16,768]{2,1,0:T(8,128)(2,1)S(1)}, bf16[4,16,768]{2,1,0:T(8,128)(2,1)S(1)}, u32[]{:S(2)}, u32[]{:S(2)}) collective-permute-start(bf16[4,16,768]{2,1,0:T(8,128)(2,1)S(1)} %get-tuple-element.49), channel_id=1, source_target_pairs={{1,2},{2,1},{5,6},{6,5},{9,10},{10,9},{13,14},{14,13},{17,18},{18,... | collective-permute-start | bytes 294920 | tf_op jit(solution)/shard_map/ppermute | solution.py:794
  3.2 0.0 copy-done
  3.2 0.0 copy-done.2
  3.2 0.0 copy-done.3
  3.2 3.8 %shard_map.109 = (bf16[4,6,576,128]{3,2,1,0:T(8,128)(2,1)S(1)}, bf16[4,6,576,128]{3,2,1,0:T(8,128)(2,1)S(1)}) custom-call(s32[1]{0:T(128)} %bitcast.base_ref, s32[4,4]{1,0:T(4,128)S(1)} %copy-done.3, bf16[4,512,768]{2,1,0:T(8,128)(2,1)S(1)} %copy-done, f32[6,768]{1,0:T(8,128)S(1)} %copy-done.2), custom_call_target="tpu_custom_call" | custom-call | flops 37748736 | bytes 12582912 | tf_op jit(solution)/shard_map/pallas_call | solution.py:654
  7.0 0.0 collective-permute-done.near_ref
  7.0 0.0 collective-permute-done.1.far_ref
  7.1 0.0 copy-done.1
  7.1 8.4 %shard_map.111 = (f32[4,6,304,128]{3,2,1,0:T(8,128)S(1)}, bf16[20,64,256]{2,1,0:T(8,128)(2,1)S(1)}, f32[4,6,304,128]{3,2,1,0:T(8,128)S(1)}, f32[6,768]{1,0:T(8,128)S(1)}) custom-call(s32[1]{0:T(128)} %bitcast.base_ref, s32[4,4]{1,0:T(4,128)S(1)} %copy-done.3, bf16[4,512,768]{2,1,0:T(8,128)(2,1)S(1)} %copy-done, bf16[4,256,768]{2,1,0:T(8,128)(2,1)S(1)} %copy-done.1, ...), custom_call_target="tpu_custom_call" | custom-call | flops 3019898880 | bytes 12582912 | tf_op jit(solution)/shard_map/pallas_call | solution.py:678
  15.5 3.9 %collective-permute-start.2 = (f32[6,768]{1,0:T(8,128)S(1)}, f32[6,768]{1,0:T(8,128)S(1)}, u32[]{:S(2)}, u32[]{:S(2)}) collective-permute-start(f32[6,768]{1,0:T(8,128)S(1)} %get-tuple-element.51), channel_id=1, source_target_pairs={{0,1},{1,0},{2,3},{3,2},{4,5},{5,4},{6,7},{7,6},{8,9},{9,8},{10,11... | collective-permute-start | bytes 55304 | tf_op jit(solution)/shard_map/ppermute | solution.py:817
  19.4 0.8 %collective-permute-done.2 = f32[6,768]{1,0:T(8,128)S(1)} collective-permute-done((f32[6,768]{1,0:T(8,128)S(1)}, f32[6,768]{1,0:T(8,128)S(1)}, u32[]{:S(2)}, u32[]{:S(2)}) %collective-permute-start.2) | collective-permute-done | bytes 18464 | tf_op jit(solution)/shard_map/ppermute | solution.py:817
  20.2 0.5 %collective-permute-start.3 = (f32[6,768]{1,0:T(8,128)S(1)}, f32[6,768]{1,0:T(8,128)S(1)}, u32[]{:S(2)}, u32[]{:S(2)}) collective-permute-start(f32[6,768]{1,0:T(8,128)S(1)} %add.12), channel_id=1, source_target_pairs={{0,2},{1,3},{2,0},{3,1},{4,6},{5,7},{6,4},{7,5},{8,10},{9,11},{10,... | collective-permute-start | bytes 55304 | tf_op jit(solution)/shard_map/ppermute | solution.py:813
  20.7 2.7 %shard_map.112 = (bf16[4,256,768]{2,1,0:T(8,128)(2,1)}, bf16[4,512,768]{2,1,0:T(8,128)(2,1)}) custom-call(s32[1]{0:T(128)} %bitcast.base_ref, s32[4,4]{1,0:T(4,128)S(1)} %copy-done.3, bf16[20,64,256]{2,1,0:T(8,128)(2,1)S(1)} %get-tuple-element.74.mat, f32[4,6,304,128]{3,2,1,0:T(8,128)S(1)} %get-tuple-element.54.g32, ...), custom_call_target="tpu_custom_call" | custom-call | flops 251658240 | bytes 1572864 | tf_op jit(solution)/shard_map/pallas_call | solution.py:725
  23.4 0.6 %collective-permute-done.3 = f32[6,768]{1,0:T(8,128)S(1)} collective-permute-done((f32[6,768]{1,0:T(8,128)S(1)}, f32[6,768]{1,0:T(8,128)S(1)}, u32[]{:S(2)}, u32[]{:S(2)}) %collective-permute-start.3) | collective-permute-done | bytes 18464 | tf_op jit(solution)/shard_map/ppermute | solution.py:813
  24.1 1.6 %collective-permute-start.4 = (f32[6,768]{1,0:T(8,128)S(1)}, f32[6,768]{1,0:T(8,128)S(1)}, u32[]{:S(2)}, u32[]{:S(2)}) collective-permute-start(f32[6,768]{1,0:T(8,128)S(1)} %add.13), channel_id=1, source_target_pairs={{0,4},{4,0},{8,12},{12,8},{16,20},{20,16},{24,28},{28,24},{1,5},{5... | collective-permute-start | bytes 55304 | tf_op jit(solution)/shard_map/ppermute | solution.py:813
  25.7 2.7 %shard_map.113 = (bf16[4,256,768]{2,1,0:T(8,128)(2,1)}, bf16[4,512,768]{2,1,0:T(8,128)(2,1)}) custom-call(s32[1]{0:T(128)} %bitcast.base_ref, s32[4,4]{1,0:T(4,128)S(1)} %copy-done.3, bf16[20,64,256]{2,1,0:T(8,128)(2,1)S(1)} %get-tuple-element.74.mat, f32[4,6,304,128]{3,2,1,0:T(8,128)S(1)} %get-tuple-element.54.g32, ...), custom_call_target="tpu_custom_call", output_to_operand_aliasing={{0}: (6, {}), {1}: (7, {})} | custom-call | flops 251658240 | bytes 1572864 | tf_op jit(solution)/shard_map/pallas_call | solution.py:725
  28.4 0.0 collective-permute-done.4
  28.4 1.7 %collective-permute-start.5 = (f32[6,768]{1,0:T(8,128)S(1)}, f32[6,768]{1,0:T(8,128)S(1)}, u32[]{:S(2)}, u32[]{:S(2)}) collective-permute-start(f32[6,768]{1,0:T(8,128)S(1)} %add.14), channel_id=1, source_target_pairs={{0,8},{4,12},{8,0},{12,4},{16,24},{20,28},{24,16},{28,20},{1,9},{5... | collective-permute-start | bytes 55304 | tf_op jit(solution)/shard_map/ppermute | solution.py:813
  30.1 2.7 %shard_map.114 = (bf16[4,256,768]{2,1,0:T(8,128)(2,1)}, bf16[4,512,768]{2,1,0:T(8,128)(2,1)}) custom-call(s32[1]{0:T(128)} %bitcast.base_ref, s32[4,4]{1,0:T(4,128)S(1)} %copy-done.3, bf16[20,64,256]{2,1,0:T(8,128)(2,1)S(1)} %get-tuple-element.74.mat, f32[4,6,304,128]{3,2,1,0:T(8,128)S(1)} %get-tuple-element.54.g32, ...), custom_call_target="tpu_custom_call", output_to_operand_aliasing={{0}: (6, {}), {1}: (7, {})} | custom-call | flops 251658240 | bytes 1572864 | tf_op jit(solution)/shard_map/pallas_call | solution.py:725
  32.8 0.0 collective-permute-done.5
  32.9 0.0 copy-start.4
  32.9 0.0 copy-start.5
  32.9 2.6 %collective-permute-start.6 = (f32[6,768]{1,0:T(8,128)S(1)}, f32[6,768]{1,0:T(8,128)S(1)}, u32[]{:S(2)}, u32[]{:S(2)}) collective-permute-start(f32[6,768]{1,0:T(8,128)S(1)} %add.15.grad_ref), channel_id=1, source_target_pairs={{0,16},{4,20},{8,24},{12,28},{16,0},{20,4},{24,8},{28,12},{1,17},{... | collective-permute-start | bytes 55304 | tf_op jit(solution)/shard_map/ppermute | solution.py:813
  35.5 2.7 %shard_map.115 = (bf16[4,256,768]{2,1,0:T(8,128)(2,1)}, bf16[4,512,768]{2,1,0:T(8,128)(2,1)}) custom-call(s32[1]{0:T(128)} %bitcast.base_ref, s32[4,4]{1,0:T(4,128)S(1)} %copy-done.3, bf16[20,64,256]{2,1,0:T(8,128)(2,1)S(1)} %get-tuple-element.74.mat, f32[4,6,304,128]{3,2,1,0:T(8,128)S(1)} %get-tuple-element.54.g32, ...), custom_call_target="tpu_custom_call", output_to_operand_aliasing={{0}: (6, {}), {1}: (7, {})} | custom-call | flops 251658240 | bytes 1572864 | tf_op jit(solution)/shard_map/pallas_call | solution.py:725
  38.2 0.0 collective-permute-done.6.other_ref
  38.2 0.0 copy-done.4
  38.3 0.0 copy-done.5
  38.3 0.8 %shard_map.116 = (f32[1,1]{1,0:T(1,128)}, f32[6,768]{1,0:T(8,128)}, f32[6,768]{1,0:T(8,128)}, f32[6,768]{1,0:T(8,128)}) custom-call(f32[6,768]{1,0:T(8,128)S(1)} %add.15.grad_ref, f32[6,768]{1,0:T(8,128)S(1)} %collective-permute-done.6.other_ref, f32[6,768]{1,0:T(8,128)S(1)} %copy-done.2, f32[6,768]{1,0:T(8,128)S(1)} %copy-done.4, f32[6,768]{1,0:T(8,128)S(1)} %copy-done.5), custom_call_target="tpu_custom_call" | custom-call | tf_op jit(solution)/shard_map/pallas_call | solution.py:770
  (4 shorter events, 0.0 us)
Async XLA Ops:
  0.6 2.5 %copy-start = (bf16[4,512,768]{2,1,0:T(8,128)(2,1)S(1)}, bf16[4,512,768]{2,1,0:T(8,128)(2,1)}, u32[]{:S(2)}) copy-start(bf16[4,512,768]{2,1,0:T(8,128)(2,1)} %x_ref.3) | copy-start | bytes 9437188
  0.6 2.5 %copy-start.2 = (f32[6,768]{1,0:T(8,128)S(1)}, f32[6,768]{1,0:T(8,128)}, u32[]{:S(2)}) copy-start(f32[6,768]{1,0:T(8,128)} %par_ref.13) | copy-start | bytes 55300
  0.7 2.5 %copy-start.3 = (s32[4,4]{1,0:T(4,128)S(1)}, s32[4,4]{1,0:T(4,128)}, u32[]{:S(2)}) copy-start(s32[4,4]{1,0:T(4,128)} %len_ref.7) | copy-start | bytes 196
  0.7 6.4 %copy-start.1 = (bf16[4,256,768]{2,1,0:T(8,128)(2,1)S(1)}, bf16[4,256,768]{2,1,0:T(8,128)(2,1)}, u32[]{:S(2)}) copy-start(bf16[4,256,768]{2,1,0:T(8,128)(2,1)} %g_ref.1) | copy-start | bytes 4718596
  2.0 5.1 %collective-permute-start = (bf16[4,16,768]{2,1,0:T(8,128)(2,1)S(1)}, bf16[4,16,768]{2,1,0:T(8,128)(2,1)S(1)}, u32[]{:S(2)}, u32[]{:S(2)}) collective-permute-start(bf16[4,16,768]{2,1,0:T(8,128)(2,1)S(1)} %get-tuple-element.48), channel_id=1, source_target_pairs={{0,1},{2,3},{1,0},{3,2},{4,5},{6,7},{5,4},{7,6},{8,9},{10,11},{9,8... | collective-permute-start | bytes 294920 | tf_op jit(solution)/shard_map/ppermute | solution.py:795
  2.5 4.6 %collective-permute-start.1 = (bf16[4,16,768]{2,1,0:T(8,128)(2,1)S(1)}, bf16[4,16,768]{2,1,0:T(8,128)(2,1)S(1)}, u32[]{:S(2)}, u32[]{:S(2)}) collective-permute-start(bf16[4,16,768]{2,1,0:T(8,128)(2,1)S(1)} %get-tuple-element.49), channel_id=1, source_target_pairs={{1,2},{2,1},{5,6},{6,5},{9,10},{10,9},{13,14},{14,13},{17,18},{18,... | collective-permute-start | bytes 294920 | tf_op jit(solution)/shard_map/ppermute | solution.py:794
  15.5 4.8 %collective-permute-start.2 = (f32[6,768]{1,0:T(8,128)S(1)}, f32[6,768]{1,0:T(8,128)S(1)}, u32[]{:S(2)}, u32[]{:S(2)}) collective-permute-start(f32[6,768]{1,0:T(8,128)S(1)} %get-tuple-element.51), channel_id=1, source_target_pairs={{0,1},{1,0},{2,3},{3,2},{4,5},{5,4},{6,7},{7,6},{8,9},{9,8},{10,11... | collective-permute-start | bytes 55304 | tf_op jit(solution)/shard_map/ppermute | solution.py:817
  20.2 3.8 %collective-permute-start.3 = (f32[6,768]{1,0:T(8,128)S(1)}, f32[6,768]{1,0:T(8,128)S(1)}, u32[]{:S(2)}, u32[]{:S(2)}) collective-permute-start(f32[6,768]{1,0:T(8,128)S(1)} %add.12), channel_id=1, source_target_pairs={{0,2},{1,3},{2,0},{3,1},{4,6},{5,7},{6,4},{7,5},{8,10},{9,11},{10,... | collective-permute-start | bytes 55304 | tf_op jit(solution)/shard_map/ppermute | solution.py:813
  24.1 4.3 %collective-permute-start.4 = (f32[6,768]{1,0:T(8,128)S(1)}, f32[6,768]{1,0:T(8,128)S(1)}, u32[]{:S(2)}, u32[]{:S(2)}) collective-permute-start(f32[6,768]{1,0:T(8,128)S(1)} %add.13), channel_id=1, source_target_pairs={{0,4},{4,0},{8,12},{12,8},{16,20},{20,16},{24,28},{28,24},{1,5},{5... | collective-permute-start | bytes 55304 | tf_op jit(solution)/shard_map/ppermute | solution.py:813
  28.4 4.4 %collective-permute-start.5 = (f32[6,768]{1,0:T(8,128)S(1)}, f32[6,768]{1,0:T(8,128)S(1)}, u32[]{:S(2)}, u32[]{:S(2)}) collective-permute-start(f32[6,768]{1,0:T(8,128)S(1)} %add.14), channel_id=1, source_target_pairs={{0,8},{4,12},{8,0},{12,4},{16,24},{20,28},{24,16},{28,20},{1,9},{5... | collective-permute-start | bytes 55304 | tf_op jit(solution)/shard_map/ppermute | solution.py:813
  32.9 5.4 %copy-start.4 = (f32[6,768]{1,0:T(8,128)S(1)}, f32[6,768]{1,0:T(8,128)}, u32[]{:S(2)}) copy-start(f32[6,768]{1,0:T(8,128)} %first_ref.1) | copy-start | bytes 55300
  32.9 5.4 %copy-start.5 = (f32[6,768]{1,0:T(8,128)S(1)}, f32[6,768]{1,0:T(8,128)}, u32[]{:S(2)}) copy-start(f32[6,768]{1,0:T(8,128)} %second_ref.1) | copy-start | bytes 55300
  32.9 5.4 %collective-permute-start.6 = (f32[6,768]{1,0:T(8,128)S(1)}, f32[6,768]{1,0:T(8,128)S(1)}, u32[]{:S(2)}, u32[]{:S(2)}) collective-permute-start(f32[6,768]{1,0:T(8,128)S(1)} %add.15.grad_ref), channel_id=1, source_target_pairs={{0,16},{4,20},{8,24},{12,28},{16,0},{20,4},{24,8},{28,12},{1,17},{... | collective-permute-start | bytes 55304 | tf_op jit(solution)/shard_map/ppermute | solution.py:813

commit v11 on v10

--- a/solution.py
+++ b/solution.py
@@ -136,14 +136,16 @@
                 for ref in (high_ref, low_ref):
                     ref[r, c, begin:, :] = jnp.zeros((rest, 128), BF16)
 
+    widened = 2 * step
+
     def widen(i, _):
-        r = i // (length // step)
-        at = pl.multiple_of((i % (length // step)) * step, step)
+        r = i // (length // widened)
+        at = pl.multiple_of((i % (length // widened)) * widened, widened)
         for c in range(chunks):
-            xf[r, c, pl.ds(at + 8, step), :] = x_ref[r, pl.ds(at, step), lanes_of(c)].astype(F32)
+            xf[r, c, pl.ds(at + 8, widened), :] = x_ref[r, pl.ds(at, widened), lanes_of(c)].astype(F32)
         return 0
 
-    lax.fori_loop(0, rows * (length // step), widen, 0)
+    lax.fori_loop(0, rows * (length // widened), widen, 0)
     copy_len.wait()
 
     def one_row(r, _):

time: 39.2 us -> 39.1 us (level)
  transfers between devices with their start and end apart: 7 -> 7, of which waited for: 2 -> 2; matrix products, arithmetic and copies ran while one was open for 0% -> 0% of each run, Pallas kernels for 38% -> 37%
where the time goes in v11:
time: 39.1 us; the launch traced here: 38.8 us
  Pallas kernels  24.9 us (64%)
  starting transfers between devices  11.6 us (30%)
  waiting for transfers between devices  1.43 us (4%)
  between operations  0.86 us (2%)
    pallas_call x4, Pallas kernels, backward(): pl.pallas_call(functools.partial(backward_kernel, shapes, r), out_shape=(...  10.8 us
    ppermute x5, starting transfers between devices, per_device(): received = lax.ppermute(grad_params, axis, exchange)  10.4 us
    pallas_call x1, Pallas kernels, forward(): pl.pallas_call(functools.partial(forward_kernel, shapes), out_shape=(jax....  8.39 us
    pallas_call x1, Pallas kernels, convolved(): pl.pallas_call(functools.partial(conv_kernel, shapes), out_shape=(part, p...  3.6 us
    ppermute x5, waiting for transfers between devices, per_device(): received = lax.ppermute(grad_params, axis, exchange)  1.42 us
    pallas_call x1, Pallas kernels, packed(): pl.pallas_call(pack_kernel, out_shape=(part, part), in_specs=[SMEM, HBM,...  1.29 us
    pallas_call x1, Pallas kernels, update(): pl.pallas_call(update_kernel, out_shape=(jax.ShapeDtypeStruct((1, 1), F32...  0.79 us
  transfers between devices with their start and end apart: 7, of which 2 were waited for; matrix products, arithmetic and copies ran while one was open for 0% of the time, Pallas kernels for 37%

profile of v11, /device:TPU:0, one launch (start us, length us, event | category | flops | bytes accessed | tf_op | source)
XLA Modules:
  0.0 38.8 jit_solution(8278963188856522582)
XLA Ops:
  0.6 0.0 copy-start
  0.6 0.0 copy-start.2
  0.7 0.0 copy-start.3
  0.7 0.0 copy-start.1
  0.7 1.3 %shard_map.110 = (bf16[4,16,768]{2,1,0:T(8,128)(2,1)S(1)}, bf16[4,16,768]{2,1,0:T(8,128)(2,1)S(1)}) custom-call(s32[1]{0:T(128)} %bitcast.base_ref, bf16[4,512,768]{2,1,0:T(8,128)(2,1)} %x_ref.3, bf16[4,256,768]{2,1,0:T(8,128)(2,1)} %g_ref.1), custom_call_target="tpu_custom_call" | custom-call | tf_op jit(solution)/shard_map/pallas_call | solution.py:639
  2.0 0.5 %collective-permute-start = (bf16[4,16,768]{2,1,0:T(8,128)(2,1)S(1)}, bf16[4,16,768]{2,1,0:T(8,128)(2,1)S(1)}, u32[]{:S(2)}, u32[]{:S(2)}) collective-permute-start(bf16[4,16,768]{2,1,0:T(8,128)(2,1)S(1)} %get-tuple-element.48), channel_id=1, source_target_pairs={{0,1},{2,3},{1,0},{3,2},{4,5},{6,7},{5,4},{7,6},{8,9},{10,11},{9,8... | collective-permute-start | bytes 294920 | tf_op jit(solution)/shard_map/ppermute | solution.py:797
  2.5 0.7 %collective-permute-start.1 = (bf16[4,16,768]{2,1,0:T(8,128)(2,1)S(1)}, bf16[4,16,768]{2,1,0:T(8,128)(2,1)S(1)}, u32[]{:S(2)}, u32[]{:S(2)}) collective-permute-start(bf16[4,16,768]{2,1,0:T(8,128)(2,1)S(1)} %get-tuple-element.49), channel_id=1, source_target_pairs={{1,2},{2,1},{5,6},{6,5},{9,10},{10,9},{13,14},{14,13},{17,18},{18,... | collective-permute-start | bytes 294920 | tf_op jit(solution)/shard_map/ppermute | solution.py:796
  3.2 0.0 copy-done
  3.2 0.0 copy-done.2
  3.2 0.0 copy-done.3
  3.2 3.6 %shard_map.109 = (bf16[4,6,576,128]{3,2,1,0:T(8,128)(2,1)S(1)}, bf16[4,6,576,128]{3,2,1,0:T(8,128)(2,1)S(1)}) custom-call(s32[1]{0:T(128)} %bitcast.base_ref, s32[4,4]{1,0:T(4,128)S(1)} %copy-done.3, bf16[4,512,768]{2,1,0:T(8,128)(2,1)S(1)} %copy-done, f32[6,768]{1,0:T(8,128)S(1)} %copy-done.2), custom_call_target="tpu_custom_call" | custom-call | flops 37748736 | bytes 12582912 | tf_op jit(solution)/shard_map/pallas_call | solution.py:656
  6.8 0.0 collective-permute-done.near_ref
  6.8 0.0 collective-permute-done.1.far_ref
  6.8 0.0 copy-done.1
  6.8 8.4 %shard_map.111 = (f32[4,6,304,128]{3,2,1,0:T(8,128)S(1)}, bf16[20,64,256]{2,1,0:T(8,128)(2,1)S(1)}, f32[4,6,304,128]{3,2,1,0:T(8,128)S(1)}, f32[6,768]{1,0:T(8,128)S(1)}) custom-call(s32[1]{0:T(128)} %bitcast.base_ref, s32[4,4]{1,0:T(4,128)S(1)} %copy-done.3, bf16[4,512,768]{2,1,0:T(8,128)(2,1)S(1)} %copy-done, bf16[4,256,768]{2,1,0:T(8,128)(2,1)S(1)} %copy-done.1, ...), custom_call_target="tpu_custom_call" | custom-call | flops 3019898880 | bytes 12582912 | tf_op jit(solution)/shard_map/pallas_call | solution.py:680
  15.2 4.1 %collective-permute-start.2 = (f32[6,768]{1,0:T(8,128)S(1)}, f32[6,768]{1,0:T(8,128)S(1)}, u32[]{:S(2)}, u32[]{:S(2)}) collective-permute-start(f32[6,768]{1,0:T(8,128)S(1)} %get-tuple-element.51), channel_id=1, source_target_pairs={{0,1},{1,0},{2,3},{3,2},{4,5},{5,4},{6,7},{7,6},{8,9},{9,8},{10,11... | collective-permute-start | bytes 55304 | tf_op jit(solution)/shard_map/ppermute | solution.py:819
  19.3 0.8 %collective-permute-done.2 = f32[6,768]{1,0:T(8,128)S(1)} collective-permute-done((f32[6,768]{1,0:T(8,128)S(1)}, f32[6,768]{1,0:T(8,128)S(1)}, u32[]{:S(2)}, u32[]{:S(2)}) %collective-permute-start.2) | collective-permute-done | bytes 18464 | tf_op jit(solution)/shard_map/ppermute | solution.py:819
  20.2 0.6 %collective-permute-start.3 = (f32[6,768]{1,0:T(8,128)S(1)}, f32[6,768]{1,0:T(8,128)S(1)}, u32[]{:S(2)}, u32[]{:S(2)}) collective-permute-start(f32[6,768]{1,0:T(8,128)S(1)} %add.12), channel_id=1, source_target_pairs={{0,2},{1,3},{2,0},{3,1},{4,6},{5,7},{6,4},{7,5},{8,10},{9,11},{10,... | collective-permute-start | bytes 55304 | tf_op jit(solution)/shard_map/ppermute | solution.py:815
  20.7 2.7 %shard_map.112 = (bf16[4,256,768]{2,1,0:T(8,128)(2,1)}, bf16[4,512,768]{2,1,0:T(8,128)(2,1)}) custom-call(s32[1]{0:T(128)} %bitcast.base_ref, s32[4,4]{1,0:T(4,128)S(1)} %copy-done.3, bf16[20,64,256]{2,1,0:T(8,128)(2,1)S(1)} %get-tuple-element.74.mat, f32[4,6,304,128]{3,2,1,0:T(8,128)S(1)} %get-tuple-element.54.g32, ...), custom_call_target="tpu_custom_call" | custom-call | flops 251658240 | bytes 1572864 | tf_op jit(solution)/shard_map/pallas_call | solution.py:727
  23.4 0.6 %collective-permute-done.3 = f32[6,768]{1,0:T(8,128)S(1)} collective-permute-done((f32[6,768]{1,0:T(8,128)S(1)}, f32[6,768]{1,0:T(8,128)S(1)}, u32[]{:S(2)}, u32[]{:S(2)}) %collective-permute-start.3) | collective-permute-done | bytes 18464 | tf_op jit(solution)/shard_map/ppermute | solution.py:815
  24.0 1.5 %collective-permute-start.4 = (f32[6,768]{1,0:T(8,128)S(1)}, f32[6,768]{1,0:T(8,128)S(1)}, u32[]{:S(2)}, u32[]{:S(2)}) collective-permute-start(f32[6,768]{1,0:T(8,128)S(1)} %add.13), channel_id=1, source_target_pairs={{0,4},{4,0},{8,12},{12,8},{16,20},{20,16},{24,28},{28,24},{1,5},{5... | collective-permute-start | bytes 55304 | tf_op jit(solution)/shard_map/ppermute | solution.py:815
  25.5 2.7 %shard_map.113 = (bf16[4,256,768]{2,1,0:T(8,128)(2,1)}, bf16[4,512,768]{2,1,0:T(8,128)(2,1)}) custom-call(s32[1]{0:T(128)} %bitcast.base_ref, s32[4,4]{1,0:T(4,128)S(1)} %copy-done.3, bf16[20,64,256]{2,1,0:T(8,128)(2,1)S(1)} %get-tuple-element.74.mat, f32[4,6,304,128]{3,2,1,0:T(8,128)S(1)} %get-tuple-element.54.g32, ...), custom_call_target="tpu_custom_call", output_to_operand_aliasing={{0}: (6, {}), {1}: (7, {})} | custom-call | flops 251658240 | bytes 1572864 | tf_op jit(solution)/shard_map/pallas_call | solution.py:727
  28.2 0.0 collective-permute-done.4
  28.2 1.6 %collective-permute-start.5 = (f32[6,768]{1,0:T(8,128)S(1)}, f32[6,768]{1,0:T(8,128)S(1)}, u32[]{:S(2)}, u32[]{:S(2)}) collective-permute-start(f32[6,768]{1,0:T(8,128)S(1)} %add.14), channel_id=1, source_target_pairs={{0,8},{4,12},{8,0},{12,4},{16,24},{20,28},{24,16},{28,20},{1,9},{5... | collective-permute-start | bytes 55304 | tf_op jit(solution)/shard_map/ppermute | solution.py:815
  29.9 2.7 %shard_map.114 = (bf16[4,256,768]{2,1,0:T(8,128)(2,1)}, bf16[4,512,768]{2,1,0:T(8,128)(2,1)}) custom-call(s32[1]{0:T(128)} %bitcast.base_ref, s32[4,4]{1,0:T(4,128)S(1)} %copy-done.3, bf16[20,64,256]{2,1,0:T(8,128)(2,1)S(1)} %get-tuple-element.74.mat, f32[4,6,304,128]{3,2,1,0:T(8,128)S(1)} %get-tuple-element.54.g32, ...), custom_call_target="tpu_custom_call", output_to_operand_aliasing={{0}: (6, {}), {1}: (7, {})} | custom-call | flops 251658240 | bytes 1572864 | tf_op jit(solution)/shard_map/pallas_call | solution.py:727
  32.6 0.0 collective-permute-done.5
  32.6 0.0 copy-start.4
  32.6 0.0 copy-start.5
  32.6 2.6 %collective-permute-start.6 = (f32[6,768]{1,0:T(8,128)S(1)}, f32[6,768]{1,0:T(8,128)S(1)}, u32[]{:S(2)}, u32[]{:S(2)}) collective-permute-start(f32[6,768]{1,0:T(8,128)S(1)} %add.15.grad_ref), channel_id=1, source_target_pairs={{0,16},{4,20},{8,24},{12,28},{16,0},{20,4},{24,8},{28,12},{1,17},{... | collective-permute-start | bytes 55304 | tf_op jit(solution)/shard_map/ppermute | solution.py:815
  35.3 2.7 %shard_map.115 = (bf16[4,256,768]{2,1,0:T(8,128)(2,1)}, bf16[4,512,768]{2,1,0:T(8,128)(2,1)}) custom-call(s32[1]{0:T(128)} %bitcast.base_ref, s32[4,4]{1,0:T(4,128)S(1)} %copy-done.3, bf16[20,64,256]{2,1,0:T(8,128)(2,1)S(1)} %get-tuple-element.74.mat, f32[4,6,304,128]{3,2,1,0:T(8,128)S(1)} %get-tuple-element.54.g32, ...), custom_call_target="tpu_custom_call", output_to_operand_aliasing={{0}: (6, {}), {1}: (7, {})} | custom-call | flops 251658240 | bytes 1572864 | tf_op jit(solution)/shard_map/pallas_call | solution.py:727
  38.0 0.0 collective-permute-done.6.other_ref
  38.0 0.0 copy-done.4
  38.0 0.0 copy-done.5
  38.0 0.8 %shard_map.116 = (f32[1,1]{1,0:T(1,128)}, f32[6,768]{1,0:T(8,128)}, f32[6,768]{1,0:T(8,128)}, f32[6,768]{1,0:T(8,128)}) custom-call(f32[6,768]{1,0:T(8,128)S(1)} %add.15.grad_ref, f32[6,768]{1,0:T(8,128)S(1)} %collective-permute-done.6.other_ref, f32[6,768]{1,0:T(8,128)S(1)} %copy-done.2, f32[6,768]{1,0:T(8,128)S(1)} %copy-done.4, f32[6,768]{1,0:T(8,128)S(1)} %copy-done.5), custom_call_target="tpu_custom_call" | custom-call | tf_op jit(solution)/shard_map/pallas_call | solution.py:772
  (4 shorter events, 0.0 us)
Async XLA Ops:
  0.6 2.5 %copy-start = (bf16[4,512,768]{2,1,0:T(8,128)(2,1)S(1)}, bf16[4,512,768]{2,1,0:T(8,128)(2,1)}, u32[]{:S(2)}) copy-start(bf16[4,512,768]{2,1,0:T(8,128)(2,1)} %x_ref.3) | copy-start | bytes 9437188
  0.6 2.5 %copy-start.2 = (f32[6,768]{1,0:T(8,128)S(1)}, f32[6,768]{1,0:T(8,128)}, u32[]{:S(2)}) copy-start(f32[6,768]{1,0:T(8,128)} %par_ref.13) | copy-start | bytes 55300
  0.7 2.5 %copy-start.3 = (s32[4,4]{1,0:T(4,128)S(1)}, s32[4,4]{1,0:T(4,128)}, u32[]{:S(2)}) copy-start(s32[4,4]{1,0:T(4,128)} %len_ref.7) | copy-start | bytes 196
  0.7 6.2 %copy-start.1 = (bf16[4,256,768]{2,1,0:T(8,128)(2,1)S(1)}, bf16[4,256,768]{2,1,0:T(8,128)(2,1)}, u32[]{:S(2)}) copy-start(bf16[4,256,768]{2,1,0:T(8,128)(2,1)} %g_ref.1) | copy-start | bytes 4718596
  2.0 4.8 %collective-permute-start = (bf16[4,16,768]{2,1,0:T(8,128)(2,1)S(1)}, bf16[4,16,768]{2,1,0:T(8,128)(2,1)S(1)}, u32[]{:S(2)}, u32[]{:S(2)}) collective-permute-start(bf16[4,16,768]{2,1,0:T(8,128)(2,1)S(1)} %get-tuple-element.48), channel_id=1, source_target_pairs={{0,1},{2,3},{1,0},{3,2},{4,5},{6,7},{5,4},{7,6},{8,9},{10,11},{9,8... | collective-permute-start | bytes 294920 | tf_op jit(solution)/shard_map/ppermute | solution.py:797
  2.5 4.3 %collective-permute-start.1 = (bf16[4,16,768]{2,1,0:T(8,128)(2,1)S(1)}, bf16[4,16,768]{2,1,0:T(8,128)(2,1)S(1)}, u32[]{:S(2)}, u32[]{:S(2)}) collective-permute-start(bf16[4,16,768]{2,1,0:T(8,128)(2,1)S(1)} %get-tuple-element.49), channel_id=1, source_target_pairs={{1,2},{2,1},{5,6},{6,5},{9,10},{10,9},{13,14},{14,13},{17,18},{18,... | collective-permute-start | bytes 294920 | tf_op jit(solution)/shard_map/ppermute | solution.py:796
  15.2 4.9 %collective-permute-start.2 = (f32[6,768]{1,0:T(8,128)S(1)}, f32[6,768]{1,0:T(8,128)S(1)}, u32[]{:S(2)}, u32[]{:S(2)}) collective-permute-start(f32[6,768]{1,0:T(8,128)S(1)} %get-tuple-element.51), channel_id=1, source_target_pairs={{0,1},{1,0},{2,3},{3,2},{4,5},{5,4},{6,7},{7,6},{8,9},{9,8},{10,11... | collective-permute-start | bytes 55304 | tf_op jit(solution)/shard_map/ppermute | solution.py:819
  20.2 3.8 %collective-permute-start.3 = (f32[6,768]{1,0:T(8,128)S(1)}, f32[6,768]{1,0:T(8,128)S(1)}, u32[]{:S(2)}, u32[]{:S(2)}) collective-permute-start(f32[6,768]{1,0:T(8,128)S(1)} %add.12), channel_id=1, source_target_pairs={{0,2},{1,3},{2,0},{3,1},{4,6},{5,7},{6,4},{7,5},{8,10},{9,11},{10,... | collective-permute-start | bytes 55304 | tf_op jit(solution)/shard_map/ppermute | solution.py:815
  24.0 4.2 %collective-permute-start.4 = (f32[6,768]{1,0:T(8,128)S(1)}, f32[6,768]{1,0:T(8,128)S(1)}, u32[]{:S(2)}, u32[]{:S(2)}) collective-permute-start(f32[6,768]{1,0:T(8,128)S(1)} %add.13), channel_id=1, source_target_pairs={{0,4},{4,0},{8,12},{12,8},{16,20},{20,16},{24,28},{28,24},{1,5},{5... | collective-permute-start | bytes 55304 | tf_op jit(solution)/shard_map/ppermute | solution.py:815
  28.2 4.4 %collective-permute-start.5 = (f32[6,768]{1,0:T(8,128)S(1)}, f32[6,768]{1,0:T(8,128)S(1)}, u32[]{:S(2)}, u32[]{:S(2)}) collective-permute-start(f32[6,768]{1,0:T(8,128)S(1)} %add.14), channel_id=1, source_target_pairs={{0,8},{4,12},{8,0},{12,4},{16,24},{20,28},{24,16},{28,20},{1,9},{5... | collective-permute-start | bytes 55304 | tf_op jit(solution)/shard_map/ppermute | solution.py:815
  32.6 5.4 %copy-start.4 = (f32[6,768]{1,0:T(8,128)S(1)}, f32[6,768]{1,0:T(8,128)}, u32[]{:S(2)}) copy-start(f32[6,768]{1,0:T(8,128)} %first_ref.1) | copy-start | bytes 55300
  32.6 5.4 %copy-start.5 = (f32[6,768]{1,0:T(8,128)S(1)}, f32[6,768]{1,0:T(8,128)}, u32[]{:S(2)}) copy-start(f32[6,768]{1,0:T(8,128)} %second_ref.1) | copy-start | bytes 55300
  32.6 5.3 %collective-permute-start.6 = (f32[6,768]{1,0:T(8,128)S(1)}, f32[6,768]{1,0:T(8,128)S(1)}, u32[]{:S(2)}, u32[]{:S(2)}) collective-permute-start(f32[6,768]{1,0:T(8,128)S(1)} %add.15.grad_ref), channel_id=1, source_target_pairs={{0,16},{4,20},{8,24},{12,28},{16,0},{20,4},{24,8},{28,12},{1,17},{... | collective-permute-start | bytes 55304 | tf_op jit(solution)/shard_map/ppermute | solution.py:815
